TPU v7x, 32 devices: a whole 2x2x4 slice. The times are simulated.
32 devices in a mesh: groups: 2 (over y), tile: 4 (over z), slab: 2 (over x), batch: 2 (over core).
Axes of the slice: x: 2, y: 2, z: 4, core: 2. Of those that a mesh axis runs over, the one named last changes fastest.
Arguments:
- phase_shift: float32 [4, 1024, 4096], P(('groups', 'slab'), 'tile'), parts along dimension 0, may hold values from -1.5 to 1.5
- absorption: float32 [4, 1024, 4096], P(('groups', 'slab'), 'tile'), parts along dimension 0, may hold values from 0.02 to 0.6
- probe_wave: float32 [2, 256, 256], replicated, may hold values from -6 to 6
- measured: float32 [64, 256, 256], P(('groups', 'tile', 'batch')), parts along dimension 0, may hold values from 0 to 3
- offsets: int32 [64, 2], P(('groups', 'tile', 'batch')), parts along dimension 0, may hold values from 0 to 3840, as said below
Outputs:
- object_gradient: float32 [2, 4, 1024, 4096], P(None, ('groups', 'slab'), 'tile'), parts along dimension 1
There are 2 independent parts, one for each index of `groups`. A program takes and returns all parts, laid end to end along the dimension named above; an argument that names none is the same for every part. Nothing has to cross between parts.
Inputs may be any that keep to these rules, and one draw needn't show every extreme that they name: `offsets`: A position's patch covers rows r to r + 255 and columns c to c + 255 of the object and lies inside it. Positions are listed by row block: the 8 positions of block b (positions b * (8) onward) have b * 256 <= r < (b + 1) * 256.
All inputs are finite; a program needn't handle non-finite values.
Results may differ from a plain program's by a relative error of at most 0.0003.
Values sent between devices are 32-bit elements; how exact they have to be, the bound alone decides.
No kernel may reach another device: no remote copies, remote signals or barrier semaphores. Data moves between devices by JAX's collectives and lax.ppermute only.
A program may use at most 128 MiB of HBM per device.

v0:
```python
from functools import partial
import math

import jax
import jax.numpy as jnp
from jax import lax
from jax.sharding import PartitionSpec as P


def from_behind(block, axis, distance):
    devices = range(lax.axis_size(axis))
    route = [(i - distance, i) for i in devices if i - distance in devices]
    return lax.ppermute(block, axis, route)


def complex_dot(left, right):
    product = partial(
        jnp.matmul, precision=lax.Precision.HIGHEST, preferred_element_type=jnp.float32
    )
    real_part = product(left[0], right[0]) - product(left[1], right[1])
    imag_part = product(left[0], right[1]) + product(left[1], right[0])
    return (real_part, imag_part)


def two_sided(matrix, wave):
    inner = complex_dot(matrix, (wave[..., 0, :, :], wave[..., 1, :, :]))
    outer = complex_dot(inner, matrix)
    return jnp.stack(outer, axis=-3)


def tables(patch_side):
    indices = jnp.arange(patch_side, dtype=jnp.int32)
    angles = (
        2.0
        * math.pi
        / patch_side
        * (indices[:, None] * indices[None, :] % patch_side).astype(jnp.float32)
    )
    fourier = (jnp.cos(angles), -jnp.sin(angles))
    conj_fourier = (fourier[0], -fourier[1])
    wavenumber = jnp.where(indices < patch_side // 2, indices, indices - patch_side)
    quadratic = (wavenumber * wavenumber % (8 * patch_side)).astype(jnp.float32)
    kernel_angle = -math.pi / (4.0 * patch_side) * quadratic
    kernel_re = jnp.cos(kernel_angle)[None, :]
    kernel_im = jnp.sin(kernel_angle)[None, :]
    scaled = (
        conj_fourier[0] * kernel_re - conj_fourier[1] * kernel_im,
        conj_fourier[0] * kernel_im + conj_fourier[1] * kernel_re,
    )
    fresnel = complex_dot(scaled, fourier)
    fresnel = (fresnel[0] / patch_side, fresnel[1] / patch_side)
    return (fourier, conj_fourier, fresnel)


def accumulate(buffer, terms, offsets, base_row):
    patch_side = terms.shape[-1]

    def add_one(index, total):
        offset_pair = lax.dynamic_index_in_dim(offsets, index, 0, keepdims=False)
        term = lax.dynamic_index_in_dim(terms, index, 0, keepdims=False)
        starts = (jnp.int32(0), offset_pair[0] - base_row, offset_pair[1])
        current = lax.dynamic_slice(total, starts, (2, patch_side, patch_side))
        return lax.dynamic_update_slice(total, current + term, starts)

    return lax.fori_loop(0, terms.shape[0], add_one, buffer)


def local(phase_shift, absorption, probe_wave, measured, offsets):
    patch_side = probe_wave.shape[-1]
    tile_rows = phase_shift.shape[1]
    slab_cols = phase_shift.shape[2]
    positions = offsets.shape[0]
    sections = lax.axis_size("slab")
    my_section = lax.axis_index("slab")
    base_row = lax.axis_index("tile") * tile_rows
    fourier, conj_fourier, fresnel = tables(patch_side)
    fresnel_back = (fresnel[0], -fresnel[1])
    own_block = jnp.stack([phase_shift, absorption])
    next_block = from_behind(own_block, "tile", -1)
    object_local = jnp.concatenate([own_block, next_block], axis=2)[:, 0]

    def cut_patch(offset_pair):
        starts = (jnp.int32(0), offset_pair[0] - base_row, offset_pair[1])
        return lax.dynamic_slice(object_local, starts, (2, patch_side, patch_side))

    patches = jax.vmap(cut_patch)(offsets)
    damping = jnp.exp(-patches[:, 1])
    transmit = jnp.stack(
        [damping * jnp.cos(patches[:, 0]), damping * jnp.sin(patches[:, 0])], axis=1
    )
    steps_total = positions + sections - 1
    wave_zero = jnp.zeros((2, patch_side, patch_side), jnp.float32)
    batch_zero = jnp.zeros((positions, 2, patch_side, patch_side), jnp.float32)

    def forward_step(step_idx, state):
        carried, stashed, exit_waves = state
        position = step_idx - my_section
        active = (position >= 0) & (position < positions)
        position = jnp.clip(position, 0, positions - 1)
        wave_in = jnp.where(my_section == 0, probe_wave, carried)
        patch_now = lax.dynamic_index_in_dim(transmit, position, 0, keepdims=False)
        products = jnp.stack(
            [
                wave_in[0] * patch_now[0] - wave_in[1] * patch_now[1],
                wave_in[0] * patch_now[1] + wave_in[1] * patch_now[0],
            ]
        )
        leaving = two_sided(fresnel, products)
        stashed = jnp.where(
            active, lax.dynamic_update_index_in_dim(stashed, wave_in, position, 0), stashed
        )
        exit_waves = jnp.where(
            active & (my_section == sections - 1),
            lax.dynamic_update_index_in_dim(exit_waves, leaving, position, 0),
            exit_waves,
        )
        carried = from_behind(leaving, "slab", 1)
        return (carried, stashed, exit_waves)

    unused_wave, stashed, exit_waves = lax.fori_loop(
        0, steps_total, forward_step, (wave_zero, batch_zero, batch_zero)
    )
    far_field = two_sided(fourier, exit_waves) / patch_side
    magnitude = jnp.sqrt(far_field[:, 0] * far_field[:, 0] + far_field[:, 1] * far_field[:, 1])
    factor = 1.0 - measured / jnp.maximum(magnitude, 0.5)
    seed_wave = far_field * factor[:, None]
    seed_back = two_sided(conj_fourier, seed_wave) / patch_side

    def adjoint_step(step_idx, state):
        carried, terms = state
        position = step_idx - (sections - 1 - my_section)
        active = (position >= 0) & (position < positions)
        position = jnp.clip(position, 0, positions - 1)
        start_wave = lax.dynamic_index_in_dim(seed_back, position, 0, keepdims=False)
        arriving = jnp.where(my_section == sections - 1, start_wave, carried)
        back_wave = two_sided(fresnel_back, arriving)
        incoming = lax.dynamic_index_in_dim(stashed, position, 0, keepdims=False)
        patch_now = lax.dynamic_index_in_dim(transmit, position, 0, keepdims=False)
        term = jnp.stack(
            [
                incoming[0] * back_wave[0] + incoming[1] * back_wave[1],
                incoming[0] * back_wave[1] - incoming[1] * back_wave[0],
            ]
        )
        leaving = jnp.stack(
            [
                patch_now[0] * back_wave[0] + patch_now[1] * back_wave[1],
                patch_now[0] * back_wave[1] - patch_now[1] * back_wave[0],
            ]
        )
        terms = jnp.where(active, lax.dynamic_update_index_in_dim(terms, term, position, 0), terms)
        carried = from_behind(leaving, "slab", -1)
        return (carried, terms)

    unused_adjoint, terms = lax.fori_loop(0, steps_total, adjoint_step, (wave_zero, batch_zero))
    buffer = jnp.zeros((2, 2 * tile_rows, slab_cols), jnp.float32)
    gradient = accumulate(buffer, terms, offsets, base_row)[:, None]
    received = from_behind(gradient[:, :, tile_rows:], "tile", 1)
    block_total = gradient[:, :, :tile_rows] + received
    object_gradient = lax.psum(block_total, "batch")
    return object_gradient


def solution(mesh):
    in_specs = (
        P(("groups", "slab"), "tile", None),
        P(("groups", "slab"), "tile", None),
        P(),
        P(("groups", "tile", "batch"), None, None),
        P(("groups", "tile", "batch"), None),
    )
    out_specs = P(None, ("groups", "slab"), "tile", None)
    return jax.shard_map(local, mesh=mesh, in_specs=in_specs, out_specs=out_specs, check_vma=False)
```

profile of v0, /device:TPU:29, one launch (start us, length us, event | category | flops | bytes accessed | tf_op | source)
XLA Modules:
  0.0 764.5 jit_solution(6175115465175073561)
XLA Ops:
  6.5 7.9 %pad_maximum_fusion.2 = f32[2,1,256,4096]{3,2,0,1:T(8,128)} fusion(f32[1,1,256,4096]{3,2,0,1:T(8,128)} %bitcast.324, f32[1,1,256,4096]{3,2,0,1:T(8,128)} %bitcast.326), kind=kLoop, calls=%fused_computation.46 | loop fusion | flops 2097152 | bytes 16777216 | tf_op jit(solution)/shard_map/stack | solution.py:78
  14.4 5.3 collective-permute-start.2
  25.9 170.0 %collective-permute-done.2 = f32[2,1,256,4096]{3,2,0,1:T(8,128)} collective-permute-done((f32[2,1,256,4096]{3,2,0,1:T(8,128)}, f32[2,1,256,4096]{3,2,0,1:T(8,128)}, u32[]{:S(2)}, u32[]{:S(2)}) %collective-permute-start.2) | collective-permute-done | bytes 8388640 | tf_op jit(solution)/shard_map/ppermute | solution.py:13
  195.9 10.8 %maximum_bitcast_fusion.1 = f32[2,512,4096]{2,1,0:T(8,128)} fusion(f32[2,1,256,4096]{3,2,0,1:T(8,128)} %collective-permute-done.2, f32[1,1,256,4096]{3,2,0,1:T(8,128)S(1)} %bitcast.325, f32[1,1,256,4096]{3,2,0,1:T(8,128)S(1)} %bitcast.327), kind=kLoop, calls=%fused_computation.44 | loop fusion | flops 8388608 | bytes 33554432 | tf_op jit(solution)/shard_map/squeeze | solution.py:80
  206.8 13.0 %while.52 = (s32[]{:T(128)}, f32[2,512,4096]{2,1,0:T(8,128)}, s32[4,3]{1,0:T(4,128)S(1)}, f32[4,2,256,256]{3,2,1,0:T(8,128)S(1)}, s32[]{:T(128)}) while((s32[]{:T(128)}, f32[2,512,4096]{2,1,0:T(8,128)}, s32[4,3]{1,0:T(4,128)S(1)}, f32[4,2,256,256]{3,2,1,0:T(8,128)S(1)}, s32[]{:T(128)}) %tuple.120), condition=%wide.while_cond, body=%wide.while_body.sunk | while | flops 2 | bytes 1048701 | solution.py:84
  207.5 2.6 bitcast_dynamic-update-slice_fusion.5
  210.7 2.6 bitcast_dynamic-update-slice_fusion.5
  214.0 2.6 bitcast_dynamic-update-slice_fusion.5
  217.3 2.6 bitcast_dynamic-update-slice_fusion.5
  219.9 3.8 cosine_multiply_fusion
  227.7 105.2 %while.49 = (s32[]{:T(128)}, f32[2,256,256]{2,1,0:T(8,128)}, f32[4,2,256,256]{3,2,1,0:T(8,128)}, f32[4,2,256,256]{3,2,0,1:T(8,128)S(1)}, pred[]{:T(512)}, /*inde...) while((s32[]{:T(128)}, f32[2,256,256]{2,1,0:T(8,128)}, ...), condition=%wide.region_1.2_spmd, body=%wide.region_0.1_spmd.sunk | while | flops 1611923456 | bytes 17302300 | solution.py:120
  227.8 2.1 fusion.296
  236.7 3.9 collective-permute-start
  240.7 9.1 %collective-permute-done = f32[2,256,256]{2,1,0:T(8,128)} collective-permute-done((f32[2,256,256]{2,1,0:T(8,128)}, f32[2,256,256]{2,1,0:T(8,128)}, u32[]{:S(2)}, u32[]{:S(2)}) %collective-permute-start) | collective-permute-done | bytes 524320 | tf_op jit(solution)/shard_map/while/body/eval_jaxpr/ppermute | solution.py:13
  249.8 2.1 fusion.296
  258.7 4.9 collective-permute-start
  263.7 8.1 %collective-permute-done = f32[2,256,256]{2,1,0:T(8,128)} collective-permute-done((f32[2,256,256]{2,1,0:T(8,128)}, f32[2,256,256]{2,1,0:T(8,128)}, u32[]{:S(2)}, u32[]{:S(2)}) %collective-permute-start) | collective-permute-done | bytes 524320 | tf_op jit(solution)/shard_map/while/body/eval_jaxpr/ppermute | solution.py:13
  271.8 2.1 fusion.296
  280.7 4.9 collective-permute-start
  285.7 7.2 collective-permute-done
  293.0 2.1 fusion.296
  301.9 4.9 collective-permute-start
  306.9 6.3 collective-permute-done
  313.2 2.1 fusion.296
  322.1 4.9 collective-permute-start
  327.1 5.5 collective-permute-done
  337.0 2.0 fusion.16
  343.1 2.2 fusion.15
  355.3 2.0 fusion.12
  357.3 2.2 fusion.41
  361.5 2.0 fusion.11
  370.5 86.2 %while.50 = (s32[]{:T(128)}, f32[2,256,256]{2,1,0:T(8,128)S(1)}, f32[4,2,256,256]{3,2,1,0:T(8,128)}, s32[]{:T(128)}, f32[4,2,256,256]{3,2,1,0:T(8,128)}, /*index...) while((s32[]{:T(128)}, f32[2,256,256]{2,1,0:T(8,128)S(1)}, ...), condition=%wide.region_3.4_spmd, body=%wide.region_2.3_spmd.sunk | while | flops 1612185600 | bytes 15728908 | solution.py:155
  381.2 6.7 collective-permute-done.1
  398.4 6.7 collective-permute-done.1
  415.6 6.7 collective-permute-done.1
  432.8 6.7 collective-permute-done.1
  450.0 6.7 collective-permute-done.1
  456.7 7.8 %broadcast_in_dim.45 = f32[2,512,4096]{2,1,0:T(8,128)} broadcast(f32[]{:T(128)} %constant.189.clone.1), dimensions={} | broadcast | bytes 16777220 | tf_op jit(solution)/shard_map/broadcast_in_dim | solution.py:156
  464.6 45.6 %while.51 = (s32[]{:T(128)}, f32[2,512,4096]{2,1,0:T(8,128)}, s32[4,2]{0,1:T(2,128)S(1)}, s32[]{:T(128)}, f32[4,2,256,256]{3,2,1,0:T(8,128)}, /*index=5*/s32[]{:T(128)}, s32[]{:T(128)}, s32[]{:T(128)}, s32[]{:T(128)}) while((s32[]{:T(128)}, f32[2,512,4096]{2,1,0:T(8,128)}, s32[4,2]{0,1:T(2,128)S(1)}, s32[]{:T(128)}, ...), condition=%wide.region_5.6_spmd, body=%wide.region_4.5_spmd.sunk | while | flops 131081 | bytes 2621673 | solution.py:65
  469.2 6.8 dynamic_update_slice.18
  480.6 6.8 dynamic_update_slice.18
  492.0 6.8 dynamic_update_slice.18
  503.5 6.7 dynamic_update_slice.18
  510.2 3.9 slice.191
  515.4 170.7 %collective-permute-done.3 = f32[2,1,256,4096]{3,2,1,0:T(8,128)} collective-permute-done((f32[2,1,256,4096]{3,2,1,0:T(8,128)S(1)}, f32[2,1,256,4096]{3,2,1,0:T(8,128)}, u32[]{:S(2)}, u32[]{:S(2)}) %collective-permute-start.3) | collective-permute-done | bytes 8388640 | tf_op jit(solution)/shard_map/ppermute | solution.py:13
  686.1 11.3 %slice_add_fusion = f32[2,1,256,4096]{3,2,1,0:T(8,128)} fusion(f32[2,1,256,4096]{3,2,1,0:T(8,128)} %collective-permute-done.3, f32[2,1,512,4096]{3,2,1,0:T(8,128)} %bitcast.323), kind=kLoop, calls=%fused_computation.45 | loop fusion | flops 2097152 | bytes 25165824 | tf_op jit(solution)/shard_map/add | solution.py:159
  697.4 52.0 %all-reduce.2.cloned.1.call-done = f32[2,1,256,4096]{3,2,1,0:T(8,128)} async-done(((f32[2,1,256,4096]{3,2,1,0:T(8,128)}), f32[2,1,256,4096]{3,2,1,0:T(8,128)}) %all-reduce.2.cloned.1.call-update) | async-done | bytes 8388624 | tf_op jit(solution)/shard_map/psum | solution.py:160
  749.5 7.8 %copy.56 = f32[2,1,256,4096]{3,2,1,0:T(8,128)} copy(f32[2,1,256,4096]{3,2,1,0:T(8,128)} %all-reduce.2.cloned.1.call-done) | data formatting | bytes 16777216
  (184 shorter events, 135.6 us)
Async XLA Ops:
  6.5 742.9 %all-reduce.2.cloned.1.call-start = ((), (), s32[]{:S(2)}) async-start(), calls=%async_computation | async-start | bytes 16777216 | tf_op jit(solution)/shard_map/psum | solution.py:160
  6.5 13.2 %copy-start.3 = (s32[4,2]{0,1:T(2,128)S(1)}, s32[4,2]{0,1:T(2,128)}, u32[]{:S(2)}) copy-start(s32[4,2]{0,1:T(2,128)} %param.15) | copy-start | bytes 100
  14.4 181.5 %collective-permute-start.2 = (f32[2,1,256,4096]{3,2,0,1:T(8,128)}, f32[2,1,256,4096]{3,2,0,1:T(8,128)}, u32[]{:S(2)}, u32[]{:S(2)}) collective-permute-start(f32[2,1,256,4096]{3,2,0,1:T(8,128)} %pad_maximum_fusion.2), channel_id=1, source_target_pairs={{4,0},{8,4},{12,8},{5,1},{9,5},{13,9},{6,2},{10,6},{14,10},{7,3},{... | collective-permute-start | bytes 25165832 | tf_op jit(solution)/shard_map/ppermute | solution.py:13
  20.1 175.8 %copy-start.1 = (f32[1,256,4096]{2,1,0:T(8,128)S(1)}, f32[1,256,4096]{2,1,0:T(8,128)}, u32[]{:S(2)}) copy-start(f32[1,256,4096]{2,1,0:T(8,128)} %param.11) | copy-start | bytes 12582916
  23.0 172.9 %copy-start = (f32[1,256,4096]{2,1,0:T(8,128)S(1)}, f32[1,256,4096]{2,1,0:T(8,128)}, u32[]{:S(2)}) copy-start(f32[1,256,4096]{2,1,0:T(8,128)} %param.12) | copy-start | bytes 12582916
  236.7 13.1 %collective-permute-start = (f32[2,256,256]{2,1,0:T(8,128)}, f32[2,256,256]{2,1,0:T(8,128)}, u32[]{:S(2)}, u32[]{:S(2)}) collective-permute-start(f32[2,256,256]{2,1,0:T(8,128)} %pad_maximum_fusion.7), channel_id=1, source_target_pairs={{0,2},{1,3},{4,6},{5,7},{8,10},{9,11},{12,14},{13,15},{16,18},{17,... | collective-permute-start | bytes 1572872 | tf_op jit(solution)/shard_map/while/body/eval_jaxpr/ppermute | solution.py:13
  258.7 13.2 %collective-permute-start = (f32[2,256,256]{2,1,0:T(8,128)}, f32[2,256,256]{2,1,0:T(8,128)}, u32[]{:S(2)}, u32[]{:S(2)}) collective-permute-start(f32[2,256,256]{2,1,0:T(8,128)} %pad_maximum_fusion.7), channel_id=1, source_target_pairs={{0,2},{1,3},{4,6},{5,7},{8,10},{9,11},{12,14},{13,15},{16,18},{17,... | collective-permute-start | bytes 1572872 | tf_op jit(solution)/shard_map/while/body/eval_jaxpr/ppermute | solution.py:13
  280.7 12.2 %collective-permute-start = (f32[2,256,256]{2,1,0:T(8,128)}, f32[2,256,256]{2,1,0:T(8,128)}, u32[]{:S(2)}, u32[]{:S(2)}) collective-permute-start(f32[2,256,256]{2,1,0:T(8,128)} %pad_maximum_fusion.7), channel_id=1, source_target_pairs={{0,2},{1,3},{4,6},{5,7},{8,10},{9,11},{12,14},{13,15},{16,18},{17,... | collective-permute-start | bytes 1572872 | tf_op jit(solution)/shard_map/while/body/eval_jaxpr/ppermute | solution.py:13
  301.9 11.3 %collective-permute-start = (f32[2,256,256]{2,1,0:T(8,128)}, f32[2,256,256]{2,1,0:T(8,128)}, u32[]{:S(2)}, u32[]{:S(2)}) collective-permute-start(f32[2,256,256]{2,1,0:T(8,128)} %pad_maximum_fusion.7), channel_id=1, source_target_pairs={{0,2},{1,3},{4,6},{5,7},{8,10},{9,11},{12,14},{13,15},{16,18},{17,... | collective-permute-start | bytes 1572872 | tf_op jit(solution)/shard_map/while/body/eval_jaxpr/ppermute | solution.py:13
  322.1 10.5 %collective-permute-start = (f32[2,256,256]{2,1,0:T(8,128)}, f32[2,256,256]{2,1,0:T(8,128)}, u32[]{:S(2)}, u32[]{:S(2)}) collective-permute-start(f32[2,256,256]{2,1,0:T(8,128)} %pad_maximum_fusion.7), channel_id=1, source_target_pairs={{0,2},{1,3},{4,6},{5,7},{8,10},{9,11},{12,14},{13,15},{16,18},{17,... | collective-permute-start | bytes 1572872 | tf_op jit(solution)/shard_map/while/body/eval_jaxpr/ppermute | solution.py:13
  349.3 1.2 copy-start.2
  378.0 9.9 %collective-permute-start.1 = (f32[2,256,256]{2,1,0:T(8,128)S(1)}, f32[2,256,256]{2,1,0:T(8,128)S(1)}, u32[]{:S(2)}, u32[]{:S(2)}) collective-permute-start(f32[2,256,256]{2,1,0:T(8,128)S(1)} %pad_maximum_fusion.8), channel_id=1, source_target_pairs={{2,0},{3,1},{6,4},{7,5},{10,8},{11,9},{14,12},{15,13},{18,16},{19,... | collective-permute-start | bytes 1572872 | tf_op jit(solution)/shard_map/while/body/eval_jaxpr/ppermute | solution.py:13
  395.2 9.9 %collective-permute-start.1 = (f32[2,256,256]{2,1,0:T(8,128)S(1)}, f32[2,256,256]{2,1,0:T(8,128)S(1)}, u32[]{:S(2)}, u32[]{:S(2)}) collective-permute-start(f32[2,256,256]{2,1,0:T(8,128)S(1)} %pad_maximum_fusion.8), channel_id=1, source_target_pairs={{2,0},{3,1},{6,4},{7,5},{10,8},{11,9},{14,12},{15,13},{18,16},{19,... | collective-permute-start | bytes 1572872 | tf_op jit(solution)/shard_map/while/body/eval_jaxpr/ppermute | solution.py:13
  412.4 9.9 %collective-permute-start.1 = (f32[2,256,256]{2,1,0:T(8,128)S(1)}, f32[2,256,256]{2,1,0:T(8,128)S(1)}, u32[]{:S(2)}, u32[]{:S(2)}) collective-permute-start(f32[2,256,256]{2,1,0:T(8,128)S(1)} %pad_maximum_fusion.8), channel_id=1, source_target_pairs={{2,0},{3,1},{6,4},{7,5},{10,8},{11,9},{14,12},{15,13},{18,16},{19,... | collective-permute-start | bytes 1572872 | tf_op jit(solution)/shard_map/while/body/eval_jaxpr/ppermute | solution.py:13
  429.6 9.9 %collective-permute-start.1 = (f32[2,256,256]{2,1,0:T(8,128)S(1)}, f32[2,256,256]{2,1,0:T(8,128)S(1)}, u32[]{:S(2)}, u32[]{:S(2)}) collective-permute-start(f32[2,256,256]{2,1,0:T(8,128)S(1)} %pad_maximum_fusion.8), channel_id=1, source_target_pairs={{2,0},{3,1},{6,4},{7,5},{10,8},{11,9},{14,12},{15,13},{18,16},{19,... | collective-permute-start | bytes 1572872 | tf_op jit(solution)/shard_map/while/body/eval_jaxpr/ppermute | solution.py:13
  446.8 9.9 %collective-permute-start.1 = (f32[2,256,256]{2,1,0:T(8,128)S(1)}, f32[2,256,256]{2,1,0:T(8,128)S(1)}, u32[]{:S(2)}, u32[]{:S(2)}) collective-permute-start(f32[2,256,256]{2,1,0:T(8,128)S(1)} %pad_maximum_fusion.8), channel_id=1, source_target_pairs={{2,0},{3,1},{6,4},{7,5},{10,8},{11,9},{14,12},{15,13},{18,16},{19,... | collective-permute-start | bytes 1572872 | tf_op jit(solution)/shard_map/while/body/eval_jaxpr/ppermute | solution.py:13
  514.1 172.0 %collective-permute-start.3 = (f32[2,1,256,4096]{3,2,1,0:T(8,128)S(1)}, f32[2,1,256,4096]{3,2,1,0:T(8,128)}, u32[]{:S(2)}, u32[]{:S(2)}) collective-permute-start(f32[2,1,256,4096]{3,2,1,0:T(8,128)S(1)} %slice.191), channel_id=1, source_target_pairs={{0,4},{4,8},{8,12},{1,5},{5,9},{9,13},{2,6},{6,10},{10,14},{3,7},{... | collective-permute-start | bytes 25165832 | tf_op jit(solution)/shard_map/ppermute | solution.py:13
Sparse Core Ops, SparseCore 0:
  697.5 51.8 all-reduce.1
where the time goes:
time: 773 us; the launch traced here: 765 us
  waiting for transfers between devices  462 us (60%)
  matrix products  92.5 us (12%)
  other arithmetic  79.7 us (10%)
  local copies, waits for them, and re-layouts  67.6 us (9%)
  starting transfers between devices  36.5 us (5%)
  between operations  14.1 us (2%)
  loops' own time  11.7 us (2%)
    ppermute x12, waiting for transfers between devices, from_behind(): return lax.ppermute(block, axis, route)  410 us
    psum x1, waiting for transfers between devices, local(): object_gradient = lax.psum(block_total, 'batch')  52 us
    dot_general x50, matrix products, complex_dot(): real_part = product(left[0], right[0]) - product(left[1], right[1])  49.2 us
    dot_general x50, matrix products, complex_dot(): imag_part = product(left[0], right[1]) + product(left[1], right[0])  43.2 us
    ppermute x12, starting transfers between devices, from_behind(): return lax.ppermute(block, axis, route)  36.5 us
    dynamic_update_slice x4, local copies, waits for them, and re-layouts, add_one(): return lax.dynamic_update_slice(total, current + term, starts)  27 us
  transfers between devices with their start and end apart: 13, of which 13 were waited for; matrix products, arithmetic and copies ran while one was open for 2% of the time, Pallas kernels for 0%

commit v1 on v0

v1 whole, which is shorter than its diff:
```python
import math

import numpy as np
import jax
import jax.numpy as jnp
from jax import lax
from jax.experimental import pallas as pl
from jax.experimental.pallas import tpu as pltpu
from jax.sharding import PartitionSpec as P

SIN = [(-1.0) ** k / math.factorial(2 * k + 1) for k in range(8)]
COS = [(-1.0) ** k / math.factorial(2 * k) for k in range(8)]


def move(block, axis, distance):
    size = lax.axis_size(axis)
    route = [(i, i + distance) for i in range(size) if 0 <= i + distance < size]
    return lax.ppermute(block, axis, route)


def rotate(block, axis, distance):
    size = lax.axis_size(axis)
    return lax.ppermute(block, axis, [(i, (i + distance) % size) for i in range(size)])


def halves(matrix):
    high = matrix.astype(np.float32).astype(jnp.bfloat16)
    low = (matrix - high.astype(np.float64)).astype(np.float32).astype(jnp.bfloat16)
    return high, low


def right_table(matrix):
    real, imag = halves(matrix.real), halves(matrix.imag)
    minus = halves(-matrix.imag)
    order = lambda pair: [pair[0], pair[1], pair[0]]
    first = np.concatenate(order(real) + order(minus), axis=0)
    second = np.concatenate(order(imag) + order(real), axis=0)
    return np.concatenate([first, second], axis=1)


def left_table(matrix):
    return np.ascontiguousarray(right_table(matrix.T).T)


def tables(side):
    index = np.arange(side)
    fourier = np.exp(-2j * np.pi * (index[:, None] * index[None, :] % side) / side)
    wavenumber = np.where(index < side // 2, index, index - side)
    kernel = np.exp(-1j * np.pi * (wavenumber * wavenumber % (8 * side)) / (4 * side))
    fresnel = (fourier.conj() * kernel[None, :]) @ fourier / side
    scaled = fourier / math.sqrt(side)
    out = []
    for matrix in (fresnel, fresnel.conj(), scaled, scaled.conj()):
        out += [left_table(matrix), right_table(matrix)]
    return out


def split(value):
    high = value.astype(jnp.bfloat16)
    low = (value - high.astype(jnp.float32)).astype(jnp.bfloat16)
    return high, low


def two_sided(left, right, real, imag):
    side = real.shape[-1]
    real_high, real_low = split(real)
    imag_high, imag_low = split(imag)
    wide = jnp.concatenate([real_high, real_high, real_low, imag_high, imag_high, imag_low], axis=1)
    inner = jnp.dot(wide, right[...], preferred_element_type=jnp.float32)
    real_high, real_low = split(inner[:, :side])
    imag_high, imag_low = split(inner[:, side:])
    tall = jnp.concatenate([real_high, real_high, real_low, imag_high, imag_high, imag_low], axis=0)
    outer = jnp.dot(left[...], tall, preferred_element_type=jnp.float32)
    return outer[:side], outer[side:]


def transmission(phase, absorption):
    square = phase * phase
    sine = jnp.full_like(phase, SIN[-1])
    cosine = jnp.full_like(phase, COS[-1])
    for a, b in zip(SIN[-2::-1], COS[-2::-1]):
        sine = sine * square + a
        cosine = cosine * square + b
    damping = jnp.exp(-absorption)
    return damping * cosine, damping * sine * phase


def slot_kernel(sections, scalars, probe, measured, *refs):
    patches = refs[:sections]
    tables_in = refs[sections : sections + 8]
    outs = refs[sections + 8 : 2 * sections + 8]
    wave, trans = refs[2 * sections + 8 :]
    slab, row, col = scalars[0], scalars[1], scalars[2]
    forward_left, forward_right, adjoint_left, adjoint_right = tables_in[:4]
    fourier_left, fourier_right, inverse_left, inverse_right = tables_in[4:]
    for distance in range(sections):
        owner = lax.rem(slab + (sections - distance), sections)
        real, imag = transmission(patches[distance][0], patches[distance][1])
        trans[owner, 0] = real
        trans[owner, 1] = imag
    for part in range(2):
        wave[0, part] = pltpu.roll(pltpu.roll(probe[part], row, 0), col, 1)
    for step in range(sections):
        a, b, c, d = wave[step, 0], wave[step, 1], trans[step, 0], trans[step, 1]
        real, imag = a * c - b * d, a * d + b * c
        if step < sections - 1:
            real, imag = two_sided(forward_left, forward_right, real, imag)
            wave[step + 1, 0] = real
            wave[step + 1, 1] = imag
    real, imag = two_sided(fourier_left, fourier_right, real, imag)
    factor = 1.0 - measured[0] * lax.rsqrt(jnp.maximum(real * real + imag * imag, 0.25))
    real, imag = two_sided(inverse_left, inverse_right, real * factor, imag * factor)
    for step in range(sections - 1, -1, -1):
        a, b = wave[step, 0], wave[step, 1]
        wave[step, 0] = a * real + b * imag
        wave[step, 1] = a * imag - b * real
        if step > 0:
            c, d = trans[step, 0], trans[step, 1]
            real, imag = c * real + d * imag, c * imag - d * real
            real, imag = two_sided(adjoint_left, adjoint_right, real, imag)
    for distance in range(sections):
        outs[distance][...] = wave[lax.rem(slab + distance, sections)]


def run_slot(scalars, probe, measured, index, patches, constants):
    sections = len(patches)
    side = probe.shape[-1]
    whole = pl.BlockSpec(memory_space=pltpu.VMEM)
    shape = jax.ShapeDtypeStruct((2, side, side), jnp.float32)
    return pl.pallas_call(
        lambda scalars, *refs: slot_kernel(sections, scalars, *refs),
        grid_spec=pltpu.PrefetchScalarGridSpec(
            num_scalar_prefetch=1,
            grid=(1,),
            in_specs=[whole, pl.BlockSpec((1, side, side), lambda i, s: (s[3], 0, 0))]
            + [whole] * (sections + 8),
            out_specs=[whole] * sections,
            scratch_shapes=[pltpu.VMEM((sections, 2, side, side), jnp.float32)] * 2,
        ),
        out_shape=[shape] * sections,
        compiler_params=pltpu.CompilerParams(vmem_limit_bytes=50 << 20),
    )(jnp.concatenate([scalars, index[None]]), probe, measured, *patches, *constants)


def cut_kernel(count, side, scalars, phase, absorption, *refs):
    outs = refs[:count]
    buffer, sems = refs[count:]
    copies = []
    for k in range(count):
        for which, source in enumerate((phase, absorption)):
            for half in range(2):
                start = pl.multiple_of(scalars[3 * k + half] * side, side)
                copies.append(
                    pltpu.make_async_copy(
                        source.at[0, :, pl.ds(start, side)],
                        buffer.at[k, which, half],
                        sems.at[k, which, half],
                    )
                )
    for copy in copies:
        copy.start()
    lane = lax.broadcasted_iota(jnp.int32, (side, side), 1)
    for k in range(count):
        own = lane >= scalars[3 * k + 2]
        for which in range(2):
            for half in range(2):
                copies[4 * k + 2 * which + half].wait()
            outs[k][which] = jnp.where(own, buffer[k, which, 0], buffer[k, which, 1])


def cut(cols, phase, absorption, side):
    count = cols.shape[0]
    blocks = phase.shape[-1] // side
    first = cols // side
    scalars = jnp.stack([first, jnp.minimum(first + 1, blocks - 1), cols % side], axis=1)
    shape = jax.ShapeDtypeStruct((2, side, side), jnp.float32)
    return pl.pallas_call(
        lambda *refs: cut_kernel(count, side, *refs),
        in_specs=[
            pl.BlockSpec(memory_space=pltpu.SMEM),
            pl.BlockSpec(memory_space=pl.ANY),
            pl.BlockSpec(memory_space=pl.ANY),
        ],
        out_specs=[pl.BlockSpec(memory_space=pltpu.VMEM)] * count,
        out_shape=[shape] * count,
        scratch_shapes=[
            pltpu.VMEM((count, 2, 2, side, side), jnp.float32),
            pltpu.SemaphoreType.DMA((count, 2, 2)),
        ],
        compiler_params=pltpu.CompilerParams(vmem_limit_bytes=50 << 20),
    )(scalars.reshape(-1), phase, absorption)


def gather_kernel(count, side, blocks, scalars, *refs):
    terms, out = refs[:count], refs[count]
    block = pl.program_id(0)
    out[...] = jnp.zeros_like(out)
    rows = lax.broadcasted_iota(jnp.int32, (side, side), 0)
    lane = lax.broadcasted_iota(jnp.int32, (side, side), 1)
    for k in range(count):
        first, col = scalars[4 * k], scalars[4 * k + 1]
        low, high = scalars[4 * k + 2], scalars[4 * k + 3]
        for half in range(2):

            @pl.when((first + half == block) & (high > low))
            def _():
                keep = (rows >= low) & (rows < high)
                keep = keep & ((lane < col) if half else (lane >= col))
                for part in range(2):
                    out[part, 0] += jnp.where(keep, terms[k][part], 0.0)


def gather_terms(terms, scalars, cols_total):
    count = len(terms)
    side = terms[0].shape[-1]
    blocks = cols_total // side
    return pl.pallas_call(
        lambda *refs: gather_kernel(count, side, blocks, *refs),
        grid_spec=pltpu.PrefetchScalarGridSpec(
            num_scalar_prefetch=1,
            grid=(blocks,),
            in_specs=[pl.BlockSpec(memory_space=pltpu.VMEM)] * count,
            out_specs=pl.BlockSpec((2, 1, side, side), lambda i, s: (0, 0, 0, i)),
        ),
        out_shape=jax.ShapeDtypeStruct((2, 1, side, cols_total), jnp.float32),
        compiler_params=pltpu.CompilerParams(vmem_limit_bytes=50 << 20),
    )(scalars.reshape(-1), *terms)


def local(phase, absorption, probe, measured, offsets):
    side = probe.shape[-1]
    cols_total = phase.shape[2]
    sections = lax.axis_size("slab")
    slab = lax.axis_index("slab")
    tile = lax.axis_index("tile")
    last = tile == lax.axis_size("tile") - 1
    each = offsets.shape[0] // sections
    n_up = each // 2
    n_here = each - n_up
    constants = [jnp.asarray(table) for table in tables(side)]

    below = move(offsets, "tile", 1)

    def here_index(k, owner):
        return owner * n_here + k

    def up_index(k, owner):
        return sections * n_here + owner * n_up + k

    def peer(distance):
        return (slab + distance) % sections

    def shifts(pair):
        return pair[0] % side, pair[1] % side

    def pick(table, index):
        return lax.dynamic_index_in_dim(table, index, 0, keepdims=False)

    distances = list(range(sections))
    here_ids = [[here_index(k, peer(d)) for d in distances] for k in range(n_here)]
    up_ids = [[up_index(k, peer(d)) for d in distances] for k in range(n_up)]
    flat = lambda lists: [i for row in lists for i in row]
    own_ids = flat(here_ids) + flat(up_ids)
    own_pairs = offsets[jnp.stack(own_ids)]
    low_pairs = below[jnp.stack(own_ids)]
    own_cut = cut(own_pairs[:, 1], phase, absorption, side)
    low_cut = cut(low_pairs[:, 1], phase, absorption, side)
    rows = lax.broadcasted_iota(jnp.int32, (1, side, 1), 1)

    def exchange(items):
        return [items[0]] + [rotate(items[d], "slab", d) for d in distances[1:]]

    terms, spans = [], []

    def add(term, pair, low, high):
        terms.append(term)
        spans.append(jnp.stack([pair[1] // side, pair[1] % side, low, high]))

    full = jnp.int32(side)
    none = jnp.int32(0)

    def slot(patches, pair, measured_in, index):
        row, col = shifts(pair)
        got = exchange(patches)
        outs = run_slot(jnp.stack([slab, row, col]), probe, measured_in, index, got, constants)
        return exchange(outs)

    for k in range(n_here):
        patches = []
        for d in distances:
            position = k * sections + d
            upper = move(low_cut[position], "tile", -1)
            row = own_pairs[position, 0] % side
            patches.append(jnp.where(rows >= row, own_cut[position], upper))
        done = slot(patches, own_pairs[k * sections], measured, here_ids[k][0])
        for d in distances:
            position = k * sections + (sections - d) % sections
            row = own_pairs[position, 0] % side
            add(done[d], own_pairs[position], row, full)
            low_row = low_pairs[position, 0] % side
            add(move(done[d], "tile", 1), low_pairs[position], none, low_row)
    for k in range(n_up):
        patches = []
        base = n_here * sections + k * sections
        for d in distances:
            lower = move(own_cut[base + d], "tile", 1)
            row = low_pairs[base + d, 0] % side
            patches.append(jnp.where(rows >= row, lower, low_cut[base + d]))
        sent = move(pick(measured, up_ids[k][0]), "tile", 1)
        done = slot(patches, low_pairs[base], sent[None], none)
        for d in distances:
            position = base + (sections - d) % sections
            add(done[d], low_pairs[position], none, low_pairs[position, 0] % side)
            row = jnp.where(last, full, own_pairs[position, 0] % side)
            add(move(done[d], "tile", -1), own_pairs[position], row, full)
        done = slot([own_cut[base + d] for d in distances], own_pairs[base], measured, up_ids[k][0])
        for d in distances:
            position = base + (sections - d) % sections
            row = jnp.where(last, own_pairs[position, 0] % side, full)
            add(done[d], own_pairs[position], row, full)

    spans = jnp.stack(spans)
    other_spans = rotate(spans, "batch", 1)
    other_terms = [rotate(term, "batch", 1) for term in terms]
    return gather_terms(terms + other_terms, jnp.concatenate([spans, other_spans]), cols_total)


def solution(mesh):
    in_specs = (
        P(("groups", "slab"), "tile", None),
        P(("groups", "slab"), "tile", None),
        P(),
        P(("groups", "tile", "batch"), None, None),
        P(("groups", "tile", "batch"), None),
    )
    out_specs = P(None, ("groups", "slab"), "tile", None)
    return jax.shard_map(local, mesh=mesh, in_specs=in_specs, out_specs=out_specs, check_vma=False)
```

time: 773 us -> 185 us (0.24)
  waiting for transfers between devices: 462 us -> 26.5 us
  matrix products: 92.5 us -> 0 us
  other arithmetic: 79.7 us -> 6.25 us
  local copies, waits for them, and re-layouts: 67.6 us -> 9.95 us
  Pallas kernels: 0 us -> 55.8 us
  between operations: 14.1 us -> 36.2 us
  starting transfers between devices: 36.5 us -> 49 us
  loops' own time: 11.7 us -> 0 us
    ppermute x12 -> x27, waiting for transfers between devices: 410 us -> 26.5 us  [the longest x10 22.2 us: move(): return lax.ppermute(block, axis, route)]
    dot_general x100 -> x0, matrix products: 92.5 us -> none  [the longest x50 49.2 us: complex_dot(): real_part = product(left[0], right[0]) - product(left[1], right[1])]
    pallas_call x0 -> x6, Pallas kernels: none -> 55.8 us  [the longest x3 34.3 us: run_slot(): pl.pallas_call(lambda scalars, *refs: slot_kernel(sections, scalars, *ref...]
    psum x1 -> x0, waiting for transfers between devices: 52 us -> none  [local(): object_gradient = lax.psum(block_total, 'batch')]
    dynamic_update_slice x4 -> x0, local copies, waits for them, and re-layouts: 27 us -> none  [add_one(): return lax.dynamic_update_slice(total, current + term, starts)]
    add x10 -> x0, other arithmetic: 22.9 us -> none  [the longest x1 11.3 us: local(): block_total = gradient[:, :, :tile_rows] + received]
    select_n x21 -> x7, other arithmetic: 26.1 us -> 5.05 us  [the longest x2 2.39 us: local(): patches.append(jnp.where(rows >= row, lower, low_cut[base + d]))]
    another operation x12 -> x10, other arithmetic: 13.7 us -> 0.77 us  [the longest x7 0.54 us: local(): spans = jnp.stack(spans)]
  transfers between devices with their start and end apart: 13 -> 27, of which waited for: 13 -> 6; matrix products, arithmetic and copies ran while one was open for 2% -> 6% of each run, Pallas kernels for 0% -> 23%
where the time goes in v1:
time: 185 us; the launch traced here: 184 us
  Pallas kernels  55.8 us (30%)
  starting transfers between devices  49 us (26%)
  between operations  36.2 us (20%)
  waiting for transfers between devices  26.5 us (14%)
  local copies, waits for them, and re-layouts  9.95 us (5%)
  other arithmetic  6.25 us (3%)
    pallas_call x3, Pallas kernels, run_slot(): pl.pallas_call(lambda scalars, *refs: slot_kernel(sections, scalars, *ref...  34.3 us
    ppermute x10, starting transfers between devices, move(): return lax.ppermute(block, axis, route)  26.7 us
    ppermute x17, starting transfers between devices, rotate(): lax.ppermute(block, axis, [(i, (i + distance) % size) for i in range(size)])  22.3 us
    ppermute x10, waiting for transfers between devices, move(): return lax.ppermute(block, axis, route)  22.2 us
    pallas_call x1, Pallas kernels, gather_terms(): pl.pallas_call(lambda *refs: gather_kernel(count, side, blocks, *refs), g...  14.1 us
    pallas_call x2, Pallas kernels, cut(): pl.pallas_call(lambda *refs: cut_kernel(count, side, *refs), in_specs=[pl...  7.44 us
    unnamed x41, local copies, waits for them, and re-layouts  5.85 us
    ppermute x17, waiting for transfers between devices, rotate(): lax.ppermute(block, axis, [(i, (i + distance) % size) for i in range(size)])  4.35 us
  transfers between devices with their start and end apart: 27, of which 6 were waited for; matrix products, arithmetic and copies ran while one was open for 6% of the time, Pallas kernels for 23%

profile of v1, /device:TPU:29, one launch (start us, length us, event | category | flops | bytes accessed | tf_op | source)
XLA Modules:
  0.0 183.8 jit_solution(4121024148804896421)
XLA Ops:
  0.0 0.8 copy.47
  0.8 1.3 collective-permute-start
  2.4 0.6 gather_fusion
  3.3 3.8 %shard_map.127 = (f32[2,256,256]{2,1,0:T(8,128)S(1)}, f32[2,256,256]{2,1,0:T(8,128)S(1)}, f32[2,256,256]{2,1,0:T(8,128)S(1)}, f32[2,256,256]{2,1,0:T(8,128)}) custom-call(s32[12]{0:T(128)S(1)} %reshape.213.refs_0_, f32[1,256,4096]{2,1,0:T(8,128)} %refs_1_.5, f32[1,256,4096]{2,1,0:T(8,128)} %refs_2_.3), custom_call_target="tpu_custom_call" | custom-call | tf_op jit(solution)/shard_map/pallas_call | solution.py:177
  7.1 0.8 copy-done.5
  7.9 1.3 collective-permute-start.15
  9.2 1.3 collective-permute-start.10
  10.5 1.3 collective-permute-start.9
  11.8 0.7 fusion.17
  31.7 0.6 gather_fusion.1
  32.3 0.7 fusion.18
  51.0 3.6 %shard_map.128 = (f32[2,256,256]{2,1,0:T(8,128)S(1)}, f32[2,256,256]{2,1,0:T(8,128)}, f32[2,256,256]{2,1,0:T(8,128)S(1)}, f32[2,256,256]{2,1,0:T(8,128)S(1)}) custom-call(s32[12]{0:T(128)S(1)} %reshape.214.refs_0_, f32[1,256,4096]{2,1,0:T(8,128)} %refs_1_.5, f32[1,256,4096]{2,1,0:T(8,128)} %refs_2_.3), custom_call_target="tpu_custom_call" | custom-call | tf_op jit(solution)/shard_map/pallas_call | solution.py:177
  54.6 0.8 copy-done.9
  55.4 0.8 copy-done.11
  56.2 0.8 copy-done.13
  57.0 5.8 %collective-permute-start.3 = (f32[2,256,256]{2,1,0:T(8,128)}, f32[2,256,256]{2,1,0:T(8,128)}, u32[]{:S(2)}, u32[]{:S(2)}) collective-permute-start(f32[2,256,256]{2,1,0:T(8,128)} %get-tuple-element.22), channel_id=1, source_target_pairs={{4,0},{8,4},{12,8},{5,1},{9,5},{13,9},{6,2},{10,6},{14,10},{7,3},{... | collective-permute-start | bytes 1572872 | tf_op jit(solution)/shard_map/ppermute | solution.py:18
  63.5 3.5 %collective-permute-start.2 = (f32[2,256,256]{2,1,0:T(8,128)}, f32[2,256,256]{2,1,0:T(8,128)}, u32[]{:S(2)}, u32[]{:S(2)}) collective-permute-start(f32[2,256,256]{2,1,0:T(8,128)} %copy-done.13), channel_id=1, source_target_pairs={{4,0},{8,4},{12,8},{5,1},{9,5},{13,9},{6,2},{10,6},{14,10},{7,3},{... | collective-permute-start | bytes 1572872 | tf_op jit(solution)/shard_map/ppermute | solution.py:18
  67.1 11.4 %shard_map.131 = (f32[2,256,256]{2,1,0:T(8,128)S(1)}, f32[2,256,256]{2,1,0:T(8,128)S(1)}) custom-call(s32[4]{0:T(128)S(1)} %pad_add_fusion.17.scalars, f32[2,256,256]{2,1,0:T(8,128)S(1)} %copy-done.1, f32[4,256,256]{2,1,0:T(8,128)S(1)} %copy-done, f32[2,256,256]{2,1,0:T(8,128)S(1)} %get-tuple-element.25.refs_2_, ...), custom_call_target="tpu_custom_call" | custom-call | tf_op jit(solution)/shard_map/pallas_call | solution.py:130
  79.0 2.4 %collective-permute-start.25 = (f32[2,256,256]{2,1,0:T(8,128)S(1)}, f32[2,256,256]{2,1,0:T(8,128)S(1)}, u32[]{:S(2)}, u32[]{:S(2)}) collective-permute-start(f32[2,256,256]{2,1,0:T(8,128)S(1)} %get-tuple-element.31.refs_9_), channel_id=1, source_target_pairs={{0,1},{1,0},{2,3},{3,2},{4,5},{5,4},{6,7},{7,6},{8,9},{9,8},{10,11... | collective-permute-start | bytes 1572872 | tf_op jit(solution)/shard_map/ppermute | solution.py:23
  81.3 1.2 broadcast_select_fusion
  82.5 1.3 collective-permute-start.11
  83.8 1.2 broadcast_select_fusion.2
  85.4 1.2 broadcast_select_fusion.1.refs_2_
  86.6 1.5 collective-permute-start.8
  88.1 1.2 broadcast_select_fusion.3.refs_2_
  89.3 7.8 %collective-permute-done.8 = f32[256,256]{1,0:T(8,128)S(1)} collective-permute-done((f32[256,256]{1,0:T(8,128)S(1)}, f32[256,256]{1,0:T(8,128)S(1)}, u32[]{:S(2)}, u32[]{:S(2)}) %collective-permute-start.8) | collective-permute-done | bytes 262176 | tf_op jit(solution)/shard_map/ppermute | solution.py:18
  97.1 1.1 collective-permute-start.1
  98.2 3.0 %collective-permute-done.11.refs_3_ = f32[2,256,256]{2,1,0:T(8,128)S(1)} collective-permute-done((f32[2,256,256]{2,1,0:T(8,128)S(1)}, f32[2,256,256]{2,1,0:T(8,128)S(1)}, u32[]{:S(2)}, u32[]{:S(2)}) %collective-permute-start.11) | collective-permute-done | bytes 524320 | tf_op jit(solution)/shard_map/ppermute | solution.py:23
  101.2 11.4 %shard_map.130 = (f32[2,256,256]{2,1,0:T(8,128)S(1)}, f32[2,256,256]{2,1,0:T(8,128)S(1)}) custom-call(s32[4]{0:T(128)S(1)} %pad_add_fusion.16.scalars, f32[2,256,256]{2,1,0:T(8,128)S(1)} %copy-done.1, f32[1,256,256]{2,1,0:T(8,128)S(1)} %bitcast.73, f32[2,256,256]{2,1,0:T(8,128)S(1)} %broadcast_select_fusion.1.refs_2_, ...), custom_call_target="tpu_custom_call" | custom-call | tf_op jit(solution)/shard_map/pallas_call | solution.py:130
  113.1 5.9 %collective-permute-start.26 = (f32[2,256,256]{2,1,0:T(8,128)S(1)}, f32[2,256,256]{2,1,0:T(8,128)S(1)}, u32[]{:S(2)}, u32[]{:S(2)}) collective-permute-start(f32[2,256,256]{2,1,0:T(8,128)S(1)} %collective-permute-done.16.refs_10_), channel_id=1, source_target_pairs={{0,1},{1,0},{2,3},{3,2},{4,5},{5,4},{6,7},{7,6},{8,9},{9,8},{10,11... | collective-permute-start | bytes 1572872 | tf_op jit(solution)/shard_map/ppermute | solution.py:23
  119.0 11.4 %shard_map.129 = (f32[2,256,256]{2,1,0:T(8,128)S(1)}, f32[2,256,256]{2,1,0:T(8,128)S(1)}) custom-call(s32[4]{0:T(128)S(1)} %pad_add_fusion.15.scalars, f32[2,256,256]{2,1,0:T(8,128)S(1)} %copy-done.1, f32[4,256,256]{2,1,0:T(8,128)S(1)} %copy-done, f32[2,256,256]{2,1,0:T(8,128)S(1)} %broadcast_select_fusion.3.refs_2_, ...), custom_call_target="tpu_custom_call" | custom-call | tf_op jit(solution)/shard_map/pallas_call | solution.py:130
  130.5 4.4 %collective-permute-start.12 = (f32[2,256,256]{2,1,0:T(8,128)S(1)}, f32[2,256,256]{2,1,0:T(8,128)S(1)}, u32[]{:S(2)}, u32[]{:S(2)}) collective-permute-start(f32[2,256,256]{2,1,0:T(8,128)S(1)} %get-tuple-element.29.refs_5_), channel_id=1, source_target_pairs={{4,0},{8,4},{12,8},{5,1},{9,5},{13,9},{6,2},{10,6},{14,10},{7,3},{... | collective-permute-start | bytes 1572872 | tf_op jit(solution)/shard_map/ppermute | solution.py:18
  134.9 1.2 collective-permute-start.6
  136.2 1.0 collective-permute-start.17
  137.2 1.3 collective-permute-start.5
  138.5 0.8 copy-done.3
  139.3 6.4 %collective-permute-done.12.refs_6_ = f32[2,256,256]{2,1,0:T(8,128)S(1)} collective-permute-done((f32[2,256,256]{2,1,0:T(8,128)S(1)}, f32[2,256,256]{2,1,0:T(8,128)S(1)}, u32[]{:S(2)}, u32[]{:S(2)}) %collective-permute-start.12) | collective-permute-done | bytes 524320 | tf_op jit(solution)/shard_map/ppermute | solution.py:18
  145.7 4.9 %collective-permute-start.14 = (f32[2,256,256]{2,1,0:T(8,128)S(1)}, f32[2,256,256]{2,1,0:T(8,128)}, u32[]{:S(2)}, u32[]{:S(2)}) collective-permute-start(f32[2,256,256]{2,1,0:T(8,128)S(1)} %collective-permute-done.13.refs_7_), channel_id=1, source_target_pairs={{4,0},{8,4},{12,8},{5,1},{9,5},{13,9},{6,2},{10,6},{14,10},{7,3},{... | collective-permute-start | bytes 1572872 | tf_op jit(solution)/shard_map/ppermute | solution.py:18
  150.7 1.5 collective-permute-start.7
  152.2 1.6 collective-permute-start.22
  153.9 0.4 collective-permute-start.18
  154.3 5.4 %collective-permute-done.14.refs_8_ = f32[2,256,256]{2,1,0:T(8,128)} collective-permute-done((f32[2,256,256]{2,1,0:T(8,128)S(1)}, f32[2,256,256]{2,1,0:T(8,128)}, u32[]{:S(2)}, u32[]{:S(2)}) %collective-permute-start.14) | collective-permute-done | bytes 524320 | tf_op jit(solution)/shard_map/ppermute | solution.py:18
  159.8 2.2 %collective-permute-start.24 = (f32[2,256,256]{2,1,0:T(8,128)}, f32[2,256,256]{2,1,0:T(8,128)}, u32[]{:S(2)}, u32[]{:S(2)}) collective-permute-start(f32[2,256,256]{2,1,0:T(8,128)} %collective-permute-done.14.refs_8_), channel_id=1, source_target_pairs={{0,1},{1,0},{2,3},{3,2},{4,5},{5,4},{6,7},{7,6},{8,9},{9,8},{10,11... | collective-permute-start | bytes 1572872 | tf_op jit(solution)/shard_map/ppermute | solution.py:23
  162.0 2.4 %collective-permute-done.7.refs_4_ = f32[2,256,256]{2,1,0:T(8,128)S(1)} collective-permute-done((f32[2,256,256]{2,1,0:T(8,128)S(1)}, f32[2,256,256]{2,1,0:T(8,128)S(1)}, u32[]{:S(2)}, u32[]{:S(2)}) %collective-permute-start.7) | collective-permute-done | bytes 524320 | tf_op jit(solution)/shard_map/ppermute | solution.py:18
  164.4 2.5 %collective-permute-start.20 = (f32[2,256,256]{2,1,0:T(8,128)S(1)}, f32[2,256,256]{2,1,0:T(8,128)}, u32[]{:S(2)}, u32[]{:S(2)}) collective-permute-start(f32[2,256,256]{2,1,0:T(8,128)S(1)} %collective-permute-done.7.refs_4_), channel_id=1, source_target_pairs={{0,1},{1,0},{2,3},{3,2},{4,5},{5,4},{6,7},{7,6},{8,9},{9,8},{10,11... | collective-permute-start | bytes 1572872 | tf_op jit(solution)/shard_map/ppermute | solution.py:23
  167.3 1.3 collective-permute-done.20.refs_14_
  168.6 1.0 copy-done.4
  169.7 14.1 %shard_map.132 = f32[2,1,256,4096]{3,2,1,0:T(8,128)} custom-call(s32[80]{0:T(128)S(1)} %reshape.212.refs_0_, f32[2,256,256]{2,1,0:T(8,128)S(1)} %copy-done.4, f32[2,256,256]{2,1,0:T(8,128)S(1)} %collective-permute-done.5.refs_2_, f32[2,256,256]{2,1,0:T(8,128)S(1)} %collective-permute-done.6.refs_3_, f32[2,256,256]{2,1,0:T(8,128)S(1)} %collective-permute-done.7.refs_4_, ...), custom_call_target="tpu_custom_call" | custom-call | tf_op jit(solution)/shard_map/pallas_call | solution.py:217
  (102 shorter events, 4.5 us)
Async XLA Ops:
  0.8 31.0 %collective-permute-start = (s32[4,2]{1,0:T(4,128)S(1)}, s32[4,2]{1,0:T(4,128)S(1)}, u32[]{:S(2)}, u32[]{:S(2)}) collective-permute-start(s32[4,2]{1,0:T(4,128)S(1)} %copy.47), channel_id=1, source_target_pairs={{0,4},{4,8},{8,12},{1,5},{5,9},{9,13},{2,6},{6,10},{10,14},{3,7},{... | collective-permute-start | bytes 104 | tf_op jit(solution)/shard_map/ppermute | solution.py:18
  3.3 28.4 %copy-start = (f32[4,256,256]{2,1,0:T(8,128)S(1)}, f32[4,256,256]{2,1,0:T(8,128)}, u32[]{:S(2)}) copy-start(f32[4,256,256]{2,1,0:T(8,128)} %refs_1_.7) | copy-start | bytes 3145732
  7.1 0.8 copy-start.5
  7.9 43.0 %copy-start.7 = (f32[2,256,256]{2,1,0:T(8,128)}, f32[2,256,256]{2,1,0:T(8,128)S(1)}, u32[]{:S(2)}) copy-start(f32[2,256,256]{2,1,0:T(8,128)S(1)} %get-tuple-element.21) | copy-start | bytes 1572868
  7.9 59.2 %collective-permute-start.15 = (f32[2,256,256]{2,1,0:T(8,128)}, f32[2,256,256]{2,1,0:T(8,128)S(1)}, u32[]{:S(2)}, u32[]{:S(2)}) collective-permute-start(f32[2,256,256]{2,1,0:T(8,128)} %get-tuple-element.27), channel_id=1, source_target_pairs={{0,2},{2,0},{1,3},{3,1},{4,6},{6,4},{5,7},{7,5},{8,10},{10,8},{9,1... | collective-permute-start | bytes 1572872 | tf_op jit(solution)/shard_map/ppermute | solution.py:23
  9.2 69.8 %collective-permute-start.10 = (f32[2,256,256]{2,1,0:T(8,128)}, f32[2,256,256]{2,1,0:T(8,128)}, u32[]{:S(2)}, u32[]{:S(2)}) collective-permute-start(f32[2,256,256]{2,1,0:T(8,128)} %get-tuple-element.27), channel_id=1, source_target_pairs={{0,4},{4,8},{8,12},{1,5},{5,9},{9,13},{2,6},{6,10},{10,14},{3,7},{... | collective-permute-start | bytes 1572872 | tf_op jit(solution)/shard_map/ppermute | solution.py:18
  10.5 74.6 %collective-permute-start.9 = (f32[2,256,256]{2,1,0:T(8,128)S(1)}, f32[2,256,256]{2,1,0:T(8,128)}, u32[]{:S(2)}, u32[]{:S(2)}) collective-permute-start(f32[2,256,256]{2,1,0:T(8,128)S(1)} %get-tuple-element.25.refs_2_), channel_id=1, source_target_pairs={{0,4},{4,8},{8,12},{1,5},{5,9},{9,13},{2,6},{6,10},{10,14},{3,7},{... | collective-permute-start | bytes 1572872 | tf_op jit(solution)/shard_map/ppermute | solution.py:18
  51.0 16.2 %copy-start.1 = (f32[2,256,256]{2,1,0:T(8,128)S(1)}, f32[2,256,256]{2,1,0:T(8,128)}, u32[]{:S(2)}) copy-start(f32[2,256,256]{2,1,0:T(8,128)} %refs_0_.5) | copy-start | bytes 1572868
  54.6 0.8 copy-start.9
  55.4 0.8 copy-start.11
  56.2 0.8 copy-start.13
  57.0 25.5 %collective-permute-start.3 = (f32[2,256,256]{2,1,0:T(8,128)}, f32[2,256,256]{2,1,0:T(8,128)}, u32[]{:S(2)}, u32[]{:S(2)}) collective-permute-start(f32[2,256,256]{2,1,0:T(8,128)} %get-tuple-element.22), channel_id=1, source_target_pairs={{4,0},{8,4},{12,8},{5,1},{9,5},{13,9},{6,2},{10,6},{14,10},{7,3},{... | collective-permute-start | bytes 1572872 | tf_op jit(solution)/shard_map/ppermute | solution.py:18
  63.5 23.1 %collective-permute-start.2 = (f32[2,256,256]{2,1,0:T(8,128)}, f32[2,256,256]{2,1,0:T(8,128)}, u32[]{:S(2)}, u32[]{:S(2)}) collective-permute-start(f32[2,256,256]{2,1,0:T(8,128)} %copy-done.13), channel_id=1, source_target_pairs={{4,0},{8,4},{12,8},{5,1},{9,5},{13,9},{6,2},{10,6},{14,10},{7,3},{... | collective-permute-start | bytes 1572872 | tf_op jit(solution)/shard_map/ppermute | solution.py:18
  67.1 14.2 %copy-start.12 = (f32[2,256,256]{2,1,0:T(8,128)S(1)}, f32[2,256,256]{2,1,0:T(8,128)}, u32[]{:S(2)}) copy-start(f32[2,256,256]{2,1,0:T(8,128)} %copy-done.11) | copy-start | bytes 1572868
  78.6 6.5 %copy-start.2 = (f32[2,256,256]{2,1,0:T(8,128)}, f32[2,256,256]{2,1,0:T(8,128)S(1)}, u32[]{:S(2)}) copy-start(f32[2,256,256]{2,1,0:T(8,128)S(1)} %get-tuple-element.31.refs_9_) | copy-start | bytes 1572868
  78.6 5.2 %copy-start.8 = (f32[2,256,256]{2,1,0:T(8,128)S(1)}, f32[2,256,256]{2,1,0:T(8,128)}, u32[]{:S(2)}) copy-start(f32[2,256,256]{2,1,0:T(8,128)} %copy-done.7) | copy-start | bytes 1572868
  78.6 34.5 %collective-permute-start.16 = (f32[2,256,256]{2,1,0:T(8,128)S(1)}, f32[2,256,256]{2,1,0:T(8,128)S(1)}, u32[]{:S(2)}, u32[]{:S(2)}) collective-permute-start(f32[2,256,256]{2,1,0:T(8,128)S(1)} %get-tuple-element.32), channel_id=1, source_target_pairs={{0,2},{2,0},{1,3},{3,1},{4,6},{6,4},{5,7},{7,5},{8,10},{10,8},{9,1... | collective-permute-start | bytes 1572872 | tf_op jit(solution)/shard_map/ppermute | solution.py:23
  79.0 56.0 %collective-permute-start.25 = (f32[2,256,256]{2,1,0:T(8,128)S(1)}, f32[2,256,256]{2,1,0:T(8,128)S(1)}, u32[]{:S(2)}, u32[]{:S(2)}) collective-permute-start(f32[2,256,256]{2,1,0:T(8,128)S(1)} %get-tuple-element.31.refs_9_), channel_id=1, source_target_pairs={{0,1},{1,0},{2,3},{3,2},{4,5},{5,4},{6,7},{7,6},{8,9},{9,8},{10,11... | collective-permute-start | bytes 1572872 | tf_op jit(solution)/shard_map/ppermute | solution.py:23
  81.3 4.1 %copy-start.10 = (f32[2,256,256]{2,1,0:T(8,128)S(1)}, f32[2,256,256]{2,1,0:T(8,128)}, u32[]{:S(2)}) copy-start(f32[2,256,256]{2,1,0:T(8,128)} %copy-done.9) | copy-start | bytes 1572868
  82.5 18.7 %collective-permute-start.11 = (f32[2,256,256]{2,1,0:T(8,128)S(1)}, f32[2,256,256]{2,1,0:T(8,128)S(1)}, u32[]{:S(2)}, u32[]{:S(2)}) collective-permute-start(f32[2,256,256]{2,1,0:T(8,128)S(1)} %broadcast_select_fusion), channel_id=1, source_target_pairs={{0,2},{2,0},{1,3},{3,1},{4,6},{6,4},{5,7},{7,5},{8,10},{10,8},{9,1... | collective-permute-start | bytes 1572872 | tf_op jit(solution)/shard_map/ppermute | solution.py:23
  83.8 4.3 %copy-start.6 = (f32[2,256,256]{2,1,0:T(8,128)S(1)}, f32[2,256,256]{2,1,0:T(8,128)}, u32[]{:S(2)}) copy-start(f32[2,256,256]{2,1,0:T(8,128)} %copy-done.5) | copy-start | bytes 1572868
  85.0 33.9 %collective-permute-start.4 = (f32[2,256,256]{2,1,0:T(8,128)S(1)}, f32[2,256,256]{2,1,0:T(8,128)S(1)}, u32[]{:S(2)}, u32[]{:S(2)}) collective-permute-start(f32[2,256,256]{2,1,0:T(8,128)S(1)} %broadcast_select_fusion.2), channel_id=1, source_target_pairs={{0,2},{2,0},{1,3},{3,1},{4,6},{6,4},{5,7},{7,5},{8,10},{10,8},{9,1... | collective-permute-start | bytes 1572872 | tf_op jit(solution)/shard_map/ppermute | solution.py:23
  86.6 10.5 %collective-permute-start.8 = (f32[256,256]{1,0:T(8,128)S(1)}, f32[256,256]{1,0:T(8,128)S(1)}, u32[]{:S(2)}, u32[]{:S(2)}) collective-permute-start(f32[256,256]{1,0:T(8,128)S(1)} %dynamic-slice_bitcast_fusion), channel_id=1, source_target_pairs={{0,4},{4,8},{8,12},{1,5},{5,9},{9,13},{2,6},{6,10},{10,14},{3,7},{... | collective-permute-start | bytes 786440 | tf_op jit(solution)/shard_map/ppermute | solution.py:18
  97.1 33.4 %collective-permute-start.1 = (s32[10,4]{0,1:T(4,128)S(1)}, s32[10,4]{0,1:T(4,128)S(1)}, u32[]{:S(2)}, u32[]{:S(2)}) collective-permute-start(s32[10,4]{0,1:T(4,128)S(1)} %stack.245), channel_id=1, source_target_pairs={{0,1},{1,0},{2,3},{3,2},{4,5},{5,4},{6,7},{7,6},{8,9},{9,8},{10,11... | collective-permute-start | bytes 488 | tf_op jit(solution)/shard_map/ppermute | solution.py:23
  112.6 24.5 %collective-permute-start.13 = (f32[2,256,256]{2,1,0:T(8,128)S(1)}, f32[2,256,256]{2,1,0:T(8,128)S(1)}, u32[]{:S(2)}, u32[]{:S(2)}) collective-permute-start(f32[2,256,256]{2,1,0:T(8,128)S(1)} %get-tuple-element.30), channel_id=1, source_target_pairs={{0,2},{2,0},{1,3},{3,1},{4,6},{6,4},{5,7},{7,5},{8,10},{10,8},{9,1... | collective-permute-start | bytes 1572872 | tf_op jit(solution)/shard_map/ppermute | solution.py:23
  113.1 17.4 %copy-start.14 = (f32[2,256,256]{2,1,0:T(8,128)}, f32[2,256,256]{2,1,0:T(8,128)S(1)}, u32[]{:S(2)}) copy-start(f32[2,256,256]{2,1,0:T(8,128)S(1)} %collective-permute-done.16.refs_10_) | copy-start | bytes 1572868
  113.1 23.1 %collective-permute-start.26 = (f32[2,256,256]{2,1,0:T(8,128)S(1)}, f32[2,256,256]{2,1,0:T(8,128)S(1)}, u32[]{:S(2)}, u32[]{:S(2)}) collective-permute-start(f32[2,256,256]{2,1,0:T(8,128)S(1)} %collective-permute-done.16.refs_10_), channel_id=1, source_target_pairs={{0,1},{1,0},{2,3},{3,2},{4,5},{5,4},{6,7},{7,6},{8,9},{9,8},{10,11... | collective-permute-start | bytes 1572872 | tf_op jit(solution)/shard_map/ppermute | solution.py:23
  119.0 20.3 %collective-permute-start.21 = (f32[2,256,256]{2,1,0:T(8,128)S(1)}, f32[2,256,256]{2,1,0:T(8,128)S(1)}, u32[]{:S(2)}, u32[]{:S(2)}) collective-permute-start(f32[2,256,256]{2,1,0:T(8,128)S(1)} %get-tuple-element.29.refs_5_), channel_id=1, source_target_pairs={{0,1},{1,0},{2,3},{3,2},{4,5},{5,4},{6,7},{7,6},{8,9},{9,8},{10,11... | collective-permute-start | bytes 1572872 | tf_op jit(solution)/shard_map/ppermute | solution.py:23
  130.5 15.2 %collective-permute-start.12 = (f32[2,256,256]{2,1,0:T(8,128)S(1)}, f32[2,256,256]{2,1,0:T(8,128)S(1)}, u32[]{:S(2)}, u32[]{:S(2)}) collective-permute-start(f32[2,256,256]{2,1,0:T(8,128)S(1)} %get-tuple-element.29.refs_5_), channel_id=1, source_target_pairs={{4,0},{8,4},{12,8},{5,1},{9,5},{13,9},{6,2},{10,6},{14,10},{7,3},{... | collective-permute-start | bytes 1572872 | tf_op jit(solution)/shard_map/ppermute | solution.py:18
  134.9 29.5 %copy-start.15 = (f32[2,256,256]{2,1,0:T(8,128)}, f32[2,256,256]{2,1,0:T(8,128)S(1)}, u32[]{:S(2)}) copy-start(f32[2,256,256]{2,1,0:T(8,128)S(1)} %collective-permute-done.25.refs_19_) | copy-start | bytes 1572868
  134.9 15.7 %collective-permute-start.6 = (f32[2,256,256]{2,1,0:T(8,128)S(1)}, f32[2,256,256]{2,1,0:T(8,128)S(1)}, u32[]{:S(2)}, u32[]{:S(2)}) collective-permute-start(f32[2,256,256]{2,1,0:T(8,128)S(1)} %get-tuple-element.24), channel_id=1, source_target_pairs={{0,2},{2,0},{1,3},{3,1},{4,6},{6,4},{5,7},{7,5},{8,10},{10,8},{9,1... | collective-permute-start | bytes 1572872 | tf_op jit(solution)/shard_map/ppermute | solution.py:23
  136.2 28.2 %copy-start.16 = (f32[2,256,256]{2,1,0:T(8,128)}, f32[2,256,256]{2,1,0:T(8,128)S(1)}, u32[]{:S(2)}) copy-start(f32[2,256,256]{2,1,0:T(8,128)S(1)} %collective-permute-done.26.refs_20_) | copy-start | bytes 1572868
  136.2 16.0 %collective-permute-start.17 = (f32[2,256,256]{2,1,0:T(8,128)S(1)}, f32[2,256,256]{2,1,0:T(8,128)S(1)}, u32[]{:S(2)}, u32[]{:S(2)}) collective-permute-start(f32[2,256,256]{2,1,0:T(8,128)S(1)} %get-tuple-element.23.refs_1_), channel_id=1, source_target_pairs={{0,1},{1,0},{2,3},{3,2},{4,5},{5,4},{6,7},{7,6},{8,9},{9,8},{10,11... | collective-permute-start | bytes 1572872 | tf_op jit(solution)/shard_map/ppermute | solution.py:23
  137.2 16.6 %collective-permute-start.5 = (f32[2,256,256]{2,1,0:T(8,128)S(1)}, f32[2,256,256]{2,1,0:T(8,128)S(1)}, u32[]{:S(2)}, u32[]{:S(2)}) collective-permute-start(f32[2,256,256]{2,1,0:T(8,128)S(1)} %get-tuple-element.23.refs_1_), channel_id=1, source_target_pairs={{0,4},{4,8},{8,12},{1,5},{5,9},{9,13},{2,6},{6,10},{10,14},{3,7},{... | collective-permute-start | bytes 1572872 | tf_op jit(solution)/shard_map/ppermute | solution.py:18
  138.5 0.8 copy-start.3
  139.3 25.1 %copy-start.17 = (f32[2,256,256]{2,1,0:T(8,128)}, f32[2,256,256]{2,1,0:T(8,128)S(1)}, u32[]{:S(2)}) copy-start(f32[2,256,256]{2,1,0:T(8,128)S(1)} %collective-permute-done.21.refs_15_) | copy-start | bytes 1572868
  139.3 14.6 %collective-permute-start.23 = (f32[2,256,256]{2,1,0:T(8,128)S(1)}, f32[2,256,256]{2,1,0:T(8,128)S(1)}, u32[]{:S(2)}, u32[]{:S(2)}) collective-permute-start(f32[2,256,256]{2,1,0:T(8,128)S(1)} %collective-permute-done.13.refs_7_), channel_id=1, source_target_pairs={{0,1},{1,0},{2,3},{3,2},{4,5},{5,4},{6,7},{7,6},{8,9},{9,8},{10,11... | collective-permute-start | bytes 1572872 | tf_op jit(solution)/shard_map/ppermute | solution.py:23
  145.7 14.0 %collective-permute-start.14 = (f32[2,256,256]{2,1,0:T(8,128)S(1)}, f32[2,256,256]{2,1,0:T(8,128)}, u32[]{:S(2)}, u32[]{:S(2)}) collective-permute-start(f32[2,256,256]{2,1,0:T(8,128)S(1)} %collective-permute-done.13.refs_7_), channel_id=1, source_target_pairs={{4,0},{8,4},{12,8},{5,1},{9,5},{13,9},{6,2},{10,6},{14,10},{7,3},{... | collective-permute-start | bytes 1572872 | tf_op jit(solution)/shard_map/ppermute | solution.py:18
  150.7 13.7 %collective-permute-start.7 = (f32[2,256,256]{2,1,0:T(8,128)S(1)}, f32[2,256,256]{2,1,0:T(8,128)S(1)}, u32[]{:S(2)}, u32[]{:S(2)}) collective-permute-start(f32[2,256,256]{2,1,0:T(8,128)S(1)} %collective-permute-done.6.refs_3_), channel_id=1, source_target_pairs={{0,4},{4,8},{8,12},{1,5},{5,9},{9,13},{2,6},{6,10},{10,14},{3,7},{... | collective-permute-start | bytes 1572872 | tf_op jit(solution)/shard_map/ppermute | solution.py:18
  152.2 12.2 %copy-start.18 = (f32[2,256,256]{2,1,0:T(8,128)}, f32[2,256,256]{2,1,0:T(8,128)S(1)}, u32[]{:S(2)}) copy-start(f32[2,256,256]{2,1,0:T(8,128)S(1)} %collective-permute-done.17.refs_11_) | copy-start | bytes 1572868
  152.2 15.1 %collective-permute-start.22 = (f32[2,256,256]{2,1,0:T(8,128)S(1)}, f32[2,256,256]{2,1,0:T(8,128)}, u32[]{:S(2)}, u32[]{:S(2)}) collective-permute-start(f32[2,256,256]{2,1,0:T(8,128)S(1)} %collective-permute-done.12.refs_6_), channel_id=1, source_target_pairs={{0,1},{1,0},{2,3},{3,2},{4,5},{5,4},{6,7},{7,6},{8,9},{9,8},{10,11... | collective-permute-start | bytes 1572872 | tf_op jit(solution)/shard_map/ppermute | solution.py:23
  153.8 13.5 %collective-permute-start.19 = (f32[2,256,256]{2,1,0:T(8,128)S(1)}, f32[2,256,256]{2,1,0:T(8,128)}, u32[]{:S(2)}, u32[]{:S(2)}) collective-permute-start(f32[2,256,256]{2,1,0:T(8,128)S(1)} %collective-permute-done.6.refs_3_), channel_id=1, source_target_pairs={{0,1},{1,0},{2,3},{3,2},{4,5},{5,4},{6,7},{7,6},{8,9},{9,8},{10,11... | collective-permute-start | bytes 1572872 | tf_op jit(solution)/shard_map/ppermute | solution.py:23
  153.9 10.5 %copy-start.19 = (f32[2,256,256]{2,1,0:T(8,128)}, f32[2,256,256]{2,1,0:T(8,128)S(1)}, u32[]{:S(2)}) copy-start(f32[2,256,256]{2,1,0:T(8,128)S(1)} %collective-permute-done.23.refs_17_) | copy-start | bytes 1572868
  153.9 13.4 %collective-permute-start.18 = (f32[2,256,256]{2,1,0:T(8,128)S(1)}, f32[2,256,256]{2,1,0:T(8,128)}, u32[]{:S(2)}, u32[]{:S(2)}) collective-permute-start(f32[2,256,256]{2,1,0:T(8,128)S(1)} %collective-permute-done.5.refs_2_), channel_id=1, source_target_pairs={{0,1},{1,0},{2,3},{3,2},{4,5},{5,4},{6,7},{7,6},{8,9},{9,8},{10,11... | collective-permute-start | bytes 1572872 | tf_op jit(solution)/shard_map/ppermute | solution.py:23
  159.8 7.5 %collective-permute-start.24 = (f32[2,256,256]{2,1,0:T(8,128)}, f32[2,256,256]{2,1,0:T(8,128)}, u32[]{:S(2)}, u32[]{:S(2)}) collective-permute-start(f32[2,256,256]{2,1,0:T(8,128)} %collective-permute-done.14.refs_8_), channel_id=1, source_target_pairs={{0,1},{1,0},{2,3},{3,2},{4,5},{5,4},{6,7},{7,6},{8,9},{9,8},{10,11... | collective-permute-start | bytes 1572872 | tf_op jit(solution)/shard_map/ppermute | solution.py:23
  164.4 4.2 %collective-permute-start.20 = (f32[2,256,256]{2,1,0:T(8,128)S(1)}, f32[2,256,256]{2,1,0:T(8,128)}, u32[]{:S(2)}, u32[]{:S(2)}) collective-permute-start(f32[2,256,256]{2,1,0:T(8,128)S(1)} %collective-permute-done.7.refs_4_), channel_id=1, source_target_pairs={{0,1},{1,0},{2,3},{3,2},{4,5},{5,4},{6,7},{7,6},{8,9},{9,8},{10,11... | collective-permute-start | bytes 1572872 | tf_op jit(solution)/shard_map/ppermute | solution.py:23
  168.6 1.0 copy-start.4

commit v2 on v1

v2 whole, which is shorter than its diff:
```python
import math

import numpy as np
import jax
import jax.numpy as jnp
from jax import lax
from jax.experimental import pallas as pl
from jax.experimental.pallas import tpu as pltpu
from jax.sharding import PartitionSpec as P

SIN = [(-1.0) ** k / math.factorial(2 * k + 1) for k in range(8)]
COS = [(-1.0) ** k / math.factorial(2 * k) for k in range(8)]
VMEM = pl.BlockSpec(memory_space=pltpu.VMEM)
SMEM = pl.BlockSpec(memory_space=pltpu.SMEM)
ANY = pl.BlockSpec(memory_space=pl.ANY)


def params(mib):
    return pltpu.CompilerParams(vmem_limit_bytes=mib << 20)


def move(block, axis, distance):
    size = lax.axis_size(axis)
    route = [(i, i + distance) for i in range(size) if 0 <= i + distance < size]
    return lax.ppermute(block, axis, route)


def rotate(block, axis, distance):
    size = lax.axis_size(axis)
    return lax.ppermute(block, axis, [(i, (i + distance) % size) for i in range(size)])


def rotate_last(block, distance):
    tiles, size = lax.axis_size("tile"), lax.axis_size("slab")
    base = (tiles - 1) * size
    route = [(base + i, base + (i + distance) % size) for i in range(size)]
    return lax.ppermute(block, ("tile", "slab"), route)


def halves(matrix):
    high = matrix.astype(np.float32).astype(jnp.bfloat16)
    low = (matrix - high.astype(np.float64)).astype(np.float32).astype(jnp.bfloat16)
    return [high, low]


def compact_tables(side):
    index = np.arange(side)
    fourier = np.exp(-2j * np.pi * (index[:, None] * index[None, :] % side) / side)
    wavenumber = np.where(index < side // 2, index, index - side)
    kernel = np.exp(-1j * np.pi * (wavenumber * wavenumber % (8 * side)) / (4 * side))
    line = np.fft.ifft(kernel)
    line = (line + line[-index % side]) / 2
    fresnel = line[(index[:, None] - index[None, :]) % side]
    scaled = fourier / math.sqrt(side)
    pieces = []
    for matrix in (fresnel, scaled):
        pieces += halves(matrix.real) + halves(matrix.imag)
    return np.stack(pieces)


def expand_kernel(pieces, *outs):
    side = pieces.shape[-1]
    for which in range(2):
        left, right = outs[2 * which], outs[2 * which + 1]
        real_high, real_low, imag_high, imag_low = [pieces[4 * which + k] for k in range(4)]
        real = [real_high, real_low, real_high]
        imag = [imag_high, imag_low, imag_high]
        minus = [-imag_high, -imag_low, -imag_high]
        for column, blocks in enumerate((real + minus, imag + real)):
            for row, block in enumerate(blocks):
                rows, cols = pl.ds(row * side, side), pl.ds(column * side, side)
                right[rows, cols] = block
                left[cols, rows] = block


def expand(side):
    pieces = jnp.asarray(compact_tables(side))
    left = jax.ShapeDtypeStruct((2 * side, 6 * side), jnp.bfloat16)
    right = jax.ShapeDtypeStruct((6 * side, 2 * side), jnp.bfloat16)
    return pl.pallas_call(
        expand_kernel,
        in_specs=[VMEM],
        out_specs=[VMEM] * 4,
        out_shape=[left, right, left, right],
        compiler_params=params(16),
        name="expand",
    )(pieces)


def split(value):
    high = value.astype(jnp.bfloat16)
    low = (value - high.astype(jnp.float32)).astype(jnp.bfloat16)
    return high, low


def two_sided(left, right, real, imag):
    side = real.shape[-1]
    real_high, real_low = split(real)
    imag_high, imag_low = split(imag)
    wide = jnp.concatenate([real_high, real_high, real_low, imag_high, imag_high, imag_low], axis=1)
    inner = jnp.dot(wide, right[...], preferred_element_type=jnp.float32)
    real_high, real_low = split(inner[:, :side])
    imag_high, imag_low = split(inner[:, side:])
    tall = jnp.concatenate([real_high, real_high, real_low, imag_high, imag_high, imag_low], axis=0)
    outer = jnp.dot(left[...], tall, preferred_element_type=jnp.float32)
    return outer[:side], outer[side:]


def transmission(phase, absorption):
    square = phase * phase
    sine = jnp.full_like(phase, SIN[-1])
    cosine = jnp.full_like(phase, COS[-1])
    for a, b in zip(SIN[-2::-1], COS[-2::-1]):
        sine = sine * square + a
        cosine = cosine * square + b
    damping = jnp.exp(-absorption)
    return damping * cosine, damping * sine * phase


def slot_kernel(kind, base, each, sections, pairs, probe, measured, *refs):
    pieces = 1 if kind == "last" else 2
    own = refs[:pieces]
    others = refs[pieces : pieces + sections - 1]
    refs = refs[pieces + sections - 1 :]
    prop_left, prop_right, dft_left, dft_right = refs[:4]
    outs = refs[4 : 4 + sections]
    wave, trans = refs[4 + sections : 6 + sections]
    side = probe.shape[-1]
    slab = lax.axis_index("slab")
    index = base + slab * each
    row = lax.rem(pairs[0, index], side)
    col = lax.rem(pairs[1, index], side)
    if kind == "up":
        amplitude = measured
        fetch = None
    else:
        amplitude, sem = refs[6 + sections :]
        fetch = pltpu.make_async_copy(measured.at[index], amplitude, sem)
        fetch.start()
    rows = lax.broadcasted_iota(jnp.int32, (side, side), 0)
    patch = [own[0][0], own[0][1]]
    if pieces == 2:
        patch = [jnp.where(rows >= row, own[0][k], own[1][k]) for k in range(2)]
    trans[slab, 0], trans[slab, 1] = transmission(patch[0], patch[1])
    for distance in range(1, sections):
        owner = lax.rem(slab + (sections - distance), sections)
        real, imag = transmission(others[distance - 1][0], others[distance - 1][1])
        trans[owner, 0] = real
        trans[owner, 1] = imag
    for part in range(2):
        wave[0, part] = pltpu.roll(pltpu.roll(probe[part], row, 0), col, 1)
    for step in range(sections):
        a, b, c, d = wave[step, 0], wave[step, 1], trans[step, 0], trans[step, 1]
        real, imag = a * c - b * d, a * d + b * c
        if step < sections - 1:
            real, imag = two_sided(prop_left, prop_right, real, imag)
            wave[step + 1, 0] = real
            wave[step + 1, 1] = imag
    real, imag = two_sided(dft_left, dft_right, real, imag)
    if fetch is not None:
        fetch.wait()
    factor = 1.0 - amplitude[...] * lax.rsqrt(jnp.maximum(real * real + imag * imag, 0.25))
    real, minus = two_sided(dft_left, dft_right, real * factor, -imag * factor)
    for step in range(sections - 1, -1, -1):
        a, b = wave[step, 0], wave[step, 1]
        wave[step, 0] = a * real - b * minus
        wave[step, 1] = -(a * minus + b * real)
        if step > 0:
            c, d = trans[step, 0], trans[step, 1]
            real, minus = c * real - d * minus, c * minus + d * real
            real, minus = two_sided(prop_left, prop_right, real, minus)
    for distance in range(sections):
        outs[distance][...] = wave[lax.rem(slab + distance, sections)]


def run_slot(kind, base, each, pairs, probe, measured, own, others, constants):
    sections = len(others) + 1
    side = probe.shape[-1]
    shape = jax.ShapeDtypeStruct((2, side, side), jnp.float32)
    scratch = [pltpu.VMEM((sections, 2, side, side), jnp.float32)] * 2
    if kind != "up":
        scratch += [pltpu.VMEM((side, side), jnp.float32), pltpu.SemaphoreType.DMA(())]
    return pl.pallas_call(
        lambda *refs: slot_kernel(kind, base, each, sections, *refs),
        in_specs=[SMEM, VMEM, VMEM if kind == "up" else ANY]
        + [VMEM] * (len(own) + len(others) + 4),
        out_specs=[VMEM] * sections,
        out_shape=[shape] * sections,
        scratch_shapes=scratch,
        compiler_params=params(32),
        name="slot_" + kind,
    )(pairs, probe, measured, *own, *others, *constants)


def position(k, bases, slab, sections):
    base, each, distance = bases[k]
    return base + lax.rem(slab + distance, sections) * each


def cut_kernel(bases, sections, send, pairs, phase, absorption, *refs):
    count = len(bases)
    side = phase.shape[1]
    blocks = phase.shape[2] // side
    slab = lax.axis_index("slab")
    if send is not None:
        measured, refs = refs[0], refs[1:]
    outs = refs[:count]
    buffer, sems = refs[-2], refs[-1]
    copies, columns = [], []
    for k in range(count):
        column = pairs[1, position(k, bases, slab, sections)]
        first = lax.div(column, side)
        columns.append(lax.rem(column, side))
        for which, source in enumerate((phase, absorption)):
            for half in range(2):
                block = first if half == 0 else jnp.minimum(first + 1, blocks - 1)
                copies.append(
                    pltpu.make_async_copy(
                        source.at[0, :, pl.ds(pl.multiple_of(block * side, side), side)],
                        buffer.at[k, which, half],
                        sems.at[k, which, half],
                    )
                )
    for copy in copies:
        copy.start()
    if send is not None:
        index = send[0] + slab * send[1]
        extra = pltpu.make_async_copy(measured.at[index], refs[count], refs[-3])
        extra.start()
    lane = lax.broadcasted_iota(jnp.int32, (side, side), 1)
    for k in range(count):
        own = lane >= columns[k]
        for which in range(2):
            for half in range(2):
                copies[4 * k + 2 * which + half].wait()
            outs[k][which] = jnp.where(own, buffer[k, which, 0], buffer[k, which, 1])
    if send is not None:
        extra.wait()


def cut(bases, pairs, phase, absorption, measured=None, send=None):
    side = phase.shape[1]
    count = len(bases)
    sections = lax.axis_size("slab")
    shape = jax.ShapeDtypeStruct((2, side, side), jnp.float32)
    shapes = [shape] * count
    scratch = [
        pltpu.VMEM((count, 2, 2, side, side), jnp.float32),
        pltpu.SemaphoreType.DMA((count, 2, 2)),
    ]
    inputs = [pairs, phase, absorption]
    if send is not None:
        shapes = shapes + [jax.ShapeDtypeStruct((side, side), jnp.float32)]
        scratch = [pltpu.SemaphoreType.DMA(())] + scratch
        inputs.append(measured)
    return pl.pallas_call(
        lambda *refs: cut_kernel(bases, sections, send, *refs),
        in_specs=[SMEM] + [ANY] * (len(inputs) - 1),
        out_specs=[VMEM] * len(shapes),
        out_shape=shapes,
        scratch_shapes=scratch,
        compiler_params=params(16),
        name="cut",
    )(*inputs)


def join_kernel(bases, sections, pairs, here, there, out):
    side = out.shape[-1]
    slab = lax.axis_index("slab")
    row = lax.rem(pairs[0, position(0, bases, slab, sections)], side)
    rows = lax.broadcasted_iota(jnp.int32, (side, side), 0)
    for part in range(2):
        out[part] = jnp.where(rows >= row, here[part], there[part])


def join(base, pairs, here, there):
    sections = lax.axis_size("slab")
    return pl.pallas_call(
        lambda *refs: join_kernel([base], sections, *refs),
        in_specs=[SMEM, VMEM, VMEM],
        out_specs=VMEM,
        out_shape=jax.ShapeDtypeStruct(here.shape, jnp.float32),
        compiler_params=params(8),
        name="join",
    )(pairs, here, there)


def spans(metas, tables, side, sections):
    slab = lax.axis_index("slab")
    last = lax.axis_index("tile") == lax.axis_size("tile") - 1
    out = []
    for source, base, mode in metas:
        index = position(0, [base], slab, sections)
        row, col = tables[source][0, index], tables[source][1, index]
        row = lax.rem(row, side)
        low, high = row, jnp.int32(side)
        if mode == "below":
            low, high = jnp.int32(0), row
        elif mode == "last":
            low = jnp.where(last, row, side)
        elif mode == "inner":
            low = jnp.where(last, side, row)
        out.append((lax.div(col, side), lax.rem(col, side), low, high))
    return out


def early_kernel(metas, sections, *refs):
    count = len(metas)
    tables, terms, out = refs[:4], refs[4 : 4 + count], refs[4 + count]
    side = terms[0].shape[-1]
    blocks = out.shape[-1] // side
    rows = lax.broadcasted_iota(jnp.int32, (side, side), 0)
    lane = lax.broadcasted_iota(jnp.int32, (side, side), 1)

    @pl.loop(0, blocks)
    def _(block):
        out[:, :, pl.ds(pl.multiple_of(block * side, side), side)] = jnp.zeros((2, side, side), jnp.float32)

    for k, (first, col, low, high) in enumerate(spans(metas, tables, side, sections)):
        for half in range(2):
            block = first + half

            @pl.when((block < blocks) & (high > low))
            def _():
                keep = (rows >= low) & (rows < high)
                keep = keep & ((lane < col) if half else (lane >= col))
                place = pl.ds(pl.multiple_of(block * side, side), side)
                for part in range(2):
                    out[part, :, place] += jnp.where(keep, terms[k][part], 0.0)


def early(metas, tables, terms, cols_total):
    side = terms[0].shape[-1]
    sections = lax.axis_size("slab")
    return pl.pallas_call(
        lambda *refs: early_kernel(metas, sections, *refs),
        in_specs=[SMEM] * 4 + [VMEM] * len(terms),
        out_specs=VMEM,
        out_shape=jax.ShapeDtypeStruct((2, side, cols_total), jnp.float32),
        compiler_params=params(20),
        name="early",
    )(*tables, *terms)


def late_kernel(metas, sections, *refs):
    count = len(metas)
    tables, total, terms = refs[:4], refs[4], refs[5 : 5 + count]
    out, stage, sems = refs[5 + count :]
    side = terms[0].shape[-1]
    blocks = out.shape[-1] // side
    rows = lax.broadcasted_iota(jnp.int32, (side, side), 0)
    lane = lax.broadcasted_iota(jnp.int32, (side, side), 1)
    ranges = spans(metas, tables, side, sections)

    def send(block):
        place = pl.ds(pl.multiple_of(block * side, side), side)
        return pltpu.make_async_copy(stage.at[:, :, place], out.at[:, 0, :, place], sems.at[block])

    @pl.loop(0, blocks)
    def _(block):
        place = pl.ds(pl.multiple_of(block * side, side), side)
        stage[:, :, place] = total[:, :, place]
        for k, (first, col, low, high) in enumerate(ranges):
            for half in range(2):

                @pl.when((first + half == block) & (high > low))
                def _():
                    keep = (rows >= low) & (rows < high)
                    keep = keep & ((lane < col) if half else (lane >= col))
                    for part in range(2):
                        stage[part, :, place] += jnp.where(keep, terms[k][part], 0.0)

        send(block).start()

    @pl.loop(0, blocks)
    def _(block):
        send(block).wait()


def late(metas, tables, total, terms):
    side = terms[0].shape[-1]
    cols_total = total.shape[-1]
    sections = lax.axis_size("slab")
    return pl.pallas_call(
        lambda *refs: late_kernel(metas, sections, *refs),
        in_specs=[SMEM] * 4 + [VMEM] * (1 + len(terms)),
        out_specs=ANY,
        out_shape=jax.ShapeDtypeStruct((2, 1, side, cols_total), jnp.float32),
        scratch_shapes=[
            pltpu.VMEM((2, side, cols_total), jnp.float32),
            pltpu.SemaphoreType.DMA((cols_total // side,)),
        ],
        compiler_params=params(28),
        name="late",
    )(*tables, total, *terms)


def local(phase, absorption, probe, measured, offsets):
    side = probe.shape[-1]
    cols_total = phase.shape[2]
    sections = lax.axis_size("slab")
    each = offsets.shape[0] // sections
    n_up = each // 2
    n_here = each - n_up
    distances = list(range(sections))

    pairs = offsets.T
    below = move(pairs, "tile", 1)
    here = lambda k, d: (k, n_here, d)
    up = lambda k, d: (sections * n_here + k, n_up, d)
    back = lambda d: (sections - d) % sections

    lower, amplitude = [], []
    for k in range(n_up):
        *cuts, send = cut(
            [up(k, d) for d in distances], pairs, phase, absorption, measured, (up(k, 0)[0], n_up)
        )
        lower.append(cuts)
        amplitude.append(send)
    raised = [[None] * sections for k in range(n_up)]
    extra = [[None] * sections for k in range(n_up)]
    for k in range(n_up):
        for d in distances[1:] + [0]:
            raised[k][d] = move(lower[k][d], "tile", 1)
            extra[k][d] = rotate_last(lower[k][d], d) if d else None
    amplitude = [move(value, "tile", 1) for value in amplitude]
    low_cuts = [cut([here(k, d) for d in distances], below, phase, absorption) for k in range(n_here)]
    lowered = [[None] * sections for k in range(n_here)]
    for k in range(n_here):
        for d in distances[1:] + [0]:
            lowered[k][d] = move(low_cuts[k][d], "tile", -1)
    constants = expand(side)
    up_cuts = [cut([up(k, d) for d in distances], below, phase, absorption) for k in range(n_up)]
    own_cuts = [cut([here(k, d) for d in distances], pairs, phase, absorption) for k in range(n_here)]

    mine, metas = [], []
    final, final_metas = [], []
    tables = [pairs, below, rotate(pairs, "batch", 1), rotate(below, "batch", 1)]

    def add(term, source, base, mode, is_final=False):
        for other in range(2):
            value = rotate(term, "batch", 1) if other else term
            (final if is_final else mine).append(value)
            (final_metas if is_final else metas).append((source + 2 * other, base, mode))

    for k in range(n_up):
        others = extra[k][1:]
        done = run_slot(
            "last", up(k, 0)[0], n_up, pairs, probe, measured, [lower[k][0]], others, constants
        )
        for d in distances:
            value = rotate_last(done[d], d) if d else done[d]
            add(value, 0, up(k, back(d)), "last")
    for k in range(n_up):
        others = [
            rotate(join(up(k, d), below, raised[k][d], up_cuts[k][d]), "slab", d)
            for d in distances[1:]
        ]
        done = run_slot(
            "up", up(k, 0)[0], n_up, below, probe, amplitude[k],
            [raised[k][0], up_cuts[k][0]], others, constants,
        )
        for d in distances:
            value = rotate(done[d], "slab", d) if d else done[d]
            add(value, 1, up(k, back(d)), "below")
            add(move(value, "tile", -1), 0, up(k, back(d)), "inner", d > 0)
    for k in range(n_here):
        others = [
            rotate(join(here(k, d), pairs, own_cuts[k][d], lowered[k][d]), "slab", d)
            for d in distances[1:]
        ]
        done = run_slot(
            "here", here(k, 0)[0], n_here, pairs, probe, measured,
            [own_cuts[k][0], lowered[k][0]], others, constants,
        )
        for d in distances:
            value = rotate(done[d], "slab", d) if d else done[d]
            add(value, 0, here(k, back(d)), "above", d > 0)
            add(move(value, "tile", 1), 1, here(k, back(d)), "below", True)
    total = early(metas, tables, mine, cols_total)
    return late(final_metas, tables, total, final)


def solution(mesh):
    in_specs = (
        P(("groups", "slab"), "tile", None),
        P(("groups", "slab"), "tile", None),
        P(),
        P(("groups", "tile", "batch"), None, None),
        P(("groups", "tile", "batch"), None),
    )
    out_specs = P(None, ("groups", "slab"), "tile", None)
    return jax.shard_map(local, mesh=mesh, in_specs=in_specs, out_specs=out_specs, check_vma=False)
```

time: 185 us -> 125 us (0.68)
  between operations: 36.2 us -> 0.52 us
  Pallas kernels: 55.8 us -> 34.5 us
  waiting for transfers between devices: 26.5 us -> 39 us
  other arithmetic: 6.25 us -> 0 us
  starting transfers between devices: 49 us -> 43.7 us
  local copies, waits for them, and re-layouts: 9.95 us -> 6.31 us
    pallas_call x6 -> x12, Pallas kernels: 55.8 us -> 34.5 us  [the longest x3 21.3 us: run_slot(): pl.pallas_call(lambda *refs: slot_kernel(kind, base, each, sections, *ref...]
    ppermute x10, waiting for transfers between devices: 22.2 us -> 29.4 us  [move(): return lax.ppermute(block, axis, route)]
    ppermute x10, starting transfers between devices: 26.7 us -> 20.3 us  [move(): return lax.ppermute(block, axis, route)]
    ppermute x0 -> x2, starting transfers between devices: none -> 5.51 us  [rotate_last(): return lax.ppermute(block, ('tile', 'slab'), route)]
    ppermute x17 -> x16, waiting for transfers between devices: 4.35 us -> 9.59 us  [rotate(): lax.ppermute(block, axis, [(i, (i + distance) % size) for i in range(size)])]
    select_n x7 -> x0, other arithmetic: 5.05 us -> none  [the longest x2 2.39 us: local(): patches.append(jnp.where(rows >= row, lower, low_cut[base + d]))]
    ppermute x17 -> x16, starting transfers between devices: 22.3 us -> 17.9 us  [rotate(): lax.ppermute(block, axis, [(i, (i + distance) % size) for i in range(size)])]
    unnamed x41 -> x20, local copies, waits for them, and re-layouts: 5.85 us -> 6.31 us
  transfers between devices with their start and end apart: 27 -> 28, of which waited for: 6 -> 5; matrix products, arithmetic and copies ran while one was open for 6% -> 0% of each run, Pallas kernels for 23% -> 23%
where the time goes in v2:
time: 125 us; the launch traced here: 124 us
  starting transfers between devices  43.7 us (35%)
  waiting for transfers between devices  39 us (31%)
  Pallas kernels  34.5 us (28%)
  local copies, waits for them, and re-layouts  6.31 us (5%)
    ppermute x10, waiting for transfers between devices, move(): return lax.ppermute(block, axis, route)  29.4 us
    pallas_call x3, Pallas kernels, run_slot(): pl.pallas_call(lambda *refs: slot_kernel(kind, base, each, sections, *ref...  21.3 us
    ppermute x10, starting transfers between devices, move(): return lax.ppermute(block, axis, route)  20.3 us
    ppermute x16, starting transfers between devices, rotate(): lax.ppermute(block, axis, [(i, (i + distance) % size) for i in range(size)])  17.9 us
    ppermute x16, waiting for transfers between devices, rotate(): lax.ppermute(block, axis, [(i, (i + distance) % size) for i in range(size)])  9.59 us
    unnamed x20, local copies, waits for them, and re-layouts  6.31 us
    ppermute x2, starting transfers between devices, rotate_last(): return lax.ppermute(block, ('tile', 'slab'), route)  5.51 us
    pallas_call x1, Pallas kernels, late(): pl.pallas_call(lambda *refs: late_kernel(metas, sections, *refs), in_spec...  4.81 us
  transfers between devices with their start and end apart: 28, of which 5 were waited for; matrix products, arithmetic and copies ran while one was open for 0% of the time, Pallas kernels for 23%

profile of v2, /device:TPU:29, one launch (start us, length us, event | category | flops | bytes accessed | tf_op | source)
XLA Modules:
  0.0 124.1 jit_solution(2690769572240774998)
XLA Ops:
  0.0 2.2 %copy-done = f32[1,256,4096]{2,1,0:T(8,128)S(1)} copy-done((f32[1,256,4096]{2,1,0:T(8,128)S(1)}, f32[1,256,4096]{2,1,0:T(8,128)}, u32[]{:S(2)}) %copy-start) | copy-done | bytes 4194328
  2.2 2.2 %copy-done.2 = f32[1,256,4096]{2,1,0:T(8,128)S(1)} copy-done((f32[1,256,4096]{2,1,0:T(8,128)S(1)}, f32[1,256,4096]{2,1,0:T(8,128)}, u32[]{:S(2)}) %copy-start.2) | copy-done | bytes 4194328
  4.4 1.2 copy-done.4
  5.6 0.7 copy-done.8
  6.3 1.0 cut.4
  7.3 1.6 %collective-permute-start.9 = (f32[2,256,256]{2,1,0:T(8,128)S(1)}, f32[2,256,256]{2,1,0:T(8,128)S(1)}, u32[]{:S(2)}, u32[]{:S(2)}) collective-permute-start(f32[2,256,256]{2,1,0:T(8,128)S(1)} %get-tuple-element.25), channel_id=1, source_target_pairs={{0,4},{4,8},{8,12},{1,5},{5,9},{9,13},{2,6},{6,10},{10,14},{3,7},{... | collective-permute-start | bytes 1572872 | tf_op jit(solution)/shard_map/ppermute | solution.py:25
  8.8 3.1 %collective-permute-start.3 = (f32[2,256,256]{2,1,0:T(8,128)S(1)}, f32[2,256,256]{2,1,0:T(8,128)S(1)}, u32[]{:S(2)}, u32[]{:S(2)}) collective-permute-start(f32[2,256,256]{2,1,0:T(8,128)S(1)} %get-tuple-element.25), channel_id=1, source_target_pairs={{12,14},{14,12},{13,15},{15,13},{28,30},{30,28},{29,31},{31,29}} | collective-permute-start | bytes 1572872 | tf_op jit(solution)/shard_map/ppermute | solution.py:37
  11.9 1.3 %collective-permute-start = (s32[2,4]{1,0:T(2,128)S(1)}, s32[2,4]{1,0:T(2,128)S(1)}, u32[]{:S(2)}, u32[]{:S(2)}) collective-permute-start(s32[2,4]{1,0:T(2,128)S(1)} %bitcast.2), channel_id=1, source_target_pairs={{0,4},{4,8},{8,12},{1,5},{5,9},{9,13},{2,6},{6,10},{10,14},{3,7},{... | collective-permute-start | bytes 104 | tf_op jit(solution)/shard_map/ppermute | solution.py:25
  13.2 9.0 %collective-permute-done.refs_0_.refs_1_ = s32[2,4]{1,0:T(2,128)S(1)} collective-permute-done((s32[2,4]{1,0:T(2,128)S(1)}, s32[2,4]{1,0:T(2,128)S(1)}, u32[]{:S(2)}, u32[]{:S(2)}) %collective-permute-start) | collective-permute-done | bytes 64 | tf_op jit(solution)/shard_map/ppermute | solution.py:25
  22.2 0.9 cut.7
  23.2 2.1 %collective-permute-start.17 = (f32[2,256,256]{2,1,0:T(8,128)S(1)}, f32[2,256,256]{2,1,0:T(8,128)S(1)}, u32[]{:S(2)}, u32[]{:S(2)}) collective-permute-start(f32[2,256,256]{2,1,0:T(8,128)S(1)} %get-tuple-element.40), channel_id=1, source_target_pairs={{4,0},{8,4},{12,8},{5,1},{9,5},{13,9},{6,2},{10,6},{14,10},{7,3},{... | collective-permute-start | bytes 1572872 | tf_op jit(solution)/shard_map/ppermute | solution.py:25
  25.3 1.3 %collective-permute-start.8 = (f32[2,256,256]{2,1,0:T(8,128)S(1)}, f32[2,256,256]{2,1,0:T(8,128)S(1)}, u32[]{:S(2)}, u32[]{:S(2)}) collective-permute-start(f32[2,256,256]{2,1,0:T(8,128)S(1)} %get-tuple-element.24.refs_3_), channel_id=1, source_target_pairs={{0,4},{4,8},{8,12},{1,5},{5,9},{9,13},{2,6},{6,10},{10,14},{3,7},{... | collective-permute-start | bytes 1572872 | tf_op jit(solution)/shard_map/ppermute | solution.py:25
  26.6 1.4 %collective-permute-start.7 = (f32[256,256]{1,0:T(8,128)S(1)}, f32[256,256]{1,0:T(8,128)S(1)}, u32[]{:S(2)}, u32[]{:S(2)}) collective-permute-start(f32[256,256]{1,0:T(8,128)S(1)} %get-tuple-element.32), channel_id=1, source_target_pairs={{0,4},{4,8},{8,12},{1,5},{5,9},{9,13},{2,6},{6,10},{10,14},{3,7},{... | collective-permute-start | bytes 786440 | tf_op jit(solution)/shard_map/ppermute | solution.py:25
  28.0 0.9 cut.6
  29.0 0.4 expand.1
  29.4 0.9 cut.5
  30.4 4.6 %collective-permute-start.16 = (f32[2,256,256]{2,1,0:T(8,128)S(1)}, f32[2,256,256]{2,1,0:T(8,128)S(1)}, u32[]{:S(2)}, u32[]{:S(2)}) collective-permute-start(f32[2,256,256]{2,1,0:T(8,128)S(1)} %get-tuple-element.38), channel_id=1, source_target_pairs={{4,0},{8,4},{12,8},{5,1},{9,5},{13,9},{6,2},{10,6},{14,10},{7,3},{... | collective-permute-start | bytes 1572872 | tf_op jit(solution)/shard_map/ppermute | solution.py:25
  35.1 0.6 join.2
  35.7 1.3 %collective-permute-start.10 = (f32[2,256,256]{2,1,0:T(8,128)S(1)}, f32[2,256,256]{2,1,0:T(8,128)S(1)}, u32[]{:S(2)}, u32[]{:S(2)}) collective-permute-start(f32[2,256,256]{2,1,0:T(8,128)S(1)} %join.2), channel_id=1, source_target_pairs={{0,2},{2,0},{1,3},{3,1},{4,6},{6,4},{5,7},{7,5},{8,10},{10,8},{9,1... | collective-permute-start | bytes 1572872 | tf_op jit(solution)/shard_map/ppermute | solution.py:30
  37.0 7.1 %slot_last.1 = (f32[2,256,256]{2,1,0:T(8,128)S(1)}, f32[2,256,256]{2,1,0:T(8,128)S(1)}) custom-call(s32[2,4]{1,0:T(2,128)S(1)} %bitcast.4, f32[2,256,256]{2,1,0:T(8,128)S(1)} %copy-done.6, f32[4,256,256]{2,1,0:T(8,128)S(1)} %copy-done.5, f32[2,256,256]{2,1,0:T(8,128)S(1)} %get-tuple-element.24.refs_3_, f32[2,256,256]{2,1,0:T(8,128)S(1)} %collective-permute-done.3.refs_4_, ...), custom_call_target="tpu_custom_call" | custom-call | tf_op jit(solution)/shard_map/slot_last/pallas_call | solution.py:183
  44.1 2.4 %collective-permute-start.5 = (f32[2,256,256]{2,1,0:T(8,128)S(1)}, f32[2,256,256]{2,1,0:T(8,128)S(1)}, u32[]{:S(2)}, u32[]{:S(2)}) collective-permute-start(f32[2,256,256]{2,1,0:T(8,128)S(1)} %get-tuple-element.31), channel_id=1, source_target_pairs={{12,14},{14,12},{13,15},{15,13},{28,30},{30,28},{29,31},{31,29}} | collective-permute-start | bytes 1572872 | tf_op jit(solution)/shard_map/ppermute | solution.py:37
  46.5 0.6 join.3
  47.1 1.2 collective-permute-start.18
  48.4 3.3 %collective-permute-start.4 = (f32[2,256,256]{2,1,0:T(8,128)S(1)}, f32[2,256,256]{2,1,0:T(8,128)S(1)}, u32[]{:S(2)}, u32[]{:S(2)}) collective-permute-start(f32[2,256,256]{2,1,0:T(8,128)S(1)} %get-tuple-element.30.refs_4_), channel_id=1, source_target_pairs={{0,1},{1,0},{2,3},{3,2},{4,5},{5,4},{6,7},{7,6},{8,9},{9,8},{10,11... | collective-permute-start | bytes 1572872 | tf_op jit(solution)/shard_map/ppermute | solution.py:30
  51.6 0.1 collective-permute-start.1
  51.7 7.0 %slot_up.1 = (f32[2,256,256]{2,1,0:T(8,128)S(1)}, f32[2,256,256]{2,1,0:T(8,128)S(1)}) custom-call(s32[2,4]{1,0:T(2,128)S(1)} %collective-permute-done.refs_0_.refs_1_, f32[2,256,256]{2,1,0:T(8,128)S(1)} %copy-done.6, f32[256,256]{1,0:T(8,128)S(1)} %collective-permute-done.7.refs_2_, f32[2,256,256]{2,1,0:T(8,128)S(1)} %collective-permute-done.8.refs_3_, ...), custom_call_target="tpu_custom_call" | custom-call | tf_op jit(solution)/shard_map/slot_up/pallas_call | solution.py:183
  58.8 0.5 collective-permute-start.2
  59.3 1.1 collective-permute-start.14
  60.4 9.5 %collective-permute-done.18.refs_5_ = f32[2,256,256]{2,1,0:T(8,128)S(1)} collective-permute-done((f32[2,256,256]{2,1,0:T(8,128)S(1)}, f32[2,256,256]{2,1,0:T(8,128)S(1)}, u32[]{:S(2)}, u32[]{:S(2)}) %collective-permute-start.18) | collective-permute-done | bytes 524320 | tf_op jit(solution)/shard_map/ppermute | solution.py:30
  69.9 4.9 %collective-permute-start.6 = (f32[2,256,256]{2,1,0:T(8,128)S(1)}, f32[2,256,256]{2,1,0:T(8,128)S(1)}, u32[]{:S(2)}, u32[]{:S(2)}) collective-permute-start(f32[2,256,256]{2,1,0:T(8,128)S(1)} %collective-permute-done.5.refs_6_), channel_id=1, source_target_pairs={{0,1},{1,0},{2,3},{3,2},{4,5},{5,4},{6,7},{7,6},{8,9},{9,8},{10,11... | collective-permute-start | bytes 1572872 | tf_op jit(solution)/shard_map/ppermute | solution.py:30
  74.8 7.1 %slot_here.1 = (f32[2,256,256]{2,1,0:T(8,128)S(1)}, f32[2,256,256]{2,1,0:T(8,128)S(1)}) custom-call(s32[2,4]{1,0:T(2,128)S(1)} %bitcast.7, f32[2,256,256]{2,1,0:T(8,128)S(1)} %copy-done.6, f32[4,256,256]{2,1,0:T(8,128)S(1)} %copy-done.5, f32[2,256,256]{2,1,0:T(8,128)S(1)} %get-tuple-element.37.refs_3_, f32[2,256,256]{2,1,0:T(8,128)S(1)} %collective-permute-done.16.refs_4_, ...), custom_call_target="tpu_custom_call" | custom-call | tf_op jit(solution)/shard_map/slot_here/pallas_call | solution.py:183
  82.0 1.3 %collective-permute-start.12 = (f32[2,256,256]{2,1,0:T(8,128)S(1)}, f32[2,256,256]{2,1,0:T(8,128)S(1)}, u32[]{:S(2)}, u32[]{:S(2)}) collective-permute-start(f32[2,256,256]{2,1,0:T(8,128)S(1)} %get-tuple-element.35.refs_8_), channel_id=1, source_target_pairs={{4,0},{8,4},{12,8},{5,1},{9,5},{13,9},{6,2},{10,6},{14,10},{7,3},{... | collective-permute-start | bytes 1572872 | tf_op jit(solution)/shard_map/ppermute | solution.py:25
  83.3 0.1 collective-permute-start.11
  83.4 0.9 collective-permute-start.24
  84.3 1.3 %collective-permute-start.22 = (f32[2,256,256]{2,1,0:T(8,128)S(1)}, f32[2,256,256]{2,1,0:T(8,128)S(1)}, u32[]{:S(2)}, u32[]{:S(2)}) collective-permute-start(f32[2,256,256]{2,1,0:T(8,128)S(1)} %get-tuple-element.41.refs_14_), channel_id=1, source_target_pairs={{0,4},{4,8},{8,12},{1,5},{5,9},{9,13},{2,6},{6,10},{10,14},{3,7},{... | collective-permute-start | bytes 1572872 | tf_op jit(solution)/shard_map/ppermute | solution.py:25
  85.6 0.8 collective-permute-start.19
  86.4 8.4 %collective-permute-done.12.refs_10_ = f32[2,256,256]{2,1,0:T(8,128)S(1)} collective-permute-done((f32[2,256,256]{2,1,0:T(8,128)S(1)}, f32[2,256,256]{2,1,0:T(8,128)S(1)}, u32[]{:S(2)}, u32[]{:S(2)}) %collective-permute-start.12) | collective-permute-done | bytes 524320 | tf_op jit(solution)/shard_map/ppermute | solution.py:25
  94.8 4.1 %collective-permute-start.20 = (f32[2,256,256]{2,1,0:T(8,128)S(1)}, f32[2,256,256]{2,1,0:T(8,128)S(1)}, u32[]{:S(2)}, u32[]{:S(2)}) collective-permute-start(f32[2,256,256]{2,1,0:T(8,128)S(1)} %collective-permute-done.14.refs_12_), channel_id=1, source_target_pairs={{4,0},{8,4},{12,8},{5,1},{9,5},{13,9},{6,2},{10,6},{14,10},{7,3},{... | collective-permute-start | bytes 1572872 | tf_op jit(solution)/shard_map/ppermute | solution.py:25
  98.9 0.9 collective-permute-start.15
  99.9 1.3 %collective-permute-start.26 = (f32[2,256,256]{2,1,0:T(8,128)S(1)}, f32[2,256,256]{2,1,0:T(8,128)S(1)}, u32[]{:S(2)}, u32[]{:S(2)}) collective-permute-start(f32[2,256,256]{2,1,0:T(8,128)S(1)} %collective-permute-done.24.refs_9_), channel_id=1, source_target_pairs={{0,4},{4,8},{8,12},{1,5},{5,9},{9,13},{2,6},{6,10},{10,14},{3,7},{... | collective-permute-start | bytes 1572872 | tf_op jit(solution)/shard_map/ppermute | solution.py:25
  101.2 0.1 collective-permute-start.13
  101.3 0.5 collective-permute-start.25
  101.7 7.8 %collective-permute-done.20.refs_5_ = f32[2,256,256]{2,1,0:T(8,128)S(1)} collective-permute-done((f32[2,256,256]{2,1,0:T(8,128)S(1)}, f32[2,256,256]{2,1,0:T(8,128)S(1)}, u32[]{:S(2)}, u32[]{:S(2)}) %collective-permute-start.20) | collective-permute-done | bytes 524320 | tf_op jit(solution)/shard_map/ppermute | solution.py:25
  109.6 1.5 %collective-permute-start.23 = (f32[2,256,256]{2,1,0:T(8,128)S(1)}, f32[2,256,256]{2,1,0:T(8,128)S(1)}, u32[]{:S(2)}, u32[]{:S(2)}) collective-permute-start(f32[2,256,256]{2,1,0:T(8,128)S(1)} %collective-permute-done.22.refs_7_), channel_id=1, source_target_pairs={{0,1},{1,0},{2,3},{3,2},{4,5},{5,4},{6,7},{7,6},{8,9},{9,8},{10,11... | collective-permute-start | bytes 1572872 | tf_op jit(solution)/shard_map/ppermute | solution.py:30
  111.0 4.3 %collective-permute-done.26.refs_11_ = f32[2,256,256]{2,1,0:T(8,128)S(1)} collective-permute-done((f32[2,256,256]{2,1,0:T(8,128)S(1)}, f32[2,256,256]{2,1,0:T(8,128)S(1)}, u32[]{:S(2)}, u32[]{:S(2)}) %collective-permute-start.26) | collective-permute-done | bytes 524320 | tf_op jit(solution)/shard_map/ppermute | solution.py:25
  115.3 0.8 collective-permute-start.27
  116.1 3.0 %early.1.refs_4_ = f32[2,256,4096]{2,1,0:T(8,128)S(1)} custom-call(s32[2,4]{1,0:T(2,128)S(1)} %bitcast.8, s32[2,4]{1,0:T(2,128)S(1)} %collective-permute-done.refs_0_.refs_1_, s32[2,4]{1,0:T(2,128)S(1)} %collective-permute-done.1.refs_2_, s32[2,4]{1,0:T(2,128)S(1)} %collective-permute-done.2.refs_3_, f32[2,256,256]{2,1,0:T(8,128)S(1)} %get-tuple-element.30.refs_4_, ...), custom_call_target="tpu_custom_call" | custom-call | tf_op jit(solution)/shard_map/early/pallas_call | solution.py:335
  119.2 4.8 %late.1 = f32[2,1,256,4096]{3,2,1,0:T(8,128)} custom-call(s32[2,4]{1,0:T(2,128)S(1)} %bitcast.9, s32[2,4]{1,0:T(2,128)S(1)} %collective-permute-done.refs_0_.refs_1_, s32[2,4]{1,0:T(2,128)S(1)} %collective-permute-done.1.refs_2_, s32[2,4]{1,0:T(2,128)S(1)} %collective-permute-done.2.refs_3_, f32[2,256,4096]{2,1,0:T(8,128)S(1)} %early.1.refs_4_, ...), custom_call_target="tpu_custom_call" | custom-call | tf_op jit(solution)/shard_map/late/pallas_call | solution.py:384
  (40 shorter events, 0.1 us)
Async XLA Ops:
  0.0 2.2 %copy-start = (f32[1,256,4096]{2,1,0:T(8,128)S(1)}, f32[1,256,4096]{2,1,0:T(8,128)}, u32[]{:S(2)}) copy-start(f32[1,256,4096]{2,1,0:T(8,128)} %refs_1_.12) | copy-start | bytes 12582916
  2.2 2.2 %copy-start.2 = (f32[1,256,4096]{2,1,0:T(8,128)S(1)}, f32[1,256,4096]{2,1,0:T(8,128)}, u32[]{:S(2)}) copy-start(f32[1,256,4096]{2,1,0:T(8,128)} %refs_2_.10) | copy-start | bytes 12582916
  4.4 1.2 copy-start.4
  5.6 0.7 copy-start.8
  6.3 15.9 %copy-start.1 = (f32[1,256,4096]{2,1,0:T(8,128)S(1)}, f32[1,256,4096]{2,1,0:T(8,128)}, u32[]{:S(2)}) copy-start(f32[1,256,4096]{2,1,0:T(8,128)} %refs_1_.12) | copy-start | bytes 12582916
  6.3 15.9 %copy-start.3 = (f32[1,256,4096]{2,1,0:T(8,128)S(1)}, f32[1,256,4096]{2,1,0:T(8,128)}, u32[]{:S(2)}) copy-start(f32[1,256,4096]{2,1,0:T(8,128)} %refs_2_.10) | copy-start | bytes 12582916
  7.3 23.1 %collective-permute-start.9 = (f32[2,256,256]{2,1,0:T(8,128)S(1)}, f32[2,256,256]{2,1,0:T(8,128)S(1)}, u32[]{:S(2)}, u32[]{:S(2)}) collective-permute-start(f32[2,256,256]{2,1,0:T(8,128)S(1)} %get-tuple-element.25), channel_id=1, source_target_pairs={{0,4},{4,8},{8,12},{1,5},{5,9},{9,13},{2,6},{6,10},{10,14},{3,7},{... | collective-permute-start | bytes 1572872 | tf_op jit(solution)/shard_map/ppermute | solution.py:25
  8.8 26.9 %collective-permute-start.3 = (f32[2,256,256]{2,1,0:T(8,128)S(1)}, f32[2,256,256]{2,1,0:T(8,128)S(1)}, u32[]{:S(2)}, u32[]{:S(2)}) collective-permute-start(f32[2,256,256]{2,1,0:T(8,128)S(1)} %get-tuple-element.25), channel_id=1, source_target_pairs={{12,14},{14,12},{13,15},{15,13},{28,30},{30,28},{29,31},{31,29}} | collective-permute-start | bytes 1572872 | tf_op jit(solution)/shard_map/ppermute | solution.py:37
  11.9 10.3 %collective-permute-start = (s32[2,4]{1,0:T(2,128)S(1)}, s32[2,4]{1,0:T(2,128)S(1)}, u32[]{:S(2)}, u32[]{:S(2)}) collective-permute-start(s32[2,4]{1,0:T(2,128)S(1)} %bitcast.2), channel_id=1, source_target_pairs={{0,4},{4,8},{8,12},{1,5},{5,9},{9,13},{2,6},{6,10},{10,14},{3,7},{... | collective-permute-start | bytes 104 | tf_op jit(solution)/shard_map/ppermute | solution.py:25
  23.2 20.9 %collective-permute-start.17 = (f32[2,256,256]{2,1,0:T(8,128)S(1)}, f32[2,256,256]{2,1,0:T(8,128)S(1)}, u32[]{:S(2)}, u32[]{:S(2)}) collective-permute-start(f32[2,256,256]{2,1,0:T(8,128)S(1)} %get-tuple-element.40), channel_id=1, source_target_pairs={{4,0},{8,4},{12,8},{5,1},{9,5},{13,9},{6,2},{10,6},{14,10},{7,3},{... | collective-permute-start | bytes 1572872 | tf_op jit(solution)/shard_map/ppermute | solution.py:25
  25.3 23.1 %collective-permute-start.8 = (f32[2,256,256]{2,1,0:T(8,128)S(1)}, f32[2,256,256]{2,1,0:T(8,128)S(1)}, u32[]{:S(2)}, u32[]{:S(2)}) collective-permute-start(f32[2,256,256]{2,1,0:T(8,128)S(1)} %get-tuple-element.24.refs_3_), channel_id=1, source_target_pairs={{0,4},{4,8},{8,12},{1,5},{5,9},{9,13},{2,6},{6,10},{10,14},{3,7},{... | collective-permute-start | bytes 1572872 | tf_op jit(solution)/shard_map/ppermute | solution.py:25
  26.6 2.4 %copy-start.7 = (bf16[8,256,256]{2,1,0:T(8,128)(2,1)S(1)}, bf16[8,256,256]{2,1,0:T(8,128)(2,1)}, u32[]{:S(2)}) copy-start(bf16[8,256,256]{2,1,0:T(8,128)(2,1)} %constant.2.clone.pieces) | copy-start | bytes 3145732
  26.6 20.5 %collective-permute-start.7 = (f32[256,256]{1,0:T(8,128)S(1)}, f32[256,256]{1,0:T(8,128)S(1)}, u32[]{:S(2)}, u32[]{:S(2)}) collective-permute-start(f32[256,256]{1,0:T(8,128)S(1)} %get-tuple-element.32), channel_id=1, source_target_pairs={{0,4},{4,8},{8,12},{1,5},{5,9},{9,13},{2,6},{6,10},{10,14},{3,7},{... | collective-permute-start | bytes 786440 | tf_op jit(solution)/shard_map/ppermute | solution.py:25
  29.4 7.6 %copy-start.5 = (f32[4,256,256]{2,1,0:T(8,128)S(1)}, f32[4,256,256]{2,1,0:T(8,128)}, u32[]{:S(2)}) copy-start(f32[4,256,256]{2,1,0:T(8,128)} %refs_2_.11) | copy-start | bytes 3145732
  29.4 7.5 %copy-start.6 = (f32[2,256,256]{2,1,0:T(8,128)S(1)}, f32[2,256,256]{2,1,0:T(8,128)}, u32[]{:S(2)}) copy-start(f32[2,256,256]{2,1,0:T(8,128)} %refs_1_.13) | copy-start | bytes 1572868
  29.4 7.5 %copy-start.9 = (s32[4,2]{0,1:T(2,128)S(1)}, s32[4,2]{0,1:T(2,128)}, u32[]{:S(2)}) copy-start(s32[4,2]{0,1:T(2,128)} %param.10) | copy-start | bytes 100
  30.4 28.4 %collective-permute-start.16 = (f32[2,256,256]{2,1,0:T(8,128)S(1)}, f32[2,256,256]{2,1,0:T(8,128)S(1)}, u32[]{:S(2)}, u32[]{:S(2)}) collective-permute-start(f32[2,256,256]{2,1,0:T(8,128)S(1)} %get-tuple-element.38), channel_id=1, source_target_pairs={{4,0},{8,4},{12,8},{5,1},{9,5},{13,9},{6,2},{10,6},{14,10},{7,3},{... | collective-permute-start | bytes 1572872 | tf_op jit(solution)/shard_map/ppermute | solution.py:25
  35.7 16.0 %collective-permute-start.10 = (f32[2,256,256]{2,1,0:T(8,128)S(1)}, f32[2,256,256]{2,1,0:T(8,128)S(1)}, u32[]{:S(2)}, u32[]{:S(2)}) collective-permute-start(f32[2,256,256]{2,1,0:T(8,128)S(1)} %join.2), channel_id=1, source_target_pairs={{0,2},{2,0},{1,3},{3,1},{4,6},{6,4},{5,7},{7,5},{8,10},{10,8},{9,1... | collective-permute-start | bytes 1572872 | tf_op jit(solution)/shard_map/ppermute | solution.py:30
  44.1 15.2 %collective-permute-start.5 = (f32[2,256,256]{2,1,0:T(8,128)S(1)}, f32[2,256,256]{2,1,0:T(8,128)S(1)}, u32[]{:S(2)}, u32[]{:S(2)}) collective-permute-start(f32[2,256,256]{2,1,0:T(8,128)S(1)} %get-tuple-element.31), channel_id=1, source_target_pairs={{12,14},{14,12},{13,15},{15,13},{28,30},{30,28},{29,31},{31,29}} | collective-permute-start | bytes 1572872 | tf_op jit(solution)/shard_map/ppermute | solution.py:37
  47.1 22.8 %collective-permute-start.18 = (f32[2,256,256]{2,1,0:T(8,128)S(1)}, f32[2,256,256]{2,1,0:T(8,128)S(1)}, u32[]{:S(2)}, u32[]{:S(2)}) collective-permute-start(f32[2,256,256]{2,1,0:T(8,128)S(1)} %join.3), channel_id=1, source_target_pairs={{0,2},{2,0},{1,3},{3,1},{4,6},{6,4},{5,7},{7,5},{8,10},{10,8},{9,1... | collective-permute-start | bytes 1572872 | tf_op jit(solution)/shard_map/ppermute | solution.py:30
  48.4 35.0 %collective-permute-start.4 = (f32[2,256,256]{2,1,0:T(8,128)S(1)}, f32[2,256,256]{2,1,0:T(8,128)S(1)}, u32[]{:S(2)}, u32[]{:S(2)}) collective-permute-start(f32[2,256,256]{2,1,0:T(8,128)S(1)} %get-tuple-element.30.refs_4_), channel_id=1, source_target_pairs={{0,1},{1,0},{2,3},{3,2},{4,5},{5,4},{6,7},{7,6},{8,9},{9,8},{10,11... | collective-permute-start | bytes 1572872 | tf_op jit(solution)/shard_map/ppermute | solution.py:30
  51.6 30.3 %collective-permute-start.1 = (s32[2,4]{1,0:T(2,128)S(1)}, s32[2,4]{1,0:T(2,128)S(1)}, u32[]{:S(2)}, u32[]{:S(2)}) collective-permute-start(s32[2,4]{1,0:T(2,128)S(1)} %bitcast.6), channel_id=1, source_target_pairs={{0,1},{1,0},{2,3},{3,2},{4,5},{5,4},{6,7},{7,6},{8,9},{9,8},{10,11... | collective-permute-start | bytes 104 | tf_op jit(solution)/shard_map/ppermute | solution.py:30
  58.8 24.5 %collective-permute-start.2 = (s32[2,4]{1,0:T(2,128)S(1)}, s32[2,4]{1,0:T(2,128)S(1)}, u32[]{:S(2)}, u32[]{:S(2)}) collective-permute-start(s32[2,4]{1,0:T(2,128)S(1)} %collective-permute-done.refs_0_.refs_1_), channel_id=1, source_target_pairs={{0,1},{1,0},{2,3},{3,2},{4,5},{5,4},{6,7},{7,6},{8,9},{9,8},{10,11... | collective-permute-start | bytes 104 | tf_op jit(solution)/shard_map/ppermute | solution.py:30
  59.3 26.3 %collective-permute-start.14 = (f32[2,256,256]{2,1,0:T(8,128)S(1)}, f32[2,256,256]{2,1,0:T(8,128)S(1)}, u32[]{:S(2)}, u32[]{:S(2)}) collective-permute-start(f32[2,256,256]{2,1,0:T(8,128)S(1)} %get-tuple-element.36), channel_id=1, source_target_pairs={{0,2},{2,0},{1,3},{3,1},{4,6},{6,4},{5,7},{7,5},{8,10},{10,8},{9,1... | collective-permute-start | bytes 1572872 | tf_op jit(solution)/shard_map/ppermute | solution.py:30
  69.9 14.4 %collective-permute-start.6 = (f32[2,256,256]{2,1,0:T(8,128)S(1)}, f32[2,256,256]{2,1,0:T(8,128)S(1)}, u32[]{:S(2)}, u32[]{:S(2)}) collective-permute-start(f32[2,256,256]{2,1,0:T(8,128)S(1)} %collective-permute-done.5.refs_6_), channel_id=1, source_target_pairs={{0,1},{1,0},{2,3},{3,2},{4,5},{5,4},{6,7},{7,6},{8,9},{9,8},{10,11... | collective-permute-start | bytes 1572872 | tf_op jit(solution)/shard_map/ppermute | solution.py:30
  82.0 12.8 %collective-permute-start.12 = (f32[2,256,256]{2,1,0:T(8,128)S(1)}, f32[2,256,256]{2,1,0:T(8,128)S(1)}, u32[]{:S(2)}, u32[]{:S(2)}) collective-permute-start(f32[2,256,256]{2,1,0:T(8,128)S(1)} %get-tuple-element.35.refs_8_), channel_id=1, source_target_pairs={{4,0},{8,4},{12,8},{5,1},{9,5},{13,9},{6,2},{10,6},{14,10},{7,3},{... | collective-permute-start | bytes 1572872 | tf_op jit(solution)/shard_map/ppermute | solution.py:25
  83.3 15.6 %collective-permute-start.11 = (f32[2,256,256]{2,1,0:T(8,128)S(1)}, f32[2,256,256]{2,1,0:T(8,128)S(1)}, u32[]{:S(2)}, u32[]{:S(2)}) collective-permute-start(f32[2,256,256]{2,1,0:T(8,128)S(1)} %get-tuple-element.35.refs_8_), channel_id=1, source_target_pairs={{0,1},{1,0},{2,3},{3,2},{4,5},{5,4},{6,7},{7,6},{8,9},{9,8},{10,11... | collective-permute-start | bytes 1572872 | tf_op jit(solution)/shard_map/ppermute | solution.py:30
  83.4 16.5 %collective-permute-start.24 = (f32[2,256,256]{2,1,0:T(8,128)S(1)}, f32[2,256,256]{2,1,0:T(8,128)S(1)}, u32[]{:S(2)}, u32[]{:S(2)}) collective-permute-start(f32[2,256,256]{2,1,0:T(8,128)S(1)} %get-tuple-element.42), channel_id=1, source_target_pairs={{0,2},{2,0},{1,3},{3,1},{4,6},{6,4},{5,7},{7,5},{8,10},{10,8},{9,1... | collective-permute-start | bytes 1572872 | tf_op jit(solution)/shard_map/ppermute | solution.py:30
  84.3 16.8 %collective-permute-start.22 = (f32[2,256,256]{2,1,0:T(8,128)S(1)}, f32[2,256,256]{2,1,0:T(8,128)S(1)}, u32[]{:S(2)}, u32[]{:S(2)}) collective-permute-start(f32[2,256,256]{2,1,0:T(8,128)S(1)} %get-tuple-element.41.refs_14_), channel_id=1, source_target_pairs={{0,4},{4,8},{8,12},{1,5},{5,9},{9,13},{2,6},{6,10},{10,14},{3,7},{... | collective-permute-start | bytes 1572872 | tf_op jit(solution)/shard_map/ppermute | solution.py:25
  85.6 15.7 %collective-permute-start.19 = (f32[2,256,256]{2,1,0:T(8,128)S(1)}, f32[2,256,256]{2,1,0:T(8,128)S(1)}, u32[]{:S(2)}, u32[]{:S(2)}) collective-permute-start(f32[2,256,256]{2,1,0:T(8,128)S(1)} %get-tuple-element.41.refs_14_), channel_id=1, source_target_pairs={{0,1},{1,0},{2,3},{3,2},{4,5},{5,4},{6,7},{7,6},{8,9},{9,8},{10,11... | collective-permute-start | bytes 1572872 | tf_op jit(solution)/shard_map/ppermute | solution.py:30
  94.8 14.8 %collective-permute-start.20 = (f32[2,256,256]{2,1,0:T(8,128)S(1)}, f32[2,256,256]{2,1,0:T(8,128)S(1)}, u32[]{:S(2)}, u32[]{:S(2)}) collective-permute-start(f32[2,256,256]{2,1,0:T(8,128)S(1)} %collective-permute-done.14.refs_12_), channel_id=1, source_target_pairs={{4,0},{8,4},{12,8},{5,1},{9,5},{13,9},{6,2},{10,6},{14,10},{7,3},{... | collective-permute-start | bytes 1572872 | tf_op jit(solution)/shard_map/ppermute | solution.py:25
  98.9 12.1 %collective-permute-start.15 = (f32[2,256,256]{2,1,0:T(8,128)S(1)}, f32[2,256,256]{2,1,0:T(8,128)S(1)}, u32[]{:S(2)}, u32[]{:S(2)}) collective-permute-start(f32[2,256,256]{2,1,0:T(8,128)S(1)} %collective-permute-done.14.refs_12_), channel_id=1, source_target_pairs={{0,1},{1,0},{2,3},{3,2},{4,5},{5,4},{6,7},{7,6},{8,9},{9,8},{10,11... | collective-permute-start | bytes 1572872 | tf_op jit(solution)/shard_map/ppermute | solution.py:30
  99.9 15.4 %collective-permute-start.26 = (f32[2,256,256]{2,1,0:T(8,128)S(1)}, f32[2,256,256]{2,1,0:T(8,128)S(1)}, u32[]{:S(2)}, u32[]{:S(2)}) collective-permute-start(f32[2,256,256]{2,1,0:T(8,128)S(1)} %collective-permute-done.24.refs_9_), channel_id=1, source_target_pairs={{0,4},{4,8},{8,12},{1,5},{5,9},{9,13},{2,6},{6,10},{10,14},{3,7},{... | collective-permute-start | bytes 1572872 | tf_op jit(solution)/shard_map/ppermute | solution.py:25
  101.2 14.9 %collective-permute-start.13 = (f32[2,256,256]{2,1,0:T(8,128)S(1)}, f32[2,256,256]{2,1,0:T(8,128)S(1)}, u32[]{:S(2)}, u32[]{:S(2)}) collective-permute-start(f32[2,256,256]{2,1,0:T(8,128)S(1)} %collective-permute-done.12.refs_10_), channel_id=1, source_target_pairs={{0,1},{1,0},{2,3},{3,2},{4,5},{5,4},{6,7},{7,6},{8,9},{9,8},{10,11... | collective-permute-start | bytes 1572872 | tf_op jit(solution)/shard_map/ppermute | solution.py:30
  101.3 17.9 %collective-permute-start.25 = (f32[2,256,256]{2,1,0:T(8,128)S(1)}, f32[2,256,256]{2,1,0:T(8,128)S(1)}, u32[]{:S(2)}, u32[]{:S(2)}) collective-permute-start(f32[2,256,256]{2,1,0:T(8,128)S(1)} %collective-permute-done.24.refs_9_), channel_id=1, source_target_pairs={{0,1},{1,0},{2,3},{3,2},{4,5},{5,4},{6,7},{7,6},{8,9},{9,8},{10,11... | collective-permute-start | bytes 1572872 | tf_op jit(solution)/shard_map/ppermute | solution.py:30
  109.6 9.6 %collective-permute-start.23 = (f32[2,256,256]{2,1,0:T(8,128)S(1)}, f32[2,256,256]{2,1,0:T(8,128)S(1)}, u32[]{:S(2)}, u32[]{:S(2)}) collective-permute-start(f32[2,256,256]{2,1,0:T(8,128)S(1)} %collective-permute-done.22.refs_7_), channel_id=1, source_target_pairs={{0,1},{1,0},{2,3},{3,2},{4,5},{5,4},{6,7},{7,6},{8,9},{9,8},{10,11... | collective-permute-start | bytes 1572872 | tf_op jit(solution)/shard_map/ppermute | solution.py:30
  111.0 8.1 %collective-permute-start.21 = (f32[2,256,256]{2,1,0:T(8,128)S(1)}, f32[2,256,256]{2,1,0:T(8,128)S(1)}, u32[]{:S(2)}, u32[]{:S(2)}) collective-permute-start(f32[2,256,256]{2,1,0:T(8,128)S(1)} %collective-permute-done.20.refs_5_), channel_id=1, source_target_pairs={{0,1},{1,0},{2,3},{3,2},{4,5},{5,4},{6,7},{7,6},{8,9},{9,8},{10,11... | collective-permute-start | bytes 1572872 | tf_op jit(solution)/shard_map/ppermute | solution.py:30
  115.3 3.9 %collective-permute-start.27 = (f32[2,256,256]{2,1,0:T(8,128)S(1)}, f32[2,256,256]{2,1,0:T(8,128)S(1)}, u32[]{:S(2)}, u32[]{:S(2)}) collective-permute-start(f32[2,256,256]{2,1,0:T(8,128)S(1)} %collective-permute-done.26.refs_11_), channel_id=1, source_target_pairs={{0,1},{1,0},{2,3},{3,2},{4,5},{5,4},{6,7},{7,6},{8,9},{9,8},{10,11... | collective-permute-start | bytes 1572872 | tf_op jit(solution)/shard_map/ppermute | solution.py:30

commit v3 on v2

--- a/solution.py
+++ b/solution.py
@@ -12,11 +12,19 @@
 COS = [(-1.0) ** k / math.factorial(2 * k) for k in range(8)]
 VMEM = pl.BlockSpec(memory_space=pltpu.VMEM)
 SMEM = pl.BlockSpec(memory_space=pltpu.SMEM)
-ANY = pl.BlockSpec(memory_space=pl.ANY)
+HBM = pl.BlockSpec(memory_space=pltpu.HBM)
 
 
 def params(mib):
     return pltpu.CompilerParams(vmem_limit_bytes=mib << 20)
+
+
+def cost(microseconds):
+    return pl.CostEstimate(flops=int(microseconds * 1e9), transcendentals=0, bytes_accessed=0)
+
+
+def after(value, *others):
+    return lax.optimization_barrier((value, *others))[0]
 
 
 def move(block, axis, distance):
@@ -117,7 +125,17 @@
     return damping * cosine, damping * sine * phase
 
 
-def slot_kernel(kind, base, each, sections, pairs, probe, measured, *refs):
+def slot_kernel(kind, *args):
+    if kind == "last":
+
+        @pl.when(lax.axis_index("tile") == lax.axis_size("tile") - 1)
+        def _():
+            slot_body(kind, *args)
+    else:
+        slot_body(kind, *args)
+
+
+def slot_body(kind, base, each, sections, pairs, probe, measured, *refs):
     pieces = 1 if kind == "last" else 2
     own = refs[:pieces]
     others = refs[pieces : pieces + sections - 1]
@@ -182,7 +200,7 @@
         scratch += [pltpu.VMEM((side, side), jnp.float32), pltpu.SemaphoreType.DMA(())]
     return pl.pallas_call(
         lambda *refs: slot_kernel(kind, base, each, sections, *refs),
-        in_specs=[SMEM, VMEM, VMEM if kind == "up" else ANY]
+        in_specs=[SMEM, VMEM, VMEM if kind == "up" else HBM]
         + [VMEM] * (len(own) + len(others) + 4),
         out_specs=[VMEM] * sections,
         out_shape=[shape] * sections,
@@ -255,7 +273,7 @@
         inputs.append(measured)
     return pl.pallas_call(
         lambda *refs: cut_kernel(bases, sections, send, *refs),
-        in_specs=[SMEM] + [ANY] * (len(inputs) - 1),
+        in_specs=[SMEM] + [HBM] * (len(inputs) - 1),
         out_specs=[VMEM] * len(shapes),
         out_shape=shapes,
         scratch_shapes=scratch,
@@ -283,6 +301,37 @@
         compiler_params=params(8),
         name="join",
     )(pairs, here, there)
+
+
+def pack_kernel(*refs):
+    out = refs[-1]
+    for k, term in enumerate(refs[:-1]):
+        out[k] = term[...]
+
+
+def pack(terms):
+    if len(terms) == 1:
+        return terms[0][None]
+    return pl.pallas_call(
+        pack_kernel,
+        in_specs=[VMEM] * len(terms),
+        out_specs=VMEM,
+        out_shape=jax.ShapeDtypeStruct((len(terms), *terms[0].shape), jnp.float32),
+        compiler_params=params(8),
+        name="pack",
+    )(*terms)
+
+
+def spread(metas, terms):
+    views, kinds = [], []
+    for kind, term in zip(metas, terms):
+        if isinstance(kind, list):
+            views += [term.at[i] for i in range(len(kind))]
+            kinds += kind
+        else:
+            views.append(term)
+            kinds.append(kind)
+    return views, kinds
 
 
 def spans(metas, tables, side, sections):
@@ -307,6 +356,7 @@
 def early_kernel(metas, sections, *refs):
     count = len(metas)
     tables, terms, out = refs[:4], refs[4 : 4 + count], refs[4 + count]
+    terms, metas = spread(metas, terms)
     side = terms[0].shape[-1]
     blocks = out.shape[-1] // side
     rows = lax.broadcasted_iota(jnp.int32, (side, side), 0)
@@ -338,6 +388,7 @@
         out_specs=VMEM,
         out_shape=jax.ShapeDtypeStruct((2, side, cols_total), jnp.float32),
         compiler_params=params(20),
+        cost_estimate=cost(4),
         name="early",
     )(*tables, *terms)
 
@@ -352,29 +403,46 @@
     lane = lax.broadcasted_iota(jnp.int32, (side, side), 1)
     ranges = spans(metas, tables, side, sections)
 
-    def send(block):
-        place = pl.ds(pl.multiple_of(block * side, side), side)
-        return pltpu.make_async_copy(stage.at[:, :, place], out.at[:, 0, :, place], sems.at[block])
+    def place(block):
+        return pl.ds(pl.multiple_of(block * side, side), side)
+
+    def send(block, source):
+        where = place(block)
+        return pltpu.make_async_copy(source.at[:, :, where], out.at[:, 0, :, where], sems.at[block])
+
+    def touched(block):
+        hit = jnp.bool_(False)
+        for first, col, low, high in ranges:
+            hit = hit | (((block == first) | (block == first + 1)) & (high > low))
+        return hit
 
     @pl.loop(0, blocks)
     def _(block):
-        place = pl.ds(pl.multiple_of(block * side, side), side)
-        stage[:, :, place] = total[:, :, place]
-        for k, (first, col, low, high) in enumerate(ranges):
-            for half in range(2):
-
-                @pl.when((first + half == block) & (high > low))
-                def _():
-                    keep = (rows >= low) & (rows < high)
-                    keep = keep & ((lane < col) if half else (lane >= col))
-                    for part in range(2):
-                        stage[part, :, place] += jnp.where(keep, terms[k][part], 0.0)
-
-        send(block).start()
+        @pl.when(jnp.logical_not(touched(block)))
+        def _():
+            send(block, total).start()
 
     @pl.loop(0, blocks)
     def _(block):
-        send(block).wait()
+        @pl.when(touched(block))
+        def _():
+            where = place(block)
+            stage[:, :, where] = total[:, :, where]
+            for k, (first, col, low, high) in enumerate(ranges):
+                for half in range(2):
+
+                    @pl.when((first + half == block) & (high > low))
+                    def _():
+                        keep = (rows >= low) & (rows < high)
+                        keep = keep & ((lane < col) if half else (lane >= col))
+                        for part in range(2):
+                            stage[part, :, where] += jnp.where(keep, terms[k][part], 0.0)
+
+            send(block, stage).start()
+
+    @pl.loop(0, blocks)
+    def _(block):
+        send(block, stage).wait()
 
 
 def late(metas, tables, total, terms):
@@ -384,7 +452,7 @@
     return pl.pallas_call(
         lambda *refs: late_kernel(metas, sections, *refs),
         in_specs=[SMEM] * 4 + [VMEM] * (1 + len(terms)),
-        out_specs=ANY,
+        out_specs=HBM,
         out_shape=jax.ShapeDtypeStruct((2, 1, side, cols_total), jnp.float32),
         scratch_shapes=[
             pltpu.VMEM((2, side, cols_total), jnp.float32),
@@ -410,75 +478,129 @@
     up = lambda k, d: (sections * n_here + k, n_up, d)
     back = lambda d: (sections - d) % sections
 
+    far = distances[1:]
+    phase = pltpu.with_memory_space_constraint(phase, pltpu.HBM)
+    absorption = pltpu.with_memory_space_constraint(absorption, pltpu.HBM)
+    measured = pltpu.with_memory_space_constraint(measured, pltpu.HBM)
+    done = [pairs]
+
+    def step(kernel, scalars, *args):
+        out = kernel(after(scalars, *done), *args)
+        done[:] = [out[0] if isinstance(out, (list, tuple)) else out]
+        return out
+
+    def cutter(table, kinds, *args):
+        return step(lambda p: cut(kinds, p, phase, absorption, *args), table)
+
+    def joiner(table, kind, *args):
+        return step(lambda p: join(kind, p, *args), table)
+
+    def slotter(table, kind, base, each, *args):
+        return step(lambda p: run_slot(kind, base, each, p, probe, *args, constants), table)
+
     lower, amplitude = [], []
     for k in range(n_up):
-        *cuts, send = cut(
-            [up(k, d) for d in distances], pairs, phase, absorption, measured, (up(k, 0)[0], n_up)
+        *cuts, send = cutter(
+            pairs, [up(k, d) for d in distances], measured, (up(k, 0)[0], n_up)
         )
         lower.append(cuts)
         amplitude.append(send)
-    raised = [[None] * sections for k in range(n_up)]
-    extra = [[None] * sections for k in range(n_up)]
+    extra = [[rotate_last(lower[k][d], d) for d in far] for k in range(n_up)]
+    raised = [[move(after(lower[k][d], below), "tile", 1) for d in far] for k in range(n_up)]
+    low_cuts = [cutter(below, [here(k, d) for d in distances]) for k in range(n_here)]
+    lowered = [[move(low_cuts[k][d], "tile", -1) for d in far] for k in range(n_here)]
+    up_cuts = [cutter(below, [up(k, d) for d in distances]) for k in range(n_up)]
+    own_cuts = [cutter(pairs, [here(k, d) for d in distances]) for k in range(n_here)]
+    constants = expand(side)
+    up_joined = [
+        [joiner(below, up(k, d), raised[k][d - 1], up_cuts[k][d]) for d in far] for k in range(n_up)
+    ]
+    up_other = [[rotate(up_joined[k][d - 1], "slab", d) for d in far] for k in range(n_up)]
     for k in range(n_up):
-        for d in distances[1:] + [0]:
-            raised[k][d] = move(lower[k][d], "tile", 1)
-            extra[k][d] = rotate_last(lower[k][d], d) if d else None
-    amplitude = [move(value, "tile", 1) for value in amplitude]
-    low_cuts = [cut([here(k, d) for d in distances], below, phase, absorption) for k in range(n_here)]
-    lowered = [[None] * sections for k in range(n_here)]
+        raised[k].insert(0, move(after(lower[k][0], *done), "tile", 1))
+        amplitude[k] = move(after(amplitude[k], *done), "tile", 1)
+    here_joined = [
+        [joiner(pairs, here(k, d), own_cuts[k][d], lowered[k][d - 1]) for d in far]
+        for k in range(n_here)
+    ]
+    here_other = [[rotate(here_joined[k][d - 1], "slab", d) for d in far] for k in range(n_here)]
     for k in range(n_here):
-        for d in distances[1:] + [0]:
-            lowered[k][d] = move(low_cuts[k][d], "tile", -1)
-    constants = expand(side)
-    up_cuts = [cut([up(k, d) for d in distances], below, phase, absorption) for k in range(n_up)]
-    own_cuts = [cut([here(k, d) for d in distances], pairs, phase, absorption) for k in range(n_here)]
-
-    mine, metas = [], []
-    final, final_metas = [], []
-    tables = [pairs, below, rotate(pairs, "batch", 1), rotate(below, "batch", 1)]
-
-    def add(term, source, base, mode, is_final=False):
-        for other in range(2):
-            value = rotate(term, "batch", 1) if other else term
-            (final if is_final else mine).append(value)
-            (final_metas if is_final else metas).append((source + 2 * other, base, mode))
-
+        lowered[k].insert(0, move(after(low_cuts[k][0], *done), "tile", -1))
+
+    other_pairs, other_below = rotate(pairs, "batch", 1), rotate(below, "batch", 1)
+    done += [other_pairs, other_below]
+    tables = [pairs, below, other_pairs, other_below]
+
+    last_outs = [
+        slotter(pairs, "last", up(k, 0)[0], n_up, measured, [lower[k][0]], extra[k])
+        for k in range(n_up)
+    ]
+    up_outs = [
+        slotter(
+            below, "up", up(k, 0)[0], n_up, amplitude[k], [raised[k][0], up_cuts[k][0]], up_other[k]
+        )
+        for k in range(n_up)
+    ]
+    up_back = [[rotate(up_outs[k][d], "slab", d) for d in far] for k in range(n_up)]
+    fallen = [move(up_outs[k][0], "tile", -1) for k in range(n_up)]
+    here_outs = [
+        slotter(
+            pairs, "here", here(k, 0)[0], n_here, measured,
+            [own_cuts[k][0], lowered[k][0]], here_other[k],
+        )
+        for k in range(n_here)
+    ]
+    here_back = [[rotate(here_outs[k][d], "slab", d) for d in far] for k in range(n_here)]
+    risen = [move(here_outs[k][0], "tile", 1) for k in range(n_here)]
+
+    twin = lambda kind: (kind[0] + 2, kind[1], kind[2])
+    terms, kinds = [], []
+
+    def group(items, gate=None):
+        values = [value for value, kind in items]
+        if gate is not None:
+            values[0] = after(values[0], gate)
+        twins = rotate(pack(values), "batch", 1)
+        terms.extend(values + [twins])
+        kinds.extend([kind for value, kind in items] + [[twin(kind) for value, kind in items]])
+        return twins
+
+    items = []
+    for k in range(n_here):
+        items.append((here_outs[k][0], (0, here(k, 0), "above")))
     for k in range(n_up):
-        others = extra[k][1:]
-        done = run_slot(
-            "last", up(k, 0)[0], n_up, pairs, probe, measured, [lower[k][0]], others, constants
-        )
-        for d in distances:
-            value = rotate_last(done[d], d) if d else done[d]
-            add(value, 0, up(k, back(d)), "last")
+        items.append((last_outs[k][0], (0, up(k, 0), "last")))
+        items.append((up_outs[k][0], (1, up(k, 0), "below")))
+        items.append((fallen[k], (0, up(k, 0), "inner")))
+        for d in far:
+            items.append((up_back[k][d - 1], (1, up(k, back(d)), "below")))
+    gate = group(items)
+    falling = [[move(value, "tile", -1) for value in row] for row in up_back]
+    rising = [[move(value, "tile", 1) for value in row] for row in here_back]
+    ending = [
+        [rotate_last(after(last_outs[k][d], *here_back[0]), d) for d in far] for k in range(n_up)
+    ]
+    items = []
+    for k in range(n_here):
+        items.append((risen[k], (1, here(k, 0), "below")))
+        for d in far:
+            items.append((here_back[k][d - 1], (0, here(k, back(d)), "above")))
+    group(items, gate)
+    total = early(kinds, tables, terms, cols_total)
+    final, final_kinds = [], []
+
+    def add(value, kind):
+        final.extend([value, rotate(after(value, total), "batch", 1)])
+        final_kinds.extend([kind, twin(kind)])
+
     for k in range(n_up):
-        others = [
-            rotate(join(up(k, d), below, raised[k][d], up_cuts[k][d]), "slab", d)
-            for d in distances[1:]
-        ]
-        done = run_slot(
-            "up", up(k, 0)[0], n_up, below, probe, amplitude[k],
-            [raised[k][0], up_cuts[k][0]], others, constants,
-        )
-        for d in distances:
-            value = rotate(done[d], "slab", d) if d else done[d]
-            add(value, 1, up(k, back(d)), "below")
-            add(move(value, "tile", -1), 0, up(k, back(d)), "inner", d > 0)
+        for d in far:
+            add(falling[k][d - 1], (0, up(k, back(d)), "inner"))
+            add(ending[k][d - 1], (0, up(k, back(d)), "last"))
     for k in range(n_here):
-        others = [
-            rotate(join(here(k, d), pairs, own_cuts[k][d], lowered[k][d]), "slab", d)
-            for d in distances[1:]
-        ]
-        done = run_slot(
-            "here", here(k, 0)[0], n_here, pairs, probe, measured,
-            [own_cuts[k][0], lowered[k][0]], others, constants,
-        )
-        for d in distances:
-            value = rotate(done[d], "slab", d) if d else done[d]
-            add(value, 0, here(k, back(d)), "above", d > 0)
-            add(move(value, "tile", 1), 1, here(k, back(d)), "below", True)
-    total = early(metas, tables, mine, cols_total)
-    return late(final_metas, tables, total, final)
+        for d in far:
+            add(rising[k][d - 1], (1, here(k, back(d)), "below"))
+    return late(final_kinds, tables, total, final)
 
 
 def solution(mesh):

time: 125 us -> 112 us (0.90)
  the two profiles are of different devices: /device:TPU:29 before, /device:TPU:0 now
where the time goes in v3:
time: 112 us; the launch traced here: 111 us
  waiting for transfers between devices  43.2 us (39%)
  starting transfers between devices  35.1 us (31%)
  Pallas kernels  31.9 us (28%)
    ppermute x10, waiting for transfers between devices, move(): return lax.ppermute(block, axis, route)  34.6 us
    ppermute x10, starting transfers between devices, move(): return lax.ppermute(block, axis, route)  28.5 us
    pallas_call x3, Pallas kernels, run_slot(): pl.pallas_call(lambda *refs: slot_kernel(kind, base, each, sections, *ref...  14.7 us
    pallas_call x4, Pallas kernels, cut(): pl.pallas_call(lambda *refs: cut_kernel(bases, sections, send, *refs), in...  8.97 us
    ppermute x11, waiting for transfers between devices, rotate(): lax.ppermute(block, axis, [(i, (i + distance) % size) for i in range(size)])  8.56 us
    ppermute x11, starting transfers between devices, rotate(): lax.ppermute(block, axis, [(i, (i + distance) % size) for i in range(size)])  5.22 us
    pallas_call x1, Pallas kernels, late(): pl.pallas_call(lambda *refs: late_kernel(metas, sections, *refs), in_spec...  4.06 us
    pallas_call x1, Pallas kernels, early(): pl.pallas_call(lambda *refs: early_kernel(metas, sections, *refs), in_spe...  2.28 us
  transfers between devices with their start and end apart: 23, of which 13 were waited for; matrix products, arithmetic and copies ran while one was open for 0% of the time, Pallas kernels for 25%

profile of v3, /device:TPU:0, one launch (start us, length us, event | category | flops | bytes accessed | tf_op | source)
XLA Modules:
  0.0 111.4 jit_solution(12205899657748517470)
XLA Ops:
  0.0 4.9 %collective-permute-start = (s32[2,4]{1,0:T(2,128)}, s32[2,4]{1,0:T(2,128)S(1)}, u32[]{:S(2)}, u32[]{:S(2)}) collective-permute-start(s32[2,4]{1,0:T(2,128)} %bitcast.1), channel_id=1, source_target_pairs={{0,4},{4,8},{8,12},{1,5},{5,9},{9,13},{2,6},{6,10},{10,14},{3,7},{... | collective-permute-start | bytes 104 | tf_op jit(solution)/shard_map/ppermute | solution.py:33
  4.9 0.7 copy-done.2
  5.6 2.2 %cut.4 = (f32[2,256,256]{2,1,0:T(8,128)S(1)}, f32[2,256,256]{2,1,0:T(8,128)S(1)}, f32[256,256]{1,0:T(8,128)S(1)}) custom-call(s32[2,4]{1,0:T(2,128)S(1)} %bitcast.2, f32[1,256,4096]{2,1,0:T(8,128)} %refs_1_.10, f32[1,256,4096]{2,1,0:T(8,128)} %refs_2_.9, f32[4,256,256]{2,1,0:T(8,128)} %refs_2_.11), custom_call_target="tpu_custom_call" | custom-call | tf_op jit(solution)/shard_map/cut/pallas_call | solution.py:274
  7.9 3.5 %collective-permute-start.3 = (f32[2,256,256]{2,1,0:T(8,128)S(1)}, f32[2,256,256]{2,1,0:T(8,128)S(1)}, u32[]{:S(2)}, u32[]{:S(2)}) collective-permute-start(f32[2,256,256]{2,1,0:T(8,128)S(1)} %get-tuple-element.52), channel_id=1, source_target_pairs={{0,4},{4,8},{8,12},{1,5},{5,9},{9,13},{2,6},{6,10},{10,14},{3,7},{... | collective-permute-start | bytes 1572872 | tf_op jit(solution)/shard_map/ppermute | solution.py:33
  11.4 2.3 %cut.5 = (f32[2,256,256]{2,1,0:T(8,128)S(1)}, f32[2,256,256]{2,1,0:T(8,128)S(1)}) custom-call(s32[2,4]{1,0:T(2,128)S(1)} %collective-permute-done.refs_0_.refs_1_, f32[1,256,4096]{2,1,0:T(8,128)} %refs_1_.10, f32[1,256,4096]{2,1,0:T(8,128)} %refs_2_.9), custom_call_target="tpu_custom_call" | custom-call | tf_op jit(solution)/shard_map/cut/pallas_call | solution.py:274
  13.7 1.3 %collective-permute-start.4 = (f32[2,256,256]{2,1,0:T(8,128)S(1)}, f32[2,256,256]{2,1,0:T(8,128)S(1)}, u32[]{:S(2)}, u32[]{:S(2)}) collective-permute-start(f32[2,256,256]{2,1,0:T(8,128)S(1)} %get-tuple-element.56), channel_id=1, source_target_pairs={{4,0},{8,4},{12,8},{5,1},{9,5},{13,9},{6,2},{10,6},{14,10},{7,3},{... | collective-permute-start | bytes 1572872 | tf_op jit(solution)/shard_map/ppermute | solution.py:33
  15.0 0.7 collective-permute-start.5
  15.7 2.3 %cut.6 = (f32[2,256,256]{2,1,0:T(8,128)S(1)}, f32[2,256,256]{2,1,0:T(8,128)S(1)}) custom-call(s32[2,4]{1,0:T(2,128)S(1)} %collective-permute-done.refs_0_.refs_1_, f32[1,256,4096]{2,1,0:T(8,128)} %refs_1_.10, f32[1,256,4096]{2,1,0:T(8,128)} %refs_2_.9), custom_call_target="tpu_custom_call" | custom-call | tf_op jit(solution)/shard_map/cut/pallas_call | solution.py:274
  18.0 2.2 %cut.7 = (f32[2,256,256]{2,1,0:T(8,128)S(1)}, f32[2,256,256]{2,1,0:T(8,128)S(1)}) custom-call(s32[2,4]{1,0:T(2,128)S(1)} %bitcast.3, f32[1,256,4096]{2,1,0:T(8,128)} %refs_1_.10, f32[1,256,4096]{2,1,0:T(8,128)} %refs_2_.9), custom_call_target="tpu_custom_call" | custom-call | tf_op jit(solution)/shard_map/cut/pallas_call | solution.py:274
  20.2 2.2 %collective-permute-done.3.refs_1_ = f32[2,256,256]{2,1,0:T(8,128)S(1)} collective-permute-done((f32[2,256,256]{2,1,0:T(8,128)S(1)}, f32[2,256,256]{2,1,0:T(8,128)S(1)}, u32[]{:S(2)}, u32[]{:S(2)}) %collective-permute-start.3) | collective-permute-done | bytes 524320 | tf_op jit(solution)/shard_map/ppermute | solution.py:33
  22.4 0.6 join.2
  23.0 4.4 %collective-permute-start.7 = (f32[2,256,256]{2,1,0:T(8,128)S(1)}, f32[2,256,256]{2,1,0:T(8,128)S(1)}, u32[]{:S(2)}, u32[]{:S(2)}) collective-permute-start(f32[2,256,256]{2,1,0:T(8,128)S(1)} %get-tuple-element.66.refs_3_), channel_id=1, source_target_pairs={{0,4},{4,8},{8,12},{1,5},{5,9},{9,13},{2,6},{6,10},{10,14},{3,7},{... | collective-permute-start | bytes 1572872 | tf_op jit(solution)/shard_map/ppermute | solution.py:33
  27.4 1.5 %collective-permute-start.8 = (f32[2,256,256]{2,1,0:T(8,128)S(1)}, f32[2,256,256]{2,1,0:T(8,128)S(1)}, u32[]{:S(2)}, u32[]{:S(2)}) collective-permute-start(f32[2,256,256]{2,1,0:T(8,128)S(1)} %join.2), channel_id=1, source_target_pairs={{0,2},{2,0},{1,3},{3,1},{4,6},{6,4},{5,7},{7,5},{8,10},{10,8},{9,1... | collective-permute-start | bytes 1572872 | tf_op jit(solution)/shard_map/ppermute | solution.py:38
  29.0 3.4 %collective-permute-start.6 = (f32[256,256]{1,0:T(8,128)S(1)}, f32[256,256]{1,0:T(8,128)S(1)}, u32[]{:S(2)}, u32[]{:S(2)}) collective-permute-start(f32[256,256]{1,0:T(8,128)S(1)} %get-tuple-element.65), channel_id=1, source_target_pairs={{0,4},{4,8},{8,12},{1,5},{5,9},{9,13},{2,6},{6,10},{10,14},{3,7},{... | collective-permute-start | bytes 786440 | tf_op jit(solution)/shard_map/ppermute | solution.py:33
  32.4 0.4 expand.1
  32.9 0.1 collective-permute-start.1
  32.9 0.6 join.3
  33.6 0.5 collective-permute-done.1.refs_2_
  34.1 0.2 collective-permute-start.2
  34.3 0.9 collective-permute-done.2.refs_3_
  35.2 0.6 collective-permute-start.10
  35.8 1.3 %collective-permute-start.9 = (f32[2,256,256]{2,1,0:T(8,128)S(1)}, f32[2,256,256]{2,1,0:T(8,128)S(1)}, u32[]{:S(2)}, u32[]{:S(2)}) collective-permute-start(f32[2,256,256]{2,1,0:T(8,128)S(1)} %get-tuple-element.69), channel_id=1, source_target_pairs={{4,0},{8,4},{12,8},{5,1},{9,5},{13,9},{6,2},{10,6},{14,10},{7,3},{... | collective-permute-start | bytes 1572872 | tf_op jit(solution)/shard_map/ppermute | solution.py:33
  37.1 0.6 slot_last.1
  37.7 5.4 %collective-permute-done.6.refs_2_ = f32[256,256]{1,0:T(8,128)S(1)} collective-permute-done((f32[256,256]{1,0:T(8,128)S(1)}, f32[256,256]{1,0:T(8,128)S(1)}, u32[]{:S(2)}, u32[]{:S(2)}) %collective-permute-start.6) | collective-permute-done | bytes 262176 | tf_op jit(solution)/shard_map/ppermute | solution.py:33
  43.1 7.0 %slot_up.1 = (f32[2,256,256]{2,1,0:T(8,128)S(1)}, f32[2,256,256]{2,1,0:T(8,128)S(1)}) custom-call(s32[2,4]{1,0:T(2,128)S(1)} %collective-permute-done.refs_0_.refs_1_, f32[2,256,256]{2,1,0:T(8,128)S(1)} %copy-done, f32[256,256]{1,0:T(8,128)S(1)} %collective-permute-done.6.refs_2_, f32[2,256,256]{2,1,0:T(8,128)S(1)} %collective-permute-done.7.refs_3_, ...), custom_call_target="tpu_custom_call" | custom-call | tf_op jit(solution)/shard_map/slot_up/pallas_call | solution.py:201
  50.1 1.6 %collective-permute-start.12 = (f32[2,256,256]{2,1,0:T(8,128)S(1)}, f32[2,256,256]{2,1,0:T(8,128)S(1)}, u32[]{:S(2)}, u32[]{:S(2)}) collective-permute-start(f32[2,256,256]{2,1,0:T(8,128)S(1)} %get-tuple-element.71), channel_id=1, source_target_pairs={{0,2},{2,0},{1,3},{3,1},{4,6},{6,4},{5,7},{7,5},{8,10},{10,8},{9,1... | collective-permute-start | bytes 1572872 | tf_op jit(solution)/shard_map/ppermute | solution.py:38
  51.7 1.5 %collective-permute-start.11 = (f32[2,256,256]{2,1,0:T(8,128)S(1)}, f32[2,256,256]{2,1,0:T(8,128)S(1)}, u32[]{:S(2)}, u32[]{:S(2)}) collective-permute-start(f32[2,256,256]{2,1,0:T(8,128)S(1)} %get-tuple-element.67.refs_2_.refs_6_), channel_id=1, source_target_pairs={{4,0},{8,4},{12,8},{5,1},{9,5},{13,9},{6,2},{10,6},{14,10},{7,3},{... | collective-permute-start | bytes 1572872 | tf_op jit(solution)/shard_map/ppermute | solution.py:33
  53.2 7.1 %slot_here.1 = (f32[2,256,256]{2,1,0:T(8,128)S(1)}, f32[2,256,256]{2,1,0:T(8,128)S(1)}) custom-call(s32[2,4]{1,0:T(2,128)S(1)} %bitcast.7, f32[2,256,256]{2,1,0:T(8,128)S(1)} %copy-done, f32[4,256,256]{2,1,0:T(8,128)} %refs_2_.11, f32[2,256,256]{2,1,0:T(8,128)S(1)} %get-tuple-element.49.refs_3_, f32[2,256,256]{2,1,0:T(8,128)S(1)} %collective-permute-done.9.refs_4_, ...), custom_call_target="tpu_custom_call" | custom-call | tf_op jit(solution)/shard_map/slot_here/pallas_call | solution.py:201
  60.4 1.9 %collective-permute-done.12.refs_4_.refs_8_ = f32[2,256,256]{2,1,0:T(8,128)S(1)} collective-permute-done((f32[2,256,256]{2,1,0:T(8,128)S(1)}, f32[2,256,256]{2,1,0:T(8,128)S(1)}, u32[]{:S(2)}, u32[]{:S(2)}) %collective-permute-start.12) | collective-permute-done | bytes 524320 | tf_op jit(solution)/shard_map/ppermute | solution.py:38
  62.3 3.5 %collective-permute-done.11.refs_3_.refs_7_ = f32[2,256,256]{2,1,0:T(8,128)S(1)} collective-permute-done((f32[2,256,256]{2,1,0:T(8,128)S(1)}, f32[2,256,256]{2,1,0:T(8,128)S(1)}, u32[]{:S(2)}, u32[]{:S(2)}) %collective-permute-start.11) | collective-permute-done | bytes 524320 | tf_op jit(solution)/shard_map/ppermute | solution.py:33
  65.8 0.2 pack.2
  65.9 0.1 collective-permute-start.13
  66.0 3.7 %collective-permute-start.14 = (f32[2,256,256]{2,1,0:T(8,128)S(1)}, f32[2,256,256]{2,1,0:T(8,128)S(1)}, u32[]{:S(2)}, u32[]{:S(2)}) collective-permute-start(f32[2,256,256]{2,1,0:T(8,128)S(1)} %get-tuple-element.70.refs_0_.refs_4_), channel_id=1, source_target_pairs={{0,4},{4,8},{8,12},{1,5},{5,9},{9,13},{2,6},{6,10},{10,14},{3,7},{... | collective-permute-start | bytes 1572872 | tf_op jit(solution)/shard_map/ppermute | solution.py:33
  69.7 0.5 collective-permute-start.15
  70.2 11.3 %collective-permute-done.14.refs_0_.refs_10_ = f32[2,256,256]{2,1,0:T(8,128)S(1)} collective-permute-done((f32[2,256,256]{2,1,0:T(8,128)S(1)}, f32[2,256,256]{2,1,0:T(8,128)S(1)}, u32[]{:S(2)}, u32[]{:S(2)}) %collective-permute-start.14) | collective-permute-done | bytes 524320 | tf_op jit(solution)/shard_map/ppermute | solution.py:33
  81.5 2.3 %collective-permute-done.15.refs_1_.refs_11_ = f32[2,256,256]{2,1,0:T(8,128)S(1)} collective-permute-done((f32[2,256,256]{2,1,0:T(8,128)S(1)}, f32[2,256,256]{2,1,0:T(8,128)S(1)}, u32[]{:S(2)}, u32[]{:S(2)}) %collective-permute-start.15) | collective-permute-done | bytes 524320 | tf_op jit(solution)/shard_map/ppermute | solution.py:38
  83.9 0.1 collective-permute-start.16
  84.0 3.2 %collective-permute-start.21 = (f32[2,256,256]{2,1,0:T(8,128)S(1)}, f32[2,256,256]{2,1,0:T(8,128)S(1)}, u32[]{:S(2)}, u32[]{:S(2)}) collective-permute-start(f32[2,256,256]{2,1,0:T(8,128)S(1)} %collective-permute-done.15.refs_1_.refs_11_), channel_id=1, source_target_pairs={{0,4},{4,8},{8,12},{1,5},{5,9},{9,13},{2,6},{6,10},{10,14},{3,7},{... | collective-permute-start | bytes 1572872 | tf_op jit(solution)/shard_map/ppermute | solution.py:33
  87.1 0.7 collective-permute-start.19
  87.8 1.3 %collective-permute-start.17 = (f32[2,256,256]{2,1,0:T(8,128)S(1)}, f32[2,256,256]{2,1,0:T(8,128)S(1)}, u32[]{:S(2)}, u32[]{:S(2)}) collective-permute-start(f32[2,256,256]{2,1,0:T(8,128)S(1)} %collective-permute-done.12.refs_4_.refs_8_), channel_id=1, source_target_pairs={{4,0},{8,4},{12,8},{5,1},{9,5},{13,9},{6,2},{10,6},{14,10},{7,3},{... | collective-permute-start | bytes 1572872 | tf_op jit(solution)/shard_map/ppermute | solution.py:33
  89.1 2.3 %early.1.refs_4_ = f32[2,256,4096]{2,1,0:T(8,128)S(1)} custom-call(s32[2,4]{1,0:T(2,128)S(1)} %bitcast.8, s32[2,4]{1,0:T(2,128)S(1)} %collective-permute-done.refs_0_.refs_1_, s32[2,4]{1,0:T(2,128)S(1)} %collective-permute-done.1.refs_2_, s32[2,4]{1,0:T(2,128)S(1)} %collective-permute-done.2.refs_3_, f32[2,256,256]{2,1,0:T(8,128)S(1)} %get-tuple-element.70.refs_0_.refs_4_, ...), custom_call_target="tpu_custom_call" | custom-call | flops 4000000000 | tf_op jit(solution)/shard_map/early/pallas_call | solution.py:385
  91.4 7.5 %collective-permute-done.21.refs_9_ = f32[2,256,256]{2,1,0:T(8,128)S(1)} collective-permute-done((f32[2,256,256]{2,1,0:T(8,128)S(1)}, f32[2,256,256]{2,1,0:T(8,128)S(1)}, u32[]{:S(2)}, u32[]{:S(2)}) %collective-permute-start.21) | collective-permute-done | bytes 524320 | tf_op jit(solution)/shard_map/ppermute | solution.py:33
  98.9 4.8 %collective-permute-done.17.refs_5_ = f32[2,256,256]{2,1,0:T(8,128)S(1)} collective-permute-done((f32[2,256,256]{2,1,0:T(8,128)S(1)}, f32[2,256,256]{2,1,0:T(8,128)S(1)}, u32[]{:S(2)}, u32[]{:S(2)}) %collective-permute-start.17) | collective-permute-done | bytes 524320 | tf_op jit(solution)/shard_map/ppermute | solution.py:33
  103.8 0.5 collective-permute-start.20
  104.3 1.4 %collective-permute-done.18.refs_6_ = f32[2,256,256]{2,1,0:T(8,128)S(1)} collective-permute-done((f32[2,256,256]{2,1,0:T(8,128)S(1)}, f32[2,256,256]{2,1,0:T(8,128)S(1)}, u32[]{:S(2)}, u32[]{:S(2)}) %collective-permute-start.18) | collective-permute-done | bytes 524320 | tf_op jit(solution)/shard_map/ppermute | solution.py:38
  105.7 0.7 collective-permute-done.20.refs_8_
  106.4 0.7 collective-permute-done.22.refs_10_
  107.2 4.1 %late.1 = f32[2,1,256,4096]{3,2,1,0:T(8,128)} custom-call(s32[2,4]{1,0:T(2,128)S(1)} %bitcast.9, s32[2,4]{1,0:T(2,128)S(1)} %collective-permute-done.refs_0_.refs_1_, s32[2,4]{1,0:T(2,128)S(1)} %collective-permute-done.1.refs_2_, s32[2,4]{1,0:T(2,128)S(1)} %collective-permute-done.2.refs_3_, f32[2,256,4096]{2,1,0:T(8,128)S(1)} %early.1.refs_4_, ...), custom_call_target="tpu_custom_call" | custom-call | tf_op jit(solution)/shard_map/late/pallas_call | solution.py:452
  (20 shorter events, 0.1 us)
Async XLA Ops:
  0.0 7.9 %collective-permute-start = (s32[2,4]{1,0:T(2,128)}, s32[2,4]{1,0:T(2,128)S(1)}, u32[]{:S(2)}, u32[]{:S(2)}) collective-permute-start(s32[2,4]{1,0:T(2,128)} %bitcast.1), channel_id=1, source_target_pairs={{0,4},{4,8},{8,12},{1,5},{5,9},{9,13},{2,6},{6,10},{10,14},{3,7},{... | collective-permute-start | bytes 104 | tf_op jit(solution)/shard_map/ppermute | solution.py:33
  4.9 0.7 copy-start.2
  7.9 14.5 %collective-permute-start.3 = (f32[2,256,256]{2,1,0:T(8,128)S(1)}, f32[2,256,256]{2,1,0:T(8,128)S(1)}, u32[]{:S(2)}, u32[]{:S(2)}) collective-permute-start(f32[2,256,256]{2,1,0:T(8,128)S(1)} %get-tuple-element.52), channel_id=1, source_target_pairs={{0,4},{4,8},{8,12},{1,5},{5,9},{9,13},{2,6},{6,10},{10,14},{3,7},{... | collective-permute-start | bytes 1572872 | tf_op jit(solution)/shard_map/ppermute | solution.py:33
  13.7 19.2 %collective-permute-start.4 = (f32[2,256,256]{2,1,0:T(8,128)S(1)}, f32[2,256,256]{2,1,0:T(8,128)S(1)}, u32[]{:S(2)}, u32[]{:S(2)}) collective-permute-start(f32[2,256,256]{2,1,0:T(8,128)S(1)} %get-tuple-element.56), channel_id=1, source_target_pairs={{4,0},{8,4},{12,8},{5,1},{9,5},{13,9},{6,2},{10,6},{14,10},{7,3},{... | collective-permute-start | bytes 1572872 | tf_op jit(solution)/shard_map/ppermute | solution.py:33
  15.0 20.8 %collective-permute-start.5 = (f32[2,256,256]{2,1,0:T(8,128)S(1)}, f32[2,256,256]{2,1,0:T(8,128)S(1)}, u32[]{:S(2)}, u32[]{:S(2)}) collective-permute-start(f32[2,256,256]{2,1,0:T(8,128)S(1)} %get-tuple-element.52), channel_id=1, source_target_pairs={{12,14},{14,12},{13,15},{15,13},{28,30},{30,28},{29,31},{31,29}} | collective-permute-start | bytes 1572872 | tf_op jit(solution)/shard_map/ppermute | solution.py:45
  15.7 2.3 %copy-start.3 = (s32[4,2]{0,1:T(2,128)S(1)}, s32[4,2]{0,1:T(2,128)}, u32[]{:S(2)}) copy-start(s32[4,2]{0,1:T(2,128)} %param.10) | copy-start | bytes 100
  18.0 14.4 %copy-start.1 = (bf16[8,256,256]{2,1,0:T(8,128)(2,1)S(1)}, bf16[8,256,256]{2,1,0:T(8,128)(2,1)}, u32[]{:S(2)}) copy-start(bf16[8,256,256]{2,1,0:T(8,128)(2,1)} %constant.2.clone.pieces) | copy-start | bytes 3145732
  20.2 16.9 %copy-start = (f32[2,256,256]{2,1,0:T(8,128)S(1)}, f32[2,256,256]{2,1,0:T(8,128)}, u32[]{:S(2)}) copy-start(f32[2,256,256]{2,1,0:T(8,128)} %refs_1_.13) | copy-start | bytes 1572868
  23.0 20.1 %collective-permute-start.7 = (f32[2,256,256]{2,1,0:T(8,128)S(1)}, f32[2,256,256]{2,1,0:T(8,128)S(1)}, u32[]{:S(2)}, u32[]{:S(2)}) collective-permute-start(f32[2,256,256]{2,1,0:T(8,128)S(1)} %get-tuple-element.66.refs_3_), channel_id=1, source_target_pairs={{0,4},{4,8},{8,12},{1,5},{5,9},{9,13},{2,6},{6,10},{10,14},{3,7},{... | collective-permute-start | bytes 1572872 | tf_op jit(solution)/shard_map/ppermute | solution.py:33
  27.4 15.7 %collective-permute-start.8 = (f32[2,256,256]{2,1,0:T(8,128)S(1)}, f32[2,256,256]{2,1,0:T(8,128)S(1)}, u32[]{:S(2)}, u32[]{:S(2)}) collective-permute-start(f32[2,256,256]{2,1,0:T(8,128)S(1)} %join.2), channel_id=1, source_target_pairs={{0,2},{2,0},{1,3},{3,1},{4,6},{6,4},{5,7},{7,5},{8,10},{10,8},{9,1... | collective-permute-start | bytes 1572872 | tf_op jit(solution)/shard_map/ppermute | solution.py:38
  29.0 14.1 %collective-permute-start.6 = (f32[256,256]{1,0:T(8,128)S(1)}, f32[256,256]{1,0:T(8,128)S(1)}, u32[]{:S(2)}, u32[]{:S(2)}) collective-permute-start(f32[256,256]{1,0:T(8,128)S(1)} %get-tuple-element.65), channel_id=1, source_target_pairs={{0,4},{4,8},{8,12},{1,5},{5,9},{9,13},{2,6},{6,10},{10,14},{3,7},{... | collective-permute-start | bytes 786440 | tf_op jit(solution)/shard_map/ppermute | solution.py:33
  32.9 1.2 %collective-permute-start.1 = (s32[2,4]{1,0:T(2,128)S(1)}, s32[2,4]{1,0:T(2,128)S(1)}, u32[]{:S(2)}, u32[]{:S(2)}) collective-permute-start(s32[2,4]{1,0:T(2,128)S(1)} %bitcast.4), channel_id=1, source_target_pairs={{0,1},{1,0},{2,3},{3,2},{4,5},{5,4},{6,7},{7,6},{8,9},{9,8},{10,11... | collective-permute-start | bytes 104 | tf_op jit(solution)/shard_map/ppermute | solution.py:38
  34.1 1.1 %collective-permute-start.2 = (s32[2,4]{1,0:T(2,128)S(1)}, s32[2,4]{1,0:T(2,128)S(1)}, u32[]{:S(2)}, u32[]{:S(2)}) collective-permute-start(s32[2,4]{1,0:T(2,128)S(1)} %collective-permute-done.refs_0_.refs_1_), channel_id=1, source_target_pairs={{0,1},{1,0},{2,3},{3,2},{4,5},{5,4},{6,7},{7,6},{8,9},{9,8},{10,11... | collective-permute-start | bytes 104 | tf_op jit(solution)/shard_map/ppermute | solution.py:38
  35.2 18.0 %collective-permute-start.10 = (f32[2,256,256]{2,1,0:T(8,128)S(1)}, f32[2,256,256]{2,1,0:T(8,128)S(1)}, u32[]{:S(2)}, u32[]{:S(2)}) collective-permute-start(f32[2,256,256]{2,1,0:T(8,128)S(1)} %join.3), channel_id=1, source_target_pairs={{0,2},{2,0},{1,3},{3,1},{4,6},{6,4},{5,7},{7,5},{8,10},{10,8},{9,1... | collective-permute-start | bytes 1572872 | tf_op jit(solution)/shard_map/ppermute | solution.py:38
  35.8 17.4 %collective-permute-start.9 = (f32[2,256,256]{2,1,0:T(8,128)S(1)}, f32[2,256,256]{2,1,0:T(8,128)S(1)}, u32[]{:S(2)}, u32[]{:S(2)}) collective-permute-start(f32[2,256,256]{2,1,0:T(8,128)S(1)} %get-tuple-element.69), channel_id=1, source_target_pairs={{4,0},{8,4},{12,8},{5,1},{9,5},{13,9},{6,2},{10,6},{14,10},{7,3},{... | collective-permute-start | bytes 1572872 | tf_op jit(solution)/shard_map/ppermute | solution.py:33
  50.1 12.1 %collective-permute-start.12 = (f32[2,256,256]{2,1,0:T(8,128)S(1)}, f32[2,256,256]{2,1,0:T(8,128)S(1)}, u32[]{:S(2)}, u32[]{:S(2)}) collective-permute-start(f32[2,256,256]{2,1,0:T(8,128)S(1)} %get-tuple-element.71), channel_id=1, source_target_pairs={{0,2},{2,0},{1,3},{3,1},{4,6},{6,4},{5,7},{7,5},{8,10},{10,8},{9,1... | collective-permute-start | bytes 1572872 | tf_op jit(solution)/shard_map/ppermute | solution.py:38
  51.7 14.0 %collective-permute-start.11 = (f32[2,256,256]{2,1,0:T(8,128)S(1)}, f32[2,256,256]{2,1,0:T(8,128)S(1)}, u32[]{:S(2)}, u32[]{:S(2)}) collective-permute-start(f32[2,256,256]{2,1,0:T(8,128)S(1)} %get-tuple-element.67.refs_2_.refs_6_), channel_id=1, source_target_pairs={{4,0},{8,4},{12,8},{5,1},{9,5},{13,9},{6,2},{10,6},{14,10},{7,3},{... | collective-permute-start | bytes 1572872 | tf_op jit(solution)/shard_map/ppermute | solution.py:33
  65.9 15.5 %collective-permute-start.13 = (f32[5,2,256,256]{3,2,1,0:T(8,128)S(1)}, f32[5,2,256,256]{3,2,1,0:T(8,128)S(1)}, u32[]{:S(2)}, u32[]{:S(2)}) collective-permute-start(f32[5,2,256,256]{3,2,1,0:T(8,128)S(1)} %pack.2), channel_id=1, source_target_pairs={{0,1},{1,0},{2,3},{3,2},{4,5},{5,4},{6,7},{7,6},{8,9},{9,8},{10,11... | collective-permute-start | bytes 7864328 | tf_op jit(solution)/shard_map/ppermute | solution.py:38
  66.0 15.5 %collective-permute-start.14 = (f32[2,256,256]{2,1,0:T(8,128)S(1)}, f32[2,256,256]{2,1,0:T(8,128)S(1)}, u32[]{:S(2)}, u32[]{:S(2)}) collective-permute-start(f32[2,256,256]{2,1,0:T(8,128)S(1)} %get-tuple-element.70.refs_0_.refs_4_), channel_id=1, source_target_pairs={{0,4},{4,8},{8,12},{1,5},{5,9},{9,13},{2,6},{6,10},{10,14},{3,7},{... | collective-permute-start | bytes 1572872 | tf_op jit(solution)/shard_map/ppermute | solution.py:33
  69.7 14.1 %collective-permute-start.15 = (f32[2,256,256]{2,1,0:T(8,128)S(1)}, f32[2,256,256]{2,1,0:T(8,128)S(1)}, u32[]{:S(2)}, u32[]{:S(2)}) collective-permute-start(f32[2,256,256]{2,1,0:T(8,128)S(1)} %get-tuple-element.73), channel_id=1, source_target_pairs={{0,2},{2,0},{1,3},{3,1},{4,6},{6,4},{5,7},{7,5},{8,10},{10,8},{9,1... | collective-permute-start | bytes 1572872 | tf_op jit(solution)/shard_map/ppermute | solution.py:38
  83.9 5.3 %collective-permute-start.16 = (f32[2,2,256,256]{3,2,1,0:T(8,128)S(1)}, f32[2,2,256,256]{3,2,1,0:T(8,128)S(1)}, u32[]{:S(2)}, u32[]{:S(2)}) collective-permute-start(f32[2,2,256,256]{3,2,1,0:T(8,128)S(1)} %pack.3), channel_id=1, source_target_pairs={{0,1},{1,0},{2,3},{3,2},{4,5},{5,4},{6,7},{7,6},{8,9},{9,8},{10,11... | collective-permute-start | bytes 3145736 | tf_op jit(solution)/shard_map/ppermute | solution.py:38
  84.0 15.0 %collective-permute-start.21 = (f32[2,256,256]{2,1,0:T(8,128)S(1)}, f32[2,256,256]{2,1,0:T(8,128)S(1)}, u32[]{:S(2)}, u32[]{:S(2)}) collective-permute-start(f32[2,256,256]{2,1,0:T(8,128)S(1)} %collective-permute-done.15.refs_1_.refs_11_), channel_id=1, source_target_pairs={{0,4},{4,8},{8,12},{1,5},{5,9},{9,13},{2,6},{6,10},{10,14},{3,7},{... | collective-permute-start | bytes 1572872 | tf_op jit(solution)/shard_map/ppermute | solution.py:33
  87.1 11.8 %collective-permute-start.19 = (f32[2,256,256]{2,1,0:T(8,128)S(1)}, f32[2,256,256]{2,1,0:T(8,128)S(1)}, u32[]{:S(2)}, u32[]{:S(2)}) collective-permute-start(f32[2,256,256]{2,1,0:T(8,128)S(1)} %get-tuple-element.76), channel_id=1, source_target_pairs={{12,14},{14,12},{13,15},{15,13},{28,30},{30,28},{29,31},{31,29}} | collective-permute-start | bytes 1572872 | tf_op jit(solution)/shard_map/ppermute | solution.py:45
  87.8 15.9 %collective-permute-start.17 = (f32[2,256,256]{2,1,0:T(8,128)S(1)}, f32[2,256,256]{2,1,0:T(8,128)S(1)}, u32[]{:S(2)}, u32[]{:S(2)}) collective-permute-start(f32[2,256,256]{2,1,0:T(8,128)S(1)} %collective-permute-done.12.refs_4_.refs_8_), channel_id=1, source_target_pairs={{4,0},{8,4},{12,8},{5,1},{9,5},{13,9},{6,2},{10,6},{14,10},{7,3},{... | collective-permute-start | bytes 1572872 | tf_op jit(solution)/shard_map/ppermute | solution.py:33
  103.8 1.9 %collective-permute-start.18 = (f32[2,256,256]{2,1,0:T(8,128)S(1)}, f32[2,256,256]{2,1,0:T(8,128)S(1)}, u32[]{:S(2)}, u32[]{:S(2)}) collective-permute-start(f32[2,256,256]{2,1,0:T(8,128)S(1)} %collective-permute-done.17.refs_5_), channel_id=1, source_target_pairs={{0,1},{1,0},{2,3},{3,2},{4,5},{5,4},{6,7},{7,6},{8,9},{9,8},{10,11... | collective-permute-start | bytes 1572872 | tf_op jit(solution)/shard_map/ppermute | solution.py:38
  103.8 2.7 %collective-permute-start.20 = (f32[2,256,256]{2,1,0:T(8,128)S(1)}, f32[2,256,256]{2,1,0:T(8,128)S(1)}, u32[]{:S(2)}, u32[]{:S(2)}) collective-permute-start(f32[2,256,256]{2,1,0:T(8,128)S(1)} %collective-permute-done.19.refs_7_), channel_id=1, source_target_pairs={{0,1},{1,0},{2,3},{3,2},{4,5},{5,4},{6,7},{7,6},{8,9},{9,8},{10,11... | collective-permute-start | bytes 1572872 | tf_op jit(solution)/shard_map/ppermute | solution.py:38
  104.3 2.9 %collective-permute-start.22 = (f32[2,256,256]{2,1,0:T(8,128)S(1)}, f32[2,256,256]{2,1,0:T(8,128)S(1)}, u32[]{:S(2)}, u32[]{:S(2)}) collective-permute-start(f32[2,256,256]{2,1,0:T(8,128)S(1)} %collective-permute-done.21.refs_9_), channel_id=1, source_target_pairs={{0,1},{1,0},{2,3},{3,2},{4,5},{5,4},{6,7},{7,6},{8,9},{9,8},{10,11... | collective-permute-start | bytes 1572872 | tf_op jit(solution)/shard_map/ppermute | solution.py:38

commit v4 on v3

--- a/solution.py
+++ b/solution.py
@@ -149,7 +149,7 @@
     row = lax.rem(pairs[0, index], side)
     col = lax.rem(pairs[1, index], side)
     if kind == "up":
-        amplitude = measured
+        amplitude = measured.at[pl.ds(0, side)]
         fetch = None
     else:
         amplitude, sem = refs[6 + sections :]
@@ -215,13 +215,11 @@
     return base + lax.rem(slab + distance, sections) * each
 
 
-def cut_kernel(bases, sections, send, pairs, phase, absorption, *refs):
+def cut_kernel(bases, sections, pairs, phase, absorption, *refs):
     count = len(bases)
     side = phase.shape[1]
     blocks = phase.shape[2] // side
     slab = lax.axis_index("slab")
-    if send is not None:
-        measured, refs = refs[0], refs[1:]
     outs = refs[:count]
     buffer, sems = refs[-2], refs[-1]
     copies, columns = [], []
@@ -241,10 +239,6 @@
                 )
     for copy in copies:
         copy.start()
-    if send is not None:
-        index = send[0] + slab * send[1]
-        extra = pltpu.make_async_copy(measured.at[index], refs[count], refs[-3])
-        extra.start()
     lane = lax.broadcasted_iota(jnp.int32, (side, side), 1)
     for k in range(count):
         own = lane >= columns[k]
@@ -252,34 +246,55 @@
             for half in range(2):
                 copies[4 * k + 2 * which + half].wait()
             outs[k][which] = jnp.where(own, buffer[k, which, 0], buffer[k, which, 1])
-    if send is not None:
-        extra.wait()
-
-
-def cut(bases, pairs, phase, absorption, measured=None, send=None):
+
+
+def cut(bases, pairs, phase, absorption):
     side = phase.shape[1]
     count = len(bases)
     sections = lax.axis_size("slab")
     shape = jax.ShapeDtypeStruct((2, side, side), jnp.float32)
-    shapes = [shape] * count
     scratch = [
         pltpu.VMEM((count, 2, 2, side, side), jnp.float32),
         pltpu.SemaphoreType.DMA((count, 2, 2)),
     ]
-    inputs = [pairs, phase, absorption]
-    if send is not None:
-        shapes = shapes + [jax.ShapeDtypeStruct((side, side), jnp.float32)]
-        scratch = [pltpu.SemaphoreType.DMA(())] + scratch
-        inputs.append(measured)
-    return pl.pallas_call(
-        lambda *refs: cut_kernel(bases, sections, send, *refs),
-        in_specs=[SMEM] + [HBM] * (len(inputs) - 1),
-        out_specs=[VMEM] * len(shapes),
-        out_shape=shapes,
+    return pl.pallas_call(
+        lambda *refs: cut_kernel(bases, sections, *refs),
+        in_specs=[SMEM, HBM, HBM],
+        out_specs=[VMEM] * count,
+        out_shape=[shape] * count,
         scratch_shapes=scratch,
         compiler_params=params(16),
         name="cut",
-    )(*inputs)
+    )(pairs, phase, absorption)
+
+
+def greet_kernel(base, each, pairs, measured, out, sem):
+    side = measured.shape[-1]
+    slab = lax.axis_index("slab")
+    copy = pltpu.make_async_copy(measured.at[base + slab * each], out.at[pl.ds(0, side)], sem)
+    copy.start()
+    rows = lax.broadcasted_iota(jnp.int32, (8, side), 0)
+    lane = lax.broadcasted_iota(jnp.int32, (8, side), 1)
+    words = jnp.zeros((8, side), jnp.float32)
+    for row in range(2):
+        for col in range(pairs.shape[1]):
+            value = pairs[row, col].astype(jnp.float32)
+            words = jnp.where((rows == row) & (lane == col), value, words)
+    out[pl.ds(side, 8)] = words
+    copy.wait()
+
+
+def greet(base, each, pairs, measured):
+    side = measured.shape[-1]
+    return pl.pallas_call(
+        lambda *refs: greet_kernel(base, each, *refs),
+        in_specs=[SMEM, HBM],
+        out_specs=VMEM,
+        out_shape=jax.ShapeDtypeStruct((side + 8, side), jnp.float32),
+        scratch_shapes=[pltpu.SemaphoreType.DMA(())],
+        compiler_params=params(4),
+        name="greet",
+    )(pairs, measured)
 
 
 def join_kernel(bases, sections, pairs, here, there, out):
@@ -473,7 +488,6 @@
     distances = list(range(sections))
 
     pairs = offsets.T
-    below = move(pairs, "tile", 1)
     here = lambda k, d: (k, n_here, d)
     up = lambda k, d: (sections * n_here + k, n_up, d)
     back = lambda d: (sections - d) % sections
@@ -498,34 +512,35 @@
     def slotter(table, kind, base, each, *args):
         return step(lambda p: run_slot(kind, base, each, p, probe, *args, constants), table)
 
-    lower, amplitude = [], []
-    for k in range(n_up):
-        *cuts, send = cutter(
-            pairs, [up(k, d) for d in distances], measured, (up(k, 0)[0], n_up)
-        )
-        lower.append(cuts)
-        amplitude.append(send)
+    greetings = [
+        move(step(lambda p: greet(up(k, 0)[0], n_up, p, measured), pairs), "tile", 1)
+        for k in range(n_up)
+    ]
+    lower = [cutter(pairs, [up(k, d) for d in distances]) for k in range(n_up)]
+    if n_up:
+        below = greetings[0][side : side + 2, : pairs.shape[1]].astype(jnp.int32)
+    else:
+        below = move(pairs, "tile", 1)
     extra = [[rotate_last(lower[k][d], d) for d in far] for k in range(n_up)]
     raised = [[move(after(lower[k][d], below), "tile", 1) for d in far] for k in range(n_up)]
+    for k in range(n_up):
+        raised[k].insert(0, move(after(lower[k][0], below), "tile", 1))
     low_cuts = [cutter(below, [here(k, d) for d in distances]) for k in range(n_here)]
     lowered = [[move(low_cuts[k][d], "tile", -1) for d in far] for k in range(n_here)]
+    for k in range(n_here):
+        lowered[k].insert(0, move(low_cuts[k][0], "tile", -1))
     up_cuts = [cutter(below, [up(k, d) for d in distances]) for k in range(n_up)]
     own_cuts = [cutter(pairs, [here(k, d) for d in distances]) for k in range(n_here)]
     constants = expand(side)
     up_joined = [
-        [joiner(below, up(k, d), raised[k][d - 1], up_cuts[k][d]) for d in far] for k in range(n_up)
+        [joiner(below, up(k, d), raised[k][d], up_cuts[k][d]) for d in far] for k in range(n_up)
     ]
     up_other = [[rotate(up_joined[k][d - 1], "slab", d) for d in far] for k in range(n_up)]
-    for k in range(n_up):
-        raised[k].insert(0, move(after(lower[k][0], *done), "tile", 1))
-        amplitude[k] = move(after(amplitude[k], *done), "tile", 1)
     here_joined = [
-        [joiner(pairs, here(k, d), own_cuts[k][d], lowered[k][d - 1]) for d in far]
+        [joiner(pairs, here(k, d), own_cuts[k][d], lowered[k][d]) for d in far]
         for k in range(n_here)
     ]
     here_other = [[rotate(here_joined[k][d - 1], "slab", d) for d in far] for k in range(n_here)]
-    for k in range(n_here):
-        lowered[k].insert(0, move(after(low_cuts[k][0], *done), "tile", -1))
 
     other_pairs, other_below = rotate(pairs, "batch", 1), rotate(below, "batch", 1)
     done += [other_pairs, other_below]
@@ -537,7 +552,7 @@
     ]
     up_outs = [
         slotter(
-            below, "up", up(k, 0)[0], n_up, amplitude[k], [raised[k][0], up_cuts[k][0]], up_other[k]
+            below, "up", up(k, 0)[0], n_up, greetings[k], [raised[k][0], up_cuts[k][0]], up_other[k]
         )
         for k in range(n_up)
     ]
@@ -566,25 +581,28 @@
         return twins
 
     items = []
-    for k in range(n_here):
-        items.append((here_outs[k][0], (0, here(k, 0), "above")))
     for k in range(n_up):
         items.append((last_outs[k][0], (0, up(k, 0), "last")))
         items.append((up_outs[k][0], (1, up(k, 0), "below")))
+    gate = group(items) if items else None
+    falling = [
+        [move(after(value, fallen[k]), "tile", -1) for value in up_back[k]] for k in range(n_up)
+    ]
+    rising = [[move(value, "tile", 1) for value in row] for row in here_back]
+    ending = [
+        [rotate_last(after(last_outs[k][d], *here_back[0]), d) for d in far] for k in range(n_up)
+    ]
+    items = []
+    for k in range(n_here):
+        items.append((here_outs[k][0], (0, here(k, 0), "above")))
+        items.append((risen[k], (1, here(k, 0), "below")))
+        for d in far:
+            items.append((here_back[k][d - 1], (0, here(k, back(d)), "above")))
+    for k in range(n_up):
         items.append((fallen[k], (0, up(k, 0), "inner")))
         for d in far:
             items.append((up_back[k][d - 1], (1, up(k, back(d)), "below")))
-    gate = group(items)
-    falling = [[move(value, "tile", -1) for value in row] for row in up_back]
-    rising = [[move(value, "tile", 1) for value in row] for row in here_back]
-    ending = [
-        [rotate_last(after(last_outs[k][d], *here_back[0]), d) for d in far] for k in range(n_up)
-    ]
-    items = []
-    for k in range(n_here):
-        items.append((risen[k], (1, here(k, 0), "below")))
-        for d in far:
-            items.append((here_back[k][d - 1], (0, here(k, back(d)), "above")))
+            items.append((falling[k][d - 1], (0, up(k, back(d)), "inner")))
     group(items, gate)
     total = early(kinds, tables, terms, cols_total)
     final, final_kinds = [], []
@@ -595,7 +613,6 @@
 
     for k in range(n_up):
         for d in far:
-            add(falling[k][d - 1], (0, up(k, back(d)), "inner"))
             add(ending[k][d - 1], (0, up(k, back(d)), "last"))
     for k in range(n_here):
         for d in far:

time: 112 us -> 112 us (level)
  the two profiles are of different devices: /device:TPU:0 before, /device:TPU:29 now
where the time goes in v4:
time: 112 us; the launch traced here: 111 us
  Pallas kernels  40.9 us (37%)
  starting transfers between devices  38 us (34%)
  waiting for transfers between devices  29.9 us (27%)
  local copies, waits for them, and re-layouts  1.37 us (1%)
    pallas_call x3, Pallas kernels, run_slot(): pl.pallas_call(lambda *refs: slot_kernel(kind, base, each, sections, *ref...  21.3 us
    ppermute x9, starting transfers between devices, move(): return lax.ppermute(block, axis, route)  20.3 us
    ppermute x9, waiting for transfers between devices, move(): return lax.ppermute(block, axis, route)  16.7 us
    ppermute x10, waiting for transfers between devices, rotate(): lax.ppermute(block, axis, [(i, (i + distance) % size) for i in range(size)])  12.9 us
    ppermute x10, starting transfers between devices, rotate(): lax.ppermute(block, axis, [(i, (i + distance) % size) for i in range(size)])  12.4 us
    pallas_call x4, Pallas kernels, cut(): pl.pallas_call(lambda *refs: cut_kernel(bases, sections, *refs), in_specs...  8.74 us
    ppermute x2, starting transfers between devices, rotate_last(): return lax.ppermute(block, ('tile', 'slab'), route)  5.24 us
    pallas_call x1, Pallas kernels, late(): pl.pallas_call(lambda *refs: late_kernel(metas, sections, *refs), in_spec...  4.1 us
  transfers between devices with their start and end apart: 21, of which 11 were waited for; matrix products, arithmetic and copies ran while one was open for 0% of the time, Pallas kernels for 32%

profile of v4, /device:TPU:29, one launch (start us, length us, event | category | flops | bytes accessed | tf_op | source)
XLA Modules:
  0.0 110.7 jit_solution(16562659054835417184)
XLA Ops:
  0.0 0.7 copy-done.2
  0.7 1.5 %greet.1 = f32[264,256]{1,0:T(8,128)S(1)} custom-call(s32[2,4]{1,0:T(2,128)S(1)} %bitcast.1, f32[4,256,256]{2,1,0:T(8,128)} %refs_2_.11), custom_call_target="tpu_custom_call" | custom-call | tf_op jit(solution)/shard_map/greet/pallas_call | solution.py:289
  2.2 1.3 %collective-permute-start = (f32[264,256]{1,0:T(8,128)S(1)}, f32[264,256]{1,0:T(8,128)S(1)}, u32[]{:S(2)}, u32[]{:S(2)}) collective-permute-start(f32[264,256]{1,0:T(8,128)S(1)} %greet.1), channel_id=1, source_target_pairs={{0,4},{4,8},{8,12},{1,5},{5,9},{9,13},{2,6},{6,10},{10,14},{3,7},{... | collective-permute-start | bytes 811016 | tf_op jit(solution)/shard_map/ppermute | solution.py:33
  3.5 0.7 copy-done.3
  4.2 2.2 %cut.4 = (f32[2,256,256]{2,1,0:T(8,128)S(1)}, f32[2,256,256]{2,1,0:T(8,128)S(1)}) custom-call(s32[2,4]{1,0:T(2,128)S(1)} %bitcast.2, f32[1,256,4096]{2,1,0:T(8,128)} %refs_1_.12, f32[1,256,4096]{2,1,0:T(8,128)} %refs_2_.9), custom_call_target="tpu_custom_call" | custom-call | tf_op jit(solution)/shard_map/cut/pallas_call | solution.py:260
  6.4 5.1 %collective-permute-done.refs_2_ = f32[264,256]{1,0:T(8,128)S(1)} collective-permute-done((f32[264,256]{1,0:T(8,128)S(1)}, f32[264,256]{1,0:T(8,128)S(1)}, u32[]{:S(2)}, u32[]{:S(2)}) %collective-permute-start) | collective-permute-done | bytes 270368 | tf_op jit(solution)/shard_map/ppermute | solution.py:33
  11.5 1.3 %collective-permute-start.3 = (f32[2,256,256]{2,1,0:T(8,128)S(1)}, f32[2,256,256]{2,1,0:T(8,128)S(1)}, u32[]{:S(2)}, u32[]{:S(2)}) collective-permute-start(f32[2,256,256]{2,1,0:T(8,128)S(1)} %get-tuple-element.51), channel_id=1, source_target_pairs={{0,4},{4,8},{8,12},{1,5},{5,9},{9,13},{2,6},{6,10},{10,14},{3,7},{... | collective-permute-start | bytes 1572872 | tf_op jit(solution)/shard_map/ppermute | solution.py:33
  12.7 2.2 %cut.5 = (f32[2,256,256]{2,1,0:T(8,128)S(1)}, f32[2,256,256]{2,1,0:T(8,128)S(1)}) custom-call(s32[2,4]{1,0:T(2,128)S(1)} %slice_convert_fusion.refs_0_.refs_1_, f32[1,256,4096]{2,1,0:T(8,128)} %refs_1_.12, f32[1,256,4096]{2,1,0:T(8,128)} %refs_2_.9), custom_call_target="tpu_custom_call" | custom-call | tf_op jit(solution)/shard_map/cut/pallas_call | solution.py:260
  14.9 4.0 %collective-permute-start.4 = (f32[2,256,256]{2,1,0:T(8,128)S(1)}, f32[2,256,256]{2,1,0:T(8,128)S(1)}, u32[]{:S(2)}, u32[]{:S(2)}) collective-permute-start(f32[2,256,256]{2,1,0:T(8,128)S(1)} %get-tuple-element.55), channel_id=1, source_target_pairs={{4,0},{8,4},{12,8},{5,1},{9,5},{13,9},{6,2},{10,6},{14,10},{7,3},{... | collective-permute-start | bytes 1572872 | tf_op jit(solution)/shard_map/ppermute | solution.py:33
  19.0 3.1 %collective-permute-start.5 = (f32[2,256,256]{2,1,0:T(8,128)S(1)}, f32[2,256,256]{2,1,0:T(8,128)S(1)}, u32[]{:S(2)}, u32[]{:S(2)}) collective-permute-start(f32[2,256,256]{2,1,0:T(8,128)S(1)} %get-tuple-element.51), channel_id=1, source_target_pairs={{12,14},{14,12},{13,15},{15,13},{28,30},{30,28},{29,31},{31,29}} | collective-permute-start | bytes 1572872 | tf_op jit(solution)/shard_map/ppermute | solution.py:45
  22.1 1.3 %collective-permute-start.6 = (f32[2,256,256]{2,1,0:T(8,128)S(1)}, f32[2,256,256]{2,1,0:T(8,128)S(1)}, u32[]{:S(2)}, u32[]{:S(2)}) collective-permute-start(f32[2,256,256]{2,1,0:T(8,128)S(1)} %get-tuple-element.63.refs_3_), channel_id=1, source_target_pairs={{0,4},{4,8},{8,12},{1,5},{5,9},{9,13},{2,6},{6,10},{10,14},{3,7},{... | collective-permute-start | bytes 1572872 | tf_op jit(solution)/shard_map/ppermute | solution.py:33
  23.4 2.2 %cut.6 = (f32[2,256,256]{2,1,0:T(8,128)S(1)}, f32[2,256,256]{2,1,0:T(8,128)S(1)}) custom-call(s32[2,4]{1,0:T(2,128)S(1)} %slice_convert_fusion.refs_0_.refs_1_, f32[1,256,4096]{2,1,0:T(8,128)} %refs_1_.12, f32[1,256,4096]{2,1,0:T(8,128)} %refs_2_.9), custom_call_target="tpu_custom_call" | custom-call | tf_op jit(solution)/shard_map/cut/pallas_call | solution.py:260
  25.6 2.2 %cut.7 = (f32[2,256,256]{2,1,0:T(8,128)S(1)}, f32[2,256,256]{2,1,0:T(8,128)S(1)}) custom-call(s32[2,4]{1,0:T(2,128)S(1)} %bitcast.3, f32[1,256,4096]{2,1,0:T(8,128)} %refs_1_.12, f32[1,256,4096]{2,1,0:T(8,128)} %refs_2_.9), custom_call_target="tpu_custom_call" | custom-call | tf_op jit(solution)/shard_map/cut/pallas_call | solution.py:260
  27.8 0.6 join.2
  28.5 0.3 collective-permute-start.7
  28.8 2.7 %collective-permute-start.1 = (s32[2,4]{1,0:T(2,128)S(1)}, s32[2,4]{1,0:T(2,128)S(1)}, u32[]{:S(2)}, u32[]{:S(2)}) collective-permute-start(s32[2,4]{1,0:T(2,128)S(1)} %bitcast.4), channel_id=1, source_target_pairs={{0,1},{1,0},{2,3},{3,2},{4,5},{5,4},{6,7},{7,6},{8,9},{9,8},{10,11... | collective-permute-start | bytes 104 | tf_op jit(solution)/shard_map/ppermute | solution.py:38
  31.5 0.4 expand.1
  31.9 0.1 collective-permute-start.2
  32.0 0.6 join.3
  32.6 4.3 %collective-permute-start.9 = (f32[2,256,256]{2,1,0:T(8,128)S(1)}, f32[2,256,256]{2,1,0:T(8,128)S(1)}, u32[]{:S(2)}, u32[]{:S(2)}) collective-permute-start(f32[2,256,256]{2,1,0:T(8,128)S(1)} %get-tuple-element.44), channel_id=1, source_target_pairs={{4,0},{8,4},{12,8},{5,1},{9,5},{13,9},{6,2},{10,6},{14,10},{7,3},{... | collective-permute-start | bytes 1572872 | tf_op jit(solution)/shard_map/ppermute | solution.py:33
  36.9 1.3 %collective-permute-start.10 = (f32[2,256,256]{2,1,0:T(8,128)S(1)}, f32[2,256,256]{2,1,0:T(8,128)S(1)}, u32[]{:S(2)}, u32[]{:S(2)}) collective-permute-start(f32[2,256,256]{2,1,0:T(8,128)S(1)} %join.3), channel_id=1, source_target_pairs={{0,2},{2,0},{1,3},{3,1},{4,6},{6,4},{5,7},{7,5},{8,10},{10,8},{9,1... | collective-permute-start | bytes 1572872 | tf_op jit(solution)/shard_map/ppermute | solution.py:38
  38.2 7.1 %slot_last.1 = (f32[2,256,256]{2,1,0:T(8,128)S(1)}, f32[2,256,256]{2,1,0:T(8,128)S(1)}) custom-call(s32[2,4]{1,0:T(2,128)S(1)} %bitcast.6, f32[2,256,256]{2,1,0:T(8,128)S(1)} %copy-done, f32[4,256,256]{2,1,0:T(8,128)} %refs_2_.11, f32[2,256,256]{2,1,0:T(8,128)S(1)} %get-tuple-element.63.refs_3_, f32[2,256,256]{2,1,0:T(8,128)S(1)} %collective-permute-done.5.refs_4_, ...), custom_call_target="tpu_custom_call" | custom-call | tf_op jit(solution)/shard_map/slot_last/pallas_call | solution.py:201
  45.4 7.0 %slot_up.1 = (f32[2,256,256]{2,1,0:T(8,128)S(1)}, f32[2,256,256]{2,1,0:T(8,128)S(1)}) custom-call(s32[2,4]{1,0:T(2,128)S(1)} %slice_convert_fusion.refs_0_.refs_1_, f32[2,256,256]{2,1,0:T(8,128)S(1)} %copy-done, f32[264,256]{1,0:T(8,128)S(1)} %collective-permute-done.refs_2_, f32[2,256,256]{2,1,0:T(8,128)S(1)} %collective-permute-done.6.refs_3_, ...), custom_call_target="tpu_custom_call" | custom-call | tf_op jit(solution)/shard_map/slot_up/pallas_call | solution.py:201
  52.4 0.1 pack.2
  52.5 3.8 %collective-permute-start.8 = (f32[2,2,256,256]{3,2,1,0:T(8,128)S(1)}, f32[2,2,256,256]{3,2,1,0:T(8,128)S(1)}, u32[]{:S(2)}, u32[]{:S(2)}) collective-permute-start(f32[2,2,256,256]{3,2,1,0:T(8,128)S(1)} %pack.2), channel_id=1, source_target_pairs={{0,1},{1,0},{2,3},{3,2},{4,5},{5,4},{6,7},{7,6},{8,9},{9,8},{10,11... | collective-permute-start | bytes 3145736 | tf_op jit(solution)/shard_map/ppermute | solution.py:38
  56.3 1.3 %collective-permute-start.14 = (f32[2,256,256]{2,1,0:T(8,128)S(1)}, f32[2,256,256]{2,1,0:T(8,128)S(1)}, u32[]{:S(2)}, u32[]{:S(2)}) collective-permute-start(f32[2,256,256]{2,1,0:T(8,128)S(1)} %get-tuple-element.69), channel_id=1, source_target_pairs={{0,2},{2,0},{1,3},{3,1},{4,6},{6,4},{5,7},{7,5},{8,10},{10,8},{9,1... | collective-permute-start | bytes 1572872 | tf_op jit(solution)/shard_map/ppermute | solution.py:38
  57.6 1.5 %collective-permute-start.13 = (f32[2,256,256]{2,1,0:T(8,128)S(1)}, f32[2,256,256]{2,1,0:T(8,128)S(1)}, u32[]{:S(2)}, u32[]{:S(2)}) collective-permute-start(f32[2,256,256]{2,1,0:T(8,128)S(1)} %get-tuple-element.64.refs_1_.refs_5_), channel_id=1, source_target_pairs={{4,0},{8,4},{12,8},{5,1},{9,5},{13,9},{6,2},{10,6},{14,10},{7,3},{... | collective-permute-start | bytes 1572872 | tf_op jit(solution)/shard_map/ppermute | solution.py:33
  59.1 7.1 %slot_here.1 = (f32[2,256,256]{2,1,0:T(8,128)S(1)}, f32[2,256,256]{2,1,0:T(8,128)S(1)}) custom-call(s32[2,4]{1,0:T(2,128)S(1)} %bitcast.7, f32[2,256,256]{2,1,0:T(8,128)S(1)} %copy-done, f32[4,256,256]{2,1,0:T(8,128)} %refs_2_.11, f32[2,256,256]{2,1,0:T(8,128)S(1)} %get-tuple-element.48.refs_3_, f32[2,256,256]{2,1,0:T(8,128)S(1)} %collective-permute-done.9.refs_4_, ...), custom_call_target="tpu_custom_call" | custom-call | tf_op jit(solution)/shard_map/slot_here/pallas_call | solution.py:201
  66.2 0.3 collective-permute-start.12
  66.5 1.3 %collective-permute-start.11 = (f32[2,256,256]{2,1,0:T(8,128)S(1)}, f32[2,256,256]{2,1,0:T(8,128)S(1)}, u32[]{:S(2)}, u32[]{:S(2)}) collective-permute-start(f32[2,256,256]{2,1,0:T(8,128)S(1)} %get-tuple-element.67.refs_0_.refs_7_), channel_id=1, source_target_pairs={{0,4},{4,8},{8,12},{1,5},{5,9},{9,13},{2,6},{6,10},{10,14},{3,7},{... | collective-permute-start | bytes 1572872 | tf_op jit(solution)/shard_map/ppermute | solution.py:33
  67.8 2.0 %collective-permute-done.14.refs_4_.refs_11_ = f32[2,256,256]{2,1,0:T(8,128)S(1)} collective-permute-done((f32[2,256,256]{2,1,0:T(8,128)S(1)}, f32[2,256,256]{2,1,0:T(8,128)S(1)}, u32[]{:S(2)}, u32[]{:S(2)}) %collective-permute-start.14) | collective-permute-done | bytes 524320 | tf_op jit(solution)/shard_map/ppermute | solution.py:38
  69.8 0.3 collective-permute-done.13.refs_3_.refs_10_
  70.1 4.1 %collective-permute-start.15 = (f32[2,256,256]{2,1,0:T(8,128)S(1)}, f32[2,256,256]{2,1,0:T(8,128)S(1)}, u32[]{:S(2)}, u32[]{:S(2)}) collective-permute-start(f32[2,256,256]{2,1,0:T(8,128)S(1)} %collective-permute-done.14.refs_4_.refs_11_), channel_id=1, source_target_pairs={{4,0},{8,4},{12,8},{5,1},{9,5},{13,9},{6,2},{10,6},{14,10},{7,3},{... | collective-permute-start | bytes 1572872 | tf_op jit(solution)/shard_map/ppermute | solution.py:33
  74.3 6.8 %collective-permute-done.12.refs_2_.refs_9_ = f32[2,256,256]{2,1,0:T(8,128)S(1)} collective-permute-done((f32[2,256,256]{2,1,0:T(8,128)S(1)}, f32[2,256,256]{2,1,0:T(8,128)S(1)}, u32[]{:S(2)}, u32[]{:S(2)}) %collective-permute-start.12) | collective-permute-done | bytes 524320 | tf_op jit(solution)/shard_map/ppermute | solution.py:38
  81.0 0.2 collective-permute-done.11.refs_1_.refs_8_
  81.3 3.3 %collective-permute-done.15.refs_5_.refs_12_ = f32[2,256,256]{2,1,0:T(8,128)S(1)} collective-permute-done((f32[2,256,256]{2,1,0:T(8,128)S(1)}, f32[2,256,256]{2,1,0:T(8,128)S(1)}, u32[]{:S(2)}, u32[]{:S(2)}) %collective-permute-start.15) | collective-permute-done | bytes 524320 | tf_op jit(solution)/shard_map/ppermute | solution.py:33
  84.6 0.2 pack.3
  84.8 1.8 %collective-permute-start.16 = (f32[6,2,256,256]{3,2,1,0:T(8,128)S(1)}, f32[6,2,256,256]{3,2,1,0:T(8,128)S(1)}, u32[]{:S(2)}, u32[]{:S(2)}) collective-permute-start(f32[6,2,256,256]{3,2,1,0:T(8,128)S(1)} %pack.3), channel_id=1, source_target_pairs={{0,1},{1,0},{2,3},{3,2},{4,5},{5,4},{6,7},{7,6},{8,9},{9,8},{10,11... | collective-permute-start | bytes 9437192 | tf_op jit(solution)/shard_map/ppermute | solution.py:38
  86.6 1.3 %collective-permute-start.19 = (f32[2,256,256]{2,1,0:T(8,128)S(1)}, f32[2,256,256]{2,1,0:T(8,128)S(1)}, u32[]{:S(2)}, u32[]{:S(2)}) collective-permute-start(f32[2,256,256]{2,1,0:T(8,128)S(1)} %collective-permute-done.12.refs_2_.refs_9_), channel_id=1, source_target_pairs={{0,4},{4,8},{8,12},{1,5},{5,9},{9,13},{2,6},{6,10},{10,14},{3,7},{... | collective-permute-start | bytes 1572872 | tf_op jit(solution)/shard_map/ppermute | solution.py:33
  87.9 2.1 %collective-permute-start.17 = (f32[2,256,256]{2,1,0:T(8,128)S(1)}, f32[2,256,256]{2,1,0:T(8,128)S(1)}, u32[]{:S(2)}, u32[]{:S(2)}) collective-permute-start(f32[2,256,256]{2,1,0:T(8,128)S(1)} %get-tuple-element.72), channel_id=1, source_target_pairs={{12,14},{14,12},{13,15},{15,13},{28,30},{30,28},{29,31},{31,29}} | collective-permute-start | bytes 1572872 | tf_op jit(solution)/shard_map/ppermute | solution.py:45
  90.0 1.9 %collective-permute-done.16.refs_13_ = f32[6,2,256,256]{3,2,1,0:T(8,128)S(1)} collective-permute-done((f32[6,2,256,256]{3,2,1,0:T(8,128)S(1)}, f32[6,2,256,256]{3,2,1,0:T(8,128)S(1)}, u32[]{:S(2)}, u32[]{:S(2)}) %collective-permute-start.16) | collective-permute-done | bytes 3145760 | tf_op jit(solution)/shard_map/ppermute | solution.py:38
  91.9 3.4 %early.1.refs_4_ = f32[2,256,4096]{2,1,0:T(8,128)S(1)} custom-call(s32[2,4]{1,0:T(2,128)S(1)} %bitcast.8, s32[2,4]{1,0:T(2,128)S(1)} %slice_convert_fusion.refs_0_.refs_1_, s32[2,4]{1,0:T(2,128)S(1)} %collective-permute-done.1.refs_2_, s32[2,4]{1,0:T(2,128)S(1)} %collective-permute-done.2.refs_3_, f32[2,256,256]{2,1,0:T(8,128)S(1)} %get-tuple-element.61.refs_0_.refs_4_, ...), custom_call_target="tpu_custom_call" | custom-call | flops 4000000000 | tf_op jit(solution)/shard_map/early/pallas_call | solution.py:400
  95.3 7.7 %collective-permute-done.19.refs_7_ = f32[2,256,256]{2,1,0:T(8,128)S(1)} collective-permute-done((f32[2,256,256]{2,1,0:T(8,128)S(1)}, f32[2,256,256]{2,1,0:T(8,128)S(1)}, u32[]{:S(2)}, u32[]{:S(2)}) %collective-permute-start.19) | collective-permute-done | bytes 524320 | tf_op jit(solution)/shard_map/ppermute | solution.py:33
  103.0 0.3 collective-permute-done.17.refs_5_
  103.3 0.8 collective-permute-start.18
  104.1 1.5 %collective-permute-done.18.refs_6_ = f32[2,256,256]{2,1,0:T(8,128)S(1)} collective-permute-done((f32[2,256,256]{2,1,0:T(8,128)S(1)}, f32[2,256,256]{2,1,0:T(8,128)S(1)}, u32[]{:S(2)}, u32[]{:S(2)}) %collective-permute-start.18) | collective-permute-done | bytes 524320 | tf_op jit(solution)/shard_map/ppermute | solution.py:38
  105.7 0.7 collective-permute-done.20.refs_8_
  106.4 4.1 %late.1 = f32[2,1,256,4096]{3,2,1,0:T(8,128)} custom-call(s32[2,4]{1,0:T(2,128)S(1)} %bitcast.9, s32[2,4]{1,0:T(2,128)S(1)} %slice_convert_fusion.refs_0_.refs_1_, s32[2,4]{1,0:T(2,128)S(1)} %collective-permute-done.1.refs_2_, s32[2,4]{1,0:T(2,128)S(1)} %collective-permute-done.2.refs_3_, f32[2,256,4096]{2,1,0:T(8,128)S(1)} %early.1.refs_4_, ...), custom_call_target="tpu_custom_call" | custom-call | tf_op jit(solution)/shard_map/late/pallas_call | solution.py:467
  (20 shorter events, 0.1 us)
Async XLA Ops:
  0.0 0.7 copy-start.2
  2.2 9.2 %collective-permute-start = (f32[264,256]{1,0:T(8,128)S(1)}, f32[264,256]{1,0:T(8,128)S(1)}, u32[]{:S(2)}, u32[]{:S(2)}) collective-permute-start(f32[264,256]{1,0:T(8,128)S(1)} %greet.1), channel_id=1, source_target_pairs={{0,4},{4,8},{8,12},{1,5},{5,9},{9,13},{2,6},{6,10},{10,14},{3,7},{... | collective-permute-start | bytes 811016 | tf_op jit(solution)/shard_map/ppermute | solution.py:33
  3.5 0.7 copy-start.3
  11.5 16.4 %collective-permute-start.3 = (f32[2,256,256]{2,1,0:T(8,128)S(1)}, f32[2,256,256]{2,1,0:T(8,128)S(1)}, u32[]{:S(2)}, u32[]{:S(2)}) collective-permute-start(f32[2,256,256]{2,1,0:T(8,128)S(1)} %get-tuple-element.51), channel_id=1, source_target_pairs={{0,4},{4,8},{8,12},{1,5},{5,9},{9,13},{2,6},{6,10},{10,14},{3,7},{... | collective-permute-start | bytes 1572872 | tf_op jit(solution)/shard_map/ppermute | solution.py:33
  14.9 17.0 %collective-permute-start.4 = (f32[2,256,256]{2,1,0:T(8,128)S(1)}, f32[2,256,256]{2,1,0:T(8,128)S(1)}, u32[]{:S(2)}, u32[]{:S(2)}) collective-permute-start(f32[2,256,256]{2,1,0:T(8,128)S(1)} %get-tuple-element.55), channel_id=1, source_target_pairs={{4,0},{8,4},{12,8},{5,1},{9,5},{13,9},{6,2},{10,6},{14,10},{7,3},{... | collective-permute-start | bytes 1572872 | tf_op jit(solution)/shard_map/ppermute | solution.py:33
  19.0 19.3 %collective-permute-start.5 = (f32[2,256,256]{2,1,0:T(8,128)S(1)}, f32[2,256,256]{2,1,0:T(8,128)S(1)}, u32[]{:S(2)}, u32[]{:S(2)}) collective-permute-start(f32[2,256,256]{2,1,0:T(8,128)S(1)} %get-tuple-element.51), channel_id=1, source_target_pairs={{12,14},{14,12},{13,15},{15,13},{28,30},{30,28},{29,31},{31,29}} | collective-permute-start | bytes 1572872 | tf_op jit(solution)/shard_map/ppermute | solution.py:45
  22.1 23.3 %collective-permute-start.6 = (f32[2,256,256]{2,1,0:T(8,128)S(1)}, f32[2,256,256]{2,1,0:T(8,128)S(1)}, u32[]{:S(2)}, u32[]{:S(2)}) collective-permute-start(f32[2,256,256]{2,1,0:T(8,128)S(1)} %get-tuple-element.63.refs_3_), channel_id=1, source_target_pairs={{0,4},{4,8},{8,12},{1,5},{5,9},{9,13},{2,6},{6,10},{10,14},{3,7},{... | collective-permute-start | bytes 1572872 | tf_op jit(solution)/shard_map/ppermute | solution.py:33
  23.4 2.2 %copy-start.4 = (s32[4,2]{0,1:T(2,128)S(1)}, s32[4,2]{0,1:T(2,128)}, u32[]{:S(2)}) copy-start(s32[4,2]{0,1:T(2,128)} %param.10) | copy-start | bytes 100
  25.6 5.9 %copy-start.1 = (bf16[8,256,256]{2,1,0:T(8,128)(2,1)S(1)}, bf16[8,256,256]{2,1,0:T(8,128)(2,1)}, u32[]{:S(2)}) copy-start(bf16[8,256,256]{2,1,0:T(8,128)(2,1)} %constant.2.clone.pieces) | copy-start | bytes 3145732
  27.8 10.4 %copy-start = (f32[2,256,256]{2,1,0:T(8,128)S(1)}, f32[2,256,256]{2,1,0:T(8,128)}, u32[]{:S(2)}) copy-start(f32[2,256,256]{2,1,0:T(8,128)} %refs_1_.15) | copy-start | bytes 1572868
  28.5 16.9 %collective-permute-start.7 = (f32[2,256,256]{2,1,0:T(8,128)S(1)}, f32[2,256,256]{2,1,0:T(8,128)S(1)}, u32[]{:S(2)}, u32[]{:S(2)}) collective-permute-start(f32[2,256,256]{2,1,0:T(8,128)S(1)} %join.2), channel_id=1, source_target_pairs={{0,2},{2,0},{1,3},{3,1},{4,6},{6,4},{5,7},{7,5},{8,10},{10,8},{9,1... | collective-permute-start | bytes 1572872 | tf_op jit(solution)/shard_map/ppermute | solution.py:38
  28.8 3.9 %collective-permute-start.1 = (s32[2,4]{1,0:T(2,128)S(1)}, s32[2,4]{1,0:T(2,128)S(1)}, u32[]{:S(2)}, u32[]{:S(2)}) collective-permute-start(s32[2,4]{1,0:T(2,128)S(1)} %bitcast.4), channel_id=1, source_target_pairs={{0,1},{1,0},{2,3},{3,2},{4,5},{5,4},{6,7},{7,6},{8,9},{9,8},{10,11... | collective-permute-start | bytes 104 | tf_op jit(solution)/shard_map/ppermute | solution.py:38
  31.9 5.0 %collective-permute-start.2 = (s32[2,4]{1,0:T(2,128)S(1)}, s32[2,4]{1,0:T(2,128)S(1)}, u32[]{:S(2)}, u32[]{:S(2)}) collective-permute-start(s32[2,4]{1,0:T(2,128)S(1)} %slice_convert_fusion.refs_0_.refs_1_), channel_id=1, source_target_pairs={{0,1},{1,0},{2,3},{3,2},{4,5},{5,4},{6,7},{7,6},{8,9},{9,8},{10,11... | collective-permute-start | bytes 104 | tf_op jit(solution)/shard_map/ppermute | solution.py:38
  32.6 26.4 %collective-permute-start.9 = (f32[2,256,256]{2,1,0:T(8,128)S(1)}, f32[2,256,256]{2,1,0:T(8,128)S(1)}, u32[]{:S(2)}, u32[]{:S(2)}) collective-permute-start(f32[2,256,256]{2,1,0:T(8,128)S(1)} %get-tuple-element.44), channel_id=1, source_target_pairs={{4,0},{8,4},{12,8},{5,1},{9,5},{13,9},{6,2},{10,6},{14,10},{7,3},{... | collective-permute-start | bytes 1572872 | tf_op jit(solution)/shard_map/ppermute | solution.py:33
  36.9 22.1 %collective-permute-start.10 = (f32[2,256,256]{2,1,0:T(8,128)S(1)}, f32[2,256,256]{2,1,0:T(8,128)S(1)}, u32[]{:S(2)}, u32[]{:S(2)}) collective-permute-start(f32[2,256,256]{2,1,0:T(8,128)S(1)} %join.3), channel_id=1, source_target_pairs={{0,2},{2,0},{1,3},{3,1},{4,6},{6,4},{5,7},{7,5},{8,10},{10,8},{9,1... | collective-permute-start | bytes 1572872 | tf_op jit(solution)/shard_map/ppermute | solution.py:38
  52.5 21.8 %collective-permute-start.8 = (f32[2,2,256,256]{3,2,1,0:T(8,128)S(1)}, f32[2,2,256,256]{3,2,1,0:T(8,128)S(1)}, u32[]{:S(2)}, u32[]{:S(2)}) collective-permute-start(f32[2,2,256,256]{3,2,1,0:T(8,128)S(1)} %pack.2), channel_id=1, source_target_pairs={{0,1},{1,0},{2,3},{3,2},{4,5},{5,4},{6,7},{7,6},{8,9},{9,8},{10,11... | collective-permute-start | bytes 3145736 | tf_op jit(solution)/shard_map/ppermute | solution.py:38
  56.3 13.5 %collective-permute-start.14 = (f32[2,256,256]{2,1,0:T(8,128)S(1)}, f32[2,256,256]{2,1,0:T(8,128)S(1)}, u32[]{:S(2)}, u32[]{:S(2)}) collective-permute-start(f32[2,256,256]{2,1,0:T(8,128)S(1)} %get-tuple-element.69), channel_id=1, source_target_pairs={{0,2},{2,0},{1,3},{3,1},{4,6},{6,4},{5,7},{7,5},{8,10},{10,8},{9,1... | collective-permute-start | bytes 1572872 | tf_op jit(solution)/shard_map/ppermute | solution.py:38
  57.6 12.6 %collective-permute-start.13 = (f32[2,256,256]{2,1,0:T(8,128)S(1)}, f32[2,256,256]{2,1,0:T(8,128)S(1)}, u32[]{:S(2)}, u32[]{:S(2)}) collective-permute-start(f32[2,256,256]{2,1,0:T(8,128)S(1)} %get-tuple-element.64.refs_1_.refs_5_), channel_id=1, source_target_pairs={{4,0},{8,4},{12,8},{5,1},{9,5},{13,9},{6,2},{10,6},{14,10},{7,3},{... | collective-permute-start | bytes 1572872 | tf_op jit(solution)/shard_map/ppermute | solution.py:33
  66.2 14.8 %collective-permute-start.12 = (f32[2,256,256]{2,1,0:T(8,128)S(1)}, f32[2,256,256]{2,1,0:T(8,128)S(1)}, u32[]{:S(2)}, u32[]{:S(2)}) collective-permute-start(f32[2,256,256]{2,1,0:T(8,128)S(1)} %get-tuple-element.68), channel_id=1, source_target_pairs={{0,2},{2,0},{1,3},{3,1},{4,6},{6,4},{5,7},{7,5},{8,10},{10,8},{9,1... | collective-permute-start | bytes 1572872 | tf_op jit(solution)/shard_map/ppermute | solution.py:38
  66.5 14.7 %collective-permute-start.11 = (f32[2,256,256]{2,1,0:T(8,128)S(1)}, f32[2,256,256]{2,1,0:T(8,128)S(1)}, u32[]{:S(2)}, u32[]{:S(2)}) collective-permute-start(f32[2,256,256]{2,1,0:T(8,128)S(1)} %get-tuple-element.67.refs_0_.refs_7_), channel_id=1, source_target_pairs={{0,4},{4,8},{8,12},{1,5},{5,9},{9,13},{2,6},{6,10},{10,14},{3,7},{... | collective-permute-start | bytes 1572872 | tf_op jit(solution)/shard_map/ppermute | solution.py:33
  70.1 14.5 %collective-permute-start.15 = (f32[2,256,256]{2,1,0:T(8,128)S(1)}, f32[2,256,256]{2,1,0:T(8,128)S(1)}, u32[]{:S(2)}, u32[]{:S(2)}) collective-permute-start(f32[2,256,256]{2,1,0:T(8,128)S(1)} %collective-permute-done.14.refs_4_.refs_11_), channel_id=1, source_target_pairs={{4,0},{8,4},{12,8},{5,1},{9,5},{13,9},{6,2},{10,6},{14,10},{7,3},{... | collective-permute-start | bytes 1572872 | tf_op jit(solution)/shard_map/ppermute | solution.py:33
  84.8 7.1 %collective-permute-start.16 = (f32[6,2,256,256]{3,2,1,0:T(8,128)S(1)}, f32[6,2,256,256]{3,2,1,0:T(8,128)S(1)}, u32[]{:S(2)}, u32[]{:S(2)}) collective-permute-start(f32[6,2,256,256]{3,2,1,0:T(8,128)S(1)} %pack.3), channel_id=1, source_target_pairs={{0,1},{1,0},{2,3},{3,2},{4,5},{5,4},{6,7},{7,6},{8,9},{9,8},{10,11... | collective-permute-start | bytes 9437192 | tf_op jit(solution)/shard_map/ppermute | solution.py:38
  86.6 16.4 %collective-permute-start.19 = (f32[2,256,256]{2,1,0:T(8,128)S(1)}, f32[2,256,256]{2,1,0:T(8,128)S(1)}, u32[]{:S(2)}, u32[]{:S(2)}) collective-permute-start(f32[2,256,256]{2,1,0:T(8,128)S(1)} %collective-permute-done.12.refs_2_.refs_9_), channel_id=1, source_target_pairs={{0,4},{4,8},{8,12},{1,5},{5,9},{9,13},{2,6},{6,10},{10,14},{3,7},{... | collective-permute-start | bytes 1572872 | tf_op jit(solution)/shard_map/ppermute | solution.py:33
  87.9 15.4 %collective-permute-start.17 = (f32[2,256,256]{2,1,0:T(8,128)S(1)}, f32[2,256,256]{2,1,0:T(8,128)S(1)}, u32[]{:S(2)}, u32[]{:S(2)}) collective-permute-start(f32[2,256,256]{2,1,0:T(8,128)S(1)} %get-tuple-element.72), channel_id=1, source_target_pairs={{12,14},{14,12},{13,15},{15,13},{28,30},{30,28},{29,31},{31,29}} | collective-permute-start | bytes 1572872 | tf_op jit(solution)/shard_map/ppermute | solution.py:45
  103.3 2.3 %collective-permute-start.18 = (f32[2,256,256]{2,1,0:T(8,128)S(1)}, f32[2,256,256]{2,1,0:T(8,128)S(1)}, u32[]{:S(2)}, u32[]{:S(2)}) collective-permute-start(f32[2,256,256]{2,1,0:T(8,128)S(1)} %collective-permute-done.17.refs_5_), channel_id=1, source_target_pairs={{0,1},{1,0},{2,3},{3,2},{4,5},{5,4},{6,7},{7,6},{8,9},{9,8},{10,11... | collective-permute-start | bytes 1572872 | tf_op jit(solution)/shard_map/ppermute | solution.py:38
  104.1 2.3 %collective-permute-start.20 = (f32[2,256,256]{2,1,0:T(8,128)S(1)}, f32[2,256,256]{2,1,0:T(8,128)S(1)}, u32[]{:S(2)}, u32[]{:S(2)}) collective-permute-start(f32[2,256,256]{2,1,0:T(8,128)S(1)} %collective-permute-done.19.refs_7_), channel_id=1, source_target_pairs={{0,1},{1,0},{2,3},{3,2},{4,5},{5,4},{6,7},{7,6},{8,9},{9,8},{10,11... | collective-permute-start | bytes 1572872 | tf_op jit(solution)/shard_map/ppermute | solution.py:38

commit v5 on v3

--- a/solution.py
+++ b/solution.py
@@ -149,7 +149,7 @@
     row = lax.rem(pairs[0, index], side)
     col = lax.rem(pairs[1, index], side)
     if kind == "up":
-        amplitude = measured
+        amplitude = own[0].at[2]
         fetch = None
     else:
         amplitude, sem = refs[6 + sections :]
@@ -200,7 +200,7 @@
         scratch += [pltpu.VMEM((side, side), jnp.float32), pltpu.SemaphoreType.DMA(())]
     return pl.pallas_call(
         lambda *refs: slot_kernel(kind, base, each, sections, *refs),
-        in_specs=[SMEM, VMEM, VMEM if kind == "up" else HBM]
+        in_specs=[SMEM, VMEM, HBM]
         + [VMEM] * (len(own) + len(others) + 4),
         out_specs=[VMEM] * sections,
         out_shape=[shape] * sections,
@@ -220,8 +220,11 @@
     side = phase.shape[1]
     blocks = phase.shape[2] // side
     slab = lax.axis_index("slab")
+    extra = None
     if send is not None:
-        measured, refs = refs[0], refs[1:]
+        extra = (refs[0].at[send[0] + slab * send[1]], refs[1].at[2], refs[-3])
+        extra = pltpu.make_async_copy(*extra)
+        refs = refs[1:]
     outs = refs[:count]
     buffer, sems = refs[-2], refs[-1]
     copies, columns = [], []
@@ -241,9 +244,7 @@
                 )
     for copy in copies:
         copy.start()
-    if send is not None:
-        index = send[0] + slab * send[1]
-        extra = pltpu.make_async_copy(measured.at[index], refs[count], refs[-3])
+    if extra is not None:
         extra.start()
     lane = lax.broadcasted_iota(jnp.int32, (side, side), 1)
     for k in range(count):
@@ -252,7 +253,7 @@
             for half in range(2):
                 copies[4 * k + 2 * which + half].wait()
             outs[k][which] = jnp.where(own, buffer[k, which, 0], buffer[k, which, 1])
-    if send is not None:
+    if extra is not None:
         extra.wait()
 
 
@@ -260,21 +261,20 @@
     side = phase.shape[1]
     count = len(bases)
     sections = lax.axis_size("slab")
-    shape = jax.ShapeDtypeStruct((2, side, side), jnp.float32)
-    shapes = [shape] * count
+    shapes = [jax.ShapeDtypeStruct((2, side, side), jnp.float32)] * count
     scratch = [
         pltpu.VMEM((count, 2, 2, side, side), jnp.float32),
         pltpu.SemaphoreType.DMA((count, 2, 2)),
     ]
     inputs = [pairs, phase, absorption]
     if send is not None:
-        shapes = shapes + [jax.ShapeDtypeStruct((side, side), jnp.float32)]
+        shapes = [jax.ShapeDtypeStruct((3, side, side), jnp.float32)] + shapes[1:]
         scratch = [pltpu.SemaphoreType.DMA(())] + scratch
         inputs.append(measured)
     return pl.pallas_call(
         lambda *refs: cut_kernel(bases, sections, send, *refs),
         in_specs=[SMEM] + [HBM] * (len(inputs) - 1),
-        out_specs=[VMEM] * len(shapes),
+        out_specs=[VMEM] * count,
         out_shape=shapes,
         scratch_shapes=scratch,
         compiler_params=params(16),
@@ -355,7 +355,8 @@
 
 def early_kernel(metas, sections, *refs):
     count = len(metas)
-    tables, terms, out = refs[:4], refs[4 : 4 + count], refs[4 + count]
+    tables, terms = refs[:4], refs[4 : 4 + count]
+    out, copied, sem = refs[4 + count :]
     terms, metas = spread(metas, terms)
     side = terms[0].shape[-1]
     blocks = out.shape[-1] // side
@@ -378,6 +379,10 @@
                 for part in range(2):
                     out[part, :, place] += jnp.where(keep, terms[k][part], 0.0)
 
+    copy = pltpu.make_async_copy(out, copied.at[:, 0], sem)
+    copy.start()
+    copy.wait()
+
 
 def early(metas, tables, terms, cols_total):
     side = terms[0].shape[-1]
@@ -385,10 +390,13 @@
     return pl.pallas_call(
         lambda *refs: early_kernel(metas, sections, *refs),
         in_specs=[SMEM] * 4 + [VMEM] * len(terms),
-        out_specs=VMEM,
-        out_shape=jax.ShapeDtypeStruct((2, side, cols_total), jnp.float32),
+        out_specs=[VMEM, HBM],
+        out_shape=[
+            jax.ShapeDtypeStruct((2, side, cols_total), jnp.float32),
+            jax.ShapeDtypeStruct((2, 1, side, cols_total), jnp.float32),
+        ],
+        scratch_shapes=[pltpu.SemaphoreType.DMA(())],
         compiler_params=params(20),
-        cost_estimate=cost(4),
         name="early",
     )(*tables, *terms)
 
@@ -396,7 +404,7 @@
 def late_kernel(metas, sections, *refs):
     count = len(metas)
     tables, total, terms = refs[:4], refs[4], refs[5 : 5 + count]
-    out, stage, sems = refs[5 + count :]
+    out, stage, sems = refs[6 + count :]
     side = terms[0].shape[-1]
     blocks = out.shape[-1] // side
     rows = lax.broadcasted_iota(jnp.int32, (side, side), 0)
@@ -406,21 +414,15 @@
     def place(block):
         return pl.ds(pl.multiple_of(block * side, side), side)
 
-    def send(block, source):
+    def send(block):
         where = place(block)
-        return pltpu.make_async_copy(source.at[:, :, where], out.at[:, 0, :, where], sems.at[block])
+        return pltpu.make_async_copy(stage.at[:, :, where], out.at[:, 0, :, where], sems.at[block])
 
     def touched(block):
         hit = jnp.bool_(False)
         for first, col, low, high in ranges:
             hit = hit | (((block == first) | (block == first + 1)) & (high > low))
         return hit
-
-    @pl.loop(0, blocks)
-    def _(block):
-        @pl.when(jnp.logical_not(touched(block)))
-        def _():
-            send(block, total).start()
 
     @pl.loop(0, blocks)
     def _(block):
@@ -438,21 +440,24 @@
                         for part in range(2):
                             stage[part, :, where] += jnp.where(keep, terms[k][part], 0.0)
 
-            send(block, stage).start()
+            send(block).start()
 
     @pl.loop(0, blocks)
     def _(block):
-        send(block, stage).wait()
-
-
-def late(metas, tables, total, terms):
+        @pl.when(touched(block))
+        def _():
+            send(block).wait()
+
+
+def late(metas, tables, total, copied, terms):
     side = terms[0].shape[-1]
     cols_total = total.shape[-1]
     sections = lax.axis_size("slab")
     return pl.pallas_call(
         lambda *refs: late_kernel(metas, sections, *refs),
-        in_specs=[SMEM] * 4 + [VMEM] * (1 + len(terms)),
+        in_specs=[SMEM] * 4 + [VMEM] * (1 + len(terms)) + [HBM],
         out_specs=HBM,
+        input_output_aliases={5 + len(terms): 0},
         out_shape=jax.ShapeDtypeStruct((2, 1, side, cols_total), jnp.float32),
         scratch_shapes=[
             pltpu.VMEM((2, side, cols_total), jnp.float32),
@@ -460,7 +465,7 @@
         ],
         compiler_params=params(28),
         name="late",
-    )(*tables, total, *terms)
+    )(*tables, total, *terms, copied)
 
 
 def local(phase, absorption, probe, measured, offsets):
@@ -473,7 +478,6 @@
     distances = list(range(sections))
 
     pairs = offsets.T
-    below = move(pairs, "tile", 1)
     here = lambda k, d: (k, n_here, d)
     up = lambda k, d: (sections * n_here + k, n_up, d)
     back = lambda d: (sections - d) % sections
@@ -498,46 +502,39 @@
     def slotter(table, kind, base, each, *args):
         return step(lambda p: run_slot(kind, base, each, p, probe, *args, constants), table)
 
-    lower, amplitude = [], []
-    for k in range(n_up):
-        *cuts, send = cutter(
-            pairs, [up(k, d) for d in distances], measured, (up(k, 0)[0], n_up)
-        )
-        lower.append(cuts)
-        amplitude.append(send)
+    below = move(pairs, "tile", 1)
+    lower = [
+        cutter(pairs, [up(k, d) for d in distances], measured, (up(k, 0)[0], n_up))
+        for k in range(n_up)
+    ]
     extra = [[rotate_last(lower[k][d], d) for d in far] for k in range(n_up)]
     raised = [[move(after(lower[k][d], below), "tile", 1) for d in far] for k in range(n_up)]
+    for k in range(n_up):
+        raised[k].insert(0, move(after(lower[k][0], below), "tile", 1))
     low_cuts = [cutter(below, [here(k, d) for d in distances]) for k in range(n_here)]
     lowered = [[move(low_cuts[k][d], "tile", -1) for d in far] for k in range(n_here)]
+    for k in range(n_here):
+        lowered[k].insert(0, move(low_cuts[k][0], "tile", -1))
     up_cuts = [cutter(below, [up(k, d) for d in distances]) for k in range(n_up)]
     own_cuts = [cutter(pairs, [here(k, d) for d in distances]) for k in range(n_here)]
     constants = expand(side)
     up_joined = [
-        [joiner(below, up(k, d), raised[k][d - 1], up_cuts[k][d]) for d in far] for k in range(n_up)
+        [joiner(below, up(k, d), raised[k][d], up_cuts[k][d]) for d in far] for k in range(n_up)
     ]
     up_other = [[rotate(up_joined[k][d - 1], "slab", d) for d in far] for k in range(n_up)]
-    for k in range(n_up):
-        raised[k].insert(0, move(after(lower[k][0], *done), "tile", 1))
-        amplitude[k] = move(after(amplitude[k], *done), "tile", 1)
     here_joined = [
-        [joiner(pairs, here(k, d), own_cuts[k][d], lowered[k][d - 1]) for d in far]
+        [joiner(pairs, here(k, d), own_cuts[k][d], lowered[k][d]) for d in far]
         for k in range(n_here)
     ]
     here_other = [[rotate(here_joined[k][d - 1], "slab", d) for d in far] for k in range(n_here)]
-    for k in range(n_here):
-        lowered[k].insert(0, move(after(low_cuts[k][0], *done), "tile", -1))
 
     other_pairs, other_below = rotate(pairs, "batch", 1), rotate(below, "batch", 1)
     done += [other_pairs, other_below]
     tables = [pairs, below, other_pairs, other_below]
 
-    last_outs = [
-        slotter(pairs, "last", up(k, 0)[0], n_up, measured, [lower[k][0]], extra[k])
-        for k in range(n_up)
-    ]
     up_outs = [
         slotter(
-            below, "up", up(k, 0)[0], n_up, amplitude[k], [raised[k][0], up_cuts[k][0]], up_other[k]
+            below, "up", up(k, 0)[0], n_up, measured, [raised[k][0], up_cuts[k][0]], up_other[k]
         )
         for k in range(n_up)
     ]
@@ -550,6 +547,10 @@
         )
         for k in range(n_here)
     ]
+    last_outs = [
+        slotter(pairs, "last", up(k, 0)[0], n_up, measured, [lower[k][0]], extra[k])
+        for k in range(n_up)
+    ]
     here_back = [[rotate(here_outs[k][d], "slab", d) for d in far] for k in range(n_here)]
     risen = [move(here_outs[k][0], "tile", 1) for k in range(n_here)]
 
@@ -566,15 +567,14 @@
         return twins
 
     items = []
-    for k in range(n_here):
-        items.append((here_outs[k][0], (0, here(k, 0), "above")))
     for k in range(n_up):
         items.append((last_outs[k][0], (0, up(k, 0), "last")))
         items.append((up_outs[k][0], (1, up(k, 0), "below")))
         items.append((fallen[k], (0, up(k, 0), "inner")))
         for d in far:
             items.append((up_back[k][d - 1], (1, up(k, back(d)), "below")))
-    gate = group(items)
+    if items:
+        group(items)
     falling = [[move(value, "tile", -1) for value in row] for row in up_back]
     rising = [[move(value, "tile", 1) for value in row] for row in here_back]
     ending = [
@@ -582,11 +582,12 @@
     ]
     items = []
     for k in range(n_here):
-        items.append((risen[k], (1, here(k, 0), "below")))
+        items.append((here_outs[k][0], (0, here(k, 0), "above")))
         for d in far:
             items.append((here_back[k][d - 1], (0, here(k, back(d)), "above")))
-    group(items, gate)
-    total = early(kinds, tables, terms, cols_total)
+        items.append((risen[k], (1, here(k, 0), "below")))
+    group(items)
+    total, copied = early(kinds, tables, terms, cols_total)
     final, final_kinds = [], []
 
     def add(value, kind):
@@ -600,7 +601,7 @@
     for k in range(n_here):
         for d in far:
             add(rising[k][d - 1], (1, here(k, back(d)), "below"))
-    return late(final_kinds, tables, total, final)
+    return late(final_kinds, tables, total, copied, final)
 
 
 def solution(mesh):

time: 112 us -> 108 us (0.964)
  the two profiles are of different devices: /device:TPU:0 before, /device:TPU:15 now
where the time goes in v5:
time: 108 us; the launch traced here: 107 us
  starting transfers between devices  50.2 us (46%)
  Pallas kernels  35.5 us (33%)
  waiting for transfers between devices  20.5 us (19%)
    ppermute x9, starting transfers between devices, move(): return lax.ppermute(block, axis, route)  33.8 us
    ppermute x11, starting transfers between devices, rotate(): lax.ppermute(block, axis, [(i, (i + distance) % size) for i in range(size)])  15.1 us
    pallas_call x3, Pallas kernels, run_slot(): pl.pallas_call(lambda *refs: slot_kernel(kind, base, each, sections, *ref...  15 us
    ppermute x11, waiting for transfers between devices, rotate(): lax.ppermute(block, axis, [(i, (i + distance) % size) for i in range(size)])  11 us
    ppermute x9, waiting for transfers between devices, move(): return lax.ppermute(block, axis, route)  9.5 us
    pallas_call x4, Pallas kernels, cut(): pl.pallas_call(lambda *refs: cut_kernel(bases, sections, send, *refs), in...  8.93 us
    pallas_call x1, Pallas kernels, early(): pl.pallas_call(lambda *refs: early_kernel(metas, sections, *refs), in_spe...  6.74 us
    pallas_call x1, Pallas kernels, late(): pl.pallas_call(lambda *refs: late_kernel(metas, sections, *refs), in_spec...  2.96 us
  transfers between devices with their start and end apart: 22, of which 12 were waited for; matrix products, arithmetic and copies ran while one was open for 0% of the time, Pallas kernels for 30%

profile of v5, /device:TPU:15, one launch (start us, length us, event | category | flops | bytes accessed | tf_op | source)
XLA Modules:
  0.0 107.4 jit_solution(11691525473669743977)
XLA Ops:
  0.0 3.2 %collective-permute-start = (s32[2,4]{1,0:T(2,128)}, s32[2,4]{1,0:T(2,128)S(1)}, u32[]{:S(2)}, u32[]{:S(2)}) collective-permute-start(s32[2,4]{1,0:T(2,128)} %bitcast.1), channel_id=1, source_target_pairs={{0,4},{4,8},{8,12},{1,5},{5,9},{9,13},{2,6},{6,10},{10,14},{3,7},{... | collective-permute-start | bytes 104 | tf_op jit(solution)/shard_map/ppermute | solution.py:33
  3.2 0.7 copy-done.2
  3.9 2.2 %cut.4 = (f32[3,256,256]{2,1,0:T(8,128)S(1)}, f32[2,256,256]{2,1,0:T(8,128)S(1)}) custom-call(s32[2,4]{1,0:T(2,128)S(1)} %bitcast.2, f32[1,256,4096]{2,1,0:T(8,128)} %refs_1_.10, f32[1,256,4096]{2,1,0:T(8,128)} %refs_2_.10, f32[4,256,256]{2,1,0:T(8,128)} %refs_2_.13), custom_call_target="tpu_custom_call" | custom-call | tf_op jit(solution)/shard_map/cut/pallas_call | solution.py:274
  6.2 3.2 %collective-permute-start.3 = (f32[2,256,256]{2,1,0:T(8,128)S(1)}, f32[2,256,256]{2,1,0:T(8,128)S(1)}, u32[]{:S(2)}, u32[]{:S(2)}) collective-permute-start(f32[2,256,256]{2,1,0:T(8,128)S(1)} %get-tuple-element.50), channel_id=1, source_target_pairs={{0,4},{4,8},{8,12},{1,5},{5,9},{9,13},{2,6},{6,10},{10,14},{3,7},{... | collective-permute-start | bytes 1572872 | tf_op jit(solution)/shard_map/ppermute | solution.py:33
  9.4 1.9 %collective-permute-start.5 = (f32[3,256,256]{2,1,0:T(8,128)S(1)}, f32[3,256,256]{2,1,0:T(8,128)S(1)}, u32[]{:S(2)}, u32[]{:S(2)}) collective-permute-start(f32[3,256,256]{2,1,0:T(8,128)S(1)} %get-tuple-element.56.refs_3_), channel_id=1, source_target_pairs={{0,4},{4,8},{8,12},{1,5},{5,9},{9,13},{2,6},{6,10},{10,14},{3,7},{... | collective-permute-start | bytes 2359304 | tf_op jit(solution)/shard_map/ppermute | solution.py:33
  11.3 2.2 %cut.5 = (f32[2,256,256]{2,1,0:T(8,128)S(1)}, f32[2,256,256]{2,1,0:T(8,128)S(1)}) custom-call(s32[2,4]{1,0:T(2,128)S(1)} %collective-permute-done.refs_0_.refs_1_, f32[1,256,4096]{2,1,0:T(8,128)} %refs_1_.10, f32[1,256,4096]{2,1,0:T(8,128)} %refs_2_.10), custom_call_target="tpu_custom_call" | custom-call | tf_op jit(solution)/shard_map/cut/pallas_call | solution.py:274
  13.5 3.5 %collective-permute-start.4 = (f32[2,256,256]{2,1,0:T(8,128)S(1)}, f32[2,256,256]{2,1,0:T(8,128)S(1)}, u32[]{:S(2)}, u32[]{:S(2)}) collective-permute-start(f32[2,256,256]{2,1,0:T(8,128)S(1)} %get-tuple-element.54), channel_id=1, source_target_pairs={{4,0},{8,4},{12,8},{5,1},{9,5},{13,9},{6,2},{10,6},{14,10},{7,3},{... | collective-permute-start | bytes 1572872 | tf_op jit(solution)/shard_map/ppermute | solution.py:33
  17.0 2.2 %cut.6 = (f32[2,256,256]{2,1,0:T(8,128)S(1)}, f32[2,256,256]{2,1,0:T(8,128)S(1)}) custom-call(s32[2,4]{1,0:T(2,128)S(1)} %collective-permute-done.refs_0_.refs_1_, f32[1,256,4096]{2,1,0:T(8,128)} %refs_1_.10, f32[1,256,4096]{2,1,0:T(8,128)} %refs_2_.10), custom_call_target="tpu_custom_call" | custom-call | tf_op jit(solution)/shard_map/cut/pallas_call | solution.py:274
  19.2 2.3 %cut.7 = (f32[2,256,256]{2,1,0:T(8,128)S(1)}, f32[2,256,256]{2,1,0:T(8,128)S(1)}) custom-call(s32[2,4]{1,0:T(2,128)S(1)} %bitcast.3, f32[1,256,4096]{2,1,0:T(8,128)} %refs_1_.10, f32[1,256,4096]{2,1,0:T(8,128)} %refs_2_.10), custom_call_target="tpu_custom_call" | custom-call | tf_op jit(solution)/shard_map/cut/pallas_call | solution.py:274
  21.6 0.6 join.2
  22.2 0.3 collective-permute-start.6
  22.5 2.6 %collective-permute-start.1 = (s32[2,4]{1,0:T(2,128)S(1)}, s32[2,4]{1,0:T(2,128)S(1)}, u32[]{:S(2)}, u32[]{:S(2)}) collective-permute-start(s32[2,4]{1,0:T(2,128)S(1)} %bitcast.4), channel_id=1, source_target_pairs={{0,1},{1,0},{2,3},{3,2},{4,5},{5,4},{6,7},{7,6},{8,9},{9,8},{10,11... | collective-permute-start | bytes 104 | tf_op jit(solution)/shard_map/ppermute | solution.py:38
  25.1 0.7 collective-permute-start.9
  25.8 0.4 expand.1
  26.2 0.6 collective-permute-done.4.refs_2_
  26.8 4.0 %collective-permute-start.7 = (f32[2,256,256]{2,1,0:T(8,128)S(1)}, f32[2,256,256]{2,1,0:T(8,128)S(1)}, u32[]{:S(2)}, u32[]{:S(2)}) collective-permute-start(f32[2,256,256]{2,1,0:T(8,128)S(1)} %get-tuple-element.43), channel_id=1, source_target_pairs={{4,0},{8,4},{12,8},{5,1},{9,5},{13,9},{6,2},{10,6},{14,10},{7,3},{... | collective-permute-start | bytes 1572872 | tf_op jit(solution)/shard_map/ppermute | solution.py:33
  30.8 0.6 join.3
  31.4 2.8 %collective-permute-start.2 = (s32[2,4]{1,0:T(2,128)S(1)}, s32[2,4]{1,0:T(2,128)S(1)}, u32[]{:S(2)}, u32[]{:S(2)}) collective-permute-start(s32[2,4]{1,0:T(2,128)S(1)} %collective-permute-done.refs_0_.refs_1_), channel_id=1, source_target_pairs={{0,1},{1,0},{2,3},{3,2},{4,5},{5,4},{6,7},{7,6},{8,9},{9,8},{10,11... | collective-permute-start | bytes 104 | tf_op jit(solution)/shard_map/ppermute | solution.py:38
  34.2 0.8 collective-permute-done.2.refs_3_
  35.0 0.3 collective-permute-start.8
  35.3 2.1 %collective-permute-done.5.refs_3_ = f32[3,256,256]{2,1,0:T(8,128)S(1)} collective-permute-done((f32[3,256,256]{2,1,0:T(8,128)S(1)}, f32[3,256,256]{2,1,0:T(8,128)S(1)}, u32[]{:S(2)}, u32[]{:S(2)}) %collective-permute-start.5) | collective-permute-done | bytes 786464 | tf_op jit(solution)/shard_map/ppermute | solution.py:33
  37.4 7.1 %slot_up.1 = (f32[2,256,256]{2,1,0:T(8,128)S(1)}, f32[2,256,256]{2,1,0:T(8,128)S(1)}) custom-call(s32[2,4]{1,0:T(2,128)S(1)} %collective-permute-done.refs_0_.refs_1_, f32[2,256,256]{2,1,0:T(8,128)S(1)} %copy-done, f32[4,256,256]{2,1,0:T(8,128)} %refs_2_.13, f32[3,256,256]{2,1,0:T(8,128)S(1)} %collective-permute-done.5.refs_3_, ...), custom_call_target="tpu_custom_call" | custom-call | tf_op jit(solution)/shard_map/slot_up/pallas_call | solution.py:201
  44.5 0.3 collective-permute-start.11
  44.8 1.9 %collective-permute-start.10 = (f32[2,256,256]{2,1,0:T(8,128)S(1)}, f32[2,256,256]{2,1,0:T(8,128)S(1)}, u32[]{:S(2)}, u32[]{:S(2)}) collective-permute-start(f32[2,256,256]{2,1,0:T(8,128)S(1)} %get-tuple-element.61.refs_1_.refs_5_), channel_id=1, source_target_pairs={{4,0},{8,4},{12,8},{5,1},{9,5},{13,9},{6,2},{10,6},{14,10},{7,3},{... | collective-permute-start | bytes 1572872 | tf_op jit(solution)/shard_map/ppermute | solution.py:33
  46.7 1.5 %collective-permute-done.8.refs_5_ = f32[2,256,256]{2,1,0:T(8,128)S(1)} collective-permute-done((f32[2,256,256]{2,1,0:T(8,128)S(1)}, f32[2,256,256]{2,1,0:T(8,128)S(1)}, u32[]{:S(2)}, u32[]{:S(2)}) %collective-permute-start.8) | collective-permute-done | bytes 524320 | tf_op jit(solution)/shard_map/ppermute | solution.py:38
  48.2 7.2 %slot_here.1 = (f32[2,256,256]{2,1,0:T(8,128)S(1)}, f32[2,256,256]{2,1,0:T(8,128)S(1)}) custom-call(s32[2,4]{1,0:T(2,128)S(1)} %bitcast.6, f32[2,256,256]{2,1,0:T(8,128)S(1)} %copy-done, f32[4,256,256]{2,1,0:T(8,128)} %refs_2_.13, f32[2,256,256]{2,1,0:T(8,128)S(1)} %get-tuple-element.47.refs_3_, f32[2,256,256]{2,1,0:T(8,128)S(1)} %collective-permute-done.7.refs_4_, ...), custom_call_target="tpu_custom_call" | custom-call | tf_op jit(solution)/shard_map/slot_here/pallas_call | solution.py:201
  55.4 1.9 %collective-permute-start.14 = (f32[2,256,256]{2,1,0:T(8,128)S(1)}, f32[2,256,256]{2,1,0:T(8,128)S(1)}, u32[]{:S(2)}, u32[]{:S(2)}) collective-permute-start(f32[2,256,256]{2,1,0:T(8,128)S(1)} %get-tuple-element.63.refs_0_.refs_9_), channel_id=1, source_target_pairs={{0,4},{4,8},{8,12},{1,5},{5,9},{9,13},{2,6},{6,10},{10,14},{3,7},{... | collective-permute-start | bytes 1572872 | tf_op jit(solution)/shard_map/ppermute | solution.py:33
  57.3 1.2 %collective-permute-start.13 = (f32[2,256,256]{2,1,0:T(8,128)S(1)}, f32[2,256,256]{2,1,0:T(8,128)S(1)}, u32[]{:S(2)}, u32[]{:S(2)}) collective-permute-start(f32[2,256,256]{2,1,0:T(8,128)S(1)} %get-tuple-element.67), channel_id=1, source_target_pairs={{0,2},{2,0},{1,3},{3,1},{4,6},{6,4},{5,7},{7,5},{8,10},{10,8},{9,1... | collective-permute-start | bytes 1572872 | tf_op jit(solution)/shard_map/ppermute | solution.py:38
  58.5 0.8 slot_last.1
  59.3 0.2 collective-permute-done.11.refs_3_.refs_7_
  59.5 0.1 pack.2
  59.6 2.9 %collective-permute-start.12 = (f32[4,2,256,256]{3,2,1,0:T(8,128)S(1)}, f32[4,2,256,256]{3,2,1,0:T(8,128)S(1)}, u32[]{:S(2)}, u32[]{:S(2)}) collective-permute-start(f32[4,2,256,256]{3,2,1,0:T(8,128)S(1)} %pack.2), channel_id=1, source_target_pairs={{0,1},{1,0},{2,3},{3,2},{4,5},{5,4},{6,7},{7,6},{8,9},{9,8},{10,11... | collective-permute-start | bytes 6291464 | tf_op jit(solution)/shard_map/ppermute | solution.py:38
  62.5 5.9 %collective-permute-done.13.refs_1_.refs_10_ = f32[2,256,256]{2,1,0:T(8,128)S(1)} collective-permute-done((f32[2,256,256]{2,1,0:T(8,128)S(1)}, f32[2,256,256]{2,1,0:T(8,128)S(1)}, u32[]{:S(2)}, u32[]{:S(2)}) %collective-permute-start.13) | collective-permute-done | bytes 524320 | tf_op jit(solution)/shard_map/ppermute | solution.py:38
  68.4 0.4 collective-permute-done.14.refs_2_.refs_11_
  68.8 0.1 pack.3
  68.9 3.1 %collective-permute-start.15 = (f32[3,2,256,256]{3,2,1,0:T(8,128)S(1)}, f32[3,2,256,256]{3,2,1,0:T(8,128)S(1)}, u32[]{:S(2)}, u32[]{:S(2)}) collective-permute-start(f32[3,2,256,256]{3,2,1,0:T(8,128)S(1)} %pack.3), channel_id=1, source_target_pairs={{0,1},{1,0},{2,3},{3,2},{4,5},{5,4},{6,7},{7,6},{8,9},{9,8},{10,11... | collective-permute-start | bytes 4718600 | tf_op jit(solution)/shard_map/ppermute | solution.py:38
  72.0 12.2 %collective-permute-start.20 = (f32[2,256,256]{2,1,0:T(8,128)S(1)}, f32[2,256,256]{2,1,0:T(8,128)S(1)}, u32[]{:S(2)}, u32[]{:S(2)}) collective-permute-start(f32[2,256,256]{2,1,0:T(8,128)S(1)} %collective-permute-done.13.refs_1_.refs_10_), channel_id=1, source_target_pairs={{0,4},{4,8},{8,12},{1,5},{5,9},{9,13},{2,6},{6,10},{10,14},{3,7},{... | collective-permute-start | bytes 1572872 | tf_op jit(solution)/shard_map/ppermute | solution.py:33
  84.3 0.7 collective-permute-start.18
  85.0 1.9 %collective-permute-start.16 = (f32[2,256,256]{2,1,0:T(8,128)S(1)}, f32[2,256,256]{2,1,0:T(8,128)S(1)}, u32[]{:S(2)}, u32[]{:S(2)}) collective-permute-start(f32[2,256,256]{2,1,0:T(8,128)S(1)} %collective-permute-done.11.refs_3_.refs_7_), channel_id=1, source_target_pairs={{4,0},{8,4},{12,8},{5,1},{9,5},{13,9},{6,2},{10,6},{14,10},{7,3},{... | collective-permute-start | bytes 1572872 | tf_op jit(solution)/shard_map/ppermute | solution.py:33
  86.9 6.7 %early.1 = (f32[2,256,4096]{2,1,0:T(8,128)S(1)}, f32[2,1,256,4096]{3,2,1,0:T(8,128)}) custom-call(s32[2,4]{1,0:T(2,128)S(1)} %bitcast.8, s32[2,4]{1,0:T(2,128)S(1)} %collective-permute-done.refs_0_.refs_1_, s32[2,4]{1,0:T(2,128)S(1)} %collective-permute-done.1.refs_2_, s32[2,4]{1,0:T(2,128)S(1)} %collective-permute-done.2.refs_3_, ...), custom_call_target="tpu_custom_call" | custom-call | tf_op jit(solution)/shard_map/early/pallas_call | solution.py:390
  93.7 1.9 %collective-permute-done.20.refs_9_ = f32[2,256,256]{2,1,0:T(8,128)S(1)} collective-permute-done((f32[2,256,256]{2,1,0:T(8,128)S(1)}, f32[2,256,256]{2,1,0:T(8,128)S(1)}, u32[]{:S(2)}, u32[]{:S(2)}) %collective-permute-start.20) | collective-permute-done | bytes 524320 | tf_op jit(solution)/shard_map/ppermute | solution.py:33
  95.6 4.5 %collective-permute-done.16.refs_5_ = f32[2,256,256]{2,1,0:T(8,128)S(1)} collective-permute-done((f32[2,256,256]{2,1,0:T(8,128)S(1)}, f32[2,256,256]{2,1,0:T(8,128)S(1)}, u32[]{:S(2)}, u32[]{:S(2)}) %collective-permute-start.16) | collective-permute-done | bytes 524320 | tf_op jit(solution)/shard_map/ppermute | solution.py:33
  100.1 1.1 %collective-permute-start.17 = (f32[2,256,256]{2,1,0:T(8,128)S(1)}, f32[2,256,256]{2,1,0:T(8,128)S(1)}, u32[]{:S(2)}, u32[]{:S(2)}) collective-permute-start(f32[2,256,256]{2,1,0:T(8,128)S(1)} %collective-permute-done.16.refs_5_), channel_id=1, source_target_pairs={{0,1},{1,0},{2,3},{3,2},{4,5},{5,4},{6,7},{7,6},{8,9},{9,8},{10,11... | collective-permute-start | bytes 1572872 | tf_op jit(solution)/shard_map/ppermute | solution.py:38
  101.2 0.5 collective-permute-start.21
  101.7 1.0 collective-permute-done.17.refs_6_
  102.7 0.7 collective-permute-done.19.refs_8_
  103.5 0.7 collective-permute-done.21.refs_10_
  104.2 3.0 %late.1 = f32[2,1,256,4096]{3,2,1,0:T(8,128)} custom-call(s32[2,4]{1,0:T(2,128)S(1)} %bitcast.9, s32[2,4]{1,0:T(2,128)S(1)} %collective-permute-done.refs_0_.refs_1_, s32[2,4]{1,0:T(2,128)S(1)} %collective-permute-done.1.refs_2_, s32[2,4]{1,0:T(2,128)S(1)} %collective-permute-done.2.refs_3_, ...), custom_call_target="tpu_custom_call", output_to_operand_aliasing={{}: (11, {})} | custom-call | tf_op jit(solution)/shard_map/late/pallas_call | solution.py:456
  (18 shorter events, 0.1 us)
Async XLA Ops:
  0.0 6.2 %collective-permute-start = (s32[2,4]{1,0:T(2,128)}, s32[2,4]{1,0:T(2,128)S(1)}, u32[]{:S(2)}, u32[]{:S(2)}) collective-permute-start(s32[2,4]{1,0:T(2,128)} %bitcast.1), channel_id=1, source_target_pairs={{0,4},{4,8},{8,12},{1,5},{5,9},{9,13},{2,6},{6,10},{10,14},{3,7},{... | collective-permute-start | bytes 104 | tf_op jit(solution)/shard_map/ppermute | solution.py:33
  3.2 0.7 copy-start.2
  6.2 15.4 %collective-permute-start.3 = (f32[2,256,256]{2,1,0:T(8,128)S(1)}, f32[2,256,256]{2,1,0:T(8,128)S(1)}, u32[]{:S(2)}, u32[]{:S(2)}) collective-permute-start(f32[2,256,256]{2,1,0:T(8,128)S(1)} %get-tuple-element.50), channel_id=1, source_target_pairs={{0,4},{4,8},{8,12},{1,5},{5,9},{9,13},{2,6},{6,10},{10,14},{3,7},{... | collective-permute-start | bytes 1572872 | tf_op jit(solution)/shard_map/ppermute | solution.py:33
  9.4 28.0 %collective-permute-start.5 = (f32[3,256,256]{2,1,0:T(8,128)S(1)}, f32[3,256,256]{2,1,0:T(8,128)S(1)}, u32[]{:S(2)}, u32[]{:S(2)}) collective-permute-start(f32[3,256,256]{2,1,0:T(8,128)S(1)} %get-tuple-element.56.refs_3_), channel_id=1, source_target_pairs={{0,4},{4,8},{8,12},{1,5},{5,9},{9,13},{2,6},{6,10},{10,14},{3,7},{... | collective-permute-start | bytes 2359304 | tf_op jit(solution)/shard_map/ppermute | solution.py:33
  13.5 5.7 %copy-start.3 = (s32[4,2]{0,1:T(2,128)S(1)}, s32[4,2]{0,1:T(2,128)}, u32[]{:S(2)}) copy-start(s32[4,2]{0,1:T(2,128)} %param.10) | copy-start | bytes 100
  13.5 13.3 %collective-permute-start.4 = (f32[2,256,256]{2,1,0:T(8,128)S(1)}, f32[2,256,256]{2,1,0:T(8,128)S(1)}, u32[]{:S(2)}, u32[]{:S(2)}) collective-permute-start(f32[2,256,256]{2,1,0:T(8,128)S(1)} %get-tuple-element.54), channel_id=1, source_target_pairs={{4,0},{8,4},{12,8},{5,1},{9,5},{13,9},{6,2},{10,6},{14,10},{7,3},{... | collective-permute-start | bytes 1572872 | tf_op jit(solution)/shard_map/ppermute | solution.py:33
  21.5 4.3 %copy-start.1 = (bf16[8,256,256]{2,1,0:T(8,128)(2,1)S(1)}, bf16[8,256,256]{2,1,0:T(8,128)(2,1)}, u32[]{:S(2)}) copy-start(bf16[8,256,256]{2,1,0:T(8,128)(2,1)} %constant.2.clone.pieces) | copy-start | bytes 3145732
  21.5 15.8 %copy-start = (f32[2,256,256]{2,1,0:T(8,128)S(1)}, f32[2,256,256]{2,1,0:T(8,128)}, u32[]{:S(2)}) copy-start(f32[2,256,256]{2,1,0:T(8,128)} %refs_1_.13) | copy-start | bytes 1572868
  22.2 15.2 %collective-permute-start.6 = (f32[2,256,256]{2,1,0:T(8,128)S(1)}, f32[2,256,256]{2,1,0:T(8,128)S(1)}, u32[]{:S(2)}, u32[]{:S(2)}) collective-permute-start(f32[2,256,256]{2,1,0:T(8,128)S(1)} %join.2), channel_id=1, source_target_pairs={{0,2},{2,0},{1,3},{3,1},{4,6},{6,4},{5,7},{7,5},{8,10},{10,8},{9,1... | collective-permute-start | bytes 1572872 | tf_op jit(solution)/shard_map/ppermute | solution.py:38
  22.5 8.9 %collective-permute-start.1 = (s32[2,4]{1,0:T(2,128)S(1)}, s32[2,4]{1,0:T(2,128)S(1)}, u32[]{:S(2)}, u32[]{:S(2)}) collective-permute-start(s32[2,4]{1,0:T(2,128)S(1)} %bitcast.4), channel_id=1, source_target_pairs={{0,1},{1,0},{2,3},{3,2},{4,5},{5,4},{6,7},{7,6},{8,9},{9,8},{10,11... | collective-permute-start | bytes 104 | tf_op jit(solution)/shard_map/ppermute | solution.py:38
  25.1 33.4 %collective-permute-start.9 = (f32[2,256,256]{2,1,0:T(8,128)S(1)}, f32[2,256,256]{2,1,0:T(8,128)S(1)}, u32[]{:S(2)}, u32[]{:S(2)}) collective-permute-start(f32[2,256,256]{2,1,0:T(8,128)S(1)} %get-tuple-element.50), channel_id=1, source_target_pairs={{12,14},{14,12},{13,15},{15,13},{28,30},{30,28},{29,31},{31,29}} | collective-permute-start | bytes 1572872 | tf_op jit(solution)/shard_map/ppermute | solution.py:45
  26.8 19.9 %collective-permute-start.7 = (f32[2,256,256]{2,1,0:T(8,128)S(1)}, f32[2,256,256]{2,1,0:T(8,128)S(1)}, u32[]{:S(2)}, u32[]{:S(2)}) collective-permute-start(f32[2,256,256]{2,1,0:T(8,128)S(1)} %get-tuple-element.43), channel_id=1, source_target_pairs={{4,0},{8,4},{12,8},{5,1},{9,5},{13,9},{6,2},{10,6},{14,10},{7,3},{... | collective-permute-start | bytes 1572872 | tf_op jit(solution)/shard_map/ppermute | solution.py:33
  31.4 3.6 %collective-permute-start.2 = (s32[2,4]{1,0:T(2,128)S(1)}, s32[2,4]{1,0:T(2,128)S(1)}, u32[]{:S(2)}, u32[]{:S(2)}) collective-permute-start(s32[2,4]{1,0:T(2,128)S(1)} %collective-permute-done.refs_0_.refs_1_), channel_id=1, source_target_pairs={{0,1},{1,0},{2,3},{3,2},{4,5},{5,4},{6,7},{7,6},{8,9},{9,8},{10,11... | collective-permute-start | bytes 104 | tf_op jit(solution)/shard_map/ppermute | solution.py:38
  35.0 13.2 %collective-permute-start.8 = (f32[2,256,256]{2,1,0:T(8,128)S(1)}, f32[2,256,256]{2,1,0:T(8,128)S(1)}, u32[]{:S(2)}, u32[]{:S(2)}) collective-permute-start(f32[2,256,256]{2,1,0:T(8,128)S(1)} %join.3), channel_id=1, source_target_pairs={{0,2},{2,0},{1,3},{3,1},{4,6},{6,4},{5,7},{7,5},{8,10},{10,8},{9,1... | collective-permute-start | bytes 1572872 | tf_op jit(solution)/shard_map/ppermute | solution.py:38
  44.5 15.0 %collective-permute-start.11 = (f32[2,256,256]{2,1,0:T(8,128)S(1)}, f32[2,256,256]{2,1,0:T(8,128)S(1)}, u32[]{:S(2)}, u32[]{:S(2)}) collective-permute-start(f32[2,256,256]{2,1,0:T(8,128)S(1)} %get-tuple-element.66), channel_id=1, source_target_pairs={{0,2},{2,0},{1,3},{3,1},{4,6},{6,4},{5,7},{7,5},{8,10},{10,8},{9,1... | collective-permute-start | bytes 1572872 | tf_op jit(solution)/shard_map/ppermute | solution.py:38
  44.8 14.7 %collective-permute-start.10 = (f32[2,256,256]{2,1,0:T(8,128)S(1)}, f32[2,256,256]{2,1,0:T(8,128)S(1)}, u32[]{:S(2)}, u32[]{:S(2)}) collective-permute-start(f32[2,256,256]{2,1,0:T(8,128)S(1)} %get-tuple-element.61.refs_1_.refs_5_), channel_id=1, source_target_pairs={{4,0},{8,4},{12,8},{5,1},{9,5},{13,9},{6,2},{10,6},{14,10},{7,3},{... | collective-permute-start | bytes 1572872 | tf_op jit(solution)/shard_map/ppermute | solution.py:33
  55.4 13.4 %collective-permute-start.14 = (f32[2,256,256]{2,1,0:T(8,128)S(1)}, f32[2,256,256]{2,1,0:T(8,128)S(1)}, u32[]{:S(2)}, u32[]{:S(2)}) collective-permute-start(f32[2,256,256]{2,1,0:T(8,128)S(1)} %get-tuple-element.63.refs_0_.refs_9_), channel_id=1, source_target_pairs={{0,4},{4,8},{8,12},{1,5},{5,9},{9,13},{2,6},{6,10},{10,14},{3,7},{... | collective-permute-start | bytes 1572872 | tf_op jit(solution)/shard_map/ppermute | solution.py:33
  57.3 11.1 %collective-permute-start.13 = (f32[2,256,256]{2,1,0:T(8,128)S(1)}, f32[2,256,256]{2,1,0:T(8,128)S(1)}, u32[]{:S(2)}, u32[]{:S(2)}) collective-permute-start(f32[2,256,256]{2,1,0:T(8,128)S(1)} %get-tuple-element.67), channel_id=1, source_target_pairs={{0,2},{2,0},{1,3},{3,1},{4,6},{6,4},{5,7},{7,5},{8,10},{10,8},{9,1... | collective-permute-start | bytes 1572872 | tf_op jit(solution)/shard_map/ppermute | solution.py:38
  59.6 27.3 %collective-permute-start.12 = (f32[4,2,256,256]{3,2,1,0:T(8,128)S(1)}, f32[4,2,256,256]{3,2,1,0:T(8,128)S(1)}, u32[]{:S(2)}, u32[]{:S(2)}) collective-permute-start(f32[4,2,256,256]{3,2,1,0:T(8,128)S(1)} %pack.2), channel_id=1, source_target_pairs={{0,1},{1,0},{2,3},{3,2},{4,5},{5,4},{6,7},{7,6},{8,9},{9,8},{10,11... | collective-permute-start | bytes 6291464 | tf_op jit(solution)/shard_map/ppermute | solution.py:38
  68.9 18.0 %collective-permute-start.15 = (f32[3,2,256,256]{3,2,1,0:T(8,128)S(1)}, f32[3,2,256,256]{3,2,1,0:T(8,128)S(1)}, u32[]{:S(2)}, u32[]{:S(2)}) collective-permute-start(f32[3,2,256,256]{3,2,1,0:T(8,128)S(1)} %pack.3), channel_id=1, source_target_pairs={{0,1},{1,0},{2,3},{3,2},{4,5},{5,4},{6,7},{7,6},{8,9},{9,8},{10,11... | collective-permute-start | bytes 4718600 | tf_op jit(solution)/shard_map/ppermute | solution.py:38
  72.0 23.6 %collective-permute-start.20 = (f32[2,256,256]{2,1,0:T(8,128)S(1)}, f32[2,256,256]{2,1,0:T(8,128)S(1)}, u32[]{:S(2)}, u32[]{:S(2)}) collective-permute-start(f32[2,256,256]{2,1,0:T(8,128)S(1)} %collective-permute-done.13.refs_1_.refs_10_), channel_id=1, source_target_pairs={{0,4},{4,8},{8,12},{1,5},{5,9},{9,13},{2,6},{6,10},{10,14},{3,7},{... | collective-permute-start | bytes 1572872 | tf_op jit(solution)/shard_map/ppermute | solution.py:33
  84.3 11.3 %collective-permute-start.18 = (f32[2,256,256]{2,1,0:T(8,128)S(1)}, f32[2,256,256]{2,1,0:T(8,128)S(1)}, u32[]{:S(2)}, u32[]{:S(2)}) collective-permute-start(f32[2,256,256]{2,1,0:T(8,128)S(1)} %get-tuple-element.71), channel_id=1, source_target_pairs={{12,14},{14,12},{13,15},{15,13},{28,30},{30,28},{29,31},{31,29}} | collective-permute-start | bytes 1572872 | tf_op jit(solution)/shard_map/ppermute | solution.py:45
  85.0 15.1 %collective-permute-start.16 = (f32[2,256,256]{2,1,0:T(8,128)S(1)}, f32[2,256,256]{2,1,0:T(8,128)S(1)}, u32[]{:S(2)}, u32[]{:S(2)}) collective-permute-start(f32[2,256,256]{2,1,0:T(8,128)S(1)} %collective-permute-done.11.refs_3_.refs_7_), channel_id=1, source_target_pairs={{4,0},{8,4},{12,8},{5,1},{9,5},{13,9},{6,2},{10,6},{14,10},{7,3},{... | collective-permute-start | bytes 1572872 | tf_op jit(solution)/shard_map/ppermute | solution.py:33
  100.1 2.7 %collective-permute-start.17 = (f32[2,256,256]{2,1,0:T(8,128)S(1)}, f32[2,256,256]{2,1,0:T(8,128)S(1)}, u32[]{:S(2)}, u32[]{:S(2)}) collective-permute-start(f32[2,256,256]{2,1,0:T(8,128)S(1)} %collective-permute-done.16.refs_5_), channel_id=1, source_target_pairs={{0,1},{1,0},{2,3},{3,2},{4,5},{5,4},{6,7},{7,6},{8,9},{9,8},{10,11... | collective-permute-start | bytes 1572872 | tf_op jit(solution)/shard_map/ppermute | solution.py:38
  101.2 2.3 %collective-permute-start.19 = (f32[2,256,256]{2,1,0:T(8,128)S(1)}, f32[2,256,256]{2,1,0:T(8,128)S(1)}, u32[]{:S(2)}, u32[]{:S(2)}) collective-permute-start(f32[2,256,256]{2,1,0:T(8,128)S(1)} %collective-permute-done.18.refs_7_), channel_id=1, source_target_pairs={{0,1},{1,0},{2,3},{3,2},{4,5},{5,4},{6,7},{7,6},{8,9},{9,8},{10,11... | collective-permute-start | bytes 1572872 | tf_op jit(solution)/shard_map/ppermute | solution.py:38
  101.2 3.0 %collective-permute-start.21 = (f32[2,256,256]{2,1,0:T(8,128)S(1)}, f32[2,256,256]{2,1,0:T(8,128)S(1)}, u32[]{:S(2)}, u32[]{:S(2)}) collective-permute-start(f32[2,256,256]{2,1,0:T(8,128)S(1)} %collective-permute-done.20.refs_9_), channel_id=1, source_target_pairs={{0,1},{1,0},{2,3},{3,2},{4,5},{5,4},{6,7},{7,6},{8,9},{9,8},{10,11... | collective-permute-start | bytes 1572872 | tf_op jit(solution)/shard_map/ppermute | solution.py:38

commit v6 on v5

--- a/solution.py
+++ b/solution.py
@@ -507,7 +507,7 @@
         cutter(pairs, [up(k, d) for d in distances], measured, (up(k, 0)[0], n_up))
         for k in range(n_up)
     ]
-    extra = [[rotate_last(lower[k][d], d) for d in far] for k in range(n_up)]
+    extra = [[rotate_last(after(lower[k][d], below), d) for d in far] for k in range(n_up)]
     raised = [[move(after(lower[k][d], below), "tile", 1) for d in far] for k in range(n_up)]
     for k in range(n_up):
         raised[k].insert(0, move(after(lower[k][0], below), "tile", 1))
@@ -518,6 +518,7 @@
     up_cuts = [cutter(below, [up(k, d) for d in distances]) for k in range(n_up)]
     own_cuts = [cutter(pairs, [here(k, d) for d in distances]) for k in range(n_here)]
     constants = expand(side)
+    done += [value for row in extra for value in row]
     up_joined = [
         [joiner(below, up(k, d), raised[k][d], up_cuts[k][d]) for d in far] for k in range(n_up)
     ]

time: 108 us -> 101 us (0.935)
  the two profiles are of different devices: /device:TPU:15 before, /device:TPU:0 now
where the time goes in v6:
time: 101 us
  Pallas kernels  34.1 us (34%)
  waiting for transfers between devices  33 us (33%)
  starting transfers between devices  32.3 us (32%)
    ppermute x9, starting transfers between devices, move(): return lax.ppermute(block, axis, route)  25.9 us
    ppermute x9, waiting for transfers between devices, move(): return lax.ppermute(block, axis, route)  19.8 us
    pallas_call x3, Pallas kernels, run_slot(): pl.pallas_call(lambda *refs: slot_kernel(kind, base, each, sections, *ref...  14.9 us
    ppermute x11, waiting for transfers between devices, rotate(): lax.ppermute(block, axis, [(i, (i + distance) % size) for i in range(size)])  13.3 us
    pallas_call x4, Pallas kernels, cut(): pl.pallas_call(lambda *refs: cut_kernel(bases, sections, send, *refs), in...  8.97 us
    pallas_call x1, Pallas kernels, early(): pl.pallas_call(lambda *refs: early_kernel(metas, sections, *refs), in_spe...  5.72 us
    ppermute x11, starting transfers between devices, rotate(): lax.ppermute(block, axis, [(i, (i + distance) % size) for i in range(size)])  5.01 us
    pallas_call x1, Pallas kernels, late(): pl.pallas_call(lambda *refs: late_kernel(metas, sections, *refs), in_spec...  2.59 us
  transfers between devices with their start and end apart: 22, of which 9 were waited for; matrix products, arithmetic and copies ran while one was open for 0% of the time, Pallas kernels for 31%

profile of v6, /device:TPU:0, one launch (start us, length us, event | category | flops | bytes accessed | tf_op | source)
XLA Modules:
  0.0 100.6 jit_solution(8495348093721202718)
XLA Ops:
  0.0 4.9 %collective-permute-start = (s32[2,4]{1,0:T(2,128)}, s32[2,4]{1,0:T(2,128)S(1)}, u32[]{:S(2)}, u32[]{:S(2)}) collective-permute-start(s32[2,4]{1,0:T(2,128)} %bitcast.1), channel_id=1, source_target_pairs={{0,4},{4,8},{8,12},{1,5},{5,9},{9,13},{2,6},{6,10},{10,14},{3,7},{... | collective-permute-start | bytes 104 | tf_op jit(solution)/shard_map/ppermute | solution.py:33
  4.9 0.0 copy-start.2
  4.9 0.7 copy-done.2
  5.6 2.2 %cut.4 = (f32[3,256,256]{2,1,0:T(8,128)S(1)}, f32[2,256,256]{2,1,0:T(8,128)S(1)}) custom-call(s32[2,4]{1,0:T(2,128)S(1)} %bitcast.2, f32[1,256,4096]{2,1,0:T(8,128)} %refs_1_.10, f32[1,256,4096]{2,1,0:T(8,128)} %refs_2_.10, f32[4,256,256]{2,1,0:T(8,128)} %refs_2_.13), custom_call_target="tpu_custom_call" | custom-call | tf_op jit(solution)/shard_map/cut/pallas_call | solution.py:274
  7.9 0.0 collective-permute-done.refs_0_.refs_1_
  7.9 0.7 collective-permute-start.3
  8.6 3.6 %collective-permute-start.4 = (f32[2,256,256]{2,1,0:T(8,128)S(1)}, f32[2,256,256]{2,1,0:T(8,128)S(1)}, u32[]{:S(2)}, u32[]{:S(2)}) collective-permute-start(f32[2,256,256]{2,1,0:T(8,128)S(1)} %get-tuple-element.49), channel_id=1, source_target_pairs={{0,4},{4,8},{8,12},{1,5},{5,9},{9,13},{2,6},{6,10},{10,14},{3,7},{... | collective-permute-start | bytes 1572872 | tf_op jit(solution)/shard_map/ppermute | solution.py:33
  12.2 3.5 %collective-permute-start.6 = (f32[3,256,256]{2,1,0:T(8,128)S(1)}, f32[3,256,256]{2,1,0:T(8,128)S(1)}, u32[]{:S(2)}, u32[]{:S(2)}) collective-permute-start(f32[3,256,256]{2,1,0:T(8,128)S(1)} %get-tuple-element.56.refs_3_), channel_id=1, source_target_pairs={{0,4},{4,8},{8,12},{1,5},{5,9},{9,13},{2,6},{6,10},{10,14},{3,7},{... | collective-permute-start | bytes 2359304 | tf_op jit(solution)/shard_map/ppermute | solution.py:33
  15.7 2.3 %cut.5 = (f32[2,256,256]{2,1,0:T(8,128)S(1)}, f32[2,256,256]{2,1,0:T(8,128)S(1)}) custom-call(s32[2,4]{1,0:T(2,128)S(1)} %collective-permute-done.refs_0_.refs_1_, f32[1,256,4096]{2,1,0:T(8,128)} %refs_1_.10, f32[1,256,4096]{2,1,0:T(8,128)} %refs_2_.10), custom_call_target="tpu_custom_call" | custom-call | tf_op jit(solution)/shard_map/cut/pallas_call | solution.py:274
  18.0 0.0 copy-start.3
  18.0 1.3 %collective-permute-start.5 = (f32[2,256,256]{2,1,0:T(8,128)S(1)}, f32[2,256,256]{2,1,0:T(8,128)S(1)}, u32[]{:S(2)}, u32[]{:S(2)}) collective-permute-start(f32[2,256,256]{2,1,0:T(8,128)S(1)} %get-tuple-element.54), channel_id=1, source_target_pairs={{4,0},{8,4},{12,8},{5,1},{9,5},{13,9},{6,2},{10,6},{14,10},{7,3},{... | collective-permute-start | bytes 1572872 | tf_op jit(solution)/shard_map/ppermute | solution.py:33
  19.3 2.3 %cut.6 = (f32[2,256,256]{2,1,0:T(8,128)S(1)}, f32[2,256,256]{2,1,0:T(8,128)S(1)}) custom-call(s32[2,4]{1,0:T(2,128)S(1)} %collective-permute-done.refs_0_.refs_1_, f32[1,256,4096]{2,1,0:T(8,128)} %refs_1_.10, f32[1,256,4096]{2,1,0:T(8,128)} %refs_2_.10), custom_call_target="tpu_custom_call" | custom-call | tf_op jit(solution)/shard_map/cut/pallas_call | solution.py:274
  21.6 2.2 %cut.7 = (f32[2,256,256]{2,1,0:T(8,128)S(1)}, f32[2,256,256]{2,1,0:T(8,128)S(1)}) custom-call(s32[2,4]{1,0:T(2,128)S(1)} %bitcast.3, f32[1,256,4096]{2,1,0:T(8,128)} %refs_1_.10, f32[1,256,4096]{2,1,0:T(8,128)} %refs_2_.10), custom_call_target="tpu_custom_call" | custom-call | tf_op jit(solution)/shard_map/cut/pallas_call | solution.py:274
  23.8 0.0 copy-start.1
  23.8 0.0 collective-permute-done.3.refs_4_
  23.8 0.7 collective-permute-done.4.refs_1_
  24.5 0.6 join.2
  25.1 1.5 %collective-permute-start.7 = (f32[2,256,256]{2,1,0:T(8,128)S(1)}, f32[2,256,256]{2,1,0:T(8,128)S(1)}, u32[]{:S(2)}, u32[]{:S(2)}) collective-permute-start(f32[2,256,256]{2,1,0:T(8,128)S(1)} %join.2), channel_id=1, source_target_pairs={{0,2},{2,0},{1,3},{3,1},{4,6},{6,4},{5,7},{7,5},{8,10},{10,8},{9,1... | collective-permute-start | bytes 1572872 | tf_op jit(solution)/shard_map/ppermute | solution.py:38
  26.6 0.4 expand.1
  27.0 1.3 %collective-permute-start.8 = (f32[2,256,256]{2,1,0:T(8,128)S(1)}, f32[2,256,256]{2,1,0:T(8,128)S(1)}, u32[]{:S(2)}, u32[]{:S(2)}) collective-permute-start(f32[2,256,256]{2,1,0:T(8,128)S(1)} %get-tuple-element.43), channel_id=1, source_target_pairs={{4,0},{8,4},{12,8},{5,1},{9,5},{13,9},{6,2},{10,6},{14,10},{7,3},{... | collective-permute-start | bytes 1572872 | tf_op jit(solution)/shard_map/ppermute | solution.py:33
  28.3 5.2 %collective-permute-done.5.refs_2_ = f32[2,256,256]{2,1,0:T(8,128)S(1)} collective-permute-done((f32[2,256,256]{2,1,0:T(8,128)S(1)}, f32[2,256,256]{2,1,0:T(8,128)S(1)}, u32[]{:S(2)}, u32[]{:S(2)}) %collective-permute-start.5) | collective-permute-done | bytes 524320 | tf_op jit(solution)/shard_map/ppermute | solution.py:33
  33.5 0.6 join.3
  34.1 0.7 collective-permute-start.9
  34.8 5.0 %collective-permute-done.6.refs_3_ = f32[3,256,256]{2,1,0:T(8,128)S(1)} collective-permute-done((f32[3,256,256]{2,1,0:T(8,128)S(1)}, f32[3,256,256]{2,1,0:T(8,128)S(1)}, u32[]{:S(2)}, u32[]{:S(2)}) %collective-permute-start.6) | collective-permute-done | bytes 786464 | tf_op jit(solution)/shard_map/ppermute | solution.py:33
  39.8 7.0 %slot_up.1 = (f32[2,256,256]{2,1,0:T(8,128)S(1)}, f32[2,256,256]{2,1,0:T(8,128)S(1)}) custom-call(s32[2,4]{1,0:T(2,128)S(1)} %collective-permute-done.refs_0_.refs_1_, f32[2,256,256]{2,1,0:T(8,128)S(1)} %copy-done, f32[4,256,256]{2,1,0:T(8,128)} %refs_2_.13, f32[3,256,256]{2,1,0:T(8,128)S(1)} %collective-permute-done.6.refs_3_, ...), custom_call_target="tpu_custom_call" | custom-call | tf_op jit(solution)/shard_map/slot_up/pallas_call | solution.py:201
  46.9 1.6 %collective-permute-start.11 = (f32[2,256,256]{2,1,0:T(8,128)S(1)}, f32[2,256,256]{2,1,0:T(8,128)S(1)}, u32[]{:S(2)}, u32[]{:S(2)}) collective-permute-start(f32[2,256,256]{2,1,0:T(8,128)S(1)} %get-tuple-element.66), channel_id=1, source_target_pairs={{0,2},{2,0},{1,3},{3,1},{4,6},{6,4},{5,7},{7,5},{8,10},{10,8},{9,1... | collective-permute-start | bytes 1572872 | tf_op jit(solution)/shard_map/ppermute | solution.py:38
  48.5 1.3 %collective-permute-start.10 = (f32[2,256,256]{2,1,0:T(8,128)S(1)}, f32[2,256,256]{2,1,0:T(8,128)S(1)}, u32[]{:S(2)}, u32[]{:S(2)}) collective-permute-start(f32[2,256,256]{2,1,0:T(8,128)S(1)} %get-tuple-element.61.refs_1_.refs_5_), channel_id=1, source_target_pairs={{4,0},{8,4},{12,8},{5,1},{9,5},{13,9},{6,2},{10,6},{14,10},{7,3},{... | collective-permute-start | bytes 1572872 | tf_op jit(solution)/shard_map/ppermute | solution.py:33
  49.8 7.1 %slot_here.1 = (f32[2,256,256]{2,1,0:T(8,128)S(1)}, f32[2,256,256]{2,1,0:T(8,128)S(1)}) custom-call(s32[2,4]{1,0:T(2,128)S(1)} %bitcast.6, f32[2,256,256]{2,1,0:T(8,128)S(1)} %copy-done, f32[4,256,256]{2,1,0:T(8,128)} %refs_2_.13, f32[2,256,256]{2,1,0:T(8,128)S(1)} %get-tuple-element.47.refs_3_, f32[2,256,256]{2,1,0:T(8,128)S(1)} %collective-permute-done.8.refs_4_, ...), custom_call_target="tpu_custom_call" | custom-call | tf_op jit(solution)/shard_map/slot_here/pallas_call | solution.py:201
  56.9 5.0 %collective-permute-start.14 = (f32[2,256,256]{2,1,0:T(8,128)S(1)}, f32[2,256,256]{2,1,0:T(8,128)S(1)}, u32[]{:S(2)}, u32[]{:S(2)}) collective-permute-start(f32[2,256,256]{2,1,0:T(8,128)S(1)} %get-tuple-element.63.refs_0_.refs_9_), channel_id=1, source_target_pairs={{0,4},{4,8},{8,12},{1,5},{5,9},{9,13},{2,6},{6,10},{10,14},{3,7},{... | collective-permute-start | bytes 1572872 | tf_op jit(solution)/shard_map/ppermute | solution.py:33
  62.0 0.6 collective-permute-start.13
  62.6 0.8 slot_last.1
  63.4 0.1 pack.2
  63.5 0.1 collective-permute-start.12
  63.6 10.4 %collective-permute-done.13.refs_1_.refs_10_ = f32[2,256,256]{2,1,0:T(8,128)S(1)} collective-permute-done((f32[2,256,256]{2,1,0:T(8,128)S(1)}, f32[2,256,256]{2,1,0:T(8,128)S(1)}, u32[]{:S(2)}, u32[]{:S(2)}) %collective-permute-start.13) | collective-permute-done | bytes 524320 | tf_op jit(solution)/shard_map/ppermute | solution.py:38
  74.0 0.1 pack.3
  74.1 0.1 collective-permute-start.15
  74.1 3.6 %collective-permute-start.20 = (f32[2,256,256]{2,1,0:T(8,128)S(1)}, f32[2,256,256]{2,1,0:T(8,128)S(1)}, u32[]{:S(2)}, u32[]{:S(2)}) collective-permute-start(f32[2,256,256]{2,1,0:T(8,128)S(1)} %collective-permute-done.13.refs_1_.refs_10_), channel_id=1, source_target_pairs={{0,4},{4,8},{8,12},{1,5},{5,9},{9,13},{2,6},{6,10},{10,14},{3,7},{... | collective-permute-start | bytes 1572872 | tf_op jit(solution)/shard_map/ppermute | solution.py:33
  77.8 0.7 collective-permute-start.18
  78.5 1.3 %collective-permute-start.16 = (f32[2,256,256]{2,1,0:T(8,128)S(1)}, f32[2,256,256]{2,1,0:T(8,128)S(1)}, u32[]{:S(2)}, u32[]{:S(2)}) collective-permute-start(f32[2,256,256]{2,1,0:T(8,128)S(1)} %collective-permute-done.11.refs_3_.refs_7_), channel_id=1, source_target_pairs={{4,0},{8,4},{12,8},{5,1},{9,5},{13,9},{6,2},{10,6},{14,10},{7,3},{... | collective-permute-start | bytes 1572872 | tf_op jit(solution)/shard_map/ppermute | solution.py:33
  79.8 5.7 %early.1 = (f32[2,256,4096]{2,1,0:T(8,128)S(1)}, f32[2,1,256,4096]{3,2,1,0:T(8,128)}) custom-call(s32[2,4]{1,0:T(2,128)S(1)} %bitcast.8, s32[2,4]{1,0:T(2,128)S(1)} %collective-permute-done.refs_0_.refs_1_, s32[2,4]{1,0:T(2,128)S(1)} %collective-permute-done.1.refs_2_, s32[2,4]{1,0:T(2,128)S(1)} %collective-permute-done.2.refs_3_, ...), custom_call_target="tpu_custom_call" | custom-call | tf_op jit(solution)/shard_map/early/pallas_call | solution.py:390
  85.5 4.0 %collective-permute-done.20.refs_9_ = f32[2,256,256]{2,1,0:T(8,128)S(1)} collective-permute-done((f32[2,256,256]{2,1,0:T(8,128)S(1)}, f32[2,256,256]{2,1,0:T(8,128)S(1)}, u32[]{:S(2)}, u32[]{:S(2)}) %collective-permute-start.20) | collective-permute-done | bytes 524320 | tf_op jit(solution)/shard_map/ppermute | solution.py:33
  89.6 4.8 %collective-permute-done.16.refs_5_ = f32[2,256,256]{2,1,0:T(8,128)S(1)} collective-permute-done((f32[2,256,256]{2,1,0:T(8,128)S(1)}, f32[2,256,256]{2,1,0:T(8,128)S(1)}, u32[]{:S(2)}, u32[]{:S(2)}) %collective-permute-start.16) | collective-permute-done | bytes 524320 | tf_op jit(solution)/shard_map/ppermute | solution.py:33
  94.4 0.5 collective-permute-start.19
  94.9 0.0 collective-permute-start.21
  94.9 1.4 %collective-permute-done.17.refs_6_ = f32[2,256,256]{2,1,0:T(8,128)S(1)} collective-permute-done((f32[2,256,256]{2,1,0:T(8,128)S(1)}, f32[2,256,256]{2,1,0:T(8,128)S(1)}, u32[]{:S(2)}, u32[]{:S(2)}) %collective-permute-start.17) | collective-permute-done | bytes 524320 | tf_op jit(solution)/shard_map/ppermute | solution.py:38
  96.3 0.7 collective-permute-done.19.refs_8_
  97.1 0.7 collective-permute-done.21.refs_10_
  97.8 2.6 %late.1 = f32[2,1,256,4096]{3,2,1,0:T(8,128)} custom-call(s32[2,4]{1,0:T(2,128)S(1)} %bitcast.9, s32[2,4]{1,0:T(2,128)S(1)} %collective-permute-done.refs_0_.refs_1_, s32[2,4]{1,0:T(2,128)S(1)} %collective-permute-done.1.refs_2_, s32[2,4]{1,0:T(2,128)S(1)} %collective-permute-done.2.refs_3_, ...), custom_call_target="tpu_custom_call", output_to_operand_aliasing={{}: (11, {})} | custom-call | tf_op jit(solution)/shard_map/late/pallas_call | solution.py:456
  (18 shorter events, 0.0 us)
Async XLA Ops:
  0.0 7.9 %collective-permute-start = (s32[2,4]{1,0:T(2,128)}, s32[2,4]{1,0:T(2,128)S(1)}, u32[]{:S(2)}, u32[]{:S(2)}) collective-permute-start(s32[2,4]{1,0:T(2,128)} %bitcast.1), channel_id=1, source_target_pairs={{0,4},{4,8},{8,12},{1,5},{5,9},{9,13},{2,6},{6,10},{10,14},{3,7},{... | collective-permute-start | bytes 104 | tf_op jit(solution)/shard_map/ppermute | solution.py:33
  4.9 0.7 copy-start.2
  7.9 15.9 %collective-permute-start.3 = (f32[2,256,256]{2,1,0:T(8,128)S(1)}, f32[2,256,256]{2,1,0:T(8,128)S(1)}, u32[]{:S(2)}, u32[]{:S(2)}) collective-permute-start(f32[2,256,256]{2,1,0:T(8,128)S(1)} %get-tuple-element.49), channel_id=1, source_target_pairs={{12,14},{14,12},{13,15},{15,13},{28,30},{30,28},{29,31},{31,29}} | collective-permute-start | bytes 1572872 | tf_op jit(solution)/shard_map/ppermute | solution.py:45
  8.6 15.9 %collective-permute-start.4 = (f32[2,256,256]{2,1,0:T(8,128)S(1)}, f32[2,256,256]{2,1,0:T(8,128)S(1)}, u32[]{:S(2)}, u32[]{:S(2)}) collective-permute-start(f32[2,256,256]{2,1,0:T(8,128)S(1)} %get-tuple-element.49), channel_id=1, source_target_pairs={{0,4},{4,8},{8,12},{1,5},{5,9},{9,13},{2,6},{6,10},{10,14},{3,7},{... | collective-permute-start | bytes 1572872 | tf_op jit(solution)/shard_map/ppermute | solution.py:33
  12.2 27.7 %collective-permute-start.6 = (f32[3,256,256]{2,1,0:T(8,128)S(1)}, f32[3,256,256]{2,1,0:T(8,128)S(1)}, u32[]{:S(2)}, u32[]{:S(2)}) collective-permute-start(f32[3,256,256]{2,1,0:T(8,128)S(1)} %get-tuple-element.56.refs_3_), channel_id=1, source_target_pairs={{0,4},{4,8},{8,12},{1,5},{5,9},{9,13},{2,6},{6,10},{10,14},{3,7},{... | collective-permute-start | bytes 2359304 | tf_op jit(solution)/shard_map/ppermute | solution.py:33
  18.0 3.6 %copy-start.3 = (s32[4,2]{0,1:T(2,128)S(1)}, s32[4,2]{0,1:T(2,128)}, u32[]{:S(2)}) copy-start(s32[4,2]{0,1:T(2,128)} %param.10) | copy-start | bytes 100
  18.0 15.5 %collective-permute-start.5 = (f32[2,256,256]{2,1,0:T(8,128)S(1)}, f32[2,256,256]{2,1,0:T(8,128)S(1)}, u32[]{:S(2)}, u32[]{:S(2)}) collective-permute-start(f32[2,256,256]{2,1,0:T(8,128)S(1)} %get-tuple-element.54), channel_id=1, source_target_pairs={{4,0},{8,4},{12,8},{5,1},{9,5},{13,9},{6,2},{10,6},{14,10},{7,3},{... | collective-permute-start | bytes 1572872 | tf_op jit(solution)/shard_map/ppermute | solution.py:33
  23.8 2.8 %copy-start.1 = (bf16[8,256,256]{2,1,0:T(8,128)(2,1)S(1)}, bf16[8,256,256]{2,1,0:T(8,128)(2,1)}, u32[]{:S(2)}) copy-start(bf16[8,256,256]{2,1,0:T(8,128)(2,1)} %constant.2.clone.pieces) | copy-start | bytes 3145732
  24.5 15.3 %copy-start = (f32[2,256,256]{2,1,0:T(8,128)S(1)}, f32[2,256,256]{2,1,0:T(8,128)}, u32[]{:S(2)}) copy-start(f32[2,256,256]{2,1,0:T(8,128)} %refs_1_.13) | copy-start | bytes 1572868
  25.1 14.7 %collective-permute-start.7 = (f32[2,256,256]{2,1,0:T(8,128)S(1)}, f32[2,256,256]{2,1,0:T(8,128)S(1)}, u32[]{:S(2)}, u32[]{:S(2)}) collective-permute-start(f32[2,256,256]{2,1,0:T(8,128)S(1)} %join.2), channel_id=1, source_target_pairs={{0,2},{2,0},{1,3},{3,1},{4,6},{6,4},{5,7},{7,5},{8,10},{10,8},{9,1... | collective-permute-start | bytes 1572872 | tf_op jit(solution)/shard_map/ppermute | solution.py:38
  26.6 7.5 %collective-permute-start.1 = (s32[2,4]{1,0:T(2,128)S(1)}, s32[2,4]{1,0:T(2,128)S(1)}, u32[]{:S(2)}, u32[]{:S(2)}) collective-permute-start(s32[2,4]{1,0:T(2,128)S(1)} %bitcast.4), channel_id=1, source_target_pairs={{0,1},{1,0},{2,3},{3,2},{4,5},{5,4},{6,7},{7,6},{8,9},{9,8},{10,11... | collective-permute-start | bytes 104 | tf_op jit(solution)/shard_map/ppermute | solution.py:38
  27.0 22.7 %collective-permute-start.8 = (f32[2,256,256]{2,1,0:T(8,128)S(1)}, f32[2,256,256]{2,1,0:T(8,128)S(1)}, u32[]{:S(2)}, u32[]{:S(2)}) collective-permute-start(f32[2,256,256]{2,1,0:T(8,128)S(1)} %get-tuple-element.43), channel_id=1, source_target_pairs={{4,0},{8,4},{12,8},{5,1},{9,5},{13,9},{6,2},{10,6},{14,10},{7,3},{... | collective-permute-start | bytes 1572872 | tf_op jit(solution)/shard_map/ppermute | solution.py:33
  33.5 1.3 %collective-permute-start.2 = (s32[2,4]{1,0:T(2,128)S(1)}, s32[2,4]{1,0:T(2,128)S(1)}, u32[]{:S(2)}, u32[]{:S(2)}) collective-permute-start(s32[2,4]{1,0:T(2,128)S(1)} %collective-permute-done.refs_0_.refs_1_), channel_id=1, source_target_pairs={{0,1},{1,0},{2,3},{3,2},{4,5},{5,4},{6,7},{7,6},{8,9},{9,8},{10,11... | collective-permute-start | bytes 104 | tf_op jit(solution)/shard_map/ppermute | solution.py:38
  34.1 15.6 %collective-permute-start.9 = (f32[2,256,256]{2,1,0:T(8,128)S(1)}, f32[2,256,256]{2,1,0:T(8,128)S(1)}, u32[]{:S(2)}, u32[]{:S(2)}) collective-permute-start(f32[2,256,256]{2,1,0:T(8,128)S(1)} %join.3), channel_id=1, source_target_pairs={{0,2},{2,0},{1,3},{3,1},{4,6},{6,4},{5,7},{7,5},{8,10},{10,8},{9,1... | collective-permute-start | bytes 1572872 | tf_op jit(solution)/shard_map/ppermute | solution.py:38
  46.9 16.5 %collective-permute-start.11 = (f32[2,256,256]{2,1,0:T(8,128)S(1)}, f32[2,256,256]{2,1,0:T(8,128)S(1)}, u32[]{:S(2)}, u32[]{:S(2)}) collective-permute-start(f32[2,256,256]{2,1,0:T(8,128)S(1)} %get-tuple-element.66), channel_id=1, source_target_pairs={{0,2},{2,0},{1,3},{3,1},{4,6},{6,4},{5,7},{7,5},{8,10},{10,8},{9,1... | collective-permute-start | bytes 1572872 | tf_op jit(solution)/shard_map/ppermute | solution.py:38
  48.5 14.9 %collective-permute-start.10 = (f32[2,256,256]{2,1,0:T(8,128)S(1)}, f32[2,256,256]{2,1,0:T(8,128)S(1)}, u32[]{:S(2)}, u32[]{:S(2)}) collective-permute-start(f32[2,256,256]{2,1,0:T(8,128)S(1)} %get-tuple-element.61.refs_1_.refs_5_), channel_id=1, source_target_pairs={{4,0},{8,4},{12,8},{5,1},{9,5},{13,9},{6,2},{10,6},{14,10},{7,3},{... | collective-permute-start | bytes 1572872 | tf_op jit(solution)/shard_map/ppermute | solution.py:33
  56.9 17.0 %collective-permute-start.14 = (f32[2,256,256]{2,1,0:T(8,128)S(1)}, f32[2,256,256]{2,1,0:T(8,128)S(1)}, u32[]{:S(2)}, u32[]{:S(2)}) collective-permute-start(f32[2,256,256]{2,1,0:T(8,128)S(1)} %get-tuple-element.63.refs_0_.refs_9_), channel_id=1, source_target_pairs={{0,4},{4,8},{8,12},{1,5},{5,9},{9,13},{2,6},{6,10},{10,14},{3,7},{... | collective-permute-start | bytes 1572872 | tf_op jit(solution)/shard_map/ppermute | solution.py:33
  62.0 12.0 %collective-permute-start.13 = (f32[2,256,256]{2,1,0:T(8,128)S(1)}, f32[2,256,256]{2,1,0:T(8,128)S(1)}, u32[]{:S(2)}, u32[]{:S(2)}) collective-permute-start(f32[2,256,256]{2,1,0:T(8,128)S(1)} %get-tuple-element.67), channel_id=1, source_target_pairs={{0,2},{2,0},{1,3},{3,1},{4,6},{6,4},{5,7},{7,5},{8,10},{10,8},{9,1... | collective-permute-start | bytes 1572872 | tf_op jit(solution)/shard_map/ppermute | solution.py:38
  63.5 16.3 %collective-permute-start.12 = (f32[4,2,256,256]{3,2,1,0:T(8,128)S(1)}, f32[4,2,256,256]{3,2,1,0:T(8,128)S(1)}, u32[]{:S(2)}, u32[]{:S(2)}) collective-permute-start(f32[4,2,256,256]{3,2,1,0:T(8,128)S(1)} %pack.2), channel_id=1, source_target_pairs={{0,1},{1,0},{2,3},{3,2},{4,5},{5,4},{6,7},{7,6},{8,9},{9,8},{10,11... | collective-permute-start | bytes 6291464 | tf_op jit(solution)/shard_map/ppermute | solution.py:38
  74.1 5.7 %collective-permute-start.15 = (f32[3,2,256,256]{3,2,1,0:T(8,128)S(1)}, f32[3,2,256,256]{3,2,1,0:T(8,128)S(1)}, u32[]{:S(2)}, u32[]{:S(2)}) collective-permute-start(f32[3,2,256,256]{3,2,1,0:T(8,128)S(1)} %pack.3), channel_id=1, source_target_pairs={{0,1},{1,0},{2,3},{3,2},{4,5},{5,4},{6,7},{7,6},{8,9},{9,8},{10,11... | collective-permute-start | bytes 4718600 | tf_op jit(solution)/shard_map/ppermute | solution.py:38
  74.1 15.4 %collective-permute-start.20 = (f32[2,256,256]{2,1,0:T(8,128)S(1)}, f32[2,256,256]{2,1,0:T(8,128)S(1)}, u32[]{:S(2)}, u32[]{:S(2)}) collective-permute-start(f32[2,256,256]{2,1,0:T(8,128)S(1)} %collective-permute-done.13.refs_1_.refs_10_), channel_id=1, source_target_pairs={{0,4},{4,8},{8,12},{1,5},{5,9},{9,13},{2,6},{6,10},{10,14},{3,7},{... | collective-permute-start | bytes 1572872 | tf_op jit(solution)/shard_map/ppermute | solution.py:33
  77.8 11.8 %collective-permute-start.18 = (f32[2,256,256]{2,1,0:T(8,128)S(1)}, f32[2,256,256]{2,1,0:T(8,128)S(1)}, u32[]{:S(2)}, u32[]{:S(2)}) collective-permute-start(f32[2,256,256]{2,1,0:T(8,128)S(1)} %get-tuple-element.71), channel_id=1, source_target_pairs={{12,14},{14,12},{13,15},{15,13},{28,30},{30,28},{29,31},{31,29}} | collective-permute-start | bytes 1572872 | tf_op jit(solution)/shard_map/ppermute | solution.py:45
  78.5 15.9 %collective-permute-start.16 = (f32[2,256,256]{2,1,0:T(8,128)S(1)}, f32[2,256,256]{2,1,0:T(8,128)S(1)}, u32[]{:S(2)}, u32[]{:S(2)}) collective-permute-start(f32[2,256,256]{2,1,0:T(8,128)S(1)} %collective-permute-done.11.refs_3_.refs_7_), channel_id=1, source_target_pairs={{4,0},{8,4},{12,8},{5,1},{9,5},{13,9},{6,2},{10,6},{14,10},{7,3},{... | collective-permute-start | bytes 1572872 | tf_op jit(solution)/shard_map/ppermute | solution.py:33
  94.4 1.9 %collective-permute-start.17 = (f32[2,256,256]{2,1,0:T(8,128)S(1)}, f32[2,256,256]{2,1,0:T(8,128)S(1)}, u32[]{:S(2)}, u32[]{:S(2)}) collective-permute-start(f32[2,256,256]{2,1,0:T(8,128)S(1)} %collective-permute-done.16.refs_5_), channel_id=1, source_target_pairs={{0,1},{1,0},{2,3},{3,2},{4,5},{5,4},{6,7},{7,6},{8,9},{9,8},{10,11... | collective-permute-start | bytes 1572872 | tf_op jit(solution)/shard_map/ppermute | solution.py:38
  94.4 2.7 %collective-permute-start.19 = (f32[2,256,256]{2,1,0:T(8,128)S(1)}, f32[2,256,256]{2,1,0:T(8,128)S(1)}, u32[]{:S(2)}, u32[]{:S(2)}) collective-permute-start(f32[2,256,256]{2,1,0:T(8,128)S(1)} %collective-permute-done.18.refs_7_), channel_id=1, source_target_pairs={{0,1},{1,0},{2,3},{3,2},{4,5},{5,4},{6,7},{7,6},{8,9},{9,8},{10,11... | collective-permute-start | bytes 1572872 | tf_op jit(solution)/shard_map/ppermute | solution.py:38
  94.9 2.9 %collective-permute-start.21 = (f32[2,256,256]{2,1,0:T(8,128)S(1)}, f32[2,256,256]{2,1,0:T(8,128)S(1)}, u32[]{:S(2)}, u32[]{:S(2)}) collective-permute-start(f32[2,256,256]{2,1,0:T(8,128)S(1)} %collective-permute-done.20.refs_9_), channel_id=1, source_target_pairs={{0,1},{1,0},{2,3},{3,2},{4,5},{5,4},{6,7},{7,6},{8,9},{9,8},{10,11... | collective-permute-start | bytes 1572872 | tf_op jit(solution)/shard_map/ppermute | solution.py:38

commit v7 on v6

--- a/solution.py
+++ b/solution.py
@@ -36,6 +36,14 @@
 def rotate(block, axis, distance):
     size = lax.axis_size(axis)
     return lax.ppermute(block, axis, [(i, (i + distance) % size) for i in range(size)])
+
+
+def swap(block, axis, phase):
+    size = lax.axis_size(axis)
+    route = []
+    for lower in range(phase, size - 1, 2):
+        route += [(lower, lower + 1), (lower + 1, lower)]
+    return lax.ppermute(block, axis, route)
 
 
 def rotate_last(block, distance):
@@ -125,40 +133,86 @@
     return damping * cosine, damping * sine * phase
 
 
+def is_lower(phase):
+    if isinstance(phase, str):
+        return phase == "lo"
+    return lax.rem(lax.axis_index("tile"), 2) == phase
+
+
+def pick(lower, first, second):
+    if isinstance(lower, bool):
+        return first if lower else second
+    return jnp.where(lower, first, second)
+
+
+def locate(spot, layout, tables, twin=0):
+    which, phase, k, distance = spot
+    sections, n_here, n_up, side = layout
+    owner = lax.rem(lax.axis_index("slab") + distance, sections)
+    here, up = owner * n_here + k, sections * n_here + owner * n_up + k
+    pairs, below = tables[2 * twin], tables[2 * twin + 1]
+    lower = True if which == "last" else is_lower(phase)
+    own, other = (here, up) if which == "slot" else (up, here)
+    row = lax.rem(pick(lower, pairs[0, own], below[0, other]), side)
+    col = pick(lower, pairs[1, own], below[1, other])
+    low, high = pick(lower, row, jnp.int32(0)), pick(lower, jnp.int32(side), row)
+    last = lax.axis_index("tile") == lax.axis_size("tile") - 1
+    if which == "last":
+        low = jnp.where(last, low, side)
+    elif which == "swap":
+        low = jnp.where(last & lower, side, low)
+    return pick(lower, own, other), row, col, low, high
+
+
 def slot_kernel(kind, *args):
     if kind == "last":
 
         @pl.when(lax.axis_index("tile") == lax.axis_size("tile") - 1)
         def _():
-            slot_body(kind, *args)
+            slot_body(*args)
     else:
-        slot_body(kind, *args)
-
-
-def slot_body(kind, base, each, sections, pairs, probe, measured, *refs):
-    pieces = 1 if kind == "last" else 2
+        slot_body(*args)
+
+
+def slot_body(spot, layout, pairs, below, probe, measured, *refs):
+    sections = layout[0]
+    which, phase = spot[:2]
+    pieces = 1 if which == "last" else 2
     own = refs[:pieces]
     others = refs[pieces : pieces + sections - 1]
     refs = refs[pieces + sections - 1 :]
     prop_left, prop_right, dft_left, dft_right = refs[:4]
     outs = refs[4 : 4 + sections]
-    wave, trans = refs[4 + sections : 6 + sections]
+    wave, trans, amplitude, sem = refs[4 + sections :]
     side = probe.shape[-1]
     slab = lax.axis_index("slab")
-    index = base + slab * each
-    row = lax.rem(pairs[0, index], side)
-    col = lax.rem(pairs[1, index], side)
-    if kind == "up":
-        amplitude = own[0].at[2]
-        fetch = None
+    index, row, col, low, high = locate(spot, layout, (pairs, below))
+    col = lax.rem(col, side)
+    lower = True if which == "last" else is_lower(phase)
+
+    def fetch():
+        return pltpu.make_async_copy(measured.at[index], amplitude, sem)
+
+    if lower is True:
+        fetch().start()
+    elif lower is False:
+        amplitude[...] = own[1][2]
     else:
-        amplitude, sem = refs[6 + sections :]
-        fetch = pltpu.make_async_copy(measured.at[index], amplitude, sem)
-        fetch.start()
+
+        @pl.when(lower)
+        def _():
+            fetch().start()
+            fetch().wait()
+
+        @pl.when(jnp.logical_not(lower))
+        def _():
+            amplitude[...] = own[1][2]
+
     rows = lax.broadcasted_iota(jnp.int32, (side, side), 0)
     patch = [own[0][0], own[0][1]]
     if pieces == 2:
-        patch = [jnp.where(rows >= row, own[0][k], own[1][k]) for k in range(2)]
+        local_rows = (rows >= low) & (rows < high)
+        patch = [jnp.where(local_rows, own[0][k], own[1][k]) for k in range(2)]
     trans[slab, 0], trans[slab, 1] = transmission(patch[0], patch[1])
     for distance in range(1, sections):
         owner = lax.rem(slab + (sections - distance), sections)
@@ -175,8 +229,8 @@
             wave[step + 1, 0] = real
             wave[step + 1, 1] = imag
     real, imag = two_sided(dft_left, dft_right, real, imag)
-    if fetch is not None:
-        fetch.wait()
+    if lower is True:
+        fetch().wait()
     factor = 1.0 - amplitude[...] * lax.rsqrt(jnp.maximum(real * real + imag * imag, 0.25))
     real, minus = two_sided(dft_left, dft_right, real * factor, -imag * factor)
     for step in range(sections - 1, -1, -1):
@@ -191,45 +245,35 @@
         outs[distance][...] = wave[lax.rem(slab + distance, sections)]
 
 
-def run_slot(kind, base, each, pairs, probe, measured, own, others, constants):
-    sections = len(others) + 1
-    side = probe.shape[-1]
+def run_slot(kind, spot, layout, pairs, below, probe, measured, own, others, constants):
+    sections, side = layout[0], layout[3]
     shape = jax.ShapeDtypeStruct((2, side, side), jnp.float32)
-    scratch = [pltpu.VMEM((sections, 2, side, side), jnp.float32)] * 2
-    if kind != "up":
-        scratch += [pltpu.VMEM((side, side), jnp.float32), pltpu.SemaphoreType.DMA(())]
     return pl.pallas_call(
-        lambda *refs: slot_kernel(kind, base, each, sections, *refs),
-        in_specs=[SMEM, VMEM, HBM]
-        + [VMEM] * (len(own) + len(others) + 4),
+        lambda *refs: slot_kernel(kind, spot, layout, *refs),
+        in_specs=[SMEM, SMEM, VMEM, HBM] + [VMEM] * (len(own) + len(others) + 4),
         out_specs=[VMEM] * sections,
         out_shape=[shape] * sections,
-        scratch_shapes=scratch,
+        scratch_shapes=[pltpu.VMEM((sections, 2, side, side), jnp.float32)] * 2
+        + [pltpu.VMEM((side, side), jnp.float32), pltpu.SemaphoreType.DMA(())],
         compiler_params=params(32),
         name="slot_" + kind,
-    )(pairs, probe, measured, *own, *others, *constants)
-
-
-def position(k, bases, slab, sections):
-    base, each, distance = bases[k]
-    return base + lax.rem(slab + distance, sections) * each
-
-
-def cut_kernel(bases, sections, send, pairs, phase, absorption, *refs):
-    count = len(bases)
-    side = phase.shape[1]
+    )(pairs, below, probe, measured, *own, *others, *constants)
+
+
+def cut_kernel(spots, layout, with_measured, pairs, below, phase, absorption, *refs):
+    count, side = len(spots), layout[3]
     blocks = phase.shape[2] // side
-    slab = lax.axis_index("slab")
     extra = None
-    if send is not None:
-        extra = (refs[0].at[send[0] + slab * send[1]], refs[1].at[2], refs[-3])
-        extra = pltpu.make_async_copy(*extra)
+    if with_measured:
+        sections, n_here, n_up, side = layout
+        index = sections * n_here + lax.axis_index("slab") * n_up + spots[0][2]
+        extra = pltpu.make_async_copy(refs[0].at[index], refs[1].at[2], refs[-3])
         refs = refs[1:]
     outs = refs[:count]
     buffer, sems = refs[-2], refs[-1]
     copies, columns = [], []
     for k in range(count):
-        column = pairs[1, position(k, bases, slab, sections)]
+        column = locate(spots[k], layout, (pairs, below))[2]
         first = lax.div(column, side)
         columns.append(lax.rem(column, side))
         for which, source in enumerate((phase, absorption)):
@@ -257,50 +301,48 @@
         extra.wait()
 
 
-def cut(bases, pairs, phase, absorption, measured=None, send=None):
-    side = phase.shape[1]
-    count = len(bases)
-    sections = lax.axis_size("slab")
+def cut(spots, layout, pairs, below, phase, absorption, measured=None):
+    side = layout[3]
+    count = len(spots)
     shapes = [jax.ShapeDtypeStruct((2, side, side), jnp.float32)] * count
     scratch = [
         pltpu.VMEM((count, 2, 2, side, side), jnp.float32),
         pltpu.SemaphoreType.DMA((count, 2, 2)),
     ]
-    inputs = [pairs, phase, absorption]
-    if send is not None:
+    inputs = [phase, absorption]
+    if measured is not None:
         shapes = [jax.ShapeDtypeStruct((3, side, side), jnp.float32)] + shapes[1:]
         scratch = [pltpu.SemaphoreType.DMA(())] + scratch
         inputs.append(measured)
     return pl.pallas_call(
-        lambda *refs: cut_kernel(bases, sections, send, *refs),
-        in_specs=[SMEM] + [HBM] * (len(inputs) - 1),
+        lambda *refs: cut_kernel(spots, layout, measured is not None, *refs),
+        in_specs=[SMEM, SMEM] + [HBM] * len(inputs),
         out_specs=[VMEM] * count,
         out_shape=shapes,
         scratch_shapes=scratch,
         compiler_params=params(16),
         name="cut",
-    )(*inputs)
-
-
-def join_kernel(bases, sections, pairs, here, there, out):
-    side = out.shape[-1]
-    slab = lax.axis_index("slab")
-    row = lax.rem(pairs[0, position(0, bases, slab, sections)], side)
+    )(pairs, below, *inputs)
+
+
+def join_kernel(spot, layout, pairs, below, here, there, out):
+    side = layout[3]
+    low, high = locate(spot, layout, (pairs, below))[3:]
     rows = lax.broadcasted_iota(jnp.int32, (side, side), 0)
+    keep = (rows >= low) & (rows < high)
     for part in range(2):
-        out[part] = jnp.where(rows >= row, here[part], there[part])
-
-
-def join(base, pairs, here, there):
-    sections = lax.axis_size("slab")
+        out[part] = jnp.where(keep, here[part], there[part])
+
+
+def join(spot, layout, pairs, below, here, there):
     return pl.pallas_call(
-        lambda *refs: join_kernel([base], sections, *refs),
-        in_specs=[SMEM, VMEM, VMEM],
+        lambda *refs: join_kernel(spot, layout, *refs),
+        in_specs=[SMEM, SMEM, VMEM, VMEM],
         out_specs=VMEM,
         out_shape=jax.ShapeDtypeStruct(here.shape, jnp.float32),
         compiler_params=params(8),
         name="join",
-    )(pairs, here, there)
+    )(pairs, below, here, there)
 
 
 def pack_kernel(*refs):
@@ -334,26 +376,16 @@
     return views, kinds
 
 
-def spans(metas, tables, side, sections):
-    slab = lax.axis_index("slab")
-    last = lax.axis_index("tile") == lax.axis_size("tile") - 1
+def spans(metas, tables, layout):
+    side = layout[3]
     out = []
-    for source, base, mode in metas:
-        index = position(0, [base], slab, sections)
-        row, col = tables[source][0, index], tables[source][1, index]
-        row = lax.rem(row, side)
-        low, high = row, jnp.int32(side)
-        if mode == "below":
-            low, high = jnp.int32(0), row
-        elif mode == "last":
-            low = jnp.where(last, row, side)
-        elif mode == "inner":
-            low = jnp.where(last, side, row)
+    for twin, spot in metas:
+        index, row, col, low, high = locate(spot, layout, tables, twin)
         out.append((lax.div(col, side), lax.rem(col, side), low, high))
     return out
 
 
-def early_kernel(metas, sections, *refs):
+def early_kernel(metas, layout, *refs):
     count = len(metas)
     tables, terms = refs[:4], refs[4 : 4 + count]
     out, copied, sem = refs[4 + count :]
@@ -367,7 +399,7 @@
     def _(block):
         out[:, :, pl.ds(pl.multiple_of(block * side, side), side)] = jnp.zeros((2, side, side), jnp.float32)
 
-    for k, (first, col, low, high) in enumerate(spans(metas, tables, side, sections)):
+    for k, (first, col, low, high) in enumerate(spans(metas, tables, layout)):
         for half in range(2):
             block = first + half
 
@@ -384,11 +416,10 @@
     copy.wait()
 
 
-def early(metas, tables, terms, cols_total):
-    side = terms[0].shape[-1]
-    sections = lax.axis_size("slab")
+def early(metas, layout, tables, terms, cols_total):
+    side = layout[3]
     return pl.pallas_call(
-        lambda *refs: early_kernel(metas, sections, *refs),
+        lambda *refs: early_kernel(metas, layout, *refs),
         in_specs=[SMEM] * 4 + [VMEM] * len(terms),
         out_specs=[VMEM, HBM],
         out_shape=[
@@ -401,7 +432,7 @@
     )(*tables, *terms)
 
 
-def late_kernel(metas, sections, *refs):
+def late_kernel(metas, layout, *refs):
     count = len(metas)
     tables, total, terms = refs[:4], refs[4], refs[5 : 5 + count]
     out, stage, sems = refs[6 + count :]
@@ -409,7 +440,7 @@
     blocks = out.shape[-1] // side
     rows = lax.broadcasted_iota(jnp.int32, (side, side), 0)
     lane = lax.broadcasted_iota(jnp.int32, (side, side), 1)
-    ranges = spans(metas, tables, side, sections)
+    ranges = spans(metas, tables, layout)
 
     def place(block):
         return pl.ds(pl.multiple_of(block * side, side), side)
@@ -449,12 +480,11 @@
             send(block).wait()
 
 
-def late(metas, tables, total, copied, terms):
-    side = terms[0].shape[-1]
+def late(metas, layout, tables, total, copied, terms):
+    side = layout[3]
     cols_total = total.shape[-1]
-    sections = lax.axis_size("slab")
     return pl.pallas_call(
-        lambda *refs: late_kernel(metas, sections, *refs),
+        lambda *refs: late_kernel(metas, layout, *refs),
         in_specs=[SMEM] * 4 + [VMEM] * (1 + len(terms)) + [HBM],
         out_specs=HBM,
         input_output_aliases={5 + len(terms): 0},
@@ -477,132 +507,112 @@
     n_here = each - n_up
     distances = list(range(sections))
 
+    layout = (sections, n_here, n_up, side)
     pairs = offsets.T
-    here = lambda k, d: (k, n_here, d)
-    up = lambda k, d: (sections * n_here + k, n_up, d)
+    below = move(pairs, "tile", 1)
     back = lambda d: (sections - d) % sections
-
     far = distances[1:]
     phase = pltpu.with_memory_space_constraint(phase, pltpu.HBM)
     absorption = pltpu.with_memory_space_constraint(absorption, pltpu.HBM)
     measured = pltpu.with_memory_space_constraint(measured, pltpu.HBM)
+
+    rounds, last_round = [], {}
+    for k in range(n_here):
+        if n_here == n_up:
+            last_round[k] = 2 * k + (lax.axis_size("tile") - 1) % 2
+            for parity in range(2):
+                there = lambda value, parity=parity: swap(value, "tile", parity)
+                rounds.append((k, parity, parity, there, there))
+        else:
+            rise = lambda value: move(value, "tile", 1)
+            fall = lambda value: move(value, "tile", -1)
+            if k < n_up:
+                last_round[k] = len(rounds)
+                rounds.append((k, "hi", "lo", rise, fall))
+            rounds.append((k, "lo", "hi", fall, rise))
+    count = len(rounds)
     done = [pairs]
 
-    def step(kernel, scalars, *args):
-        out = kernel(after(scalars, *done), *args)
+    def step(kernel):
+        out = kernel(after(pairs, *done))
         done[:] = [out[0] if isinstance(out, (list, tuple)) else out]
         return out
 
-    def cutter(table, kinds, *args):
-        return step(lambda p: cut(kinds, p, phase, absorption, *args), table)
-
-    def joiner(table, kind, *args):
-        return step(lambda p: join(kind, p, *args), table)
-
-    def slotter(table, kind, base, each, *args):
-        return step(lambda p: run_slot(kind, base, each, p, probe, *args, constants), table)
-
-    below = move(pairs, "tile", 1)
-    lower = [
-        cutter(pairs, [up(k, d) for d in distances], measured, (up(k, 0)[0], n_up))
-        for k in range(n_up)
-    ]
-    extra = [[rotate_last(after(lower[k][d], below), d) for d in far] for k in range(n_up)]
-    raised = [[move(after(lower[k][d], below), "tile", 1) for d in far] for k in range(n_up)]
-    for k in range(n_up):
-        raised[k].insert(0, move(after(lower[k][0], below), "tile", 1))
-    low_cuts = [cutter(below, [here(k, d) for d in distances]) for k in range(n_here)]
-    lowered = [[move(low_cuts[k][d], "tile", -1) for d in far] for k in range(n_here)]
-    for k in range(n_here):
-        lowered[k].insert(0, move(low_cuts[k][0], "tile", -1))
-    up_cuts = [cutter(below, [up(k, d) for d in distances]) for k in range(n_up)]
-    own_cuts = [cutter(pairs, [here(k, d) for d in distances]) for k in range(n_here)]
+    spots = [("send", rounds[i][2], rounds[i][0], d) for i in range(count) for d in far]
+    pieces = step(lambda p: cut(spots, layout, p, below, phase, absorption)) if spots else []
+    sent, got = [], []
+    for i, (k, role, send_role, there, home) in enumerate(rounds):
+        sent.append([None, *pieces[i * len(far) : (i + 1) * len(far)]])
+        got.append([None] + [there(piece) for piece in sent[i][1:]])
+    for i, (k, role, send_role, there, home) in enumerate(rounds):
+        extra_input = [] if role == "lo" else [measured]
+        spots = [("send", send_role, k, 0)]
+        sent[i][0] = step(lambda p: cut(spots, layout, p, below, phase, absorption, *extra_input))[0]
+        got[i][0] = there(sent[i][0])
+    ends = sorted(last_round)
+    extra = [[rotate_last(sent[last_round[k]][d], d) for d in far] for k in ends]
+    held = []
+    for k, role, send_role, there, home in rounds:
+        spots = [("slot", role, k, d) for d in distances]
+        held.append(step(lambda p: cut(spots, layout, p, below, phase, absorption)))
     constants = expand(side)
     done += [value for row in extra for value in row]
-    up_joined = [
-        [joiner(below, up(k, d), raised[k][d], up_cuts[k][d]) for d in far] for k in range(n_up)
-    ]
-    up_other = [[rotate(up_joined[k][d - 1], "slab", d) for d in far] for k in range(n_up)]
-    here_joined = [
-        [joiner(pairs, here(k, d), own_cuts[k][d], lowered[k][d]) for d in far]
-        for k in range(n_here)
-    ]
-    here_other = [[rotate(here_joined[k][d - 1], "slab", d) for d in far] for k in range(n_here)]
+    others = []
+    for i, (k, role, send_role, there, home) in enumerate(rounds):
+        joined = []
+        for d in far:
+            spot = ("slot", role, k, d)
+            joined.append(step(lambda p: join(spot, layout, p, below, held[i][d], got[i][d])))
+        others.append([rotate(joined[d - 1], "slab", d) for d in far])
 
     other_pairs, other_below = rotate(pairs, "batch", 1), rotate(below, "batch", 1)
     done += [other_pairs, other_below]
     tables = [pairs, below, other_pairs, other_below]
 
-    up_outs = [
-        slotter(
-            below, "up", up(k, 0)[0], n_up, measured, [raised[k][0], up_cuts[k][0]], up_other[k]
+    def slot(kind, spot, own, rest):
+        return step(
+            lambda p: run_slot(kind, spot, layout, p, below, probe, measured, own, rest, constants)
         )
-        for k in range(n_up)
+
+    outs, backs, homes = [], [], []
+    for i, (k, role, send_role, there, home) in enumerate(rounds):
+        outs.append(slot(f"{i}", ("slot", role, k, 0), [held[i][0], got[i][0]], others[i]))
+        backs.append([rotate(outs[i][d], "slab", d) for d in far])
+        homes.append(home(outs[i][0]))
+    last_outs = [
+        slot("last", ("last", "lo", k, 0), [sent[last_round[k]][0]], extra[n])
+        for n, k in enumerate(ends)
     ]
-    up_back = [[rotate(up_outs[k][d], "slab", d) for d in far] for k in range(n_up)]
-    fallen = [move(up_outs[k][0], "tile", -1) for k in range(n_up)]
-    here_outs = [
-        slotter(
-            pairs, "here", here(k, 0)[0], n_here, measured,
-            [own_cuts[k][0], lowered[k][0]], here_other[k],
-        )
-        for k in range(n_here)
-    ]
-    last_outs = [
-        slotter(pairs, "last", up(k, 0)[0], n_up, measured, [lower[k][0]], extra[k])
-        for k in range(n_up)
-    ]
-    here_back = [[rotate(here_outs[k][d], "slab", d) for d in far] for k in range(n_here)]
-    risen = [move(here_outs[k][0], "tile", 1) for k in range(n_here)]
-
-    twin = lambda kind: (kind[0] + 2, kind[1], kind[2])
     terms, kinds = [], []
 
-    def group(items, gate=None):
-        values = [value for value, kind in items]
-        if gate is not None:
-            values[0] = after(values[0], gate)
+    def group(items):
+        values = [value for value, spot in items]
         twins = rotate(pack(values), "batch", 1)
         terms.extend(values + [twins])
-        kinds.extend([kind for value, kind in items] + [[twin(kind) for value, kind in items]])
-        return twins
-
-    items = []
-    for k in range(n_up):
-        items.append((last_outs[k][0], (0, up(k, 0), "last")))
-        items.append((up_outs[k][0], (1, up(k, 0), "below")))
-        items.append((fallen[k], (0, up(k, 0), "inner")))
+        kinds.extend([(0, spot) for value, spot in items] + [[(1, spot) for value, spot in items]])
+
+    final, final_kinds = [], []
+    ending = [
+        [rotate_last(after(last_outs[n][d], *backs[-1]), d) for d in far] for n in range(len(ends))
+    ]
+    last_items = [(last_outs[n][0], ("last", "lo", k, 0)) for n, k in enumerate(ends)]
+    for i, (k, role, send_role, there, home) in enumerate(rounds):
+        items = [(outs[i][0], ("slot", role, k, 0))]
+        items += [(backs[i][d - 1], ("slot", role, k, back(d))) for d in far]
+        items.append((homes[i], ("swap", send_role, k, 0)))
+        if i == 0:
+            items = last_items + items
+        group(items)
         for d in far:
-            items.append((up_back[k][d - 1], (1, up(k, back(d)), "below")))
-    if items:
-        group(items)
-    falling = [[move(value, "tile", -1) for value in row] for row in up_back]
-    rising = [[move(value, "tile", 1) for value in row] for row in here_back]
-    ending = [
-        [rotate_last(after(last_outs[k][d], *here_back[0]), d) for d in far] for k in range(n_up)
-    ]
-    items = []
-    for k in range(n_here):
-        items.append((here_outs[k][0], (0, here(k, 0), "above")))
-        for d in far:
-            items.append((here_back[k][d - 1], (0, here(k, back(d)), "above")))
-        items.append((risen[k], (1, here(k, 0), "below")))
-    group(items)
-    total, copied = early(kinds, tables, terms, cols_total)
-    final, final_kinds = [], []
-
-    def add(value, kind):
-        final.extend([value, rotate(after(value, total), "batch", 1)])
-        final_kinds.extend([kind, twin(kind)])
-
-    for k in range(n_up):
-        for d in far:
-            add(falling[k][d - 1], (0, up(k, back(d)), "inner"))
-            add(ending[k][d - 1], (0, up(k, back(d)), "last"))
-    for k in range(n_here):
-        for d in far:
-            add(rising[k][d - 1], (1, here(k, back(d)), "below"))
-    return late(final_kinds, tables, total, copied, final)
+            final.append((home(backs[i][d - 1]), ("swap", send_role, k, back(d))))
+    for n, k in enumerate(ends):
+        final += [(ending[n][d - 1], ("last", "lo", k, back(d))) for d in far]
+    total, copied = early(kinds, layout, tables, terms, cols_total)
+    values = []
+    for value, spot in final:
+        values += [value, rotate(after(value, total), "batch", 1)]
+        final_kinds += [(0, spot), (1, spot)]
+    return late(final_kinds, layout, tables, total, copied, values)
 
 
 def solution(mesh):

time: 101 us -> 98.2 us (0.972)
  starting transfers between devices: 32.3 us -> 25.9 us
  Pallas kernels: 34.1 us -> 36.6 us
  waiting for transfers between devices: 33 us -> 34.2 us
    ppermute x9 -> x1, starting transfers between devices: 25.9 us -> 4.92 us  [move(): return lax.ppermute(block, axis, route)]
    ppermute x0 -> x8, waiting for transfers between devices: none -> 19.7 us  [swap(): return lax.ppermute(block, axis, route)]
    ppermute x9 -> x1, waiting for transfers between devices: 19.8 us -> 1.49 us  [move(): return lax.ppermute(block, axis, route)]
    ppermute x0 -> x8, starting transfers between devices: none -> 12.6 us  [swap(): return lax.ppermute(block, axis, route)]
    pallas_call x11 -> x12, Pallas kernels: 33.5 us -> 36 us  [the longest x3 15.6 us: run_slot(): pl.pallas_call(lambda *refs: slot_kernel(kind, spot, layout, *refs), in_s...]
    ppermute x11, starting transfers between devices: 5.01 us -> 7.02 us  [rotate(): lax.ppermute(block, axis, [(i, (i + distance) % size) for i in range(size)])]
  transfers between devices with their start and end apart: 22 -> 22, of which waited for: 9 -> 9; matrix products, arithmetic and copies ran while one was open for 0% -> 0% of each run, Pallas kernels for 31% -> 32%
where the time goes in v7:
time: 98.2 us; the launch traced here: 97.8 us
  Pallas kernels  36.6 us (37%)
  waiting for transfers between devices  34.2 us (35%)
  starting transfers between devices  25.9 us (26%)
    ppermute x8, waiting for transfers between devices, swap(): return lax.ppermute(block, axis, route)  19.7 us
    pallas_call x3, Pallas kernels, run_slot(): pl.pallas_call(lambda *refs: slot_kernel(kind, spot, layout, *refs), in_s...  15.6 us
    ppermute x11, waiting for transfers between devices, rotate(): lax.ppermute(block, axis, [(i, (i + distance) % size) for i in range(size)])  13 us
    ppermute x8, starting transfers between devices, swap(): return lax.ppermute(block, axis, route)  12.6 us
    pallas_call x5, Pallas kernels, cut(): pl.pallas_call(lambda *refs: cut_kernel(spots, layout, measured is not No...  10.5 us
    ppermute x11, starting transfers between devices, rotate(): lax.ppermute(block, axis, [(i, (i + distance) % size) for i in range(size)])  7.02 us
    pallas_call x1, Pallas kernels, early(): pl.pallas_call(lambda *refs: early_kernel(metas, layout, *refs), in_specs...  5.82 us
    ppermute x1, starting transfers between devices, move(): return lax.ppermute(block, axis, route)  4.92 us
  transfers between devices with their start and end apart: 22, of which 9 were waited for; matrix products, arithmetic and copies ran while one was open for 0% of the time, Pallas kernels for 32%

profile of v7, /device:TPU:0, one launch (start us, length us, event | category | flops | bytes accessed | tf_op | source)
XLA Modules:
  0.0 97.8 jit_solution(17941987581896133052)
XLA Ops:
  0.0 4.9 %collective-permute-start = (s32[2,4]{1,0:T(2,128)}, s32[2,4]{1,0:T(2,128)S(1)}, u32[]{:S(2)}, u32[]{:S(2)}) collective-permute-start(s32[2,4]{1,0:T(2,128)} %bitcast.1), channel_id=1, source_target_pairs={{0,4},{4,8},{8,12},{1,5},{5,9},{9,13},{2,6},{6,10},{10,14},{3,7},{... | collective-permute-start | bytes 104 | tf_op jit(solution)/shard_map/ppermute | solution.py:33
  4.9 1.5 %collective-permute-done.refs_1_ = s32[2,4]{1,0:T(2,128)S(1)} collective-permute-done((s32[2,4]{1,0:T(2,128)}, s32[2,4]{1,0:T(2,128)S(1)}, u32[]{:S(2)}, u32[]{:S(2)}) %collective-permute-start) | collective-permute-done | bytes 64 | tf_op jit(solution)/shard_map/ppermute | solution.py:33
  6.4 0.7 copy-done.2
  7.1 2.2 %cut.5 = (f32[2,256,256]{2,1,0:T(8,128)S(1)}, f32[2,256,256]{2,1,0:T(8,128)S(1)}) custom-call(s32[2,4]{1,0:T(2,128)S(1)} %bitcast.2, s32[2,4]{1,0:T(2,128)S(1)} %collective-permute-done.refs_1_, f32[1,256,4096]{2,1,0:T(8,128)} %refs_2_.12, f32[1,256,4096]{2,1,0:T(8,128)} %refs_3_.12), custom_call_target="tpu_custom_call" | custom-call | tf_op jit(solution)/shard_map/cut/pallas_call | solution.py:317
  9.3 0.7 collective-permute-start.3
  10.0 2.3 %collective-permute-start.4 = (f32[2,256,256]{2,1,0:T(8,128)S(1)}, f32[2,256,256]{2,1,0:T(8,128)S(1)}, u32[]{:S(2)}, u32[]{:S(2)}) collective-permute-start(f32[2,256,256]{2,1,0:T(8,128)S(1)} %get-tuple-element.38), channel_id=1, source_target_pairs={{0,4},{4,0},{8,12},{12,8},{1,5},{5,1},{9,13},{13,9},{2,6},{6,2},{1... | collective-permute-start | bytes 1572872 | tf_op jit(solution)/shard_map/ppermute | solution.py:46
  12.3 1.9 %cut.6 = f32[3,256,256]{2,1,0:T(8,128)S(1)} custom-call(s32[2,4]{1,0:T(2,128)S(1)} %bitcast.3, s32[2,4]{1,0:T(2,128)S(1)} %collective-permute-done.refs_1_, f32[1,256,4096]{2,1,0:T(8,128)} %refs_2_.12, f32[1,256,4096]{2,1,0:T(8,128)} %refs_3_.12, f32[4,256,256]{2,1,0:T(8,128)} %refs_3_.15), custom_call_target="tpu_custom_call" | custom-call | tf_op jit(solution)/shard_map/cut/pallas_call | solution.py:317
  14.3 0.1 collective-permute-start.6
  14.4 0.7 collective-permute-start.5
  15.1 1.9 %cut.7.refs_4_ = f32[3,256,256]{2,1,0:T(8,128)S(1)} custom-call(s32[2,4]{1,0:T(2,128)S(1)} %bitcast.4, s32[2,4]{1,0:T(2,128)S(1)} %collective-permute-done.refs_1_, f32[1,256,4096]{2,1,0:T(8,128)} %refs_2_.12, f32[1,256,4096]{2,1,0:T(8,128)} %refs_3_.12, f32[4,256,256]{2,1,0:T(8,128)} %refs_3_.15), custom_call_target="tpu_custom_call" | custom-call | tf_op jit(solution)/shard_map/cut/pallas_call | solution.py:317
  17.0 2.2 %cut.8 = (f32[2,256,256]{2,1,0:T(8,128)S(1)}, f32[2,256,256]{2,1,0:T(8,128)S(1)}) custom-call(s32[2,4]{1,0:T(2,128)S(1)} %bitcast.5, s32[2,4]{1,0:T(2,128)S(1)} %collective-permute-done.refs_1_, f32[1,256,4096]{2,1,0:T(8,128)} %refs_2_.12, f32[1,256,4096]{2,1,0:T(8,128)} %refs_3_.12), custom_call_target="tpu_custom_call" | custom-call | tf_op jit(solution)/shard_map/cut/pallas_call | solution.py:317
  19.2 2.3 %cut.9 = (f32[2,256,256]{2,1,0:T(8,128)S(1)}, f32[2,256,256]{2,1,0:T(8,128)S(1)}) custom-call(s32[2,4]{1,0:T(2,128)S(1)} %bitcast.6, s32[2,4]{1,0:T(2,128)S(1)} %collective-permute-done.refs_1_, f32[1,256,4096]{2,1,0:T(8,128)} %refs_2_.12, f32[1,256,4096]{2,1,0:T(8,128)} %refs_3_.12), custom_call_target="tpu_custom_call" | custom-call | tf_op jit(solution)/shard_map/cut/pallas_call | solution.py:317
  21.5 0.0 copy-start.1
  21.5 3.7 %collective-permute-done.4.refs_3_ = f32[2,256,256]{2,1,0:T(8,128)S(1)} collective-permute-done((f32[2,256,256]{2,1,0:T(8,128)S(1)}, f32[2,256,256]{2,1,0:T(8,128)S(1)}, u32[]{:S(2)}, u32[]{:S(2)}) %collective-permute-start.4) | collective-permute-done | bytes 524320 | tf_op jit(solution)/shard_map/ppermute | solution.py:46
  25.2 0.6 join.2
  25.8 1.6 %collective-permute-start.7 = (f32[2,256,256]{2,1,0:T(8,128)S(1)}, f32[2,256,256]{2,1,0:T(8,128)S(1)}, u32[]{:S(2)}, u32[]{:S(2)}) collective-permute-start(f32[2,256,256]{2,1,0:T(8,128)S(1)} %join.2), channel_id=1, source_target_pairs={{0,2},{2,0},{1,3},{3,1},{4,6},{6,4},{5,7},{7,5},{8,10},{10,8},{9,1... | collective-permute-start | bytes 1572872 | tf_op jit(solution)/shard_map/ppermute | solution.py:38
  27.4 0.7 collective-permute-start.8
  28.1 0.1 collective-permute-start.1
  28.2 0.4 expand.1
  28.6 0.0 collective-permute-done.5.refs_3_
  28.6 0.5 collective-permute-start.2
  29.2 0.6 join.3
  29.8 0.6 collective-permute-start.9
  30.4 9.5 %collective-permute-done.6.refs_5_ = f32[3,256,256]{2,1,0:T(8,128)S(1)} collective-permute-done((f32[3,256,256]{2,1,0:T(8,128)S(1)}, f32[3,256,256]{2,1,0:T(8,128)S(1)}, u32[]{:S(2)}, u32[]{:S(2)}) %collective-permute-start.6) | collective-permute-done | bytes 786464 | tf_op jit(solution)/shard_map/ppermute | solution.py:46
  40.0 7.9 %slot_0.1 = (f32[2,256,256]{2,1,0:T(8,128)S(1)}, f32[2,256,256]{2,1,0:T(8,128)S(1)}) custom-call(s32[2,4]{1,0:T(2,128)S(1)} %bitcast.10, s32[2,4]{1,0:T(2,128)S(1)} %collective-permute-done.refs_1_, f32[2,256,256]{2,1,0:T(8,128)S(1)} %copy-done, f32[4,256,256]{2,1,0:T(8,128)} %refs_3_.15, f32[2,256,256]{2,1,0:T(8,128)S(1)} %get-tuple-element.42.refs_4_, ...), custom_call_target="tpu_custom_call" | custom-call | tf_op jit(solution)/shard_map/slot_0/pallas_call | solution.py:251
  47.9 1.6 %collective-permute-start.10 = (f32[2,256,256]{2,1,0:T(8,128)S(1)}, f32[2,256,256]{2,1,0:T(8,128)S(1)}, u32[]{:S(2)}, u32[]{:S(2)}) collective-permute-start(f32[2,256,256]{2,1,0:T(8,128)S(1)} %get-tuple-element.60), channel_id=1, source_target_pairs={{0,2},{2,0},{1,3},{3,1},{4,6},{6,4},{5,7},{7,5},{8,10},{10,8},{9,1... | collective-permute-start | bytes 1572872 | tf_op jit(solution)/shard_map/ppermute | solution.py:38
  49.5 0.8 collective-permute-start.11
  50.3 7.0 %slot_1.1 = (f32[2,256,256]{2,1,0:T(8,128)S(1)}, f32[2,256,256]{2,1,0:T(8,128)S(1)}) custom-call(s32[2,4]{1,0:T(2,128)S(1)} %bitcast.11, s32[2,4]{1,0:T(2,128)S(1)} %collective-permute-done.refs_1_, f32[2,256,256]{2,1,0:T(8,128)S(1)} %copy-done, f32[4,256,256]{2,1,0:T(8,128)} %refs_3_.15, f32[2,256,256]{2,1,0:T(8,128)S(1)} %get-tuple-element.44.refs_4_, ...), custom_call_target="tpu_custom_call" | custom-call | tf_op jit(solution)/shard_map/slot_1/pallas_call | solution.py:251
  57.3 0.7 collective-permute-start.14
  58.0 2.0 %collective-permute-start.13 = (f32[2,256,256]{2,1,0:T(8,128)S(1)}, f32[2,256,256]{2,1,0:T(8,128)S(1)}, u32[]{:S(2)}, u32[]{:S(2)}) collective-permute-start(f32[2,256,256]{2,1,0:T(8,128)S(1)} %get-tuple-element.61), channel_id=1, source_target_pairs={{0,2},{2,0},{1,3},{3,1},{4,6},{6,4},{5,7},{7,5},{8,10},{10,8},{9,1... | collective-permute-start | bytes 1572872 | tf_op jit(solution)/shard_map/ppermute | solution.py:38
  60.0 0.8 slot_last.1
  60.7 1.0 %collective-permute-done.10.refs_2_.refs_6_ = f32[2,256,256]{2,1,0:T(8,128)S(1)} collective-permute-done((f32[2,256,256]{2,1,0:T(8,128)S(1)}, f32[2,256,256]{2,1,0:T(8,128)S(1)}, u32[]{:S(2)}, u32[]{:S(2)}) %collective-permute-start.10) | collective-permute-done | bytes 524320 | tf_op jit(solution)/shard_map/ppermute | solution.py:38
  61.8 0.1 pack.2
  61.9 0.1 collective-permute-start.12
  62.0 9.1 %collective-permute-done.13.refs_1_.refs_10_ = f32[2,256,256]{2,1,0:T(8,128)S(1)} collective-permute-done((f32[2,256,256]{2,1,0:T(8,128)S(1)}, f32[2,256,256]{2,1,0:T(8,128)S(1)}, u32[]{:S(2)}, u32[]{:S(2)}) %collective-permute-start.13) | collective-permute-done | bytes 524320 | tf_op jit(solution)/shard_map/ppermute | solution.py:38
  71.1 0.1 pack.3
  71.2 0.1 collective-permute-start.15
  71.3 0.7 collective-permute-start.20
  72.0 0.7 collective-permute-start.18
  72.7 6.6 %collective-permute-start.16 = (f32[2,256,256]{2,1,0:T(8,128)S(1)}, f32[2,256,256]{2,1,0:T(8,128)S(1)}, u32[]{:S(2)}, u32[]{:S(2)}) collective-permute-start(f32[2,256,256]{2,1,0:T(8,128)S(1)} %collective-permute-done.10.refs_2_.refs_6_), channel_id=1, source_target_pairs={{0,4},{4,0},{8,12},{12,8},{1,5},{5,1},{9,13},{13,9},{2,6},{6,2},{1... | collective-permute-start | bytes 1572872 | tf_op jit(solution)/shard_map/ppermute | solution.py:46
  79.2 5.8 %early.1 = (f32[2,256,4096]{2,1,0:T(8,128)S(1)}, f32[2,1,256,4096]{3,2,1,0:T(8,128)}) custom-call(s32[2,4]{1,0:T(2,128)S(1)} %bitcast.13, s32[2,4]{1,0:T(2,128)S(1)} %collective-permute-done.refs_1_, s32[2,4]{1,0:T(2,128)S(1)} %collective-permute-done.1.refs_2_, s32[2,4]{1,0:T(2,128)S(1)} %collective-permute-done.2.refs_3_, ...), custom_call_target="tpu_custom_call" | custom-call | tf_op jit(solution)/shard_map/early/pallas_call | solution.py:421
  85.1 6.4 %collective-permute-done.16.refs_5_ = f32[2,256,256]{2,1,0:T(8,128)S(1)} collective-permute-done((f32[2,256,256]{2,1,0:T(8,128)S(1)}, f32[2,256,256]{2,1,0:T(8,128)S(1)}, u32[]{:S(2)}, u32[]{:S(2)}) %collective-permute-start.16) | collective-permute-done | bytes 524320 | tf_op jit(solution)/shard_map/ppermute | solution.py:46
  91.5 0.5 collective-permute-start.19
  92.0 0.0 collective-permute-start.21
  92.0 1.4 %collective-permute-done.17.refs_6_ = f32[2,256,256]{2,1,0:T(8,128)S(1)} collective-permute-done((f32[2,256,256]{2,1,0:T(8,128)S(1)}, f32[2,256,256]{2,1,0:T(8,128)S(1)}, u32[]{:S(2)}, u32[]{:S(2)}) %collective-permute-start.17) | collective-permute-done | bytes 524320 | tf_op jit(solution)/shard_map/ppermute | solution.py:38
  93.4 0.7 collective-permute-done.19.refs_8_
  94.2 0.7 collective-permute-done.21.refs_10_
  94.9 2.7 %late.1 = f32[2,1,256,4096]{3,2,1,0:T(8,128)} custom-call(s32[2,4]{1,0:T(2,128)S(1)} %bitcast.14, s32[2,4]{1,0:T(2,128)S(1)} %collective-permute-done.refs_1_, s32[2,4]{1,0:T(2,128)S(1)} %collective-permute-done.1.refs_2_, s32[2,4]{1,0:T(2,128)S(1)} %collective-permute-done.2.refs_3_, ...), custom_call_target="tpu_custom_call", output_to_operand_aliasing={{}: (11, {})} | custom-call | tf_op jit(solution)/shard_map/late/pallas_call | solution.py:486
  (19 shorter events, 0.0 us)
Async XLA Ops:
  0.0 6.4 %collective-permute-start = (s32[2,4]{1,0:T(2,128)}, s32[2,4]{1,0:T(2,128)S(1)}, u32[]{:S(2)}, u32[]{:S(2)}) collective-permute-start(s32[2,4]{1,0:T(2,128)} %bitcast.1), channel_id=1, source_target_pairs={{0,4},{4,8},{8,12},{1,5},{5,9},{9,13},{2,6},{6,10},{10,14},{3,7},{... | collective-permute-start | bytes 104 | tf_op jit(solution)/shard_map/ppermute | solution.py:33
  6.4 0.7 copy-start.2
  9.3 12.2 %collective-permute-start.3 = (f32[2,256,256]{2,1,0:T(8,128)S(1)}, f32[2,256,256]{2,1,0:T(8,128)S(1)}, u32[]{:S(2)}, u32[]{:S(2)}) collective-permute-start(f32[2,256,256]{2,1,0:T(8,128)S(1)} %get-tuple-element.45), channel_id=1, source_target_pairs={{12,14},{14,12},{13,15},{15,13},{28,30},{30,28},{29,31},{31,29}} | collective-permute-start | bytes 1572872 | tf_op jit(solution)/shard_map/ppermute | solution.py:53
  10.0 15.2 %collective-permute-start.4 = (f32[2,256,256]{2,1,0:T(8,128)S(1)}, f32[2,256,256]{2,1,0:T(8,128)S(1)}, u32[]{:S(2)}, u32[]{:S(2)}) collective-permute-start(f32[2,256,256]{2,1,0:T(8,128)S(1)} %get-tuple-element.38), channel_id=1, source_target_pairs={{0,4},{4,0},{8,12},{12,8},{1,5},{5,1},{9,13},{13,9},{2,6},{6,2},{1... | collective-permute-start | bytes 1572872 | tf_op jit(solution)/shard_map/ppermute | solution.py:46
  14.3 25.7 %collective-permute-start.6 = (f32[3,256,256]{2,1,0:T(8,128)S(1)}, f32[3,256,256]{2,1,0:T(8,128)S(1)}, u32[]{:S(2)}, u32[]{:S(2)}) collective-permute-start(f32[3,256,256]{2,1,0:T(8,128)S(1)} %cut.6), channel_id=1, source_target_pairs={{0,4},{4,0},{8,12},{12,8},{1,5},{5,1},{9,13},{13,9},{2,6},{6,2},{1... | collective-permute-start | bytes 2359304 | tf_op jit(solution)/shard_map/ppermute | solution.py:46
  14.4 14.3 %collective-permute-start.5 = (f32[2,256,256]{2,1,0:T(8,128)S(1)}, f32[2,256,256]{2,1,0:T(8,128)S(1)}, u32[]{:S(2)}, u32[]{:S(2)}) collective-permute-start(f32[2,256,256]{2,1,0:T(8,128)S(1)} %get-tuple-element.45), channel_id=1, source_target_pairs={{4,8},{8,4},{5,9},{9,5},{6,10},{10,6},{7,11},{11,7},{20,24},{24,20... | collective-permute-start | bytes 1572872 | tf_op jit(solution)/shard_map/ppermute | solution.py:46
  21.5 6.7 %copy-start.1 = (bf16[8,256,256]{2,1,0:T(8,128)(2,1)S(1)}, bf16[8,256,256]{2,1,0:T(8,128)(2,1)}, u32[]{:S(2)}) copy-start(bf16[8,256,256]{2,1,0:T(8,128)(2,1)} %constant.2.clone.pieces) | copy-start | bytes 3145732
  25.2 14.8 %copy-start = (f32[2,256,256]{2,1,0:T(8,128)S(1)}, f32[2,256,256]{2,1,0:T(8,128)}, u32[]{:S(2)}) copy-start(f32[2,256,256]{2,1,0:T(8,128)} %refs_2_.15) | copy-start | bytes 1572868
  25.2 14.8 %copy-start.3 = (s32[4,2]{0,1:T(2,128)S(1)}, s32[4,2]{0,1:T(2,128)}, u32[]{:S(2)}) copy-start(s32[4,2]{0,1:T(2,128)} %param.10) | copy-start | bytes 100
  25.8 14.1 %collective-permute-start.7 = (f32[2,256,256]{2,1,0:T(8,128)S(1)}, f32[2,256,256]{2,1,0:T(8,128)S(1)}, u32[]{:S(2)}, u32[]{:S(2)}) collective-permute-start(f32[2,256,256]{2,1,0:T(8,128)S(1)} %join.2), channel_id=1, source_target_pairs={{0,2},{2,0},{1,3},{3,1},{4,6},{6,4},{5,7},{7,5},{8,10},{10,8},{9,1... | collective-permute-start | bytes 1572872 | tf_op jit(solution)/shard_map/ppermute | solution.py:38
  27.4 22.9 %collective-permute-start.8 = (f32[3,256,256]{2,1,0:T(8,128)S(1)}, f32[3,256,256]{2,1,0:T(8,128)S(1)}, u32[]{:S(2)}, u32[]{:S(2)}) collective-permute-start(f32[3,256,256]{2,1,0:T(8,128)S(1)} %cut.7.refs_4_), channel_id=1, source_target_pairs={{4,8},{8,4},{5,9},{9,5},{6,10},{10,6},{7,11},{11,7},{20,24},{24,20... | collective-permute-start | bytes 2359304 | tf_op jit(solution)/shard_map/ppermute | solution.py:46
  28.1 1.7 %collective-permute-start.1 = (s32[2,4]{1,0:T(2,128)S(1)}, s32[2,4]{1,0:T(2,128)S(1)}, u32[]{:S(2)}, u32[]{:S(2)}) collective-permute-start(s32[2,4]{1,0:T(2,128)S(1)} %bitcast.8), channel_id=1, source_target_pairs={{0,1},{1,0},{2,3},{3,2},{4,5},{5,4},{6,7},{7,6},{8,9},{9,8},{10,11... | collective-permute-start | bytes 104 | tf_op jit(solution)/shard_map/ppermute | solution.py:38
  28.6 1.8 %collective-permute-start.2 = (s32[2,4]{1,0:T(2,128)S(1)}, s32[2,4]{1,0:T(2,128)S(1)}, u32[]{:S(2)}, u32[]{:S(2)}) collective-permute-start(s32[2,4]{1,0:T(2,128)S(1)} %collective-permute-done.refs_1_), channel_id=1, source_target_pairs={{0,1},{1,0},{2,3},{3,2},{4,5},{5,4},{6,7},{7,6},{8,9},{9,8},{10,11... | collective-permute-start | bytes 104 | tf_op jit(solution)/shard_map/ppermute | solution.py:38
  29.8 20.5 %collective-permute-start.9 = (f32[2,256,256]{2,1,0:T(8,128)S(1)}, f32[2,256,256]{2,1,0:T(8,128)S(1)}, u32[]{:S(2)}, u32[]{:S(2)}) collective-permute-start(f32[2,256,256]{2,1,0:T(8,128)S(1)} %join.3), channel_id=1, source_target_pairs={{0,2},{2,0},{1,3},{3,1},{4,6},{6,4},{5,7},{7,5},{8,10},{10,8},{9,1... | collective-permute-start | bytes 1572872 | tf_op jit(solution)/shard_map/ppermute | solution.py:38
  47.9 13.9 %collective-permute-start.10 = (f32[2,256,256]{2,1,0:T(8,128)S(1)}, f32[2,256,256]{2,1,0:T(8,128)S(1)}, u32[]{:S(2)}, u32[]{:S(2)}) collective-permute-start(f32[2,256,256]{2,1,0:T(8,128)S(1)} %get-tuple-element.60), channel_id=1, source_target_pairs={{0,2},{2,0},{1,3},{3,1},{4,6},{6,4},{5,7},{7,5},{8,10},{10,8},{9,1... | collective-permute-start | bytes 1572872 | tf_op jit(solution)/shard_map/ppermute | solution.py:38
  49.5 12.3 %collective-permute-start.11 = (f32[2,256,256]{2,1,0:T(8,128)S(1)}, f32[2,256,256]{2,1,0:T(8,128)S(1)}, u32[]{:S(2)}, u32[]{:S(2)}) collective-permute-start(f32[2,256,256]{2,1,0:T(8,128)S(1)} %get-tuple-element.55.refs_1_.refs_5_), channel_id=1, source_target_pairs={{0,4},{4,0},{8,12},{12,8},{1,5},{5,1},{9,13},{13,9},{2,6},{6,2},{1... | collective-permute-start | bytes 1572872 | tf_op jit(solution)/shard_map/ppermute | solution.py:46
  57.3 13.8 %collective-permute-start.14 = (f32[2,256,256]{2,1,0:T(8,128)S(1)}, f32[2,256,256]{2,1,0:T(8,128)S(1)}, u32[]{:S(2)}, u32[]{:S(2)}) collective-permute-start(f32[2,256,256]{2,1,0:T(8,128)S(1)} %get-tuple-element.57.refs_0_.refs_9_), channel_id=1, source_target_pairs={{4,8},{8,4},{5,9},{9,5},{6,10},{10,6},{7,11},{11,7},{20,24},{24,20... | collective-permute-start | bytes 1572872 | tf_op jit(solution)/shard_map/ppermute | solution.py:46
  58.0 13.1 %collective-permute-start.13 = (f32[2,256,256]{2,1,0:T(8,128)S(1)}, f32[2,256,256]{2,1,0:T(8,128)S(1)}, u32[]{:S(2)}, u32[]{:S(2)}) collective-permute-start(f32[2,256,256]{2,1,0:T(8,128)S(1)} %get-tuple-element.61), channel_id=1, source_target_pairs={{0,2},{2,0},{1,3},{3,1},{4,6},{6,4},{5,7},{7,5},{8,10},{10,8},{9,1... | collective-permute-start | bytes 1572872 | tf_op jit(solution)/shard_map/ppermute | solution.py:38
  61.9 17.3 %collective-permute-start.12 = (f32[4,2,256,256]{3,2,1,0:T(8,128)S(1)}, f32[4,2,256,256]{3,2,1,0:T(8,128)S(1)}, u32[]{:S(2)}, u32[]{:S(2)}) collective-permute-start(f32[4,2,256,256]{3,2,1,0:T(8,128)S(1)} %pack.2), channel_id=1, source_target_pairs={{0,1},{1,0},{2,3},{3,2},{4,5},{5,4},{6,7},{7,6},{8,9},{9,8},{10,11... | collective-permute-start | bytes 6291464 | tf_op jit(solution)/shard_map/ppermute | solution.py:38
  71.2 8.1 %collective-permute-start.15 = (f32[3,2,256,256]{3,2,1,0:T(8,128)S(1)}, f32[3,2,256,256]{3,2,1,0:T(8,128)S(1)}, u32[]{:S(2)}, u32[]{:S(2)}) collective-permute-start(f32[3,2,256,256]{3,2,1,0:T(8,128)S(1)} %pack.3), channel_id=1, source_target_pairs={{0,1},{1,0},{2,3},{3,2},{4,5},{5,4},{6,7},{7,6},{8,9},{9,8},{10,11... | collective-permute-start | bytes 4718600 | tf_op jit(solution)/shard_map/ppermute | solution.py:38
  71.3 13.8 %collective-permute-start.20 = (f32[2,256,256]{2,1,0:T(8,128)S(1)}, f32[2,256,256]{2,1,0:T(8,128)S(1)}, u32[]{:S(2)}, u32[]{:S(2)}) collective-permute-start(f32[2,256,256]{2,1,0:T(8,128)S(1)} %get-tuple-element.66), channel_id=1, source_target_pairs={{12,14},{14,12},{13,15},{15,13},{28,30},{30,28},{29,31},{31,29}} | collective-permute-start | bytes 1572872 | tf_op jit(solution)/shard_map/ppermute | solution.py:53
  72.0 13.1 %collective-permute-start.18 = (f32[2,256,256]{2,1,0:T(8,128)S(1)}, f32[2,256,256]{2,1,0:T(8,128)S(1)}, u32[]{:S(2)}, u32[]{:S(2)}) collective-permute-start(f32[2,256,256]{2,1,0:T(8,128)S(1)} %collective-permute-done.13.refs_1_.refs_10_), channel_id=1, source_target_pairs={{4,8},{8,4},{5,9},{9,5},{6,10},{10,6},{7,11},{11,7},{20,24},{24,20... | collective-permute-start | bytes 1572872 | tf_op jit(solution)/shard_map/ppermute | solution.py:46
  72.7 18.9 %collective-permute-start.16 = (f32[2,256,256]{2,1,0:T(8,128)S(1)}, f32[2,256,256]{2,1,0:T(8,128)S(1)}, u32[]{:S(2)}, u32[]{:S(2)}) collective-permute-start(f32[2,256,256]{2,1,0:T(8,128)S(1)} %collective-permute-done.10.refs_2_.refs_6_), channel_id=1, source_target_pairs={{0,4},{4,0},{8,12},{12,8},{1,5},{5,1},{9,13},{13,9},{2,6},{6,2},{1... | collective-permute-start | bytes 1572872 | tf_op jit(solution)/shard_map/ppermute | solution.py:46
  91.5 1.9 %collective-permute-start.17 = (f32[2,256,256]{2,1,0:T(8,128)S(1)}, f32[2,256,256]{2,1,0:T(8,128)S(1)}, u32[]{:S(2)}, u32[]{:S(2)}) collective-permute-start(f32[2,256,256]{2,1,0:T(8,128)S(1)} %collective-permute-done.16.refs_5_), channel_id=1, source_target_pairs={{0,1},{1,0},{2,3},{3,2},{4,5},{5,4},{6,7},{7,6},{8,9},{9,8},{10,11... | collective-permute-start | bytes 1572872 | tf_op jit(solution)/shard_map/ppermute | solution.py:38
  91.5 2.7 %collective-permute-start.19 = (f32[2,256,256]{2,1,0:T(8,128)S(1)}, f32[2,256,256]{2,1,0:T(8,128)S(1)}, u32[]{:S(2)}, u32[]{:S(2)}) collective-permute-start(f32[2,256,256]{2,1,0:T(8,128)S(1)} %collective-permute-done.18.refs_7_), channel_id=1, source_target_pairs={{0,1},{1,0},{2,3},{3,2},{4,5},{5,4},{6,7},{7,6},{8,9},{9,8},{10,11... | collective-permute-start | bytes 1572872 | tf_op jit(solution)/shard_map/ppermute | solution.py:38
  92.0 2.9 %collective-permute-start.21 = (f32[2,256,256]{2,1,0:T(8,128)S(1)}, f32[2,256,256]{2,1,0:T(8,128)S(1)}, u32[]{:S(2)}, u32[]{:S(2)}) collective-permute-start(f32[2,256,256]{2,1,0:T(8,128)S(1)} %collective-permute-done.20.refs_9_), channel_id=1, source_target_pairs={{0,1},{1,0},{2,3},{3,2},{4,5},{5,4},{6,7},{7,6},{8,9},{9,8},{10,11... | collective-permute-start | bytes 1572872 | tf_op jit(solution)/shard_map/ppermute | solution.py:38

commit v8 on v7

--- a/solution.py
+++ b/solution.py
@@ -150,7 +150,9 @@
     sections, n_here, n_up, side = layout
     owner = lax.rem(lax.axis_index("slab") + distance, sections)
     here, up = owner * n_here + k, sections * n_here + owner * n_up + k
-    pairs, below = tables[2 * twin], tables[2 * twin + 1]
+    width = len(tables) // 2 if len(tables) > 3 else len(tables)
+    pairs = tables[width * twin]
+    below = tables[width * twin + 1 + (0 if isinstance(phase, str) else phase)]
     lower = True if which == "last" else is_lower(phase)
     own, other = (here, up) if which == "slot" else (up, here)
     row = lax.rem(pick(lower, pairs[0, own], below[0, other]), side)
@@ -174,7 +176,8 @@
         slot_body(*args)
 
 
-def slot_body(spot, layout, pairs, below, probe, measured, *refs):
+def slot_body(spot, layout, n_tables, *refs):
+    tables, (probe, measured), refs = refs[:n_tables], refs[n_tables : n_tables + 2], refs[n_tables + 2 :]
     sections = layout[0]
     which, phase = spot[:2]
     pieces = 1 if which == "last" else 2
@@ -186,7 +189,7 @@
     wave, trans, amplitude, sem = refs[4 + sections :]
     side = probe.shape[-1]
     slab = lax.axis_index("slab")
-    index, row, col, low, high = locate(spot, layout, (pairs, below))
+    index, row, col, low, high = locate(spot, layout, tables)
     col = lax.rem(col, side)
     lower = True if which == "last" else is_lower(phase)
 
@@ -245,22 +248,24 @@
         outs[distance][...] = wave[lax.rem(slab + distance, sections)]
 
 
-def run_slot(kind, spot, layout, pairs, below, probe, measured, own, others, constants):
+def run_slot(kind, spot, layout, tables, probe, measured, own, others, constants):
     sections, side = layout[0], layout[3]
     shape = jax.ShapeDtypeStruct((2, side, side), jnp.float32)
     return pl.pallas_call(
-        lambda *refs: slot_kernel(kind, spot, layout, *refs),
-        in_specs=[SMEM, SMEM, VMEM, HBM] + [VMEM] * (len(own) + len(others) + 4),
+        lambda *refs: slot_kernel(kind, spot, layout, len(tables), *refs),
+        in_specs=[SMEM] * len(tables) + [VMEM, HBM] + [VMEM] * (len(own) + len(others) + 4),
         out_specs=[VMEM] * sections,
         out_shape=[shape] * sections,
         scratch_shapes=[pltpu.VMEM((sections, 2, side, side), jnp.float32)] * 2
         + [pltpu.VMEM((side, side), jnp.float32), pltpu.SemaphoreType.DMA(())],
         compiler_params=params(32),
         name="slot_" + kind,
-    )(pairs, below, probe, measured, *own, *others, *constants)
-
-
-def cut_kernel(spots, layout, with_measured, pairs, below, phase, absorption, *refs):
+    )(*tables, probe, measured, *own, *others, *constants)
+
+
+def cut_kernel(spots, layout, with_measured, n_tables, *refs):
+    tables, (phase, absorption) = refs[:n_tables], refs[n_tables : n_tables + 2]
+    refs = refs[n_tables + 2 :]
     count, side = len(spots), layout[3]
     blocks = phase.shape[2] // side
     extra = None
@@ -273,7 +278,7 @@
     buffer, sems = refs[-2], refs[-1]
     copies, columns = [], []
     for k in range(count):
-        column = locate(spots[k], layout, (pairs, below))[2]
+        column = locate(spots[k], layout, tables)[2]
         first = lax.div(column, side)
         columns.append(lax.rem(column, side))
         for which, source in enumerate((phase, absorption)):
@@ -301,7 +306,7 @@
         extra.wait()
 
 
-def cut(spots, layout, pairs, below, phase, absorption, measured=None):
+def cut(spots, layout, tables, phase, absorption, measured=None):
     side = layout[3]
     count = len(spots)
     shapes = [jax.ShapeDtypeStruct((2, side, side), jnp.float32)] * count
@@ -315,34 +320,35 @@
         scratch = [pltpu.SemaphoreType.DMA(())] + scratch
         inputs.append(measured)
     return pl.pallas_call(
-        lambda *refs: cut_kernel(spots, layout, measured is not None, *refs),
-        in_specs=[SMEM, SMEM] + [HBM] * len(inputs),
+        lambda *refs: cut_kernel(spots, layout, measured is not None, len(tables), *refs),
+        in_specs=[SMEM] * len(tables) + [HBM] * len(inputs),
         out_specs=[VMEM] * count,
         out_shape=shapes,
         scratch_shapes=scratch,
         compiler_params=params(16),
         name="cut",
-    )(pairs, below, *inputs)
-
-
-def join_kernel(spot, layout, pairs, below, here, there, out):
+    )(*tables, *inputs)
+
+
+def join_kernel(spot, layout, *refs):
+    tables, (here, there, out) = refs[:-3], refs[-3:]
     side = layout[3]
-    low, high = locate(spot, layout, (pairs, below))[3:]
+    low, high = locate(spot, layout, tables)[3:]
     rows = lax.broadcasted_iota(jnp.int32, (side, side), 0)
     keep = (rows >= low) & (rows < high)
     for part in range(2):
         out[part] = jnp.where(keep, here[part], there[part])
 
 
-def join(spot, layout, pairs, below, here, there):
+def join(spot, layout, tables, here, there):
     return pl.pallas_call(
         lambda *refs: join_kernel(spot, layout, *refs),
-        in_specs=[SMEM, SMEM, VMEM, VMEM],
+        in_specs=[SMEM] * len(tables) + [VMEM, VMEM],
         out_specs=VMEM,
         out_shape=jax.ShapeDtypeStruct(here.shape, jnp.float32),
         compiler_params=params(8),
         name="join",
-    )(pairs, below, here, there)
+    )(*tables, here, there)
 
 
 def pack_kernel(*refs):
@@ -386,9 +392,9 @@
 
 
 def early_kernel(metas, layout, *refs):
-    count = len(metas)
-    tables, terms = refs[:4], refs[4 : 4 + count]
-    out, copied, sem = refs[4 + count :]
+    out, copied, sem = refs[-3:]
+    width = len(refs) - 3 - len(metas)
+    tables, terms = refs[:width], refs[width:-3]
     terms, metas = spread(metas, terms)
     side = terms[0].shape[-1]
     blocks = out.shape[-1] // side
@@ -420,7 +426,7 @@
     side = layout[3]
     return pl.pallas_call(
         lambda *refs: early_kernel(metas, layout, *refs),
-        in_specs=[SMEM] * 4 + [VMEM] * len(terms),
+        in_specs=[SMEM] * len(tables) + [VMEM] * len(terms),
         out_specs=[VMEM, HBM],
         out_shape=[
             jax.ShapeDtypeStruct((2, side, cols_total), jnp.float32),
@@ -433,9 +439,9 @@
 
 
 def late_kernel(metas, layout, *refs):
-    count = len(metas)
-    tables, total, terms = refs[:4], refs[4], refs[5 : 5 + count]
-    out, stage, sems = refs[6 + count :]
+    width = len(refs) - 5 - len(metas)
+    tables, total, terms = refs[:width], refs[width], refs[width + 1 : -4]
+    out, stage, sems = refs[-3:]
     side = terms[0].shape[-1]
     blocks = out.shape[-1] // side
     rows = lax.broadcasted_iota(jnp.int32, (side, side), 0)
@@ -485,9 +491,9 @@
     cols_total = total.shape[-1]
     return pl.pallas_call(
         lambda *refs: late_kernel(metas, layout, *refs),
-        in_specs=[SMEM] * 4 + [VMEM] * (1 + len(terms)) + [HBM],
+        in_specs=[SMEM] * len(tables) + [VMEM] * (1 + len(terms)) + [HBM],
         out_specs=HBM,
-        input_output_aliases={5 + len(terms): 0},
+        input_output_aliases={len(tables) + 1 + len(terms): 0},
         out_shape=jax.ShapeDtypeStruct((2, 1, side, cols_total), jnp.float32),
         scratch_shapes=[
             pltpu.VMEM((2, side, cols_total), jnp.float32),
@@ -509,7 +515,10 @@
 
     layout = (sections, n_here, n_up, side)
     pairs = offsets.T
-    below = move(pairs, "tile", 1)
+    if n_here == n_up:
+        tables = [pairs] + [swap(pairs, "tile", parity) for parity in range(2)]
+    else:
+        tables = [pairs, move(pairs, "tile", 1)]
     back = lambda d: (sections - d) % sections
     far = distances[1:]
     phase = pltpu.with_memory_space_constraint(phase, pltpu.HBM)
@@ -534,12 +543,12 @@
     done = [pairs]
 
     def step(kernel):
-        out = kernel(after(pairs, *done))
+        out = kernel([after(pairs, *done)] + tables[1:])
         done[:] = [out[0] if isinstance(out, (list, tuple)) else out]
         return out
 
     spots = [("send", rounds[i][2], rounds[i][0], d) for i in range(count) for d in far]
-    pieces = step(lambda p: cut(spots, layout, p, below, phase, absorption)) if spots else []
+    pieces = step(lambda p: cut(spots, layout, p, phase, absorption)) if spots else []
     sent, got = [], []
     for i, (k, role, send_role, there, home) in enumerate(rounds):
         sent.append([None, *pieces[i * len(far) : (i + 1) * len(far)]])
@@ -547,31 +556,31 @@
     for i, (k, role, send_role, there, home) in enumerate(rounds):
         extra_input = [] if role == "lo" else [measured]
         spots = [("send", send_role, k, 0)]
-        sent[i][0] = step(lambda p: cut(spots, layout, p, below, phase, absorption, *extra_input))[0]
+        sent[i][0] = step(lambda p: cut(spots, layout, p, phase, absorption, *extra_input))[0]
         got[i][0] = there(sent[i][0])
     ends = sorted(last_round)
     extra = [[rotate_last(sent[last_round[k]][d], d) for d in far] for k in ends]
     held = []
     for k, role, send_role, there, home in rounds:
         spots = [("slot", role, k, d) for d in distances]
-        held.append(step(lambda p: cut(spots, layout, p, below, phase, absorption)))
+        held.append(step(lambda p: cut(spots, layout, p, phase, absorption)))
     constants = expand(side)
-    done += [value for row in extra for value in row]
     others = []
     for i, (k, role, send_role, there, home) in enumerate(rounds):
         joined = []
         for d in far:
             spot = ("slot", role, k, d)
-            joined.append(step(lambda p: join(spot, layout, p, below, held[i][d], got[i][d])))
+            joined.append(step(lambda p: join(spot, layout, p, held[i][d], got[i][d])))
         others.append([rotate(joined[d - 1], "slab", d) for d in far])
-
-    other_pairs, other_below = rotate(pairs, "batch", 1), rotate(below, "batch", 1)
-    done += [other_pairs, other_below]
-    tables = [pairs, below, other_pairs, other_below]
+        if i == 0:
+            done += [value for row in extra for value in row]
+
+    twin_tables = [rotate(table, "batch", 1) for table in tables]
+    done += twin_tables
 
     def slot(kind, spot, own, rest):
         return step(
-            lambda p: run_slot(kind, spot, layout, p, below, probe, measured, own, rest, constants)
+            lambda p: run_slot(kind, spot, layout, p, probe, measured, own, rest, constants)
         )
 
     outs, backs, homes = [], [], []
@@ -590,11 +599,14 @@
         twins = rotate(pack(values), "batch", 1)
         terms.extend(values + [twins])
         kinds.extend([(0, spot) for value, spot in items] + [[(1, spot) for value, spot in items]])
+        return twins
 
     final, final_kinds = [], []
     ending = [
         [rotate_last(after(last_outs[n][d], *backs[-1]), d) for d in far] for n in range(len(ends))
     ]
+    for n, k in enumerate(ends):
+        final += [(ending[n][d - 1], ("last", "lo", k, back(d))) for d in far]
     last_items = [(last_outs[n][0], ("last", "lo", k, 0)) for n, k in enumerate(ends)]
     for i, (k, role, send_role, there, home) in enumerate(rounds):
         items = [(outs[i][0], ("slot", role, k, 0))]
@@ -602,17 +614,15 @@
         items.append((homes[i], ("swap", send_role, k, 0)))
         if i == 0:
             items = last_items + items
-        group(items)
+        twins = group(items)
         for d in far:
             final.append((home(backs[i][d - 1]), ("swap", send_role, k, back(d))))
-    for n, k in enumerate(ends):
-        final += [(ending[n][d - 1], ("last", "lo", k, back(d))) for d in far]
-    total, copied = early(kinds, layout, tables, terms, cols_total)
+    total, copied = early(kinds, layout, tables + twin_tables, terms, cols_total)
     values = []
     for value, spot in final:
         values += [value, rotate(after(value, total), "batch", 1)]
         final_kinds += [(0, spot), (1, spot)]
-    return late(final_kinds, layout, tables, total, copied, values)
+    return late(final_kinds, layout, tables + twin_tables, total, copied, values)
 
 
 def solution(mesh):

time: 98.2 us -> 97 us (0.988)
  the two profiles are of different devices: /device:TPU:0 before, /device:TPU:29 now
where the time goes in v8:
time: 97 us; the launch traced here: 96.7 us
  Pallas kernels  45.1 us (46%)
  starting transfers between devices  36.2 us (37%)
  waiting for transfers between devices  14.2 us (15%)
    pallas_call x3, Pallas kernels, run_slot(): pl.pallas_call(lambda *refs: slot_kernel(kind, spot, layout, len(tables),...  22.3 us
    ppermute x12, starting transfers between devices, rotate(): lax.ppermute(block, axis, [(i, (i + distance) % size) for i in range(size)])  20.9 us
    pallas_call x5, Pallas kernels, cut(): pl.pallas_call(lambda *refs: cut_kernel(spots, layout, measured is not No...  10.5 us
    ppermute x10, starting transfers between devices, swap(): return lax.ppermute(block, axis, route)  10.1 us
    ppermute x10, waiting for transfers between devices, swap(): return lax.ppermute(block, axis, route)  6.99 us
    pallas_call x1, Pallas kernels, early(): pl.pallas_call(lambda *refs: early_kernel(metas, layout, *refs), in_specs...  6.92 us
    ppermute x2, starting transfers between devices, rotate_last(): return lax.ppermute(block, ('tile', 'slab'), route)  5.26 us
    ppermute x12, waiting for transfers between devices, rotate(): lax.ppermute(block, axis, [(i, (i + distance) % size) for i in range(size)])  3.7 us
  transfers between devices with their start and end apart: 24, of which 12 were waited for; matrix products, arithmetic and copies ran while one was open for 0% of the time, Pallas kernels for 41%

profile of v8, /device:TPU:29, one launch (start us, length us, event | category | flops | bytes accessed | tf_op | source)
XLA Modules:
  0.0 96.7 jit_solution(1152741523075903720)
XLA Ops:
  0.0 0.6 collective-permute-start.1
  0.7 1.7 %collective-permute-start = (s32[2,4]{1,0:T(2,128)}, s32[2,4]{1,0:T(2,128)S(1)}, u32[]{:S(2)}, u32[]{:S(2)}) collective-permute-start(s32[2,4]{1,0:T(2,128)} %bitcast.2), channel_id=1, source_target_pairs={{0,4},{4,0},{8,12},{12,8},{1,5},{5,1},{9,13},{13,9},{2,6},{6,2},{1... | collective-permute-start | bytes 104 | tf_op jit(solution)/shard_map/ppermute | solution.py:46
  2.3 1.2 %collective-permute-done.refs_1_ = s32[2,4]{1,0:T(2,128)S(1)} collective-permute-done((s32[2,4]{1,0:T(2,128)}, s32[2,4]{1,0:T(2,128)S(1)}, u32[]{:S(2)}, u32[]{:S(2)}) %collective-permute-start) | collective-permute-done | bytes 64 | tf_op jit(solution)/shard_map/ppermute | solution.py:46
  3.5 0.7 copy-done.2
  4.2 2.2 %cut.5 = (f32[2,256,256]{2,1,0:T(8,128)S(1)}, f32[2,256,256]{2,1,0:T(8,128)S(1)}) custom-call(s32[2,4]{1,0:T(2,128)S(1)} %bitcast.3, s32[2,4]{1,0:T(2,128)S(1)} %collective-permute-done.refs_1_, s32[2,4]{1,0:T(2,128)S(1)} %collective-permute-done.1.refs_2_, f32[1,256,4096]{2,1,0:T(8,128)} %refs_3_.12, f32[1,256,4096]{2,1,0:T(8,128)} %refs_4_.12), custom_call_target="tpu_custom_call" | custom-call | tf_op jit(solution)/shard_map/cut/pallas_call | solution.py:322
  6.4 1.5 %collective-permute-start.5 = (f32[2,256,256]{2,1,0:T(8,128)S(1)}, f32[2,256,256]{2,1,0:T(8,128)S(1)}, u32[]{:S(2)}, u32[]{:S(2)}) collective-permute-start(f32[2,256,256]{2,1,0:T(8,128)S(1)} %get-tuple-element.38), channel_id=1, source_target_pairs={{0,4},{4,0},{8,12},{12,8},{1,5},{5,1},{9,13},{13,9},{2,6},{6,2},{1... | collective-permute-start | bytes 1572872 | tf_op jit(solution)/shard_map/ppermute | solution.py:46
  7.9 2.0 %cut.6 = f32[3,256,256]{2,1,0:T(8,128)S(1)} custom-call(s32[2,4]{1,0:T(2,128)S(1)} %bitcast.4, s32[2,4]{1,0:T(2,128)S(1)} %collective-permute-done.refs_1_, s32[2,4]{1,0:T(2,128)S(1)} %collective-permute-done.1.refs_2_, f32[1,256,4096]{2,1,0:T(8,128)} %refs_3_.12, f32[1,256,4096]{2,1,0:T(8,128)} %refs_4_.12, f32[4,256,256]{2,1,0:T(8,128)} %refs_4_.15), custom_call_target="tpu_custom_call" | custom-call | tf_op jit(solution)/shard_map/cut/pallas_call | solution.py:322
  10.0 0.7 collective-permute-start.7
  10.7 3.1 %collective-permute-start.6 = (f32[2,256,256]{2,1,0:T(8,128)S(1)}, f32[2,256,256]{2,1,0:T(8,128)S(1)}, u32[]{:S(2)}, u32[]{:S(2)}) collective-permute-start(f32[2,256,256]{2,1,0:T(8,128)S(1)} %get-tuple-element.47), channel_id=1, source_target_pairs={{12,14},{14,12},{13,15},{15,13},{28,30},{30,28},{29,31},{31,29}} | collective-permute-start | bytes 1572872 | tf_op jit(solution)/shard_map/ppermute | solution.py:53
  13.8 1.9 %cut.7.refs_5_ = f32[3,256,256]{2,1,0:T(8,128)S(1)} custom-call(s32[2,4]{1,0:T(2,128)S(1)} %bitcast.5, s32[2,4]{1,0:T(2,128)S(1)} %collective-permute-done.refs_1_, s32[2,4]{1,0:T(2,128)S(1)} %collective-permute-done.1.refs_2_, f32[1,256,4096]{2,1,0:T(8,128)} %refs_3_.12, f32[1,256,4096]{2,1,0:T(8,128)} %refs_4_.12, f32[4,256,256]{2,1,0:T(8,128)} %refs_4_.15), custom_call_target="tpu_custom_call" | custom-call | tf_op jit(solution)/shard_map/cut/pallas_call | solution.py:322
  15.7 2.2 %cut.8 = (f32[2,256,256]{2,1,0:T(8,128)S(1)}, f32[2,256,256]{2,1,0:T(8,128)S(1)}) custom-call(s32[2,4]{1,0:T(2,128)S(1)} %bitcast.6, s32[2,4]{1,0:T(2,128)S(1)} %collective-permute-done.refs_1_, s32[2,4]{1,0:T(2,128)S(1)} %collective-permute-done.1.refs_2_, f32[1,256,4096]{2,1,0:T(8,128)} %refs_3_.12, f32[1,256,4096]{2,1,0:T(8,128)} %refs_4_.12), custom_call_target="tpu_custom_call" | custom-call | tf_op jit(solution)/shard_map/cut/pallas_call | solution.py:322
  17.9 2.2 %cut.9 = (f32[2,256,256]{2,1,0:T(8,128)S(1)}, f32[2,256,256]{2,1,0:T(8,128)S(1)}) custom-call(s32[2,4]{1,0:T(2,128)S(1)} %bitcast.7, s32[2,4]{1,0:T(2,128)S(1)} %collective-permute-done.refs_1_, s32[2,4]{1,0:T(2,128)S(1)} %collective-permute-done.1.refs_2_, f32[1,256,4096]{2,1,0:T(8,128)} %refs_3_.12, f32[1,256,4096]{2,1,0:T(8,128)} %refs_4_.12), custom_call_target="tpu_custom_call" | custom-call | tf_op jit(solution)/shard_map/cut/pallas_call | solution.py:322
  20.2 0.7 join.2
  20.9 0.3 collective-permute-start.9
  21.2 0.7 collective-permute-start.10
  21.9 0.4 expand.1
  22.3 1.2 %collective-permute-done.6.refs_6_ = f32[2,256,256]{2,1,0:T(8,128)S(1)} collective-permute-done((f32[2,256,256]{2,1,0:T(8,128)S(1)}, f32[2,256,256]{2,1,0:T(8,128)S(1)}, u32[]{:S(2)}, u32[]{:S(2)}) %collective-permute-start.6) | collective-permute-done | bytes 524320 | tf_op jit(solution)/shard_map/ppermute | solution.py:53
  23.6 6.1 %collective-permute-start.2 = (s32[2,4]{1,0:T(2,128)S(1)}, s32[2,4]{1,0:T(2,128)S(1)}, u32[]{:S(2)}, u32[]{:S(2)}) collective-permute-start(s32[2,4]{1,0:T(2,128)S(1)} %bitcast.9), channel_id=1, source_target_pairs={{0,1},{1,0},{2,3},{3,2},{4,5},{5,4},{6,7},{7,6},{8,9},{9,8},{10,11... | collective-permute-start | bytes 104 | tf_op jit(solution)/shard_map/ppermute | solution.py:38
  29.7 0.7 join.3
  30.3 0.1 collective-permute-done.2.refs_3_
  30.5 0.4 collective-permute-start.3
  30.9 1.4 %collective-permute-start.11 = (f32[2,256,256]{2,1,0:T(8,128)S(1)}, f32[2,256,256]{2,1,0:T(8,128)S(1)}, u32[]{:S(2)}, u32[]{:S(2)}) collective-permute-start(f32[2,256,256]{2,1,0:T(8,128)S(1)} %join.3), channel_id=1, source_target_pairs={{0,2},{2,0},{1,3},{3,1},{4,6},{6,4},{5,7},{7,5},{8,10},{10,8},{9,1... | collective-permute-start | bytes 1572872 | tf_op jit(solution)/shard_map/ppermute | solution.py:38
  32.3 2.6 %collective-permute-done.8.refs_6_ = f32[3,256,256]{2,1,0:T(8,128)S(1)} collective-permute-done((f32[3,256,256]{2,1,0:T(8,128)S(1)}, f32[3,256,256]{2,1,0:T(8,128)S(1)}, u32[]{:S(2)}, u32[]{:S(2)}) %collective-permute-start.8) | collective-permute-done | bytes 786464 | tf_op jit(solution)/shard_map/ppermute | solution.py:46
  35.0 7.1 %slot_0.1 = (f32[2,256,256]{2,1,0:T(8,128)S(1)}, f32[2,256,256]{2,1,0:T(8,128)S(1)}) custom-call(s32[2,4]{1,0:T(2,128)S(1)} %bitcast.11, s32[2,4]{1,0:T(2,128)S(1)} %collective-permute-done.refs_1_, s32[2,4]{1,0:T(2,128)S(1)} %collective-permute-done.1.refs_2_, f32[2,256,256]{2,1,0:T(8,128)S(1)} %copy-done, f32[4,256,256]{2,1,0:T(8,128)} %refs_4_.15, ...), custom_call_target="tpu_custom_call" | custom-call | tf_op jit(solution)/shard_map/slot_0/pallas_call | solution.py:254
  42.1 1.3 %collective-permute-start.12 = (f32[2,256,256]{2,1,0:T(8,128)S(1)}, f32[2,256,256]{2,1,0:T(8,128)S(1)}, u32[]{:S(2)}, u32[]{:S(2)}) collective-permute-start(f32[2,256,256]{2,1,0:T(8,128)S(1)} %get-tuple-element.60), channel_id=1, source_target_pairs={{0,2},{2,0},{1,3},{3,1},{4,6},{6,4},{5,7},{7,5},{8,10},{10,8},{9,1... | collective-permute-start | bytes 1572872 | tf_op jit(solution)/shard_map/ppermute | solution.py:38
  43.3 2.1 %collective-permute-start.13 = (f32[2,256,256]{2,1,0:T(8,128)S(1)}, f32[2,256,256]{2,1,0:T(8,128)S(1)}, u32[]{:S(2)}, u32[]{:S(2)}) collective-permute-start(f32[2,256,256]{2,1,0:T(8,128)S(1)} %get-tuple-element.55.refs_1_.refs_7_), channel_id=1, source_target_pairs={{0,4},{4,0},{8,12},{12,8},{1,5},{5,1},{9,13},{13,9},{2,6},{6,2},{1... | collective-permute-start | bytes 1572872 | tf_op jit(solution)/shard_map/ppermute | solution.py:46
  45.4 0.7 collective-permute-done.11.refs_7_
  46.2 8.0 %slot_1.1 = (f32[2,256,256]{2,1,0:T(8,128)S(1)}, f32[2,256,256]{2,1,0:T(8,128)S(1)}) custom-call(s32[2,4]{1,0:T(2,128)S(1)} %bitcast.12, s32[2,4]{1,0:T(2,128)S(1)} %collective-permute-done.refs_1_, s32[2,4]{1,0:T(2,128)S(1)} %collective-permute-done.1.refs_2_, f32[2,256,256]{2,1,0:T(8,128)S(1)} %copy-done, f32[4,256,256]{2,1,0:T(8,128)} %refs_4_.15, ...), custom_call_target="tpu_custom_call" | custom-call | tf_op jit(solution)/shard_map/slot_1/pallas_call | solution.py:254
  54.2 0.9 collective-permute-start.16
  55.1 1.2 %collective-permute-start.15 = (f32[2,256,256]{2,1,0:T(8,128)S(1)}, f32[2,256,256]{2,1,0:T(8,128)S(1)}, u32[]{:S(2)}, u32[]{:S(2)}) collective-permute-start(f32[2,256,256]{2,1,0:T(8,128)S(1)} %get-tuple-element.61), channel_id=1, source_target_pairs={{0,2},{2,0},{1,3},{3,1},{4,6},{6,4},{5,7},{7,5},{8,10},{10,8},{9,1... | collective-permute-start | bytes 1572872 | tf_op jit(solution)/shard_map/ppermute | solution.py:38
  56.3 7.1 %slot_last.1 = (f32[2,256,256]{2,1,0:T(8,128)S(1)}, f32[2,256,256]{2,1,0:T(8,128)S(1)}) custom-call(s32[2,4]{1,0:T(2,128)S(1)} %bitcast.13, s32[2,4]{1,0:T(2,128)S(1)} %collective-permute-done.refs_1_, s32[2,4]{1,0:T(2,128)S(1)} %collective-permute-done.1.refs_2_, f32[2,256,256]{2,1,0:T(8,128)S(1)} %copy-done, f32[4,256,256]{2,1,0:T(8,128)} %refs_4_.15, ...), custom_call_target="tpu_custom_call" | custom-call | tf_op jit(solution)/shard_map/slot_last/pallas_call | solution.py:254
  63.4 0.1 pack.2
  63.6 6.6 %collective-permute-start.14 = (f32[4,2,256,256]{3,2,1,0:T(8,128)S(1)}, f32[4,2,256,256]{3,2,1,0:T(8,128)S(1)}, u32[]{:S(2)}, u32[]{:S(2)}) collective-permute-start(f32[4,2,256,256]{3,2,1,0:T(8,128)S(1)} %pack.2), channel_id=1, source_target_pairs={{0,1},{1,0},{2,3},{3,2},{4,5},{5,4},{6,7},{7,6},{8,9},{9,8},{10,11... | collective-permute-start | bytes 6291464 | tf_op jit(solution)/shard_map/ppermute | solution.py:38
  70.2 0.1 pack.3
  70.3 1.7 %collective-permute-start.17 = (f32[3,2,256,256]{3,2,1,0:T(8,128)S(1)}, f32[3,2,256,256]{3,2,1,0:T(8,128)S(1)}, u32[]{:S(2)}, u32[]{:S(2)}) collective-permute-start(f32[3,2,256,256]{3,2,1,0:T(8,128)S(1)} %pack.3), channel_id=1, source_target_pairs={{0,1},{1,0},{2,3},{3,2},{4,5},{5,4},{6,7},{7,6},{8,9},{9,8},{10,11... | collective-permute-start | bytes 4718600 | tf_op jit(solution)/shard_map/ppermute | solution.py:38
  72.0 0.7 collective-permute-start.22
  72.7 1.1 %collective-permute-start.20 = (f32[2,256,256]{2,1,0:T(8,128)S(1)}, f32[2,256,256]{2,1,0:T(8,128)S(1)}, u32[]{:S(2)}, u32[]{:S(2)}) collective-permute-start(f32[2,256,256]{2,1,0:T(8,128)S(1)} %collective-permute-done.12.refs_2_.refs_8_), channel_id=1, source_target_pairs={{0,4},{4,0},{8,12},{12,8},{1,5},{5,1},{9,13},{13,9},{2,6},{6,2},{1... | collective-permute-start | bytes 1572872 | tf_op jit(solution)/shard_map/ppermute | solution.py:46
  73.8 2.1 %collective-permute-start.18 = (f32[2,256,256]{2,1,0:T(8,128)S(1)}, f32[2,256,256]{2,1,0:T(8,128)S(1)}, u32[]{:S(2)}, u32[]{:S(2)}) collective-permute-start(f32[2,256,256]{2,1,0:T(8,128)S(1)} %get-tuple-element.64), channel_id=1, source_target_pairs={{12,14},{14,12},{13,15},{15,13},{28,30},{30,28},{29,31},{31,29}} | collective-permute-start | bytes 1572872 | tf_op jit(solution)/shard_map/ppermute | solution.py:53
  76.0 0.2 collective-permute-done.17.refs_14_
  76.2 6.9 %early.1 = (f32[2,256,4096]{2,1,0:T(8,128)S(1)}, f32[2,1,256,4096]{3,2,1,0:T(8,128)}) custom-call(s32[2,4]{1,0:T(2,128)S(1)} %bitcast.14, s32[2,4]{1,0:T(2,128)S(1)} %collective-permute-done.refs_1_, s32[2,4]{1,0:T(2,128)S(1)} %collective-permute-done.1.refs_2_, s32[2,4]{1,0:T(2,128)S(1)} %collective-permute-done.2.refs_3_, ...), custom_call_target="tpu_custom_call" | custom-call | tf_op jit(solution)/shard_map/early/pallas_call | solution.py:427
  83.1 3.2 %collective-permute-done.20.refs_9_ = f32[2,256,256]{2,1,0:T(8,128)S(1)} collective-permute-done((f32[2,256,256]{2,1,0:T(8,128)S(1)}, f32[2,256,256]{2,1,0:T(8,128)S(1)}, u32[]{:S(2)}, u32[]{:S(2)}) %collective-permute-start.20) | collective-permute-done | bytes 524320 | tf_op jit(solution)/shard_map/ppermute | solution.py:46
  86.3 2.3 %collective-permute-done.18.refs_7_ = f32[2,256,256]{2,1,0:T(8,128)S(1)} collective-permute-done((f32[2,256,256]{2,1,0:T(8,128)S(1)}, f32[2,256,256]{2,1,0:T(8,128)S(1)}, u32[]{:S(2)}, u32[]{:S(2)}) %collective-permute-start.18) | collective-permute-done | bytes 524320 | tf_op jit(solution)/shard_map/ppermute | solution.py:53
  88.6 1.4 %collective-permute-start.19 = (f32[2,256,256]{2,1,0:T(8,128)S(1)}, f32[2,256,256]{2,1,0:T(8,128)S(1)}, u32[]{:S(2)}, u32[]{:S(2)}) collective-permute-start(f32[2,256,256]{2,1,0:T(8,128)S(1)} %collective-permute-done.18.refs_7_), channel_id=1, source_target_pairs={{0,1},{1,0},{2,3},{3,2},{4,5},{5,4},{6,7},{7,6},{8,9},{9,8},{10,11... | collective-permute-start | bytes 1572872 | tf_op jit(solution)/shard_map/ppermute | solution.py:38
  90.0 0.5 collective-permute-start.23
  90.6 1.0 %collective-permute-done.19.refs_8_ = f32[2,256,256]{2,1,0:T(8,128)S(1)} collective-permute-done((f32[2,256,256]{2,1,0:T(8,128)S(1)}, f32[2,256,256]{2,1,0:T(8,128)S(1)}, u32[]{:S(2)}, u32[]{:S(2)}) %collective-permute-start.19) | collective-permute-done | bytes 524320 | tf_op jit(solution)/shard_map/ppermute | solution.py:38
  91.6 0.7 collective-permute-done.21.refs_10_
  92.3 0.7 collective-permute-done.23.refs_12_
  93.1 3.4 %late.1 = f32[2,1,256,4096]{3,2,1,0:T(8,128)} custom-call(s32[2,4]{1,0:T(2,128)S(1)} %bitcast.15, s32[2,4]{1,0:T(2,128)S(1)} %collective-permute-done.refs_1_, s32[2,4]{1,0:T(2,128)S(1)} %collective-permute-done.1.refs_2_, s32[2,4]{1,0:T(2,128)S(1)} %collective-permute-done.2.refs_3_, ...), custom_call_target="tpu_custom_call", output_to_operand_aliasing={{}: (13, {})} | custom-call | tf_op jit(solution)/shard_map/late/pallas_call | solution.py:492
  (23 shorter events, 0.2 us)
Async XLA Ops:
  0.0 2.3 %collective-permute-start.1 = (s32[2,4]{1,0:T(2,128)}, s32[2,4]{1,0:T(2,128)S(1)}, u32[]{:S(2)}, u32[]{:S(2)}) collective-permute-start(s32[2,4]{1,0:T(2,128)} %bitcast.1), channel_id=1, source_target_pairs={{4,8},{8,4},{5,9},{9,5},{6,10},{10,6},{7,11},{11,7},{20,24},{24,20... | collective-permute-start | bytes 104 | tf_op jit(solution)/shard_map/ppermute | solution.py:46
  0.7 2.8 %collective-permute-start = (s32[2,4]{1,0:T(2,128)}, s32[2,4]{1,0:T(2,128)S(1)}, u32[]{:S(2)}, u32[]{:S(2)}) collective-permute-start(s32[2,4]{1,0:T(2,128)} %bitcast.2), channel_id=1, source_target_pairs={{0,4},{4,0},{8,12},{12,8},{1,5},{5,1},{9,13},{13,9},{2,6},{6,2},{1... | collective-permute-start | bytes 104 | tf_op jit(solution)/shard_map/ppermute | solution.py:46
  3.5 0.7 copy-start.2
  6.4 13.8 %collective-permute-start.5 = (f32[2,256,256]{2,1,0:T(8,128)S(1)}, f32[2,256,256]{2,1,0:T(8,128)S(1)}, u32[]{:S(2)}, u32[]{:S(2)}) collective-permute-start(f32[2,256,256]{2,1,0:T(8,128)S(1)} %get-tuple-element.38), channel_id=1, source_target_pairs={{0,4},{4,0},{8,12},{12,8},{1,5},{5,1},{9,13},{13,9},{2,6},{6,2},{1... | collective-permute-start | bytes 1572872 | tf_op jit(solution)/shard_map/ppermute | solution.py:46
  9.9 25.0 %collective-permute-start.8 = (f32[3,256,256]{2,1,0:T(8,128)S(1)}, f32[3,256,256]{2,1,0:T(8,128)S(1)}, u32[]{:S(2)}, u32[]{:S(2)}) collective-permute-start(f32[3,256,256]{2,1,0:T(8,128)S(1)} %cut.6), channel_id=1, source_target_pairs={{0,4},{4,0},{8,12},{12,8},{1,5},{5,1},{9,13},{13,9},{2,6},{6,2},{1... | collective-permute-start | bytes 2359304 | tf_op jit(solution)/shard_map/ppermute | solution.py:46
  10.0 19.7 %collective-permute-start.7 = (f32[2,256,256]{2,1,0:T(8,128)S(1)}, f32[2,256,256]{2,1,0:T(8,128)S(1)}, u32[]{:S(2)}, u32[]{:S(2)}) collective-permute-start(f32[2,256,256]{2,1,0:T(8,128)S(1)} %get-tuple-element.47), channel_id=1, source_target_pairs={{4,8},{8,4},{5,9},{9,5},{6,10},{10,6},{7,11},{11,7},{20,24},{24,20... | collective-permute-start | bytes 1572872 | tf_op jit(solution)/shard_map/ppermute | solution.py:46
  10.7 12.9 %collective-permute-start.6 = (f32[2,256,256]{2,1,0:T(8,128)S(1)}, f32[2,256,256]{2,1,0:T(8,128)S(1)}, u32[]{:S(2)}, u32[]{:S(2)}) collective-permute-start(f32[2,256,256]{2,1,0:T(8,128)S(1)} %get-tuple-element.47), channel_id=1, source_target_pairs={{12,14},{14,12},{13,15},{15,13},{28,30},{30,28},{29,31},{31,29}} | collective-permute-start | bytes 1572872 | tf_op jit(solution)/shard_map/ppermute | solution.py:53
  20.2 1.8 %copy-start.1 = (bf16[8,256,256]{2,1,0:T(8,128)(2,1)S(1)}, bf16[8,256,256]{2,1,0:T(8,128)(2,1)}, u32[]{:S(2)}) copy-start(bf16[8,256,256]{2,1,0:T(8,128)(2,1)} %constant.2.clone.pieces) | copy-start | bytes 3145732
  20.2 14.8 %copy-start = (f32[2,256,256]{2,1,0:T(8,128)S(1)}, f32[2,256,256]{2,1,0:T(8,128)}, u32[]{:S(2)}) copy-start(f32[2,256,256]{2,1,0:T(8,128)} %refs_3_.15) | copy-start | bytes 1572868
  20.2 14.8 %copy-start.3 = (s32[4,2]{0,1:T(2,128)S(1)}, s32[4,2]{0,1:T(2,128)}, u32[]{:S(2)}) copy-start(s32[4,2]{0,1:T(2,128)} %param.10) | copy-start | bytes 100
  20.9 14.1 %collective-permute-start.9 = (f32[2,256,256]{2,1,0:T(8,128)S(1)}, f32[2,256,256]{2,1,0:T(8,128)S(1)}, u32[]{:S(2)}, u32[]{:S(2)}) collective-permute-start(f32[2,256,256]{2,1,0:T(8,128)S(1)} %join.2), channel_id=1, source_target_pairs={{0,2},{2,0},{1,3},{3,1},{4,6},{6,4},{5,7},{7,5},{8,10},{10,8},{9,1... | collective-permute-start | bytes 1572872 | tf_op jit(solution)/shard_map/ppermute | solution.py:38
  21.2 24.2 %collective-permute-start.10 = (f32[3,256,256]{2,1,0:T(8,128)S(1)}, f32[3,256,256]{2,1,0:T(8,128)S(1)}, u32[]{:S(2)}, u32[]{:S(2)}) collective-permute-start(f32[3,256,256]{2,1,0:T(8,128)S(1)} %cut.7.refs_5_), channel_id=1, source_target_pairs={{4,8},{8,4},{5,9},{9,5},{6,10},{10,6},{7,11},{11,7},{20,24},{24,20... | collective-permute-start | bytes 2359304 | tf_op jit(solution)/shard_map/ppermute | solution.py:46
  23.6 6.9 %collective-permute-start.2 = (s32[2,4]{1,0:T(2,128)S(1)}, s32[2,4]{1,0:T(2,128)S(1)}, u32[]{:S(2)}, u32[]{:S(2)}) collective-permute-start(s32[2,4]{1,0:T(2,128)S(1)} %bitcast.9), channel_id=1, source_target_pairs={{0,1},{1,0},{2,3},{3,2},{4,5},{5,4},{6,7},{7,6},{8,9},{9,8},{10,11... | collective-permute-start | bytes 104 | tf_op jit(solution)/shard_map/ppermute | solution.py:38
  29.7 1.3 %collective-permute-start.4 = (s32[2,4]{1,0:T(2,128)S(1)}, s32[2,4]{1,0:T(2,128)S(1)}, u32[]{:S(2)}, u32[]{:S(2)}) collective-permute-start(s32[2,4]{1,0:T(2,128)S(1)} %collective-permute-done.1.refs_2_), channel_id=1, source_target_pairs={{0,1},{1,0},{2,3},{3,2},{4,5},{5,4},{6,7},{7,6},{8,9},{9,8},{10,11... | collective-permute-start | bytes 104 | tf_op jit(solution)/shard_map/ppermute | solution.py:38
  30.5 1.8 %collective-permute-start.3 = (s32[2,4]{1,0:T(2,128)S(1)}, s32[2,4]{1,0:T(2,128)S(1)}, u32[]{:S(2)}, u32[]{:S(2)}) collective-permute-start(s32[2,4]{1,0:T(2,128)S(1)} %collective-permute-done.refs_1_), channel_id=1, source_target_pairs={{0,1},{1,0},{2,3},{3,2},{4,5},{5,4},{6,7},{7,6},{8,9},{9,8},{10,11... | collective-permute-start | bytes 104 | tf_op jit(solution)/shard_map/ppermute | solution.py:38
  30.9 15.3 %collective-permute-start.11 = (f32[2,256,256]{2,1,0:T(8,128)S(1)}, f32[2,256,256]{2,1,0:T(8,128)S(1)}, u32[]{:S(2)}, u32[]{:S(2)}) collective-permute-start(f32[2,256,256]{2,1,0:T(8,128)S(1)} %join.3), channel_id=1, source_target_pairs={{0,2},{2,0},{1,3},{3,1},{4,6},{6,4},{5,7},{7,5},{8,10},{10,8},{9,1... | collective-permute-start | bytes 1572872 | tf_op jit(solution)/shard_map/ppermute | solution.py:38
  42.1 21.4 %collective-permute-start.12 = (f32[2,256,256]{2,1,0:T(8,128)S(1)}, f32[2,256,256]{2,1,0:T(8,128)S(1)}, u32[]{:S(2)}, u32[]{:S(2)}) collective-permute-start(f32[2,256,256]{2,1,0:T(8,128)S(1)} %get-tuple-element.60), channel_id=1, source_target_pairs={{0,2},{2,0},{1,3},{3,1},{4,6},{6,4},{5,7},{7,5},{8,10},{10,8},{9,1... | collective-permute-start | bytes 1572872 | tf_op jit(solution)/shard_map/ppermute | solution.py:38
  43.3 20.1 %collective-permute-start.13 = (f32[2,256,256]{2,1,0:T(8,128)S(1)}, f32[2,256,256]{2,1,0:T(8,128)S(1)}, u32[]{:S(2)}, u32[]{:S(2)}) collective-permute-start(f32[2,256,256]{2,1,0:T(8,128)S(1)} %get-tuple-element.55.refs_1_.refs_7_), channel_id=1, source_target_pairs={{0,4},{4,0},{8,12},{12,8},{1,5},{5,1},{9,13},{13,9},{2,6},{6,2},{1... | collective-permute-start | bytes 1572872 | tf_op jit(solution)/shard_map/ppermute | solution.py:46
  54.2 15.9 %collective-permute-start.16 = (f32[2,256,256]{2,1,0:T(8,128)S(1)}, f32[2,256,256]{2,1,0:T(8,128)S(1)}, u32[]{:S(2)}, u32[]{:S(2)}) collective-permute-start(f32[2,256,256]{2,1,0:T(8,128)S(1)} %get-tuple-element.57.refs_0_.refs_11_), channel_id=1, source_target_pairs={{4,8},{8,4},{5,9},{9,5},{6,10},{10,6},{7,11},{11,7},{20,24},{24,20... | collective-permute-start | bytes 1572872 | tf_op jit(solution)/shard_map/ppermute | solution.py:46
  55.1 15.0 %collective-permute-start.15 = (f32[2,256,256]{2,1,0:T(8,128)S(1)}, f32[2,256,256]{2,1,0:T(8,128)S(1)}, u32[]{:S(2)}, u32[]{:S(2)}) collective-permute-start(f32[2,256,256]{2,1,0:T(8,128)S(1)} %get-tuple-element.61), channel_id=1, source_target_pairs={{0,2},{2,0},{1,3},{3,1},{4,6},{6,4},{5,7},{7,5},{8,10},{10,8},{9,1... | collective-permute-start | bytes 1572872 | tf_op jit(solution)/shard_map/ppermute | solution.py:38
  63.6 12.6 %collective-permute-start.14 = (f32[4,2,256,256]{3,2,1,0:T(8,128)S(1)}, f32[4,2,256,256]{3,2,1,0:T(8,128)S(1)}, u32[]{:S(2)}, u32[]{:S(2)}) collective-permute-start(f32[4,2,256,256]{3,2,1,0:T(8,128)S(1)} %pack.2), channel_id=1, source_target_pairs={{0,1},{1,0},{2,3},{3,2},{4,5},{5,4},{6,7},{7,6},{8,9},{9,8},{10,11... | collective-permute-start | bytes 6291464 | tf_op jit(solution)/shard_map/ppermute | solution.py:38
  70.3 5.9 %collective-permute-start.17 = (f32[3,2,256,256]{3,2,1,0:T(8,128)S(1)}, f32[3,2,256,256]{3,2,1,0:T(8,128)S(1)}, u32[]{:S(2)}, u32[]{:S(2)}) collective-permute-start(f32[3,2,256,256]{3,2,1,0:T(8,128)S(1)} %pack.3), channel_id=1, source_target_pairs={{0,1},{1,0},{2,3},{3,2},{4,5},{5,4},{6,7},{7,6},{8,9},{9,8},{10,11... | collective-permute-start | bytes 4718600 | tf_op jit(solution)/shard_map/ppermute | solution.py:38
  72.0 11.1 %collective-permute-start.22 = (f32[2,256,256]{2,1,0:T(8,128)S(1)}, f32[2,256,256]{2,1,0:T(8,128)S(1)}, u32[]{:S(2)}, u32[]{:S(2)}) collective-permute-start(f32[2,256,256]{2,1,0:T(8,128)S(1)} %collective-permute-done.15.refs_1_.refs_12_), channel_id=1, source_target_pairs={{4,8},{8,4},{5,9},{9,5},{6,10},{10,6},{7,11},{11,7},{20,24},{24,20... | collective-permute-start | bytes 1572872 | tf_op jit(solution)/shard_map/ppermute | solution.py:46
  72.7 13.6 %collective-permute-start.20 = (f32[2,256,256]{2,1,0:T(8,128)S(1)}, f32[2,256,256]{2,1,0:T(8,128)S(1)}, u32[]{:S(2)}, u32[]{:S(2)}) collective-permute-start(f32[2,256,256]{2,1,0:T(8,128)S(1)} %collective-permute-done.12.refs_2_.refs_8_), channel_id=1, source_target_pairs={{0,4},{4,0},{8,12},{12,8},{1,5},{5,1},{9,13},{13,9},{2,6},{6,2},{1... | collective-permute-start | bytes 1572872 | tf_op jit(solution)/shard_map/ppermute | solution.py:46
  73.8 14.8 %collective-permute-start.18 = (f32[2,256,256]{2,1,0:T(8,128)S(1)}, f32[2,256,256]{2,1,0:T(8,128)S(1)}, u32[]{:S(2)}, u32[]{:S(2)}) collective-permute-start(f32[2,256,256]{2,1,0:T(8,128)S(1)} %get-tuple-element.64), channel_id=1, source_target_pairs={{12,14},{14,12},{13,15},{15,13},{28,30},{30,28},{29,31},{31,29}} | collective-permute-start | bytes 1572872 | tf_op jit(solution)/shard_map/ppermute | solution.py:53
  88.6 3.0 %collective-permute-start.19 = (f32[2,256,256]{2,1,0:T(8,128)S(1)}, f32[2,256,256]{2,1,0:T(8,128)S(1)}, u32[]{:S(2)}, u32[]{:S(2)}) collective-permute-start(f32[2,256,256]{2,1,0:T(8,128)S(1)} %collective-permute-done.18.refs_7_), channel_id=1, source_target_pairs={{0,1},{1,0},{2,3},{3,2},{4,5},{5,4},{6,7},{7,6},{8,9},{9,8},{10,11... | collective-permute-start | bytes 1572872 | tf_op jit(solution)/shard_map/ppermute | solution.py:38
  90.0 2.3 %collective-permute-start.21 = (f32[2,256,256]{2,1,0:T(8,128)S(1)}, f32[2,256,256]{2,1,0:T(8,128)S(1)}, u32[]{:S(2)}, u32[]{:S(2)}) collective-permute-start(f32[2,256,256]{2,1,0:T(8,128)S(1)} %collective-permute-done.20.refs_9_), channel_id=1, source_target_pairs={{0,1},{1,0},{2,3},{3,2},{4,5},{5,4},{6,7},{7,6},{8,9},{9,8},{10,11... | collective-permute-start | bytes 1572872 | tf_op jit(solution)/shard_map/ppermute | solution.py:38
  90.0 3.0 %collective-permute-start.23 = (f32[2,256,256]{2,1,0:T(8,128)S(1)}, f32[2,256,256]{2,1,0:T(8,128)S(1)}, u32[]{:S(2)}, u32[]{:S(2)}) collective-permute-start(f32[2,256,256]{2,1,0:T(8,128)S(1)} %collective-permute-done.22.refs_11_), channel_id=1, source_target_pairs={{0,1},{1,0},{2,3},{3,2},{4,5},{5,4},{6,7},{7,6},{8,9},{9,8},{10,11... | collective-permute-start | bytes 1572872 | tf_op jit(solution)/shard_map/ppermute | solution.py:38

commit v9 on v8

--- a/solution.py
+++ b/solution.py
@@ -152,7 +152,10 @@
     here, up = owner * n_here + k, sections * n_here + owner * n_up + k
     width = len(tables) // 2 if len(tables) > 3 else len(tables)
     pairs = tables[width * twin]
-    below = tables[width * twin + 1 + (0 if isinstance(phase, str) else phase)]
+    if which == "last":
+        below = pairs
+    else:
+        below = tables[width * twin + 1 + (0 if isinstance(phase, str) else phase)]
     lower = True if which == "last" else is_lower(phase)
     own, other = (here, up) if which == "slot" else (up, here)
     row = lax.rem(pick(lower, pairs[0, own], below[0, other]), side)
@@ -205,7 +208,6 @@
         @pl.when(lower)
         def _():
             fetch().start()
-            fetch().wait()
 
         @pl.when(jnp.logical_not(lower))
         def _():
@@ -234,6 +236,12 @@
     real, imag = two_sided(dft_left, dft_right, real, imag)
     if lower is True:
         fetch().wait()
+    elif lower is not False:
+
+        @pl.when(lower)
+        def _():
+            fetch().wait()
+
     factor = 1.0 - amplitude[...] * lax.rsqrt(jnp.maximum(real * real + imag * imag, 0.25))
     real, minus = two_sided(dft_left, dft_right, real * factor, -imag * factor)
     for step in range(sections - 1, -1, -1):
@@ -547,23 +555,32 @@
         done[:] = [out[0] if isinstance(out, (list, tuple)) else out]
         return out
 
+    ends = sorted(last_round)
+    spots = [("last", "lo", k, d) for k in ends for d in far]
+    pieces = step(lambda p: cut(spots, layout, p[:1], phase, absorption)) if spots else []
+    extra = []
+    for n in range(len(ends)):
+        row = pieces[n * len(far) : (n + 1) * len(far)]
+        extra.append([rotate_last(piece, d) for piece, d in zip(row, far)])
     spots = [("send", rounds[i][2], rounds[i][0], d) for i in range(count) for d in far]
     pieces = step(lambda p: cut(spots, layout, p, phase, absorption)) if spots else []
-    sent, got = [], []
+    got = []
     for i, (k, role, send_role, there, home) in enumerate(rounds):
-        sent.append([None, *pieces[i * len(far) : (i + 1) * len(far)]])
-        got.append([None] + [there(piece) for piece in sent[i][1:]])
-    for i, (k, role, send_role, there, home) in enumerate(rounds):
-        extra_input = [] if role == "lo" else [measured]
-        spots = [("send", send_role, k, 0)]
-        sent[i][0] = step(lambda p: cut(spots, layout, p, phase, absorption, *extra_input))[0]
-        got[i][0] = there(sent[i][0])
-    ends = sorted(last_round)
-    extra = [[rotate_last(sent[last_round[k]][d], d) for d in far] for k in ends]
+        row = pieces[i * len(far) : (i + 1) * len(far)]
+        got.append([None] + [there(piece) for piece in row])
+    done += [value for row in extra for value in row]
     held = []
     for k, role, send_role, there, home in rounds:
         spots = [("slot", role, k, d) for d in distances]
         held.append(step(lambda p: cut(spots, layout, p, phase, absorption)))
+    for i, (k, role, send_role, there, home) in enumerate(rounds):
+        extra_input = [] if role == "lo" else [measured]
+        spots = [("send", send_role, k, 0)]
+        piece = step(lambda p: cut(spots, layout, p, phase, absorption, *extra_input))[0]
+        got[i][0] = there(piece)
+    own_cut = [
+        step(lambda p: cut([("last", "lo", k, 0)], layout, p[:1], phase, absorption)) for k in ends
+    ]
     constants = expand(side)
     others = []
     for i, (k, role, send_role, there, home) in enumerate(rounds):
@@ -572,8 +589,6 @@
             spot = ("slot", role, k, d)
             joined.append(step(lambda p: join(spot, layout, p, held[i][d], got[i][d])))
         others.append([rotate(joined[d - 1], "slab", d) for d in far])
-        if i == 0:
-            done += [value for row in extra for value in row]
 
     twin_tables = [rotate(table, "batch", 1) for table in tables]
     done += twin_tables
@@ -587,11 +602,14 @@
     for i, (k, role, send_role, there, home) in enumerate(rounds):
         outs.append(slot(f"{i}", ("slot", role, k, 0), [held[i][0], got[i][0]], others[i]))
         backs.append([rotate(outs[i][d], "slab", d) for d in far])
-        homes.append(home(outs[i][0]))
+        homes.append(home)
     last_outs = [
-        slot("last", ("last", "lo", k, 0), [sent[last_round[k]][0]], extra[n])
+        slot("last", ("last", "lo", k, 0), [own_cut[n][0]], extra[n])
         for n, k in enumerate(ends)
     ]
+    for i in range(count):
+        gates = backs[0] if i and i == count - 1 else []
+        homes[i] = homes[i](after(outs[i][0], *gates))
     terms, kinds = [], []
 
     def group(items):

time: 97 us -> 110 us (1.13)
  waiting for transfers between devices: 14.2 us -> 23.3 us
  Pallas kernels: 45.1 us -> 47.9 us
    ppermute x10, starting transfers between devices: 10.1 us -> 17.3 us  [swap(): return lax.ppermute(block, axis, route)]
    ppermute x12, starting transfers between devices: 20.9 us -> 13.8 us  [rotate(): lax.ppermute(block, axis, [(i, (i + distance) % size) for i in range(size)])]
    ppermute x12, waiting for transfers between devices: 3.7 us -> 9.82 us  [rotate(): lax.ppermute(block, axis, [(i, (i + distance) % size) for i in range(size)])]
    ppermute x2, waiting for transfers between devices: 3.55 us -> 8.51 us  [rotate_last(): return lax.ppermute(block, ('tile', 'slab'), route)]
    pallas_call x5 -> x7, Pallas kernels: 10.5 us -> 14.2 us  [cut(): pl.pallas_call(lambda *refs: cut_kernel(spots, layout, measured is not No...]
    ppermute x10, waiting for transfers between devices: 6.99 us -> 5 us  [swap(): return lax.ppermute(block, axis, route)]
  transfers between devices with their start and end apart: 24 -> 24, of which waited for: 12 -> 11; matrix products, arithmetic and copies ran while one was open for 0% -> 0% of each run, Pallas kernels for 41% -> 39%
where the time goes in v9:
time: 110 us
  Pallas kernels  47.9 us (44%)
  starting transfers between devices  37.3 us (34%)
  waiting for transfers between devices  23.3 us (21%)
    pallas_call x3, Pallas kernels, run_slot(): pl.pallas_call(lambda *refs: slot_kernel(kind, spot, layout, len(tables),...  21.7 us
    ppermute x10, starting transfers between devices, swap(): return lax.ppermute(block, axis, route)  17.3 us
    pallas_call x7, Pallas kernels, cut(): pl.pallas_call(lambda *refs: cut_kernel(spots, layout, measured is not No...  14.2 us
    ppermute x12, starting transfers between devices, rotate(): lax.ppermute(block, axis, [(i, (i + distance) % size) for i in range(size)])  13.8 us
    ppermute x12, waiting for transfers between devices, rotate(): lax.ppermute(block, axis, [(i, (i + distance) % size) for i in range(size)])  9.82 us
    ppermute x2, waiting for transfers between devices, rotate_last(): return lax.ppermute(block, ('tile', 'slab'), route)  8.51 us
    pallas_call x1, Pallas kernels, early(): pl.pallas_call(lambda *refs: early_kernel(metas, layout, *refs), in_specs...  6.96 us
    ppermute x2, starting transfers between devices, rotate_last(): return lax.ppermute(block, ('tile', 'slab'), route)  6.23 us
  transfers between devices with their start and end apart: 24, of which 11 were waited for; matrix products, arithmetic and copies ran while one was open for 0% of the time, Pallas kernels for 39%

profile of v9, /device:TPU:29, one launch (start us, length us, event | category | flops | bytes accessed | tf_op | source)
XLA Modules:
  0.0 109.7 jit_solution(14513651899719731250)
XLA Ops:
  0.0 0.7 copy-done.2
  0.7 1.8 %cut.7 = f32[2,256,256]{2,1,0:T(8,128)S(1)} custom-call(s32[2,4]{1,0:T(2,128)S(1)} %bitcast.1, f32[1,256,4096]{2,1,0:T(8,128)} %refs_1_.3, f32[1,256,4096]{2,1,0:T(8,128)} %refs_2_.3), custom_call_target="tpu_custom_call" | custom-call | tf_op jit(solution)/shard_map/cut/pallas_call | solution.py:330
  2.5 3.1 %collective-permute-start.5 = (f32[2,256,256]{2,1,0:T(8,128)S(1)}, f32[2,256,256]{2,1,0:T(8,128)S(1)}, u32[]{:S(2)}, u32[]{:S(2)}) collective-permute-start(f32[2,256,256]{2,1,0:T(8,128)S(1)} %cut.7), channel_id=1, source_target_pairs={{12,14},{14,12},{13,15},{15,13},{28,30},{30,28},{29,31},{31,29}} | collective-permute-start | bytes 1572872 | tf_op jit(solution)/shard_map/ppermute | solution.py:53
  5.6 0.7 collective-permute-start.1
  6.4 2.7 %collective-permute-done.refs_1_ = s32[2,4]{1,0:T(2,128)S(1)} collective-permute-done((s32[2,4]{1,0:T(2,128)S(1)}, s32[2,4]{1,0:T(2,128)S(1)}, u32[]{:S(2)}, u32[]{:S(2)}) %collective-permute-start) | collective-permute-done | bytes 64 | tf_op jit(solution)/shard_map/ppermute | solution.py:46
  9.1 2.2 %cut.8 = (f32[2,256,256]{2,1,0:T(8,128)S(1)}, f32[2,256,256]{2,1,0:T(8,128)S(1)}) custom-call(s32[2,4]{1,0:T(2,128)S(1)} %bitcast.4, s32[2,4]{1,0:T(2,128)S(1)} %collective-permute-done.refs_1_, s32[2,4]{1,0:T(2,128)S(1)} %collective-permute-done.1.refs_2_, f32[1,256,4096]{2,1,0:T(8,128)} %refs_1_.3, f32[1,256,4096]{2,1,0:T(8,128)} %refs_2_.3), custom_call_target="tpu_custom_call" | custom-call | tf_op jit(solution)/shard_map/cut/pallas_call | solution.py:330
  11.4 5.8 %collective-permute-done.5.refs_6_ = f32[2,256,256]{2,1,0:T(8,128)S(1)} collective-permute-done((f32[2,256,256]{2,1,0:T(8,128)S(1)}, f32[2,256,256]{2,1,0:T(8,128)S(1)}, u32[]{:S(2)}, u32[]{:S(2)}) %collective-permute-start.5) | collective-permute-done | bytes 524320 | tf_op jit(solution)/shard_map/ppermute | solution.py:53
  17.2 2.2 %cut.9 = (f32[2,256,256]{2,1,0:T(8,128)S(1)}, f32[2,256,256]{2,1,0:T(8,128)S(1)}) custom-call(s32[2,4]{1,0:T(2,128)S(1)} %bitcast.5, s32[2,4]{1,0:T(2,128)S(1)} %collective-permute-done.refs_1_, s32[2,4]{1,0:T(2,128)S(1)} %collective-permute-done.1.refs_2_, f32[1,256,4096]{2,1,0:T(8,128)} %refs_1_.3, f32[1,256,4096]{2,1,0:T(8,128)} %refs_2_.3), custom_call_target="tpu_custom_call" | custom-call | tf_op jit(solution)/shard_map/cut/pallas_call | solution.py:330
  19.4 2.3 %cut.10 = (f32[2,256,256]{2,1,0:T(8,128)S(1)}, f32[2,256,256]{2,1,0:T(8,128)S(1)}) custom-call(s32[2,4]{1,0:T(2,128)S(1)} %bitcast.6, s32[2,4]{1,0:T(2,128)S(1)} %collective-permute-done.refs_1_, s32[2,4]{1,0:T(2,128)S(1)} %collective-permute-done.1.refs_2_, f32[1,256,4096]{2,1,0:T(8,128)} %refs_1_.3, f32[1,256,4096]{2,1,0:T(8,128)} %refs_2_.3), custom_call_target="tpu_custom_call" | custom-call | tf_op jit(solution)/shard_map/cut/pallas_call | solution.py:330
  21.7 1.9 %cut.11 = f32[3,256,256]{2,1,0:T(8,128)S(1)} custom-call(s32[2,4]{1,0:T(2,128)S(1)} %bitcast.7, s32[2,4]{1,0:T(2,128)S(1)} %collective-permute-done.refs_1_, s32[2,4]{1,0:T(2,128)S(1)} %collective-permute-done.1.refs_2_, f32[1,256,4096]{2,1,0:T(8,128)} %refs_1_.3, f32[1,256,4096]{2,1,0:T(8,128)} %refs_2_.3, f32[4,256,256]{2,1,0:T(8,128)} %refs_4_.15), custom_call_target="tpu_custom_call" | custom-call | tf_op jit(solution)/shard_map/cut/pallas_call | solution.py:330
  23.7 0.7 collective-permute-start.7
  24.4 1.9 %cut.12 = f32[3,256,256]{2,1,0:T(8,128)S(1)} custom-call(s32[2,4]{1,0:T(2,128)S(1)} %bitcast.8, s32[2,4]{1,0:T(2,128)S(1)} %collective-permute-done.refs_1_, s32[2,4]{1,0:T(2,128)S(1)} %collective-permute-done.1.refs_2_, f32[1,256,4096]{2,1,0:T(8,128)} %refs_1_.3, f32[1,256,4096]{2,1,0:T(8,128)} %refs_2_.3, f32[4,256,256]{2,1,0:T(8,128)} %refs_4_.15), custom_call_target="tpu_custom_call" | custom-call | tf_op jit(solution)/shard_map/cut/pallas_call | solution.py:330
  26.4 1.8 %cut.13.refs_5_ = f32[2,256,256]{2,1,0:T(8,128)S(1)} custom-call(s32[2,4]{1,0:T(2,128)S(1)} %bitcast.9, f32[1,256,4096]{2,1,0:T(8,128)} %refs_1_.3, f32[1,256,4096]{2,1,0:T(8,128)} %refs_2_.3), custom_call_target="tpu_custom_call" | custom-call | tf_op jit(solution)/shard_map/cut/pallas_call | solution.py:330
  28.2 0.7 join.2
  28.9 1.3 %collective-permute-start.9 = (f32[2,256,256]{2,1,0:T(8,128)S(1)}, f32[2,256,256]{2,1,0:T(8,128)S(1)}, u32[]{:S(2)}, u32[]{:S(2)}) collective-permute-start(f32[2,256,256]{2,1,0:T(8,128)S(1)} %join.2), channel_id=1, source_target_pairs={{0,2},{2,0},{1,3},{3,1},{4,6},{6,4},{5,7},{7,5},{8,10},{10,8},{9,1... | collective-permute-start | bytes 1572872 | tf_op jit(solution)/shard_map/ppermute | solution.py:38
  30.2 0.7 collective-permute-start.10
  30.9 1.9 %collective-permute-start.2 = (s32[2,4]{1,0:T(2,128)S(1)}, s32[2,4]{1,0:T(2,128)S(1)}, u32[]{:S(2)}, u32[]{:S(2)}) collective-permute-start(s32[2,4]{1,0:T(2,128)S(1)} %bitcast.11), channel_id=1, source_target_pairs={{0,1},{1,0},{2,3},{3,2},{4,5},{5,4},{6,7},{7,6},{8,9},{9,8},{10,11... | collective-permute-start | bytes 104 | tf_op jit(solution)/shard_map/ppermute | solution.py:38
  32.8 0.4 expand.1
  33.3 0.7 join.3
  33.9 0.5 collective-permute-start.3
  34.5 0.3 collective-permute-start.11
  34.8 0.5 collective-permute-done.3.refs_4_
  35.3 5.6 %collective-permute-done.9.refs_7_ = f32[2,256,256]{2,1,0:T(8,128)S(1)} collective-permute-done((f32[2,256,256]{2,1,0:T(8,128)S(1)}, f32[2,256,256]{2,1,0:T(8,128)S(1)}, u32[]{:S(2)}, u32[]{:S(2)}) %collective-permute-start.9) | collective-permute-done | bytes 524320 | tf_op jit(solution)/shard_map/ppermute | solution.py:38
  40.9 0.3 collective-permute-done.8.refs_6_
  41.2 7.2 %slot_0.1 = (f32[2,256,256]{2,1,0:T(8,128)S(1)}, f32[2,256,256]{2,1,0:T(8,128)S(1)}) custom-call(s32[2,4]{1,0:T(2,128)S(1)} %bitcast.13, s32[2,4]{1,0:T(2,128)S(1)} %collective-permute-done.refs_1_, s32[2,4]{1,0:T(2,128)S(1)} %collective-permute-done.1.refs_2_, f32[2,256,256]{2,1,0:T(8,128)S(1)} %copy-done, f32[4,256,256]{2,1,0:T(8,128)} %refs_4_.15, ...), custom_call_target="tpu_custom_call" | custom-call | tf_op jit(solution)/shard_map/slot_0/pallas_call | solution.py:262
  48.4 1.3 %collective-permute-start.12 = (f32[2,256,256]{2,1,0:T(8,128)S(1)}, f32[2,256,256]{2,1,0:T(8,128)S(1)}, u32[]{:S(2)}, u32[]{:S(2)}) collective-permute-start(f32[2,256,256]{2,1,0:T(8,128)S(1)} %get-tuple-element.65), channel_id=1, source_target_pairs={{0,2},{2,0},{1,3},{3,1},{4,6},{6,4},{5,7},{7,5},{8,10},{10,8},{9,1... | collective-permute-start | bytes 1572872 | tf_op jit(solution)/shard_map/ppermute | solution.py:38
  49.7 4.4 %collective-permute-start.13 = (f32[2,256,256]{2,1,0:T(8,128)S(1)}, f32[2,256,256]{2,1,0:T(8,128)S(1)}, u32[]{:S(2)}, u32[]{:S(2)}) collective-permute-start(f32[2,256,256]{2,1,0:T(8,128)S(1)} %get-tuple-element.60.refs_1_.refs_7_), channel_id=1, source_target_pairs={{0,4},{4,0},{8,12},{12,8},{1,5},{5,1},{9,13},{13,9},{2,6},{6,2},{1... | collective-permute-start | bytes 1572872 | tf_op jit(solution)/shard_map/ppermute | solution.py:46
  54.1 7.4 %slot_1.1 = (f32[2,256,256]{2,1,0:T(8,128)S(1)}, f32[2,256,256]{2,1,0:T(8,128)S(1)}) custom-call(s32[2,4]{1,0:T(2,128)S(1)} %bitcast.14, s32[2,4]{1,0:T(2,128)S(1)} %collective-permute-done.refs_1_, s32[2,4]{1,0:T(2,128)S(1)} %collective-permute-done.1.refs_2_, f32[2,256,256]{2,1,0:T(8,128)S(1)} %copy-done, f32[4,256,256]{2,1,0:T(8,128)} %refs_4_.15, ...), custom_call_target="tpu_custom_call" | custom-call | tf_op jit(solution)/shard_map/slot_1/pallas_call | solution.py:262
  61.5 0.5 collective-permute-start.15
  61.9 7.1 %slot_last.1 = (f32[2,256,256]{2,1,0:T(8,128)S(1)}, f32[2,256,256]{2,1,0:T(8,128)S(1)}) custom-call(s32[2,4]{1,0:T(2,128)S(1)} %bitcast.15, s32[2,4]{1,0:T(2,128)S(1)} %collective-permute-done.refs_1_, s32[2,4]{1,0:T(2,128)S(1)} %collective-permute-done.1.refs_2_, f32[2,256,256]{2,1,0:T(8,128)S(1)} %copy-done, f32[4,256,256]{2,1,0:T(8,128)} %refs_4_.15, ...), custom_call_target="tpu_custom_call" | custom-call | tf_op jit(solution)/shard_map/slot_last/pallas_call | solution.py:262
  69.1 0.7 collective-permute-start.16
  69.8 0.1 pack.2
  70.0 3.7 %collective-permute-start.14 = (f32[4,2,256,256]{3,2,1,0:T(8,128)S(1)}, f32[4,2,256,256]{3,2,1,0:T(8,128)S(1)}, u32[]{:S(2)}, u32[]{:S(2)}) collective-permute-start(f32[4,2,256,256]{3,2,1,0:T(8,128)S(1)} %pack.2), channel_id=1, source_target_pairs={{0,1},{1,0},{2,3},{3,2},{4,5},{5,4},{6,7},{7,6},{8,9},{9,8},{10,11... | collective-permute-start | bytes 6291464 | tf_op jit(solution)/shard_map/ppermute | solution.py:38
  73.6 1.1 %collective-permute-done.15.refs_1_.refs_12_ = f32[2,256,256]{2,1,0:T(8,128)S(1)} collective-permute-done((f32[2,256,256]{2,1,0:T(8,128)S(1)}, f32[2,256,256]{2,1,0:T(8,128)S(1)}, u32[]{:S(2)}, u32[]{:S(2)}) %collective-permute-start.15) | collective-permute-done | bytes 524320 | tf_op jit(solution)/shard_map/ppermute | solution.py:38
  74.8 0.1 pack.3
  74.9 2.3 %collective-permute-start.17 = (f32[3,2,256,256]{3,2,1,0:T(8,128)S(1)}, f32[3,2,256,256]{3,2,1,0:T(8,128)S(1)}, u32[]{:S(2)}, u32[]{:S(2)}) collective-permute-start(f32[3,2,256,256]{3,2,1,0:T(8,128)S(1)} %pack.3), channel_id=1, source_target_pairs={{0,1},{1,0},{2,3},{3,2},{4,5},{5,4},{6,7},{7,6},{8,9},{9,8},{10,11... | collective-permute-start | bytes 4718600 | tf_op jit(solution)/shard_map/ppermute | solution.py:38
  77.2 0.7 collective-permute-start.22
  77.9 9.3 %collective-permute-start.20 = (f32[2,256,256]{2,1,0:T(8,128)S(1)}, f32[2,256,256]{2,1,0:T(8,128)S(1)}, u32[]{:S(2)}, u32[]{:S(2)}) collective-permute-start(f32[2,256,256]{2,1,0:T(8,128)S(1)} %collective-permute-done.12.refs_2_.refs_8_), channel_id=1, source_target_pairs={{0,4},{4,0},{8,12},{12,8},{1,5},{5,1},{9,13},{13,9},{2,6},{6,2},{1... | collective-permute-start | bytes 1572872 | tf_op jit(solution)/shard_map/ppermute | solution.py:46
  87.2 3.1 %collective-permute-start.18 = (f32[2,256,256]{2,1,0:T(8,128)S(1)}, f32[2,256,256]{2,1,0:T(8,128)S(1)}, u32[]{:S(2)}, u32[]{:S(2)}) collective-permute-start(f32[2,256,256]{2,1,0:T(8,128)S(1)} %get-tuple-element.70), channel_id=1, source_target_pairs={{12,14},{14,12},{13,15},{15,13},{28,30},{30,28},{29,31},{31,29}} | collective-permute-start | bytes 1572872 | tf_op jit(solution)/shard_map/ppermute | solution.py:53
  90.3 7.0 %early.1 = (f32[2,256,4096]{2,1,0:T(8,128)S(1)}, f32[2,1,256,4096]{3,2,1,0:T(8,128)}) custom-call(s32[2,4]{1,0:T(2,128)S(1)} %bitcast.16, s32[2,4]{1,0:T(2,128)S(1)} %collective-permute-done.refs_1_, s32[2,4]{1,0:T(2,128)S(1)} %collective-permute-done.1.refs_2_, s32[2,4]{1,0:T(2,128)S(1)} %collective-permute-done.2.refs_3_, ...), custom_call_target="tpu_custom_call" | custom-call | tf_op jit(solution)/shard_map/early/pallas_call | solution.py:435
  97.3 2.0 %collective-permute-done.20.refs_9_ = f32[2,256,256]{2,1,0:T(8,128)S(1)} collective-permute-done((f32[2,256,256]{2,1,0:T(8,128)S(1)}, f32[2,256,256]{2,1,0:T(8,128)S(1)}, u32[]{:S(2)}, u32[]{:S(2)}) %collective-permute-start.20) | collective-permute-done | bytes 524320 | tf_op jit(solution)/shard_map/ppermute | solution.py:46
  99.3 2.7 %collective-permute-done.18.refs_7_ = f32[2,256,256]{2,1,0:T(8,128)S(1)} collective-permute-done((f32[2,256,256]{2,1,0:T(8,128)S(1)}, f32[2,256,256]{2,1,0:T(8,128)S(1)}, u32[]{:S(2)}, u32[]{:S(2)}) %collective-permute-start.18) | collective-permute-done | bytes 524320 | tf_op jit(solution)/shard_map/ppermute | solution.py:53
  102.0 1.4 %collective-permute-start.19 = (f32[2,256,256]{2,1,0:T(8,128)S(1)}, f32[2,256,256]{2,1,0:T(8,128)S(1)}, u32[]{:S(2)}, u32[]{:S(2)}) collective-permute-start(f32[2,256,256]{2,1,0:T(8,128)S(1)} %collective-permute-done.18.refs_7_), channel_id=1, source_target_pairs={{0,1},{1,0},{2,3},{3,2},{4,5},{5,4},{6,7},{7,6},{8,9},{9,8},{10,11... | collective-permute-start | bytes 1572872 | tf_op jit(solution)/shard_map/ppermute | solution.py:38
  103.4 0.5 collective-permute-start.23
  103.9 1.0 collective-permute-done.19.refs_8_
  105.0 0.7 collective-permute-done.21.refs_10_
  105.7 0.7 collective-permute-done.23.refs_12_
  106.5 3.1 %late.1 = f32[2,1,256,4096]{3,2,1,0:T(8,128)} custom-call(s32[2,4]{1,0:T(2,128)S(1)} %bitcast.17, s32[2,4]{1,0:T(2,128)S(1)} %collective-permute-done.refs_1_, s32[2,4]{1,0:T(2,128)S(1)} %collective-permute-done.1.refs_2_, s32[2,4]{1,0:T(2,128)S(1)} %collective-permute-done.2.refs_3_, ...), custom_call_target="tpu_custom_call", output_to_operand_aliasing={{}: (13, {})} | custom-call | tf_op jit(solution)/shard_map/late/pallas_call | solution.py:500
  (25 shorter events, 0.4 us)
Async XLA Ops:
  0.0 0.7 copy-start.2
  2.5 14.7 %collective-permute-start.5 = (f32[2,256,256]{2,1,0:T(8,128)S(1)}, f32[2,256,256]{2,1,0:T(8,128)S(1)}, u32[]{:S(2)}, u32[]{:S(2)}) collective-permute-start(f32[2,256,256]{2,1,0:T(8,128)S(1)} %cut.7), channel_id=1, source_target_pairs={{12,14},{14,12},{13,15},{15,13},{28,30},{30,28},{29,31},{31,29}} | collective-permute-start | bytes 1572872 | tf_op jit(solution)/shard_map/ppermute | solution.py:53
  5.6 0.8 collective-permute-start.1
  6.3 2.8 %collective-permute-start = (s32[2,4]{1,0:T(2,128)S(1)}, s32[2,4]{1,0:T(2,128)S(1)}, u32[]{:S(2)}, u32[]{:S(2)}) collective-permute-start(s32[2,4]{1,0:T(2,128)S(1)} %bitcast.3), channel_id=1, source_target_pairs={{0,4},{4,0},{8,12},{12,8},{1,5},{5,1},{9,13},{13,9},{2,6},{6,2},{1... | collective-permute-start | bytes 104 | tf_op jit(solution)/shard_map/ppermute | solution.py:46
  11.3 16.9 %collective-permute-start.6 = (f32[2,256,256]{2,1,0:T(8,128)S(1)}, f32[2,256,256]{2,1,0:T(8,128)S(1)}, u32[]{:S(2)}, u32[]{:S(2)}) collective-permute-start(f32[2,256,256]{2,1,0:T(8,128)S(1)} %get-tuple-element.42), channel_id=1, source_target_pairs={{0,4},{4,0},{8,12},{12,8},{1,5},{5,1},{9,13},{13,9},{2,6},{6,2},{1... | collective-permute-start | bytes 1572872 | tf_op jit(solution)/shard_map/ppermute | solution.py:46
  23.6 17.6 %collective-permute-start.8 = (f32[3,256,256]{2,1,0:T(8,128)S(1)}, f32[3,256,256]{2,1,0:T(8,128)S(1)}, u32[]{:S(2)}, u32[]{:S(2)}) collective-permute-start(f32[3,256,256]{2,1,0:T(8,128)S(1)} %cut.11), channel_id=1, source_target_pairs={{0,4},{4,0},{8,12},{12,8},{1,5},{5,1},{9,13},{13,9},{2,6},{6,2},{1... | collective-permute-start | bytes 2359304 | tf_op jit(solution)/shard_map/ppermute | solution.py:46
  23.7 9.4 %collective-permute-start.7 = (f32[2,256,256]{2,1,0:T(8,128)S(1)}, f32[2,256,256]{2,1,0:T(8,128)S(1)}, u32[]{:S(2)}, u32[]{:S(2)}) collective-permute-start(f32[2,256,256]{2,1,0:T(8,128)S(1)} %get-tuple-element.54), channel_id=1, source_target_pairs={{4,8},{8,4},{5,9},{9,5},{6,10},{10,6},{7,11},{11,7},{20,24},{24,20... | collective-permute-start | bytes 1572872 | tf_op jit(solution)/shard_map/ppermute | solution.py:46
  28.2 4.6 %copy-start.1 = (bf16[8,256,256]{2,1,0:T(8,128)(2,1)S(1)}, bf16[8,256,256]{2,1,0:T(8,128)(2,1)}, u32[]{:S(2)}) copy-start(bf16[8,256,256]{2,1,0:T(8,128)(2,1)} %constant.2.clone.pieces) | copy-start | bytes 3145732
  28.2 13.0 %copy-start = (f32[2,256,256]{2,1,0:T(8,128)S(1)}, f32[2,256,256]{2,1,0:T(8,128)}, u32[]{:S(2)}) copy-start(f32[2,256,256]{2,1,0:T(8,128)} %refs_3_.15) | copy-start | bytes 1572868
  28.2 13.0 %copy-start.3 = (s32[4,2]{0,1:T(2,128)S(1)}, s32[4,2]{0,1:T(2,128)}, u32[]{:S(2)}) copy-start(s32[4,2]{0,1:T(2,128)} %param.10) | copy-start | bytes 100
  28.9 12.0 %collective-permute-start.9 = (f32[2,256,256]{2,1,0:T(8,128)S(1)}, f32[2,256,256]{2,1,0:T(8,128)S(1)}, u32[]{:S(2)}, u32[]{:S(2)}) collective-permute-start(f32[2,256,256]{2,1,0:T(8,128)S(1)} %join.2), channel_id=1, source_target_pairs={{0,2},{2,0},{1,3},{3,1},{4,6},{6,4},{5,7},{7,5},{8,10},{10,8},{9,1... | collective-permute-start | bytes 1572872 | tf_op jit(solution)/shard_map/ppermute | solution.py:38
  30.2 23.9 %collective-permute-start.10 = (f32[3,256,256]{2,1,0:T(8,128)S(1)}, f32[3,256,256]{2,1,0:T(8,128)S(1)}, u32[]{:S(2)}, u32[]{:S(2)}) collective-permute-start(f32[3,256,256]{2,1,0:T(8,128)S(1)} %cut.12), channel_id=1, source_target_pairs={{4,8},{8,4},{5,9},{9,5},{6,10},{10,6},{7,11},{11,7},{20,24},{24,20... | collective-permute-start | bytes 2359304 | tf_op jit(solution)/shard_map/ppermute | solution.py:46
  30.9 3.0 %collective-permute-start.2 = (s32[2,4]{1,0:T(2,128)S(1)}, s32[2,4]{1,0:T(2,128)S(1)}, u32[]{:S(2)}, u32[]{:S(2)}) collective-permute-start(s32[2,4]{1,0:T(2,128)S(1)} %bitcast.11), channel_id=1, source_target_pairs={{0,1},{1,0},{2,3},{3,2},{4,5},{5,4},{6,7},{7,6},{8,9},{9,8},{10,11... | collective-permute-start | bytes 104 | tf_op jit(solution)/shard_map/ppermute | solution.py:38
  33.2 1.3 %collective-permute-start.4 = (s32[2,4]{1,0:T(2,128)S(1)}, s32[2,4]{1,0:T(2,128)S(1)}, u32[]{:S(2)}, u32[]{:S(2)}) collective-permute-start(s32[2,4]{1,0:T(2,128)S(1)} %collective-permute-done.1.refs_2_), channel_id=1, source_target_pairs={{0,1},{1,0},{2,3},{3,2},{4,5},{5,4},{6,7},{7,6},{8,9},{9,8},{10,11... | collective-permute-start | bytes 104 | tf_op jit(solution)/shard_map/ppermute | solution.py:38
  33.9 1.4 %collective-permute-start.3 = (s32[2,4]{1,0:T(2,128)S(1)}, s32[2,4]{1,0:T(2,128)S(1)}, u32[]{:S(2)}, u32[]{:S(2)}) collective-permute-start(s32[2,4]{1,0:T(2,128)S(1)} %collective-permute-done.refs_1_), channel_id=1, source_target_pairs={{0,1},{1,0},{2,3},{3,2},{4,5},{5,4},{6,7},{7,6},{8,9},{9,8},{10,11... | collective-permute-start | bytes 104 | tf_op jit(solution)/shard_map/ppermute | solution.py:38
  34.5 19.6 %collective-permute-start.11 = (f32[2,256,256]{2,1,0:T(8,128)S(1)}, f32[2,256,256]{2,1,0:T(8,128)S(1)}, u32[]{:S(2)}, u32[]{:S(2)}) collective-permute-start(f32[2,256,256]{2,1,0:T(8,128)S(1)} %join.3), channel_id=1, source_target_pairs={{0,2},{2,0},{1,3},{3,1},{4,6},{6,4},{5,7},{7,5},{8,10},{10,8},{9,1... | collective-permute-start | bytes 1572872 | tf_op jit(solution)/shard_map/ppermute | solution.py:38
  48.4 20.7 %collective-permute-start.12 = (f32[2,256,256]{2,1,0:T(8,128)S(1)}, f32[2,256,256]{2,1,0:T(8,128)S(1)}, u32[]{:S(2)}, u32[]{:S(2)}) collective-permute-start(f32[2,256,256]{2,1,0:T(8,128)S(1)} %get-tuple-element.65), channel_id=1, source_target_pairs={{0,2},{2,0},{1,3},{3,1},{4,6},{6,4},{5,7},{7,5},{8,10},{10,8},{9,1... | collective-permute-start | bytes 1572872 | tf_op jit(solution)/shard_map/ppermute | solution.py:38
  49.7 20.1 %collective-permute-start.13 = (f32[2,256,256]{2,1,0:T(8,128)S(1)}, f32[2,256,256]{2,1,0:T(8,128)S(1)}, u32[]{:S(2)}, u32[]{:S(2)}) collective-permute-start(f32[2,256,256]{2,1,0:T(8,128)S(1)} %get-tuple-element.60.refs_1_.refs_7_), channel_id=1, source_target_pairs={{0,4},{4,0},{8,12},{12,8},{1,5},{5,1},{9,13},{13,9},{2,6},{6,2},{1... | collective-permute-start | bytes 1572872 | tf_op jit(solution)/shard_map/ppermute | solution.py:46
  61.5 13.3 %collective-permute-start.15 = (f32[2,256,256]{2,1,0:T(8,128)S(1)}, f32[2,256,256]{2,1,0:T(8,128)S(1)}, u32[]{:S(2)}, u32[]{:S(2)}) collective-permute-start(f32[2,256,256]{2,1,0:T(8,128)S(1)} %get-tuple-element.66), channel_id=1, source_target_pairs={{0,2},{2,0},{1,3},{3,1},{4,6},{6,4},{5,7},{7,5},{8,10},{10,8},{9,1... | collective-permute-start | bytes 1572872 | tf_op jit(solution)/shard_map/ppermute | solution.py:38
  69.1 5.7 %collective-permute-start.16 = (f32[2,256,256]{2,1,0:T(8,128)S(1)}, f32[2,256,256]{2,1,0:T(8,128)S(1)}, u32[]{:S(2)}, u32[]{:S(2)}) collective-permute-start(f32[2,256,256]{2,1,0:T(8,128)S(1)} %get-tuple-element.67.refs_0_.refs_11_), channel_id=1, source_target_pairs={{4,8},{8,4},{5,9},{9,5},{6,10},{10,6},{7,11},{11,7},{20,24},{24,20... | collective-permute-start | bytes 1572872 | tf_op jit(solution)/shard_map/ppermute | solution.py:46
  70.0 20.4 %collective-permute-start.14 = (f32[4,2,256,256]{3,2,1,0:T(8,128)S(1)}, f32[4,2,256,256]{3,2,1,0:T(8,128)S(1)}, u32[]{:S(2)}, u32[]{:S(2)}) collective-permute-start(f32[4,2,256,256]{3,2,1,0:T(8,128)S(1)} %pack.2), channel_id=1, source_target_pairs={{0,1},{1,0},{2,3},{3,2},{4,5},{5,4},{6,7},{7,6},{8,9},{9,8},{10,11... | collective-permute-start | bytes 6291464 | tf_op jit(solution)/shard_map/ppermute | solution.py:38
  74.9 15.4 %collective-permute-start.17 = (f32[3,2,256,256]{3,2,1,0:T(8,128)S(1)}, f32[3,2,256,256]{3,2,1,0:T(8,128)S(1)}, u32[]{:S(2)}, u32[]{:S(2)}) collective-permute-start(f32[3,2,256,256]{3,2,1,0:T(8,128)S(1)} %pack.3), channel_id=1, source_target_pairs={{0,1},{1,0},{2,3},{3,2},{4,5},{5,4},{6,7},{7,6},{8,9},{9,8},{10,11... | collective-permute-start | bytes 4718600 | tf_op jit(solution)/shard_map/ppermute | solution.py:38
  77.2 20.1 %collective-permute-start.22 = (f32[2,256,256]{2,1,0:T(8,128)S(1)}, f32[2,256,256]{2,1,0:T(8,128)S(1)}, u32[]{:S(2)}, u32[]{:S(2)}) collective-permute-start(f32[2,256,256]{2,1,0:T(8,128)S(1)} %collective-permute-done.15.refs_1_.refs_12_), channel_id=1, source_target_pairs={{4,8},{8,4},{5,9},{9,5},{6,10},{10,6},{7,11},{11,7},{20,24},{24,20... | collective-permute-start | bytes 1572872 | tf_op jit(solution)/shard_map/ppermute | solution.py:46
  77.9 21.4 %collective-permute-start.20 = (f32[2,256,256]{2,1,0:T(8,128)S(1)}, f32[2,256,256]{2,1,0:T(8,128)S(1)}, u32[]{:S(2)}, u32[]{:S(2)}) collective-permute-start(f32[2,256,256]{2,1,0:T(8,128)S(1)} %collective-permute-done.12.refs_2_.refs_8_), channel_id=1, source_target_pairs={{0,4},{4,0},{8,12},{12,8},{1,5},{5,1},{9,13},{13,9},{2,6},{6,2},{1... | collective-permute-start | bytes 1572872 | tf_op jit(solution)/shard_map/ppermute | solution.py:46
  87.2 14.8 %collective-permute-start.18 = (f32[2,256,256]{2,1,0:T(8,128)S(1)}, f32[2,256,256]{2,1,0:T(8,128)S(1)}, u32[]{:S(2)}, u32[]{:S(2)}) collective-permute-start(f32[2,256,256]{2,1,0:T(8,128)S(1)} %get-tuple-element.70), channel_id=1, source_target_pairs={{12,14},{14,12},{13,15},{15,13},{28,30},{30,28},{29,31},{31,29}} | collective-permute-start | bytes 1572872 | tf_op jit(solution)/shard_map/ppermute | solution.py:53
  102.0 3.0 %collective-permute-start.19 = (f32[2,256,256]{2,1,0:T(8,128)S(1)}, f32[2,256,256]{2,1,0:T(8,128)S(1)}, u32[]{:S(2)}, u32[]{:S(2)}) collective-permute-start(f32[2,256,256]{2,1,0:T(8,128)S(1)} %collective-permute-done.18.refs_7_), channel_id=1, source_target_pairs={{0,1},{1,0},{2,3},{3,2},{4,5},{5,4},{6,7},{7,6},{8,9},{9,8},{10,11... | collective-permute-start | bytes 1572872 | tf_op jit(solution)/shard_map/ppermute | solution.py:38
  103.4 2.3 %collective-permute-start.21 = (f32[2,256,256]{2,1,0:T(8,128)S(1)}, f32[2,256,256]{2,1,0:T(8,128)S(1)}, u32[]{:S(2)}, u32[]{:S(2)}) collective-permute-start(f32[2,256,256]{2,1,0:T(8,128)S(1)} %collective-permute-done.20.refs_9_), channel_id=1, source_target_pairs={{0,1},{1,0},{2,3},{3,2},{4,5},{5,4},{6,7},{7,6},{8,9},{9,8},{10,11... | collective-permute-start | bytes 1572872 | tf_op jit(solution)/shard_map/ppermute | solution.py:38
  103.4 3.0 %collective-permute-start.23 = (f32[2,256,256]{2,1,0:T(8,128)S(1)}, f32[2,256,256]{2,1,0:T(8,128)S(1)}, u32[]{:S(2)}, u32[]{:S(2)}) collective-permute-start(f32[2,256,256]{2,1,0:T(8,128)S(1)} %collective-permute-done.22.refs_11_), channel_id=1, source_target_pairs={{0,1},{1,0},{2,3},{3,2},{4,5},{5,4},{6,7},{7,6},{8,9},{9,8},{10,11... | collective-permute-start | bytes 1572872 | tf_op jit(solution)/shard_map/ppermute | solution.py:38

commit v10 on v8

--- a/solution.py
+++ b/solution.py
@@ -77,27 +77,22 @@
 def expand_kernel(pieces, *outs):
     side = pieces.shape[-1]
     for which in range(2):
-        left, right = outs[2 * which], outs[2 * which + 1]
         real_high, real_low, imag_high, imag_low = [pieces[4 * which + k] for k in range(4)]
         real = [real_high, real_low, real_high]
         imag = [imag_high, imag_low, imag_high]
         minus = [-imag_high, -imag_low, -imag_high]
         for column, blocks in enumerate((real + minus, imag + real)):
             for row, block in enumerate(blocks):
-                rows, cols = pl.ds(row * side, side), pl.ds(column * side, side)
-                right[rows, cols] = block
-                left[cols, rows] = block
+                outs[which][pl.ds(row * side, side), pl.ds(column * side, side)] = block
 
 
 def expand(side):
     pieces = jnp.asarray(compact_tables(side))
-    left = jax.ShapeDtypeStruct((2 * side, 6 * side), jnp.bfloat16)
-    right = jax.ShapeDtypeStruct((6 * side, 2 * side), jnp.bfloat16)
     return pl.pallas_call(
         expand_kernel,
         in_specs=[VMEM],
-        out_specs=[VMEM] * 4,
-        out_shape=[left, right, left, right],
+        out_specs=[VMEM] * 2,
+        out_shape=[jax.ShapeDtypeStruct((6 * side, 2 * side), jnp.bfloat16)] * 2,
         compiler_params=params(16),
         name="expand",
     )(pieces)
@@ -109,17 +104,23 @@
     return high, low
 
 
-def two_sided(left, right, real, imag):
+def right_product(table, real, imag):
     side = real.shape[-1]
     real_high, real_low = split(real)
     imag_high, imag_low = split(imag)
     wide = jnp.concatenate([real_high, real_high, real_low, imag_high, imag_high, imag_low], axis=1)
-    inner = jnp.dot(wide, right[...], preferred_element_type=jnp.float32)
-    real_high, real_low = split(inner[:, :side])
-    imag_high, imag_low = split(inner[:, side:])
-    tall = jnp.concatenate([real_high, real_high, real_low, imag_high, imag_high, imag_low], axis=0)
-    outer = jnp.dot(left[...], tall, preferred_element_type=jnp.float32)
-    return outer[:side], outer[side:]
+    out = jnp.dot(wide, table[...], preferred_element_type=jnp.float32)
+    return out[:, :side], out[:, side:]
+
+
+def two_sided_transposed(table, real, imag):
+    real, imag = right_product(table, real, imag)
+    return right_product(table, real.T, imag.T)
+
+
+def two_sided(table, real, imag):
+    real, imag = two_sided_transposed(table, real, imag)
+    return real.T, imag.T
 
 
 def transmission(phase, absorption):
@@ -184,9 +185,9 @@
     own = refs[:pieces]
     others = refs[pieces : pieces + sections - 1]
     refs = refs[pieces + sections - 1 :]
-    prop_left, prop_right, dft_left, dft_right = refs[:4]
-    outs = refs[4 : 4 + sections]
-    wave, trans, amplitude, sem = refs[4 + sections :]
+    prop, dft = refs[:2]
+    outs = refs[2 : 2 + sections]
+    wave, trans, amplitude, sem = refs[2 + sections :]
     side = probe.shape[-1]
     slab = lax.axis_index("slab")
     index, row, col, low, high = locate(spot, layout, tables)
@@ -205,7 +206,6 @@
         @pl.when(lower)
         def _():
             fetch().start()
-            fetch().wait()
 
         @pl.when(jnp.logical_not(lower))
         def _():
@@ -228,14 +228,20 @@
         a, b, c, d = wave[step, 0], wave[step, 1], trans[step, 0], trans[step, 1]
         real, imag = a * c - b * d, a * d + b * c
         if step < sections - 1:
-            real, imag = two_sided(prop_left, prop_right, real, imag)
+            real, imag = two_sided(prop, real, imag)
             wave[step + 1, 0] = real
             wave[step + 1, 1] = imag
-    real, imag = two_sided(dft_left, dft_right, real, imag)
+    real, imag = two_sided_transposed(dft, real, imag)
     if lower is True:
         fetch().wait()
-    factor = 1.0 - amplitude[...] * lax.rsqrt(jnp.maximum(real * real + imag * imag, 0.25))
-    real, minus = two_sided(dft_left, dft_right, real * factor, -imag * factor)
+    elif lower is not False:
+
+        @pl.when(lower)
+        def _():
+            fetch().wait()
+
+    factor = 1.0 - amplitude[...].T * lax.rsqrt(jnp.maximum(real * real + imag * imag, 0.25))
+    real, minus = two_sided_transposed(dft, real * factor, -imag * factor)
     for step in range(sections - 1, -1, -1):
         a, b = wave[step, 0], wave[step, 1]
         wave[step, 0] = a * real - b * minus
@@ -243,7 +249,7 @@
         if step > 0:
             c, d = trans[step, 0], trans[step, 1]
             real, minus = c * real - d * minus, c * minus + d * real
-            real, minus = two_sided(prop_left, prop_right, real, minus)
+            real, minus = two_sided(prop, real, minus)
     for distance in range(sections):
         outs[distance][...] = wave[lax.rem(slab + distance, sections)]
 
@@ -253,7 +259,7 @@
     shape = jax.ShapeDtypeStruct((2, side, side), jnp.float32)
     return pl.pallas_call(
         lambda *refs: slot_kernel(kind, spot, layout, len(tables), *refs),
-        in_specs=[SMEM] * len(tables) + [VMEM, HBM] + [VMEM] * (len(own) + len(others) + 4),
+        in_specs=[SMEM] * len(tables) + [VMEM, HBM] + [VMEM] * (len(own) + len(others) + 2),
         out_specs=[VMEM] * sections,
         out_shape=[shape] * sections,
         scratch_shapes=[pltpu.VMEM((sections, 2, side, side), jnp.float32)] * 2

time: 97 us -> 96.2 us (level)
  Pallas kernels: 45.1 us -> 42.7 us
  waiting for transfers between devices: 14.2 us -> 15.3 us
    pallas_call x3, Pallas kernels: 22.3 us -> 20.2 us  [run_slot(): pl.pallas_call(lambda *refs: slot_kernel(kind, spot, layout, len(tables),...]
    ppermute x10, starting transfers between devices: 10.1 us -> 8.11 us  [swap(): return lax.ppermute(block, axis, route)]
    ppermute x12, waiting for transfers between devices: 3.7 us -> 5.4 us  [rotate(): lax.ppermute(block, axis, [(i, (i + distance) % size) for i in range(size)])]
    ppermute x12, starting transfers between devices: 20.9 us -> 22.2 us  [rotate(): lax.ppermute(block, axis, [(i, (i + distance) % size) for i in range(size)])]
  transfers between devices with their start and end apart: 24 -> 24, of which waited for: 12 -> 12; matrix products, arithmetic and copies ran while one was open for 0% -> 0% of each run, Pallas kernels for 41% -> 39%
where the time goes in v10:
time: 96.2 us; the launch traced here: 95.6 us
  Pallas kernels  42.7 us (44%)
  starting transfers between devices  36.4 us (38%)
  waiting for transfers between devices  15.3 us (16%)
    ppermute x12, starting transfers between devices, rotate(): lax.ppermute(block, axis, [(i, (i + distance) % size) for i in range(size)])  22.2 us
    pallas_call x3, Pallas kernels, run_slot(): pl.pallas_call(lambda *refs: slot_kernel(kind, spot, layout, len(tables),...  20.2 us
    pallas_call x5, Pallas kernels, cut(): pl.pallas_call(lambda *refs: cut_kernel(spots, layout, measured is not No...  10.6 us
    ppermute x10, starting transfers between devices, swap(): return lax.ppermute(block, axis, route)  8.11 us
    ppermute x10, waiting for transfers between devices, swap(): return lax.ppermute(block, axis, route)  7.16 us
    pallas_call x1, Pallas kernels, early(): pl.pallas_call(lambda *refs: early_kernel(metas, layout, *refs), in_specs...  6.94 us
    ppermute x2, starting transfers between devices, rotate_last(): return lax.ppermute(block, ('tile', 'slab'), route)  6.1 us
    ppermute x12, waiting for transfers between devices, rotate(): lax.ppermute(block, axis, [(i, (i + distance) % size) for i in range(size)])  5.4 us
  transfers between devices with their start and end apart: 24, of which 12 were waited for; matrix products, arithmetic and copies ran while one was open for 0% of the time, Pallas kernels for 39%

profile of v10, /device:TPU:29, one launch (start us, length us, event | category | flops | bytes accessed | tf_op | source)
XLA Modules:
  0.0 95.6 jit_solution(7954905437938710313)
XLA Ops:
  0.0 0.6 collective-permute-start.1
  0.7 1.7 %collective-permute-start = (s32[2,4]{1,0:T(2,128)}, s32[2,4]{1,0:T(2,128)S(1)}, u32[]{:S(2)}, u32[]{:S(2)}) collective-permute-start(s32[2,4]{1,0:T(2,128)} %bitcast.2), channel_id=1, source_target_pairs={{0,4},{4,0},{8,12},{12,8},{1,5},{5,1},{9,13},{13,9},{2,6},{6,2},{1... | collective-permute-start | bytes 104 | tf_op jit(solution)/shard_map/ppermute | solution.py:46
  2.3 1.2 %collective-permute-done.refs_1_ = s32[2,4]{1,0:T(2,128)S(1)} collective-permute-done((s32[2,4]{1,0:T(2,128)}, s32[2,4]{1,0:T(2,128)S(1)}, u32[]{:S(2)}, u32[]{:S(2)}) %collective-permute-start) | collective-permute-done | bytes 64 | tf_op jit(solution)/shard_map/ppermute | solution.py:46
  3.5 0.7 copy-done.2
  4.2 2.2 %cut.5 = (f32[2,256,256]{2,1,0:T(8,128)S(1)}, f32[2,256,256]{2,1,0:T(8,128)S(1)}) custom-call(s32[2,4]{1,0:T(2,128)S(1)} %bitcast.3, s32[2,4]{1,0:T(2,128)S(1)} %collective-permute-done.refs_1_, s32[2,4]{1,0:T(2,128)S(1)} %collective-permute-done.1.refs_2_, f32[1,256,4096]{2,1,0:T(8,128)} %refs_3_.12, f32[1,256,4096]{2,1,0:T(8,128)} %refs_4_.12), custom_call_target="tpu_custom_call" | custom-call | tf_op jit(solution)/shard_map/cut/pallas_call | solution.py:328
  6.4 1.5 %collective-permute-start.5 = (f32[2,256,256]{2,1,0:T(8,128)S(1)}, f32[2,256,256]{2,1,0:T(8,128)S(1)}, u32[]{:S(2)}, u32[]{:S(2)}) collective-permute-start(f32[2,256,256]{2,1,0:T(8,128)S(1)} %get-tuple-element.36), channel_id=1, source_target_pairs={{0,4},{4,0},{8,12},{12,8},{1,5},{5,1},{9,13},{13,9},{2,6},{6,2},{1... | collective-permute-start | bytes 1572872 | tf_op jit(solution)/shard_map/ppermute | solution.py:46
  7.9 1.9 %cut.6 = f32[3,256,256]{2,1,0:T(8,128)S(1)} custom-call(s32[2,4]{1,0:T(2,128)S(1)} %bitcast.4, s32[2,4]{1,0:T(2,128)S(1)} %collective-permute-done.refs_1_, s32[2,4]{1,0:T(2,128)S(1)} %collective-permute-done.1.refs_2_, f32[1,256,4096]{2,1,0:T(8,128)} %refs_3_.12, f32[1,256,4096]{2,1,0:T(8,128)} %refs_4_.12, f32[4,256,256]{2,1,0:T(8,128)} %refs_4_.15), custom_call_target="tpu_custom_call" | custom-call | tf_op jit(solution)/shard_map/cut/pallas_call | solution.py:328
  10.0 0.7 collective-permute-start.7
  10.7 3.1 %collective-permute-start.6 = (f32[2,256,256]{2,1,0:T(8,128)S(1)}, f32[2,256,256]{2,1,0:T(8,128)S(1)}, u32[]{:S(2)}, u32[]{:S(2)}) collective-permute-start(f32[2,256,256]{2,1,0:T(8,128)S(1)} %get-tuple-element.45), channel_id=1, source_target_pairs={{12,14},{14,12},{13,15},{15,13},{28,30},{30,28},{29,31},{31,29}} | collective-permute-start | bytes 1572872 | tf_op jit(solution)/shard_map/ppermute | solution.py:53
  13.8 1.9 %cut.7.refs_5_ = f32[3,256,256]{2,1,0:T(8,128)S(1)} custom-call(s32[2,4]{1,0:T(2,128)S(1)} %bitcast.5, s32[2,4]{1,0:T(2,128)S(1)} %collective-permute-done.refs_1_, s32[2,4]{1,0:T(2,128)S(1)} %collective-permute-done.1.refs_2_, f32[1,256,4096]{2,1,0:T(8,128)} %refs_3_.12, f32[1,256,4096]{2,1,0:T(8,128)} %refs_4_.12, f32[4,256,256]{2,1,0:T(8,128)} %refs_4_.15), custom_call_target="tpu_custom_call" | custom-call | tf_op jit(solution)/shard_map/cut/pallas_call | solution.py:328
  15.7 2.2 %cut.8 = (f32[2,256,256]{2,1,0:T(8,128)S(1)}, f32[2,256,256]{2,1,0:T(8,128)S(1)}) custom-call(s32[2,4]{1,0:T(2,128)S(1)} %bitcast.6, s32[2,4]{1,0:T(2,128)S(1)} %collective-permute-done.refs_1_, s32[2,4]{1,0:T(2,128)S(1)} %collective-permute-done.1.refs_2_, f32[1,256,4096]{2,1,0:T(8,128)} %refs_3_.12, f32[1,256,4096]{2,1,0:T(8,128)} %refs_4_.12), custom_call_target="tpu_custom_call" | custom-call | tf_op jit(solution)/shard_map/cut/pallas_call | solution.py:328
  17.9 2.3 %cut.9 = (f32[2,256,256]{2,1,0:T(8,128)S(1)}, f32[2,256,256]{2,1,0:T(8,128)S(1)}) custom-call(s32[2,4]{1,0:T(2,128)S(1)} %bitcast.7, s32[2,4]{1,0:T(2,128)S(1)} %collective-permute-done.refs_1_, s32[2,4]{1,0:T(2,128)S(1)} %collective-permute-done.1.refs_2_, f32[1,256,4096]{2,1,0:T(8,128)} %refs_3_.12, f32[1,256,4096]{2,1,0:T(8,128)} %refs_4_.12), custom_call_target="tpu_custom_call" | custom-call | tf_op jit(solution)/shard_map/cut/pallas_call | solution.py:328
  20.3 0.7 join.2
  20.9 0.3 collective-permute-start.9
  21.3 0.7 collective-permute-start.10
  22.0 0.2 expand.1
  22.2 1.4 %collective-permute-done.6.refs_6_ = f32[2,256,256]{2,1,0:T(8,128)S(1)} collective-permute-done((f32[2,256,256]{2,1,0:T(8,128)S(1)}, f32[2,256,256]{2,1,0:T(8,128)S(1)}, u32[]{:S(2)}, u32[]{:S(2)}) %collective-permute-start.6) | collective-permute-done | bytes 524320 | tf_op jit(solution)/shard_map/ppermute | solution.py:53
  23.6 6.0 %collective-permute-start.2 = (s32[2,4]{1,0:T(2,128)S(1)}, s32[2,4]{1,0:T(2,128)S(1)}, u32[]{:S(2)}, u32[]{:S(2)}) collective-permute-start(s32[2,4]{1,0:T(2,128)S(1)} %bitcast.9), channel_id=1, source_target_pairs={{0,1},{1,0},{2,3},{3,2},{4,5},{5,4},{6,7},{7,6},{8,9},{9,8},{10,11... | collective-permute-start | bytes 104 | tf_op jit(solution)/shard_map/ppermute | solution.py:38
  29.6 0.7 join.3
  30.3 0.1 collective-permute-done.2.refs_3_
  30.4 0.4 collective-permute-start.3
  30.9 1.4 %collective-permute-start.11 = (f32[2,256,256]{2,1,0:T(8,128)S(1)}, f32[2,256,256]{2,1,0:T(8,128)S(1)}, u32[]{:S(2)}, u32[]{:S(2)}) collective-permute-start(f32[2,256,256]{2,1,0:T(8,128)S(1)} %join.3), channel_id=1, source_target_pairs={{0,2},{2,0},{1,3},{3,1},{4,6},{6,4},{5,7},{7,5},{8,10},{10,8},{9,1... | collective-permute-start | bytes 1572872 | tf_op jit(solution)/shard_map/ppermute | solution.py:38
  32.3 2.6 %collective-permute-done.8.refs_6_ = f32[3,256,256]{2,1,0:T(8,128)S(1)} collective-permute-done((f32[3,256,256]{2,1,0:T(8,128)S(1)}, f32[3,256,256]{2,1,0:T(8,128)S(1)}, u32[]{:S(2)}, u32[]{:S(2)}) %collective-permute-start.8) | collective-permute-done | bytes 786464 | tf_op jit(solution)/shard_map/ppermute | solution.py:46
  34.9 0.1 collective-permute-done.9.refs_7_
  35.0 6.7 %slot_0.1 = (f32[2,256,256]{2,1,0:T(8,128)S(1)}, f32[2,256,256]{2,1,0:T(8,128)S(1)}) custom-call(s32[2,4]{1,0:T(2,128)S(1)} %bitcast.11, s32[2,4]{1,0:T(2,128)S(1)} %collective-permute-done.refs_1_, s32[2,4]{1,0:T(2,128)S(1)} %collective-permute-done.1.refs_2_, f32[2,256,256]{2,1,0:T(8,128)S(1)} %copy-done, f32[4,256,256]{2,1,0:T(8,128)} %refs_4_.15, ...), custom_call_target="tpu_custom_call" | custom-call | tf_op jit(solution)/shard_map/slot_0/pallas_call | solution.py:260
  41.7 1.2 %collective-permute-start.12 = (f32[2,256,256]{2,1,0:T(8,128)S(1)}, f32[2,256,256]{2,1,0:T(8,128)S(1)}, u32[]{:S(2)}, u32[]{:S(2)}) collective-permute-start(f32[2,256,256]{2,1,0:T(8,128)S(1)} %get-tuple-element.56), channel_id=1, source_target_pairs={{0,2},{2,0},{1,3},{3,1},{4,6},{6,4},{5,7},{7,5},{8,10},{10,8},{9,1... | collective-permute-start | bytes 1572872 | tf_op jit(solution)/shard_map/ppermute | solution.py:38
  42.9 1.2 %collective-permute-start.13 = (f32[2,256,256]{2,1,0:T(8,128)S(1)}, f32[2,256,256]{2,1,0:T(8,128)S(1)}, u32[]{:S(2)}, u32[]{:S(2)}) collective-permute-start(f32[2,256,256]{2,1,0:T(8,128)S(1)} %get-tuple-element.51.refs_1_.refs_7_), channel_id=1, source_target_pairs={{0,4},{4,0},{8,12},{12,8},{1,5},{5,1},{9,13},{13,9},{2,6},{6,2},{1... | collective-permute-start | bytes 1572872 | tf_op jit(solution)/shard_map/ppermute | solution.py:46
  44.1 2.1 %collective-permute-done.11.refs_7_ = f32[2,256,256]{2,1,0:T(8,128)S(1)} collective-permute-done((f32[2,256,256]{2,1,0:T(8,128)S(1)}, f32[2,256,256]{2,1,0:T(8,128)S(1)}, u32[]{:S(2)}, u32[]{:S(2)}) %collective-permute-start.11) | collective-permute-done | bytes 524320 | tf_op jit(solution)/shard_map/ppermute | solution.py:38
  46.2 6.7 %slot_1.1 = (f32[2,256,256]{2,1,0:T(8,128)S(1)}, f32[2,256,256]{2,1,0:T(8,128)S(1)}) custom-call(s32[2,4]{1,0:T(2,128)S(1)} %bitcast.12, s32[2,4]{1,0:T(2,128)S(1)} %collective-permute-done.refs_1_, s32[2,4]{1,0:T(2,128)S(1)} %collective-permute-done.1.refs_2_, f32[2,256,256]{2,1,0:T(8,128)S(1)} %copy-done, f32[4,256,256]{2,1,0:T(8,128)} %refs_4_.15, ...), custom_call_target="tpu_custom_call" | custom-call | tf_op jit(solution)/shard_map/slot_1/pallas_call | solution.py:260
  52.9 0.7 collective-permute-start.16
  53.6 1.1 %collective-permute-start.15 = (f32[2,256,256]{2,1,0:T(8,128)S(1)}, f32[2,256,256]{2,1,0:T(8,128)S(1)}, u32[]{:S(2)}, u32[]{:S(2)}) collective-permute-start(f32[2,256,256]{2,1,0:T(8,128)S(1)} %get-tuple-element.57), channel_id=1, source_target_pairs={{0,2},{2,0},{1,3},{3,1},{4,6},{6,4},{5,7},{7,5},{8,10},{10,8},{9,1... | collective-permute-start | bytes 1572872 | tf_op jit(solution)/shard_map/ppermute | solution.py:38
  54.7 6.8 %slot_last.1 = (f32[2,256,256]{2,1,0:T(8,128)S(1)}, f32[2,256,256]{2,1,0:T(8,128)S(1)}) custom-call(s32[2,4]{1,0:T(2,128)S(1)} %bitcast.13, s32[2,4]{1,0:T(2,128)S(1)} %collective-permute-done.refs_1_, s32[2,4]{1,0:T(2,128)S(1)} %collective-permute-done.1.refs_2_, f32[2,256,256]{2,1,0:T(8,128)S(1)} %copy-done, f32[4,256,256]{2,1,0:T(8,128)} %refs_4_.15, ...), custom_call_target="tpu_custom_call" | custom-call | tf_op jit(solution)/shard_map/slot_last/pallas_call | solution.py:260
  61.6 0.1 pack.2
  61.7 6.6 %collective-permute-start.14 = (f32[4,2,256,256]{3,2,1,0:T(8,128)S(1)}, f32[4,2,256,256]{3,2,1,0:T(8,128)S(1)}, u32[]{:S(2)}, u32[]{:S(2)}) collective-permute-start(f32[4,2,256,256]{3,2,1,0:T(8,128)S(1)} %pack.2), channel_id=1, source_target_pairs={{0,1},{1,0},{2,3},{3,2},{4,5},{5,4},{6,7},{7,6},{8,9},{9,8},{10,11... | collective-permute-start | bytes 6291464 | tf_op jit(solution)/shard_map/ppermute | solution.py:38
  68.3 0.4 collective-permute-done.15.refs_1_.refs_12_
  68.8 3.2 %collective-permute-start.17 = (f32[3,2,256,256]{3,2,1,0:T(8,128)S(1)}, f32[3,2,256,256]{3,2,1,0:T(8,128)S(1)}, u32[]{:S(2)}, u32[]{:S(2)}) collective-permute-start(f32[3,2,256,256]{3,2,1,0:T(8,128)S(1)} %pack.3), channel_id=1, source_target_pairs={{0,1},{1,0},{2,3},{3,2},{4,5},{5,4},{6,7},{7,6},{8,9},{9,8},{10,11... | collective-permute-start | bytes 4718600 | tf_op jit(solution)/shard_map/ppermute | solution.py:38
  72.0 0.7 collective-permute-start.22
  72.7 0.2 collective-permute-start.20
  72.9 3.0 %collective-permute-start.18 = (f32[2,256,256]{2,1,0:T(8,128)S(1)}, f32[2,256,256]{2,1,0:T(8,128)S(1)}, u32[]{:S(2)}, u32[]{:S(2)}) collective-permute-start(f32[2,256,256]{2,1,0:T(8,128)S(1)} %get-tuple-element.60), channel_id=1, source_target_pairs={{12,14},{14,12},{13,15},{15,13},{28,30},{30,28},{29,31},{31,29}} | collective-permute-start | bytes 1572872 | tf_op jit(solution)/shard_map/ppermute | solution.py:53
  76.0 6.9 %early.1 = (f32[2,256,4096]{2,1,0:T(8,128)S(1)}, f32[2,1,256,4096]{3,2,1,0:T(8,128)}) custom-call(s32[2,4]{1,0:T(2,128)S(1)} %bitcast.14, s32[2,4]{1,0:T(2,128)S(1)} %collective-permute-done.refs_1_, s32[2,4]{1,0:T(2,128)S(1)} %collective-permute-done.1.refs_2_, s32[2,4]{1,0:T(2,128)S(1)} %collective-permute-done.2.refs_3_, ...), custom_call_target="tpu_custom_call" | custom-call | tf_op jit(solution)/shard_map/early/pallas_call | solution.py:433
  82.9 3.4 %collective-permute-done.20.refs_9_ = f32[2,256,256]{2,1,0:T(8,128)S(1)} collective-permute-done((f32[2,256,256]{2,1,0:T(8,128)S(1)}, f32[2,256,256]{2,1,0:T(8,128)S(1)}, u32[]{:S(2)}, u32[]{:S(2)}) %collective-permute-start.20) | collective-permute-done | bytes 524320 | tf_op jit(solution)/shard_map/ppermute | solution.py:46
  86.3 1.4 %collective-permute-done.18.refs_7_ = f32[2,256,256]{2,1,0:T(8,128)S(1)} collective-permute-done((f32[2,256,256]{2,1,0:T(8,128)S(1)}, f32[2,256,256]{2,1,0:T(8,128)S(1)}, u32[]{:S(2)}, u32[]{:S(2)}) %collective-permute-start.18) | collective-permute-done | bytes 524320 | tf_op jit(solution)/shard_map/ppermute | solution.py:53
  87.7 1.4 %collective-permute-start.19 = (f32[2,256,256]{2,1,0:T(8,128)S(1)}, f32[2,256,256]{2,1,0:T(8,128)S(1)}, u32[]{:S(2)}, u32[]{:S(2)}) collective-permute-start(f32[2,256,256]{2,1,0:T(8,128)S(1)} %collective-permute-done.18.refs_7_), channel_id=1, source_target_pairs={{0,1},{1,0},{2,3},{3,2},{4,5},{5,4},{6,7},{7,6},{8,9},{9,8},{10,11... | collective-permute-start | bytes 1572872 | tf_op jit(solution)/shard_map/ppermute | solution.py:38
  89.2 0.5 collective-permute-start.23
  89.7 1.0 %collective-permute-done.19.refs_8_ = f32[2,256,256]{2,1,0:T(8,128)S(1)} collective-permute-done((f32[2,256,256]{2,1,0:T(8,128)S(1)}, f32[2,256,256]{2,1,0:T(8,128)S(1)}, u32[]{:S(2)}, u32[]{:S(2)}) %collective-permute-start.19) | collective-permute-done | bytes 524320 | tf_op jit(solution)/shard_map/ppermute | solution.py:38
  90.7 0.7 collective-permute-done.21.refs_10_
  91.4 0.7 collective-permute-done.23.refs_12_
  92.2 3.3 %late.1 = f32[2,1,256,4096]{3,2,1,0:T(8,128)} custom-call(s32[2,4]{1,0:T(2,128)S(1)} %bitcast.15, s32[2,4]{1,0:T(2,128)S(1)} %collective-permute-done.refs_1_, s32[2,4]{1,0:T(2,128)S(1)} %collective-permute-done.1.refs_2_, s32[2,4]{1,0:T(2,128)S(1)} %collective-permute-done.2.refs_3_, ...), custom_call_target="tpu_custom_call", output_to_operand_aliasing={{}: (13, {})} | custom-call | tf_op jit(solution)/shard_map/late/pallas_call | solution.py:498
  (23 shorter events, 0.3 us)
Async XLA Ops:
  0.0 2.3 %collective-permute-start.1 = (s32[2,4]{1,0:T(2,128)}, s32[2,4]{1,0:T(2,128)S(1)}, u32[]{:S(2)}, u32[]{:S(2)}) collective-permute-start(s32[2,4]{1,0:T(2,128)} %bitcast.1), channel_id=1, source_target_pairs={{4,8},{8,4},{5,9},{9,5},{6,10},{10,6},{7,11},{11,7},{20,24},{24,20... | collective-permute-start | bytes 104 | tf_op jit(solution)/shard_map/ppermute | solution.py:46
  0.7 2.8 %collective-permute-start = (s32[2,4]{1,0:T(2,128)}, s32[2,4]{1,0:T(2,128)S(1)}, u32[]{:S(2)}, u32[]{:S(2)}) collective-permute-start(s32[2,4]{1,0:T(2,128)} %bitcast.2), channel_id=1, source_target_pairs={{0,4},{4,0},{8,12},{12,8},{1,5},{5,1},{9,13},{13,9},{2,6},{6,2},{1... | collective-permute-start | bytes 104 | tf_op jit(solution)/shard_map/ppermute | solution.py:46
  3.5 0.7 copy-start.2
  6.4 13.8 %collective-permute-start.5 = (f32[2,256,256]{2,1,0:T(8,128)S(1)}, f32[2,256,256]{2,1,0:T(8,128)S(1)}, u32[]{:S(2)}, u32[]{:S(2)}) collective-permute-start(f32[2,256,256]{2,1,0:T(8,128)S(1)} %get-tuple-element.36), channel_id=1, source_target_pairs={{0,4},{4,0},{8,12},{12,8},{1,5},{5,1},{9,13},{13,9},{2,6},{6,2},{1... | collective-permute-start | bytes 1572872 | tf_op jit(solution)/shard_map/ppermute | solution.py:46
  9.9 25.0 %collective-permute-start.8 = (f32[3,256,256]{2,1,0:T(8,128)S(1)}, f32[3,256,256]{2,1,0:T(8,128)S(1)}, u32[]{:S(2)}, u32[]{:S(2)}) collective-permute-start(f32[3,256,256]{2,1,0:T(8,128)S(1)} %cut.6), channel_id=1, source_target_pairs={{0,4},{4,0},{8,12},{12,8},{1,5},{5,1},{9,13},{13,9},{2,6},{6,2},{1... | collective-permute-start | bytes 2359304 | tf_op jit(solution)/shard_map/ppermute | solution.py:46
  10.0 19.7 %collective-permute-start.7 = (f32[2,256,256]{2,1,0:T(8,128)S(1)}, f32[2,256,256]{2,1,0:T(8,128)S(1)}, u32[]{:S(2)}, u32[]{:S(2)}) collective-permute-start(f32[2,256,256]{2,1,0:T(8,128)S(1)} %get-tuple-element.45), channel_id=1, source_target_pairs={{4,8},{8,4},{5,9},{9,5},{6,10},{10,6},{7,11},{11,7},{20,24},{24,20... | collective-permute-start | bytes 1572872 | tf_op jit(solution)/shard_map/ppermute | solution.py:46
  10.7 12.9 %collective-permute-start.6 = (f32[2,256,256]{2,1,0:T(8,128)S(1)}, f32[2,256,256]{2,1,0:T(8,128)S(1)}, u32[]{:S(2)}, u32[]{:S(2)}) collective-permute-start(f32[2,256,256]{2,1,0:T(8,128)S(1)} %get-tuple-element.45), channel_id=1, source_target_pairs={{12,14},{14,12},{13,15},{15,13},{28,30},{30,28},{29,31},{31,29}} | collective-permute-start | bytes 1572872 | tf_op jit(solution)/shard_map/ppermute | solution.py:53
  20.2 1.8 %copy-start.1 = (bf16[8,256,256]{2,1,0:T(8,128)(2,1)S(1)}, bf16[8,256,256]{2,1,0:T(8,128)(2,1)}, u32[]{:S(2)}) copy-start(bf16[8,256,256]{2,1,0:T(8,128)(2,1)} %constant.2.clone.pieces) | copy-start | bytes 3145732
  20.2 14.8 %copy-start = (f32[2,256,256]{2,1,0:T(8,128)S(1)}, f32[2,256,256]{2,1,0:T(8,128)}, u32[]{:S(2)}) copy-start(f32[2,256,256]{2,1,0:T(8,128)} %refs_3_.15) | copy-start | bytes 1572868
  20.3 14.8 %copy-start.3 = (s32[4,2]{0,1:T(2,128)S(1)}, s32[4,2]{0,1:T(2,128)}, u32[]{:S(2)}) copy-start(s32[4,2]{0,1:T(2,128)} %param.10) | copy-start | bytes 100
  20.9 14.1 %collective-permute-start.9 = (f32[2,256,256]{2,1,0:T(8,128)S(1)}, f32[2,256,256]{2,1,0:T(8,128)S(1)}, u32[]{:S(2)}, u32[]{:S(2)}) collective-permute-start(f32[2,256,256]{2,1,0:T(8,128)S(1)} %join.2), channel_id=1, source_target_pairs={{0,2},{2,0},{1,3},{3,1},{4,6},{6,4},{5,7},{7,5},{8,10},{10,8},{9,1... | collective-permute-start | bytes 1572872 | tf_op jit(solution)/shard_map/ppermute | solution.py:38
  21.3 22.8 %collective-permute-start.10 = (f32[3,256,256]{2,1,0:T(8,128)S(1)}, f32[3,256,256]{2,1,0:T(8,128)S(1)}, u32[]{:S(2)}, u32[]{:S(2)}) collective-permute-start(f32[3,256,256]{2,1,0:T(8,128)S(1)} %cut.7.refs_5_), channel_id=1, source_target_pairs={{4,8},{8,4},{5,9},{9,5},{6,10},{10,6},{7,11},{11,7},{20,24},{24,20... | collective-permute-start | bytes 2359304 | tf_op jit(solution)/shard_map/ppermute | solution.py:46
  23.6 6.9 %collective-permute-start.2 = (s32[2,4]{1,0:T(2,128)S(1)}, s32[2,4]{1,0:T(2,128)S(1)}, u32[]{:S(2)}, u32[]{:S(2)}) collective-permute-start(s32[2,4]{1,0:T(2,128)S(1)} %bitcast.9), channel_id=1, source_target_pairs={{0,1},{1,0},{2,3},{3,2},{4,5},{5,4},{6,7},{7,6},{8,9},{9,8},{10,11... | collective-permute-start | bytes 104 | tf_op jit(solution)/shard_map/ppermute | solution.py:38
  29.6 1.3 %collective-permute-start.4 = (s32[2,4]{1,0:T(2,128)S(1)}, s32[2,4]{1,0:T(2,128)S(1)}, u32[]{:S(2)}, u32[]{:S(2)}) collective-permute-start(s32[2,4]{1,0:T(2,128)S(1)} %collective-permute-done.1.refs_2_), channel_id=1, source_target_pairs={{0,1},{1,0},{2,3},{3,2},{4,5},{5,4},{6,7},{7,6},{8,9},{9,8},{10,11... | collective-permute-start | bytes 104 | tf_op jit(solution)/shard_map/ppermute | solution.py:38
  30.4 1.8 %collective-permute-start.3 = (s32[2,4]{1,0:T(2,128)S(1)}, s32[2,4]{1,0:T(2,128)S(1)}, u32[]{:S(2)}, u32[]{:S(2)}) collective-permute-start(s32[2,4]{1,0:T(2,128)S(1)} %collective-permute-done.refs_1_), channel_id=1, source_target_pairs={{0,1},{1,0},{2,3},{3,2},{4,5},{5,4},{6,7},{7,6},{8,9},{9,8},{10,11... | collective-permute-start | bytes 104 | tf_op jit(solution)/shard_map/ppermute | solution.py:38
  30.9 15.4 %collective-permute-start.11 = (f32[2,256,256]{2,1,0:T(8,128)S(1)}, f32[2,256,256]{2,1,0:T(8,128)S(1)}, u32[]{:S(2)}, u32[]{:S(2)}) collective-permute-start(f32[2,256,256]{2,1,0:T(8,128)S(1)} %join.3), channel_id=1, source_target_pairs={{0,2},{2,0},{1,3},{3,1},{4,6},{6,4},{5,7},{7,5},{8,10},{10,8},{9,1... | collective-permute-start | bytes 1572872 | tf_op jit(solution)/shard_map/ppermute | solution.py:38
  41.7 19.9 %collective-permute-start.12 = (f32[2,256,256]{2,1,0:T(8,128)S(1)}, f32[2,256,256]{2,1,0:T(8,128)S(1)}, u32[]{:S(2)}, u32[]{:S(2)}) collective-permute-start(f32[2,256,256]{2,1,0:T(8,128)S(1)} %get-tuple-element.56), channel_id=1, source_target_pairs={{0,2},{2,0},{1,3},{3,1},{4,6},{6,4},{5,7},{7,5},{8,10},{10,8},{9,1... | collective-permute-start | bytes 1572872 | tf_op jit(solution)/shard_map/ppermute | solution.py:38
  42.9 18.7 %collective-permute-start.13 = (f32[2,256,256]{2,1,0:T(8,128)S(1)}, f32[2,256,256]{2,1,0:T(8,128)S(1)}, u32[]{:S(2)}, u32[]{:S(2)}) collective-permute-start(f32[2,256,256]{2,1,0:T(8,128)S(1)} %get-tuple-element.51.refs_1_.refs_7_), channel_id=1, source_target_pairs={{0,4},{4,0},{8,12},{12,8},{1,5},{5,1},{9,13},{13,9},{2,6},{6,2},{1... | collective-permute-start | bytes 1572872 | tf_op jit(solution)/shard_map/ppermute | solution.py:46
  52.9 15.8 %collective-permute-start.16 = (f32[2,256,256]{2,1,0:T(8,128)S(1)}, f32[2,256,256]{2,1,0:T(8,128)S(1)}, u32[]{:S(2)}, u32[]{:S(2)}) collective-permute-start(f32[2,256,256]{2,1,0:T(8,128)S(1)} %get-tuple-element.53.refs_0_.refs_11_), channel_id=1, source_target_pairs={{4,8},{8,4},{5,9},{9,5},{6,10},{10,6},{7,11},{11,7},{20,24},{24,20... | collective-permute-start | bytes 1572872 | tf_op jit(solution)/shard_map/ppermute | solution.py:46
  53.6 15.1 %collective-permute-start.15 = (f32[2,256,256]{2,1,0:T(8,128)S(1)}, f32[2,256,256]{2,1,0:T(8,128)S(1)}, u32[]{:S(2)}, u32[]{:S(2)}) collective-permute-start(f32[2,256,256]{2,1,0:T(8,128)S(1)} %get-tuple-element.57), channel_id=1, source_target_pairs={{0,2},{2,0},{1,3},{3,1},{4,6},{6,4},{5,7},{7,5},{8,10},{10,8},{9,1... | collective-permute-start | bytes 1572872 | tf_op jit(solution)/shard_map/ppermute | solution.py:38
  61.7 14.2 %collective-permute-start.14 = (f32[4,2,256,256]{3,2,1,0:T(8,128)S(1)}, f32[4,2,256,256]{3,2,1,0:T(8,128)S(1)}, u32[]{:S(2)}, u32[]{:S(2)}) collective-permute-start(f32[4,2,256,256]{3,2,1,0:T(8,128)S(1)} %pack.2), channel_id=1, source_target_pairs={{0,1},{1,0},{2,3},{3,2},{4,5},{5,4},{6,7},{7,6},{8,9},{9,8},{10,11... | collective-permute-start | bytes 6291464 | tf_op jit(solution)/shard_map/ppermute | solution.py:38
  68.8 7.1 %collective-permute-start.17 = (f32[3,2,256,256]{3,2,1,0:T(8,128)S(1)}, f32[3,2,256,256]{3,2,1,0:T(8,128)S(1)}, u32[]{:S(2)}, u32[]{:S(2)}) collective-permute-start(f32[3,2,256,256]{3,2,1,0:T(8,128)S(1)} %pack.3), channel_id=1, source_target_pairs={{0,1},{1,0},{2,3},{3,2},{4,5},{5,4},{6,7},{7,6},{8,9},{9,8},{10,11... | collective-permute-start | bytes 4718600 | tf_op jit(solution)/shard_map/ppermute | solution.py:38
  72.0 10.9 %collective-permute-start.22 = (f32[2,256,256]{2,1,0:T(8,128)S(1)}, f32[2,256,256]{2,1,0:T(8,128)S(1)}, u32[]{:S(2)}, u32[]{:S(2)}) collective-permute-start(f32[2,256,256]{2,1,0:T(8,128)S(1)} %collective-permute-done.15.refs_1_.refs_12_), channel_id=1, source_target_pairs={{4,8},{8,4},{5,9},{9,5},{6,10},{10,6},{7,11},{11,7},{20,24},{24,20... | collective-permute-start | bytes 1572872 | tf_op jit(solution)/shard_map/ppermute | solution.py:46
  72.7 13.6 %collective-permute-start.20 = (f32[2,256,256]{2,1,0:T(8,128)S(1)}, f32[2,256,256]{2,1,0:T(8,128)S(1)}, u32[]{:S(2)}, u32[]{:S(2)}) collective-permute-start(f32[2,256,256]{2,1,0:T(8,128)S(1)} %collective-permute-done.12.refs_2_.refs_8_), channel_id=1, source_target_pairs={{0,4},{4,0},{8,12},{12,8},{1,5},{5,1},{9,13},{13,9},{2,6},{6,2},{1... | collective-permute-start | bytes 1572872 | tf_op jit(solution)/shard_map/ppermute | solution.py:46
  72.9 14.8 %collective-permute-start.18 = (f32[2,256,256]{2,1,0:T(8,128)S(1)}, f32[2,256,256]{2,1,0:T(8,128)S(1)}, u32[]{:S(2)}, u32[]{:S(2)}) collective-permute-start(f32[2,256,256]{2,1,0:T(8,128)S(1)} %get-tuple-element.60), channel_id=1, source_target_pairs={{12,14},{14,12},{13,15},{15,13},{28,30},{30,28},{29,31},{31,29}} | collective-permute-start | bytes 1572872 | tf_op jit(solution)/shard_map/ppermute | solution.py:53
  87.7 3.0 %collective-permute-start.19 = (f32[2,256,256]{2,1,0:T(8,128)S(1)}, f32[2,256,256]{2,1,0:T(8,128)S(1)}, u32[]{:S(2)}, u32[]{:S(2)}) collective-permute-start(f32[2,256,256]{2,1,0:T(8,128)S(1)} %collective-permute-done.18.refs_7_), channel_id=1, source_target_pairs={{0,1},{1,0},{2,3},{3,2},{4,5},{5,4},{6,7},{7,6},{8,9},{9,8},{10,11... | collective-permute-start | bytes 1572872 | tf_op jit(solution)/shard_map/ppermute | solution.py:38
  89.2 2.3 %collective-permute-start.21 = (f32[2,256,256]{2,1,0:T(8,128)S(1)}, f32[2,256,256]{2,1,0:T(8,128)S(1)}, u32[]{:S(2)}, u32[]{:S(2)}) collective-permute-start(f32[2,256,256]{2,1,0:T(8,128)S(1)} %collective-permute-done.20.refs_9_), channel_id=1, source_target_pairs={{0,1},{1,0},{2,3},{3,2},{4,5},{5,4},{6,7},{7,6},{8,9},{9,8},{10,11... | collective-permute-start | bytes 1572872 | tf_op jit(solution)/shard_map/ppermute | solution.py:38
  89.2 3.0 %collective-permute-start.23 = (f32[2,256,256]{2,1,0:T(8,128)S(1)}, f32[2,256,256]{2,1,0:T(8,128)S(1)}, u32[]{:S(2)}, u32[]{:S(2)}) collective-permute-start(f32[2,256,256]{2,1,0:T(8,128)S(1)} %collective-permute-done.22.refs_11_), channel_id=1, source_target_pairs={{0,1},{1,0},{2,3},{3,2},{4,5},{5,4},{6,7},{7,6},{8,9},{9,8},{10,11... | collective-permute-start | bytes 1572872 | tf_op jit(solution)/shard_map/ppermute | solution.py:38

commit v11 on v10

--- a/solution.py
+++ b/solution.py
@@ -51,6 +51,12 @@
     base = (tiles - 1) * size
     route = [(base + i, base + (i + distance) % size) for i in range(size)]
     return lax.ppermute(block, ("tile", "slab"), route)
+
+
+def twin_last(block):
+    tiles = lax.axis_size("tile")
+    base = (tiles - 1) * 2
+    return lax.ppermute(block, ("tile", "batch"), [(base, base + 1), (base + 1, base)])
 
 
 def halves(matrix):
@@ -446,7 +452,7 @@
 
 def late_kernel(metas, layout, *refs):
     width = len(refs) - 5 - len(metas)
-    tables, total, terms = refs[:width], refs[width], refs[width + 1 : -4]
+    tables, terms = refs[:width], refs[width + 1 : -4]
     out, stage, sems = refs[-3:]
     side = terms[0].shape[-1]
     blocks = out.shape[-1] // side
@@ -472,7 +478,6 @@
         @pl.when(touched(block))
         def _():
             where = place(block)
-            stage[:, :, where] = total[:, :, where]
             for k, (first, col, low, high) in enumerate(ranges):
                 for half in range(2):
 
@@ -498,16 +503,16 @@
     return pl.pallas_call(
         lambda *refs: late_kernel(metas, layout, *refs),
         in_specs=[SMEM] * len(tables) + [VMEM] * (1 + len(terms)) + [HBM],
-        out_specs=HBM,
-        input_output_aliases={len(tables) + 1 + len(terms): 0},
-        out_shape=jax.ShapeDtypeStruct((2, 1, side, cols_total), jnp.float32),
-        scratch_shapes=[
-            pltpu.VMEM((2, side, cols_total), jnp.float32),
-            pltpu.SemaphoreType.DMA((cols_total // side,)),
+        out_specs=[HBM, VMEM],
+        input_output_aliases={len(tables) + 1 + len(terms): 0, len(tables): 1},
+        out_shape=[
+            jax.ShapeDtypeStruct((2, 1, side, cols_total), jnp.float32),
+            jax.ShapeDtypeStruct((2, side, cols_total), jnp.float32),
         ],
-        compiler_params=params(28),
+        scratch_shapes=[pltpu.SemaphoreType.DMA((cols_total // side,))],
+        compiler_params=params(20),
         name="late",
-    )(*tables, total, *terms, copied)
+    )(*tables, total, *terms, copied)[0]
 
 
 def local(phase, absorption, probe, measured, offsets):
@@ -553,24 +558,31 @@
         done[:] = [out[0] if isinstance(out, (list, tuple)) else out]
         return out
 
-    spots = [("send", rounds[i][2], rounds[i][0], d) for i in range(count) for d in far]
-    pieces = step(lambda p: cut(spots, layout, p, phase, absorption)) if spots else []
-    sent, got = [], []
+    sent, got, early_pieces = [], [], []
     for i, (k, role, send_role, there, home) in enumerate(rounds):
-        sent.append([None, *pieces[i * len(far) : (i + 1) * len(far)]])
-        got.append([None] + [there(piece) for piece in sent[i][1:]])
+        spots = [("send", send_role, k, d) for d in far]
+        if i == 0:
+            spots += [("last", "lo", n, d) for n in sorted(last_round) for d in far]
+        pieces = step(lambda p: cut(spots, layout, p, phase, absorption)) if far else []
+        if i == 0:
+            pieces, early_pieces = pieces[: len(far)], pieces[len(far) :]
+        sent.append([None, *pieces])
+        got.append([None] + [there(piece) for piece in pieces])
     for i, (k, role, send_role, there, home) in enumerate(rounds):
         extra_input = [] if role == "lo" else [measured]
         spots = [("send", send_role, k, 0)]
         sent[i][0] = step(lambda p: cut(spots, layout, p, phase, absorption, *extra_input))[0]
         got[i][0] = there(sent[i][0])
     ends = sorted(last_round)
-    extra = [[rotate_last(sent[last_round[k]][d], d) for d in far] for k in ends]
+    extra = [
+        [rotate_last(early_pieces[n * len(far) + d - 1], d) for d in far] for n in range(len(ends))
+    ]
     held = []
     for k, role, send_role, there, home in rounds:
         spots = [("slot", role, k, d) for d in distances]
         held.append(step(lambda p: cut(spots, layout, p, phase, absorption)))
     constants = expand(side)
+    done += [value for row in extra for value in row]
     others = []
     for i, (k, role, send_role, there, home) in enumerate(rounds):
         joined = []
@@ -578,8 +590,6 @@
             spot = ("slot", role, k, d)
             joined.append(step(lambda p: join(spot, layout, p, held[i][d], got[i][d])))
         others.append([rotate(joined[d - 1], "slab", d) for d in far])
-        if i == 0:
-            done += [value for row in extra for value in row]
 
     twin_tables = [rotate(table, "batch", 1) for table in tables]
     done += twin_tables
@@ -626,7 +636,8 @@
     total, copied = early(kinds, layout, tables + twin_tables, terms, cols_total)
     values = []
     for value, spot in final:
-        values += [value, rotate(after(value, total), "batch", 1)]
+        gated = after(value, total)
+        values += [value, twin_last(gated) if spot[0] == "last" else rotate(gated, "batch", 1)]
         final_kinds += [(0, spot), (1, spot)]
     return late(final_kinds, layout, tables + twin_tables, total, copied, values)
 

time: 96.2 us -> 101 us (1.050)
  waiting for transfers between devices: 15.3 us -> 18 us
  Pallas kernels: 42.7 us -> 44.4 us
    ppermute x12 -> x11, starting transfers between devices: 22.2 us -> 16.8 us  [rotate(): lax.ppermute(block, axis, [(i, (i + distance) % size) for i in range(size)])]
    ppermute x0 -> x1, starting transfers between devices: none -> 3.35 us  [twin_last(): lax.ppermute(block, ('tile', 'batch'), [(base, base + 1), (base + 1, base)])]
    ppermute x10, waiting for transfers between devices: 7.16 us -> 10.4 us  [swap(): return lax.ppermute(block, axis, route)]
    ppermute x10, starting transfers between devices: 8.11 us -> 11 us  [swap(): return lax.ppermute(block, axis, route)]
    pallas_call x5 -> x6, Pallas kernels: 10.6 us -> 12.4 us  [cut(): pl.pallas_call(lambda *refs: cut_kernel(spots, layout, measured is not No...]
    ppermute x12 -> x11, waiting for transfers between devices: 5.4 us -> 4.03 us  [rotate(): lax.ppermute(block, axis, [(i, (i + distance) % size) for i in range(size)])]
  transfers between devices with their start and end apart: 24 -> 24, of which waited for: 12 -> 8; matrix products, arithmetic and copies ran while one was open for 0% -> 0% of each run, Pallas kernels for 39% -> 39%
where the time goes in v11:
time: 101 us; the launch traced here: 100 us
  Pallas kernels  44.4 us (44%)
  starting transfers between devices  36.5 us (36%)
  waiting for transfers between devices  18 us (18%)
    pallas_call x3, Pallas kernels, run_slot(): pl.pallas_call(lambda *refs: slot_kernel(kind, spot, layout, len(tables),...  20.2 us
    ppermute x11, starting transfers between devices, rotate(): lax.ppermute(block, axis, [(i, (i + distance) % size) for i in range(size)])  16.8 us
    pallas_call x6, Pallas kernels, cut(): pl.pallas_call(lambda *refs: cut_kernel(spots, layout, measured is not No...  12.4 us
    ppermute x10, starting transfers between devices, swap(): return lax.ppermute(block, axis, route)  11 us
    ppermute x10, waiting for transfers between devices, swap(): return lax.ppermute(block, axis, route)  10.4 us
    pallas_call x1, Pallas kernels, early(): pl.pallas_call(lambda *refs: early_kernel(metas, layout, *refs), in_specs...  6.94 us
    ppermute x2, starting transfers between devices, rotate_last(): return lax.ppermute(block, ('tile', 'slab'), route)  5.42 us
    ppermute x11, waiting for transfers between devices, rotate(): lax.ppermute(block, axis, [(i, (i + distance) % size) for i in range(size)])  4.03 us
  transfers between devices with their start and end apart: 24, of which 8 were waited for; matrix products, arithmetic and copies ran while one was open for 0% of the time, Pallas kernels for 39%

profile of v11, /device:TPU:29, one launch (start us, length us, event | category | flops | bytes accessed | tf_op | source)
XLA Modules:
  0.0 100.1 jit_solution(13883269823034016445)
XLA Ops:
  0.0 0.6 collective-permute-start.1
  0.7 1.7 %collective-permute-start = (s32[2,4]{1,0:T(2,128)}, s32[2,4]{1,0:T(2,128)S(1)}, u32[]{:S(2)}, u32[]{:S(2)}) collective-permute-start(s32[2,4]{1,0:T(2,128)} %bitcast.2), channel_id=1, source_target_pairs={{0,4},{4,0},{8,12},{12,8},{1,5},{5,1},{9,13},{13,9},{2,6},{6,2},{1... | collective-permute-start | bytes 104 | tf_op jit(solution)/shard_map/ppermute | solution.py:46
  2.3 1.2 %collective-permute-done.refs_1_ = s32[2,4]{1,0:T(2,128)S(1)} collective-permute-done((s32[2,4]{1,0:T(2,128)}, s32[2,4]{1,0:T(2,128)S(1)}, u32[]{:S(2)}, u32[]{:S(2)}) %collective-permute-start) | collective-permute-done | bytes 64 | tf_op jit(solution)/shard_map/ppermute | solution.py:46
  3.5 0.7 copy-done.2
  4.2 2.2 %cut.6 = (f32[2,256,256]{2,1,0:T(8,128)S(1)}, f32[2,256,256]{2,1,0:T(8,128)S(1)}) custom-call(s32[2,4]{1,0:T(2,128)S(1)} %bitcast.3, s32[2,4]{1,0:T(2,128)S(1)} %collective-permute-done.refs_1_, s32[2,4]{1,0:T(2,128)S(1)} %collective-permute-done.1.refs_2_, f32[1,256,4096]{2,1,0:T(8,128)} %refs_3_.14, f32[1,256,4096]{2,1,0:T(8,128)} %refs_4_.14), custom_call_target="tpu_custom_call" | custom-call | tf_op jit(solution)/shard_map/cut/pallas_call | solution.py:334
  6.4 3.1 %collective-permute-start.5 = (f32[2,256,256]{2,1,0:T(8,128)S(1)}, f32[2,256,256]{2,1,0:T(8,128)S(1)}, u32[]{:S(2)}, u32[]{:S(2)}) collective-permute-start(f32[2,256,256]{2,1,0:T(8,128)S(1)} %get-tuple-element.46), channel_id=1, source_target_pairs={{12,14},{14,12},{13,15},{15,13},{28,30},{30,28},{29,31},{31,29}} | collective-permute-start | bytes 1572872 | tf_op jit(solution)/shard_map/ppermute | solution.py:53
  9.6 1.9 %cut.7 = f32[2,256,256]{2,1,0:T(8,128)S(1)} custom-call(s32[2,4]{1,0:T(2,128)S(1)} %bitcast.4, s32[2,4]{1,0:T(2,128)S(1)} %collective-permute-done.refs_1_, s32[2,4]{1,0:T(2,128)S(1)} %collective-permute-done.1.refs_2_, f32[1,256,4096]{2,1,0:T(8,128)} %refs_3_.14, f32[1,256,4096]{2,1,0:T(8,128)} %refs_4_.14), custom_call_target="tpu_custom_call" | custom-call | tf_op jit(solution)/shard_map/cut/pallas_call | solution.py:334
  11.5 1.9 %cut.8 = f32[3,256,256]{2,1,0:T(8,128)S(1)} custom-call(s32[2,4]{1,0:T(2,128)S(1)} %bitcast.5, s32[2,4]{1,0:T(2,128)S(1)} %collective-permute-done.refs_1_, s32[2,4]{1,0:T(2,128)S(1)} %collective-permute-done.1.refs_2_, f32[1,256,4096]{2,1,0:T(8,128)} %refs_3_.14, f32[1,256,4096]{2,1,0:T(8,128)} %refs_4_.14, f32[4,256,256]{2,1,0:T(8,128)} %refs_4_.17), custom_call_target="tpu_custom_call" | custom-call | tf_op jit(solution)/shard_map/cut/pallas_call | solution.py:334
  13.4 1.5 %collective-permute-start.8 = (f32[3,256,256]{2,1,0:T(8,128)S(1)}, f32[3,256,256]{2,1,0:T(8,128)S(1)}, u32[]{:S(2)}, u32[]{:S(2)}) collective-permute-start(f32[3,256,256]{2,1,0:T(8,128)S(1)} %cut.8), channel_id=1, source_target_pairs={{0,4},{4,0},{8,12},{12,8},{1,5},{5,1},{9,13},{13,9},{2,6},{6,2},{1... | collective-permute-start | bytes 2359304 | tf_op jit(solution)/shard_map/ppermute | solution.py:46
  14.9 0.7 collective-permute-start.7
  15.6 1.9 %cut.9.refs_5_ = f32[3,256,256]{2,1,0:T(8,128)S(1)} custom-call(s32[2,4]{1,0:T(2,128)S(1)} %bitcast.6, s32[2,4]{1,0:T(2,128)S(1)} %collective-permute-done.refs_1_, s32[2,4]{1,0:T(2,128)S(1)} %collective-permute-done.1.refs_2_, f32[1,256,4096]{2,1,0:T(8,128)} %refs_3_.14, f32[1,256,4096]{2,1,0:T(8,128)} %refs_4_.14, f32[4,256,256]{2,1,0:T(8,128)} %refs_4_.17), custom_call_target="tpu_custom_call" | custom-call | tf_op jit(solution)/shard_map/cut/pallas_call | solution.py:334
  17.6 2.2 %cut.10 = (f32[2,256,256]{2,1,0:T(8,128)S(1)}, f32[2,256,256]{2,1,0:T(8,128)S(1)}) custom-call(s32[2,4]{1,0:T(2,128)S(1)} %bitcast.7, s32[2,4]{1,0:T(2,128)S(1)} %collective-permute-done.refs_1_, s32[2,4]{1,0:T(2,128)S(1)} %collective-permute-done.1.refs_2_, f32[1,256,4096]{2,1,0:T(8,128)} %refs_3_.14, f32[1,256,4096]{2,1,0:T(8,128)} %refs_4_.14), custom_call_target="tpu_custom_call" | custom-call | tf_op jit(solution)/shard_map/cut/pallas_call | solution.py:334
  19.8 2.2 %cut.11 = (f32[2,256,256]{2,1,0:T(8,128)S(1)}, f32[2,256,256]{2,1,0:T(8,128)S(1)}) custom-call(s32[2,4]{1,0:T(2,128)S(1)} %bitcast.8, s32[2,4]{1,0:T(2,128)S(1)} %collective-permute-done.refs_1_, s32[2,4]{1,0:T(2,128)S(1)} %collective-permute-done.1.refs_2_, f32[1,256,4096]{2,1,0:T(8,128)} %refs_3_.14, f32[1,256,4096]{2,1,0:T(8,128)} %refs_4_.14), custom_call_target="tpu_custom_call" | custom-call | tf_op jit(solution)/shard_map/cut/pallas_call | solution.py:334
  22.1 0.7 join.2
  22.7 0.3 collective-permute-start.9
  23.1 0.7 collective-permute-start.10
  23.8 4.8 %collective-permute-start.2 = (s32[2,4]{1,0:T(2,128)S(1)}, s32[2,4]{1,0:T(2,128)S(1)}, u32[]{:S(2)}, u32[]{:S(2)}) collective-permute-start(s32[2,4]{1,0:T(2,128)S(1)} %bitcast.10), channel_id=1, source_target_pairs={{0,1},{1,0},{2,3},{3,2},{4,5},{5,4},{6,7},{7,6},{8,9},{9,8},{10,11... | collective-permute-start | bytes 104 | tf_op jit(solution)/shard_map/ppermute | solution.py:38
  28.6 0.2 expand.1
  28.8 0.1 collective-permute-start.4
  28.9 0.7 join.3
  29.6 0.5 collective-permute-start.3
  30.1 1.2 %collective-permute-start.11 = (f32[2,256,256]{2,1,0:T(8,128)S(1)}, f32[2,256,256]{2,1,0:T(8,128)S(1)}, u32[]{:S(2)}, u32[]{:S(2)}) collective-permute-start(f32[2,256,256]{2,1,0:T(8,128)S(1)} %join.3), channel_id=1, source_target_pairs={{0,2},{2,0},{1,3},{3,1},{4,6},{6,4},{5,7},{7,5},{8,10},{10,8},{9,1... | collective-permute-start | bytes 1572872 | tf_op jit(solution)/shard_map/ppermute | solution.py:38
  31.3 6.4 %collective-permute-done.8.refs_6_ = f32[3,256,256]{2,1,0:T(8,128)S(1)} collective-permute-done((f32[3,256,256]{2,1,0:T(8,128)S(1)}, f32[3,256,256]{2,1,0:T(8,128)S(1)}, u32[]{:S(2)}, u32[]{:S(2)}) %collective-permute-start.8) | collective-permute-done | bytes 786464 | tf_op jit(solution)/shard_map/ppermute | solution.py:46
  37.8 6.7 %slot_0.1 = (f32[2,256,256]{2,1,0:T(8,128)S(1)}, f32[2,256,256]{2,1,0:T(8,128)S(1)}) custom-call(s32[2,4]{1,0:T(2,128)S(1)} %bitcast.12, s32[2,4]{1,0:T(2,128)S(1)} %collective-permute-done.refs_1_, s32[2,4]{1,0:T(2,128)S(1)} %collective-permute-done.1.refs_2_, f32[2,256,256]{2,1,0:T(8,128)S(1)} %copy-done, f32[4,256,256]{2,1,0:T(8,128)} %refs_4_.17, ...), custom_call_target="tpu_custom_call" | custom-call | tf_op jit(solution)/shard_map/slot_0/pallas_call | solution.py:266
  44.5 0.4 collective-permute-start.12
  44.8 0.3 collective-permute-start.13
  45.2 6.7 %slot_1.1 = (f32[2,256,256]{2,1,0:T(8,128)S(1)}, f32[2,256,256]{2,1,0:T(8,128)S(1)}) custom-call(s32[2,4]{1,0:T(2,128)S(1)} %bitcast.13, s32[2,4]{1,0:T(2,128)S(1)} %collective-permute-done.refs_1_, s32[2,4]{1,0:T(2,128)S(1)} %collective-permute-done.1.refs_2_, f32[2,256,256]{2,1,0:T(8,128)S(1)} %copy-done, f32[4,256,256]{2,1,0:T(8,128)} %refs_4_.17, ...), custom_call_target="tpu_custom_call" | custom-call | tf_op jit(solution)/shard_map/slot_1/pallas_call | solution.py:266
  51.8 0.7 collective-permute-start.16
  52.5 1.2 %collective-permute-start.15 = (f32[2,256,256]{2,1,0:T(8,128)S(1)}, f32[2,256,256]{2,1,0:T(8,128)S(1)}, u32[]{:S(2)}, u32[]{:S(2)}) collective-permute-start(f32[2,256,256]{2,1,0:T(8,128)S(1)} %get-tuple-element.60), channel_id=1, source_target_pairs={{0,2},{2,0},{1,3},{3,1},{4,6},{6,4},{5,7},{7,5},{8,10},{10,8},{9,1... | collective-permute-start | bytes 1572872 | tf_op jit(solution)/shard_map/ppermute | solution.py:38
  53.8 6.8 %slot_last.1 = (f32[2,256,256]{2,1,0:T(8,128)S(1)}, f32[2,256,256]{2,1,0:T(8,128)S(1)}) custom-call(s32[2,4]{1,0:T(2,128)S(1)} %bitcast.14, s32[2,4]{1,0:T(2,128)S(1)} %collective-permute-done.refs_1_, s32[2,4]{1,0:T(2,128)S(1)} %collective-permute-done.1.refs_2_, f32[2,256,256]{2,1,0:T(8,128)S(1)} %copy-done, f32[4,256,256]{2,1,0:T(8,128)} %refs_4_.17, ...), custom_call_target="tpu_custom_call" | custom-call | tf_op jit(solution)/shard_map/slot_last/pallas_call | solution.py:266
  60.6 0.1 pack.2
  60.7 4.2 %collective-permute-start.14 = (f32[4,2,256,256]{3,2,1,0:T(8,128)S(1)}, f32[4,2,256,256]{3,2,1,0:T(8,128)S(1)}, u32[]{:S(2)}, u32[]{:S(2)}) collective-permute-start(f32[4,2,256,256]{3,2,1,0:T(8,128)S(1)} %pack.2), channel_id=1, source_target_pairs={{0,1},{1,0},{2,3},{3,2},{4,5},{5,4},{6,7},{7,6},{8,9},{9,8},{10,11... | collective-permute-start | bytes 6291464 | tf_op jit(solution)/shard_map/ppermute | solution.py:38
  65.0 2.5 %collective-permute-done.15.refs_1_.refs_12_ = f32[2,256,256]{2,1,0:T(8,128)S(1)} collective-permute-done((f32[2,256,256]{2,1,0:T(8,128)S(1)}, f32[2,256,256]{2,1,0:T(8,128)S(1)}, u32[]{:S(2)}, u32[]{:S(2)}) %collective-permute-start.15) | collective-permute-done | bytes 524320 | tf_op jit(solution)/shard_map/ppermute | solution.py:38
  67.5 0.1 pack.3
  67.6 3.4 %collective-permute-start.17 = (f32[3,2,256,256]{3,2,1,0:T(8,128)S(1)}, f32[3,2,256,256]{3,2,1,0:T(8,128)S(1)}, u32[]{:S(2)}, u32[]{:S(2)}) collective-permute-start(f32[3,2,256,256]{3,2,1,0:T(8,128)S(1)} %pack.3), channel_id=1, source_target_pairs={{0,1},{1,0},{2,3},{3,2},{4,5},{5,4},{6,7},{7,6},{8,9},{9,8},{10,11... | collective-permute-start | bytes 4718600 | tf_op jit(solution)/shard_map/ppermute | solution.py:38
  71.0 0.7 collective-permute-start.22
  71.7 4.0 %collective-permute-start.20 = (f32[2,256,256]{2,1,0:T(8,128)S(1)}, f32[2,256,256]{2,1,0:T(8,128)S(1)}, u32[]{:S(2)}, u32[]{:S(2)}) collective-permute-start(f32[2,256,256]{2,1,0:T(8,128)S(1)} %collective-permute-done.12.refs_2_.refs_8_), channel_id=1, source_target_pairs={{0,4},{4,0},{8,12},{12,8},{1,5},{5,1},{9,13},{13,9},{2,6},{6,2},{1... | collective-permute-start | bytes 1572872 | tf_op jit(solution)/shard_map/ppermute | solution.py:46
  75.7 2.3 %collective-permute-start.18 = (f32[2,256,256]{2,1,0:T(8,128)S(1)}, f32[2,256,256]{2,1,0:T(8,128)S(1)}, u32[]{:S(2)}, u32[]{:S(2)}) collective-permute-start(f32[2,256,256]{2,1,0:T(8,128)S(1)} %get-tuple-element.63), channel_id=1, source_target_pairs={{12,14},{14,12},{13,15},{15,13},{28,30},{30,28},{29,31},{31,29}} | collective-permute-start | bytes 1572872 | tf_op jit(solution)/shard_map/ppermute | solution.py:53
  78.0 6.9 %early.1 = (f32[2,256,4096]{2,1,0:T(8,128)S(1)}, f32[2,1,256,4096]{3,2,1,0:T(8,128)}) custom-call(s32[2,4]{1,0:T(2,128)S(1)} %bitcast.15, s32[2,4]{1,0:T(2,128)S(1)} %collective-permute-done.refs_1_, s32[2,4]{1,0:T(2,128)S(1)} %collective-permute-done.1.refs_2_, s32[2,4]{1,0:T(2,128)S(1)} %collective-permute-done.2.refs_3_, ...), custom_call_target="tpu_custom_call" | custom-call | tf_op jit(solution)/shard_map/early/pallas_call | solution.py:439
  85.0 2.8 %collective-permute-done.20.refs_9_ = f32[2,256,256]{2,1,0:T(8,128)S(1)} collective-permute-done((f32[2,256,256]{2,1,0:T(8,128)S(1)}, f32[2,256,256]{2,1,0:T(8,128)S(1)}, u32[]{:S(2)}, u32[]{:S(2)}) %collective-permute-start.20) | collective-permute-done | bytes 524320 | tf_op jit(solution)/shard_map/ppermute | solution.py:46
  87.8 2.7 %collective-permute-done.18.refs_7_ = f32[2,256,256]{2,1,0:T(8,128)S(1)} collective-permute-done((f32[2,256,256]{2,1,0:T(8,128)S(1)}, f32[2,256,256]{2,1,0:T(8,128)S(1)}, u32[]{:S(2)}, u32[]{:S(2)}) %collective-permute-start.18) | collective-permute-done | bytes 524320 | tf_op jit(solution)/shard_map/ppermute | solution.py:53
  90.5 3.3 %collective-permute-start.19 = (f32[2,256,256]{2,1,0:T(8,128)S(1)}, f32[2,256,256]{2,1,0:T(8,128)S(1)}, u32[]{:S(2)}, u32[]{:S(2)}) collective-permute-start(f32[2,256,256]{2,1,0:T(8,128)S(1)} %collective-permute-done.18.refs_7_), channel_id=1, source_target_pairs={{12,13},{13,12},{14,15},{15,14},{28,29},{29,28},{30,31},{31,30}} | collective-permute-start | bytes 1572872 | tf_op jit(solution)/shard_map/ppermute | solution.py:59
  93.8 0.1 collective-permute-start.21
  93.9 0.5 collective-permute-start.23
  94.4 0.9 collective-permute-done.19.refs_8_
  95.3 0.7 collective-permute-done.21.refs_10_
  96.1 0.7 collective-permute-done.23.refs_12_
  96.8 3.1 %late.1 = (f32[2,1,256,4096]{3,2,1,0:T(8,128)}, f32[2,256,4096]{2,1,0:T(8,128)S(1)}) custom-call(s32[2,4]{1,0:T(2,128)S(1)} %bitcast.16, s32[2,4]{1,0:T(2,128)S(1)} %collective-permute-done.refs_1_, s32[2,4]{1,0:T(2,128)S(1)} %collective-permute-done.1.refs_2_, ...), custom_call_target="tpu_custom_call", output_to_operand_aliasing={{0}: (13, {}), {1}: (6, {})} | custom-call | tf_op jit(solution)/shard_map/late/pallas_call | solution.py:503
  (24 shorter events, 0.1 us)
Async XLA Ops:
  0.0 2.3 %collective-permute-start.1 = (s32[2,4]{1,0:T(2,128)}, s32[2,4]{1,0:T(2,128)S(1)}, u32[]{:S(2)}, u32[]{:S(2)}) collective-permute-start(s32[2,4]{1,0:T(2,128)} %bitcast.1), channel_id=1, source_target_pairs={{4,8},{8,4},{5,9},{9,5},{6,10},{10,6},{7,11},{11,7},{20,24},{24,20... | collective-permute-start | bytes 104 | tf_op jit(solution)/shard_map/ppermute | solution.py:46
  0.7 2.8 %collective-permute-start = (s32[2,4]{1,0:T(2,128)}, s32[2,4]{1,0:T(2,128)S(1)}, u32[]{:S(2)}, u32[]{:S(2)}) collective-permute-start(s32[2,4]{1,0:T(2,128)} %bitcast.2), channel_id=1, source_target_pairs={{0,4},{4,0},{8,12},{12,8},{1,5},{5,1},{9,13},{13,9},{2,6},{6,2},{1... | collective-permute-start | bytes 104 | tf_op jit(solution)/shard_map/ppermute | solution.py:46
  3.5 0.7 copy-start.2
  6.4 15.7 %collective-permute-start.5 = (f32[2,256,256]{2,1,0:T(8,128)S(1)}, f32[2,256,256]{2,1,0:T(8,128)S(1)}, u32[]{:S(2)}, u32[]{:S(2)}) collective-permute-start(f32[2,256,256]{2,1,0:T(8,128)S(1)} %get-tuple-element.46), channel_id=1, source_target_pairs={{12,14},{14,12},{13,15},{15,13},{28,30},{30,28},{29,31},{31,29}} | collective-permute-start | bytes 1572872 | tf_op jit(solution)/shard_map/ppermute | solution.py:53
  9.5 12.6 %collective-permute-start.6 = (f32[2,256,256]{2,1,0:T(8,128)S(1)}, f32[2,256,256]{2,1,0:T(8,128)S(1)}, u32[]{:S(2)}, u32[]{:S(2)}) collective-permute-start(f32[2,256,256]{2,1,0:T(8,128)S(1)} %get-tuple-element.38), channel_id=1, source_target_pairs={{0,4},{4,0},{8,12},{12,8},{1,5},{5,1},{9,13},{13,9},{2,6},{6,2},{1... | collective-permute-start | bytes 1572872 | tf_op jit(solution)/shard_map/ppermute | solution.py:46
  13.4 24.3 %collective-permute-start.8 = (f32[3,256,256]{2,1,0:T(8,128)S(1)}, f32[3,256,256]{2,1,0:T(8,128)S(1)}, u32[]{:S(2)}, u32[]{:S(2)}) collective-permute-start(f32[3,256,256]{2,1,0:T(8,128)S(1)} %cut.8), channel_id=1, source_target_pairs={{0,4},{4,0},{8,12},{12,8},{1,5},{5,1},{9,13},{13,9},{2,6},{6,2},{1... | collective-permute-start | bytes 2359304 | tf_op jit(solution)/shard_map/ppermute | solution.py:46
  14.9 13.9 %collective-permute-start.7 = (f32[2,256,256]{2,1,0:T(8,128)S(1)}, f32[2,256,256]{2,1,0:T(8,128)S(1)}, u32[]{:S(2)}, u32[]{:S(2)}) collective-permute-start(f32[2,256,256]{2,1,0:T(8,128)S(1)} %cut.7), channel_id=1, source_target_pairs={{4,8},{8,4},{5,9},{9,5},{6,10},{10,6},{7,11},{11,7},{20,24},{24,20... | collective-permute-start | bytes 1572872 | tf_op jit(solution)/shard_map/ppermute | solution.py:46
  19.8 8.8 %copy-start.1 = (bf16[8,256,256]{2,1,0:T(8,128)(2,1)S(1)}, bf16[8,256,256]{2,1,0:T(8,128)(2,1)}, u32[]{:S(2)}) copy-start(bf16[8,256,256]{2,1,0:T(8,128)(2,1)} %constant.2.clone.pieces) | copy-start | bytes 3145732
  22.0 15.7 %copy-start = (f32[2,256,256]{2,1,0:T(8,128)S(1)}, f32[2,256,256]{2,1,0:T(8,128)}, u32[]{:S(2)}) copy-start(f32[2,256,256]{2,1,0:T(8,128)} %refs_3_.17) | copy-start | bytes 1572868
  22.0 15.7 %copy-start.3 = (s32[4,2]{0,1:T(2,128)S(1)}, s32[4,2]{0,1:T(2,128)}, u32[]{:S(2)}) copy-start(s32[4,2]{0,1:T(2,128)} %param.10) | copy-start | bytes 100
  22.7 15.0 %collective-permute-start.9 = (f32[2,256,256]{2,1,0:T(8,128)S(1)}, f32[2,256,256]{2,1,0:T(8,128)S(1)}, u32[]{:S(2)}, u32[]{:S(2)}) collective-permute-start(f32[2,256,256]{2,1,0:T(8,128)S(1)} %join.2), channel_id=1, source_target_pairs={{0,2},{2,0},{1,3},{3,1},{4,6},{6,4},{5,7},{7,5},{8,10},{10,8},{9,1... | collective-permute-start | bytes 1572872 | tf_op jit(solution)/shard_map/ppermute | solution.py:38
  23.1 22.1 %collective-permute-start.10 = (f32[3,256,256]{2,1,0:T(8,128)S(1)}, f32[3,256,256]{2,1,0:T(8,128)S(1)}, u32[]{:S(2)}, u32[]{:S(2)}) collective-permute-start(f32[3,256,256]{2,1,0:T(8,128)S(1)} %cut.9.refs_5_), channel_id=1, source_target_pairs={{4,8},{8,4},{5,9},{9,5},{6,10},{10,6},{7,11},{11,7},{20,24},{24,20... | collective-permute-start | bytes 2359304 | tf_op jit(solution)/shard_map/ppermute | solution.py:46
  23.8 5.8 %collective-permute-start.2 = (s32[2,4]{1,0:T(2,128)S(1)}, s32[2,4]{1,0:T(2,128)S(1)}, u32[]{:S(2)}, u32[]{:S(2)}) collective-permute-start(s32[2,4]{1,0:T(2,128)S(1)} %bitcast.10), channel_id=1, source_target_pairs={{0,1},{1,0},{2,3},{3,2},{4,5},{5,4},{6,7},{7,6},{8,9},{9,8},{10,11... | collective-permute-start | bytes 104 | tf_op jit(solution)/shard_map/ppermute | solution.py:38
  28.8 1.3 %collective-permute-start.4 = (s32[2,4]{1,0:T(2,128)S(1)}, s32[2,4]{1,0:T(2,128)S(1)}, u32[]{:S(2)}, u32[]{:S(2)}) collective-permute-start(s32[2,4]{1,0:T(2,128)S(1)} %collective-permute-done.1.refs_2_), channel_id=1, source_target_pairs={{0,1},{1,0},{2,3},{3,2},{4,5},{5,4},{6,7},{7,6},{8,9},{9,8},{10,11... | collective-permute-start | bytes 104 | tf_op jit(solution)/shard_map/ppermute | solution.py:38
  29.6 1.8 %collective-permute-start.3 = (s32[2,4]{1,0:T(2,128)S(1)}, s32[2,4]{1,0:T(2,128)S(1)}, u32[]{:S(2)}, u32[]{:S(2)}) collective-permute-start(s32[2,4]{1,0:T(2,128)S(1)} %collective-permute-done.refs_1_), channel_id=1, source_target_pairs={{0,1},{1,0},{2,3},{3,2},{4,5},{5,4},{6,7},{7,6},{8,9},{9,8},{10,11... | collective-permute-start | bytes 104 | tf_op jit(solution)/shard_map/ppermute | solution.py:38
  30.1 15.0 %collective-permute-start.11 = (f32[2,256,256]{2,1,0:T(8,128)S(1)}, f32[2,256,256]{2,1,0:T(8,128)S(1)}, u32[]{:S(2)}, u32[]{:S(2)}) collective-permute-start(f32[2,256,256]{2,1,0:T(8,128)S(1)} %join.3), channel_id=1, source_target_pairs={{0,2},{2,0},{1,3},{3,1},{4,6},{6,4},{5,7},{7,5},{8,10},{10,8},{9,1... | collective-permute-start | bytes 1572872 | tf_op jit(solution)/shard_map/ppermute | solution.py:38
  44.5 16.1 %collective-permute-start.12 = (f32[2,256,256]{2,1,0:T(8,128)S(1)}, f32[2,256,256]{2,1,0:T(8,128)S(1)}, u32[]{:S(2)}, u32[]{:S(2)}) collective-permute-start(f32[2,256,256]{2,1,0:T(8,128)S(1)} %get-tuple-element.59), channel_id=1, source_target_pairs={{0,2},{2,0},{1,3},{3,1},{4,6},{6,4},{5,7},{7,5},{8,10},{10,8},{9,1... | collective-permute-start | bytes 1572872 | tf_op jit(solution)/shard_map/ppermute | solution.py:38
  44.8 15.8 %collective-permute-start.13 = (f32[2,256,256]{2,1,0:T(8,128)S(1)}, f32[2,256,256]{2,1,0:T(8,128)S(1)}, u32[]{:S(2)}, u32[]{:S(2)}) collective-permute-start(f32[2,256,256]{2,1,0:T(8,128)S(1)} %get-tuple-element.54.refs_1_.refs_7_), channel_id=1, source_target_pairs={{0,4},{4,0},{8,12},{12,8},{1,5},{5,1},{9,13},{13,9},{2,6},{6,2},{1... | collective-permute-start | bytes 1572872 | tf_op jit(solution)/shard_map/ppermute | solution.py:46
  51.8 15.6 %collective-permute-start.16 = (f32[2,256,256]{2,1,0:T(8,128)S(1)}, f32[2,256,256]{2,1,0:T(8,128)S(1)}, u32[]{:S(2)}, u32[]{:S(2)}) collective-permute-start(f32[2,256,256]{2,1,0:T(8,128)S(1)} %get-tuple-element.56.refs_0_.refs_11_), channel_id=1, source_target_pairs={{4,8},{8,4},{5,9},{9,5},{6,10},{10,6},{7,11},{11,7},{20,24},{24,20... | collective-permute-start | bytes 1572872 | tf_op jit(solution)/shard_map/ppermute | solution.py:46
  52.5 14.9 %collective-permute-start.15 = (f32[2,256,256]{2,1,0:T(8,128)S(1)}, f32[2,256,256]{2,1,0:T(8,128)S(1)}, u32[]{:S(2)}, u32[]{:S(2)}) collective-permute-start(f32[2,256,256]{2,1,0:T(8,128)S(1)} %get-tuple-element.60), channel_id=1, source_target_pairs={{0,2},{2,0},{1,3},{3,1},{4,6},{6,4},{5,7},{7,5},{8,10},{10,8},{9,1... | collective-permute-start | bytes 1572872 | tf_op jit(solution)/shard_map/ppermute | solution.py:38
  60.7 17.3 %collective-permute-start.14 = (f32[4,2,256,256]{3,2,1,0:T(8,128)S(1)}, f32[4,2,256,256]{3,2,1,0:T(8,128)S(1)}, u32[]{:S(2)}, u32[]{:S(2)}) collective-permute-start(f32[4,2,256,256]{3,2,1,0:T(8,128)S(1)} %pack.2), channel_id=1, source_target_pairs={{0,1},{1,0},{2,3},{3,2},{4,5},{5,4},{6,7},{7,6},{8,9},{9,8},{10,11... | collective-permute-start | bytes 6291464 | tf_op jit(solution)/shard_map/ppermute | solution.py:38
  67.6 10.4 %collective-permute-start.17 = (f32[3,2,256,256]{3,2,1,0:T(8,128)S(1)}, f32[3,2,256,256]{3,2,1,0:T(8,128)S(1)}, u32[]{:S(2)}, u32[]{:S(2)}) collective-permute-start(f32[3,2,256,256]{3,2,1,0:T(8,128)S(1)} %pack.3), channel_id=1, source_target_pairs={{0,1},{1,0},{2,3},{3,2},{4,5},{5,4},{6,7},{7,6},{8,9},{9,8},{10,11... | collective-permute-start | bytes 4718600 | tf_op jit(solution)/shard_map/ppermute | solution.py:38
  71.0 14.0 %collective-permute-start.22 = (f32[2,256,256]{2,1,0:T(8,128)S(1)}, f32[2,256,256]{2,1,0:T(8,128)S(1)}, u32[]{:S(2)}, u32[]{:S(2)}) collective-permute-start(f32[2,256,256]{2,1,0:T(8,128)S(1)} %collective-permute-done.15.refs_1_.refs_12_), channel_id=1, source_target_pairs={{4,8},{8,4},{5,9},{9,5},{6,10},{10,6},{7,11},{11,7},{20,24},{24,20... | collective-permute-start | bytes 1572872 | tf_op jit(solution)/shard_map/ppermute | solution.py:46
  71.7 16.1 %collective-permute-start.20 = (f32[2,256,256]{2,1,0:T(8,128)S(1)}, f32[2,256,256]{2,1,0:T(8,128)S(1)}, u32[]{:S(2)}, u32[]{:S(2)}) collective-permute-start(f32[2,256,256]{2,1,0:T(8,128)S(1)} %collective-permute-done.12.refs_2_.refs_8_), channel_id=1, source_target_pairs={{0,4},{4,0},{8,12},{12,8},{1,5},{5,1},{9,13},{13,9},{2,6},{6,2},{1... | collective-permute-start | bytes 1572872 | tf_op jit(solution)/shard_map/ppermute | solution.py:46
  75.7 14.8 %collective-permute-start.18 = (f32[2,256,256]{2,1,0:T(8,128)S(1)}, f32[2,256,256]{2,1,0:T(8,128)S(1)}, u32[]{:S(2)}, u32[]{:S(2)}) collective-permute-start(f32[2,256,256]{2,1,0:T(8,128)S(1)} %get-tuple-element.63), channel_id=1, source_target_pairs={{12,14},{14,12},{13,15},{15,13},{28,30},{30,28},{29,31},{31,29}} | collective-permute-start | bytes 1572872 | tf_op jit(solution)/shard_map/ppermute | solution.py:53
  90.5 4.9 %collective-permute-start.19 = (f32[2,256,256]{2,1,0:T(8,128)S(1)}, f32[2,256,256]{2,1,0:T(8,128)S(1)}, u32[]{:S(2)}, u32[]{:S(2)}) collective-permute-start(f32[2,256,256]{2,1,0:T(8,128)S(1)} %collective-permute-done.18.refs_7_), channel_id=1, source_target_pairs={{12,13},{13,12},{14,15},{15,14},{28,29},{29,28},{30,31},{31,30}} | collective-permute-start | bytes 1572872 | tf_op jit(solution)/shard_map/ppermute | solution.py:59
  93.8 2.3 %collective-permute-start.21 = (f32[2,256,256]{2,1,0:T(8,128)S(1)}, f32[2,256,256]{2,1,0:T(8,128)S(1)}, u32[]{:S(2)}, u32[]{:S(2)}) collective-permute-start(f32[2,256,256]{2,1,0:T(8,128)S(1)} %collective-permute-done.20.refs_9_), channel_id=1, source_target_pairs={{0,1},{1,0},{2,3},{3,2},{4,5},{5,4},{6,7},{7,6},{8,9},{9,8},{10,11... | collective-permute-start | bytes 1572872 | tf_op jit(solution)/shard_map/ppermute | solution.py:38
  93.9 2.9 %collective-permute-start.23 = (f32[2,256,256]{2,1,0:T(8,128)S(1)}, f32[2,256,256]{2,1,0:T(8,128)S(1)}, u32[]{:S(2)}, u32[]{:S(2)}) collective-permute-start(f32[2,256,256]{2,1,0:T(8,128)S(1)} %collective-permute-done.22.refs_11_), channel_id=1, source_target_pairs={{0,1},{1,0},{2,3},{3,2},{4,5},{5,4},{6,7},{7,6},{8,9},{9,8},{10,11... | collective-permute-start | bytes 1572872 | tf_op jit(solution)/shard_map/ppermute | solution.py:38

commit v12 on v10

--- a/solution.py
+++ b/solution.py
@@ -153,7 +153,7 @@
     here, up = owner * n_here + k, sections * n_here + owner * n_up + k
     width = len(tables) // 2 if len(tables) > 3 else len(tables)
     pairs = tables[width * twin]
-    below = tables[width * twin + 1 + (0 if isinstance(phase, str) else phase)]
+    below = tables[width * twin + 1]
     lower = True if which == "last" else is_lower(phase)
     own, other = (here, up) if which == "slot" else (up, here)
     row = lax.rem(pick(lower, pairs[0, own], below[0, other]), side)
@@ -521,10 +521,7 @@
 
     layout = (sections, n_here, n_up, side)
     pairs = offsets.T
-    if n_here == n_up:
-        tables = [pairs] + [swap(pairs, "tile", parity) for parity in range(2)]
-    else:
-        tables = [pairs, move(pairs, "tile", 1)]
+    tables = [pairs, move(pairs, "tile", 1)]
     back = lambda d: (sections - d) % sections
     far = distances[1:]
     phase = pltpu.with_memory_space_constraint(phase, pltpu.HBM)

time: 96.2 us -> 96.8 us (level)
  waiting for transfers between devices: 15.3 us -> 19.1 us
  starting transfers between devices: 36.4 us -> 34.2 us
    ppermute x10 -> x8, starting transfers between devices: 8.11 us -> 4.55 us  [swap(): return lax.ppermute(block, axis, route)]
    ppermute x0 -> x1, waiting for transfers between devices: none -> 3.23 us  [move(): return lax.ppermute(block, axis, route)]
    ppermute x0 -> x1, starting transfers between devices: none -> 1.28 us  [move(): return lax.ppermute(block, axis, route)]
    ppermute x12 -> x11, waiting for transfers between devices: 5.4 us -> 6.64 us  [rotate(): lax.ppermute(block, axis, [(i, (i + distance) % size) for i in range(size)])]
    ppermute x10 -> x8, waiting for transfers between devices: 7.16 us -> 6.41 us  [swap(): return lax.ppermute(block, axis, route)]
    ppermute x12 -> x11, starting transfers between devices: 22.2 us -> 22.1 us  [rotate(): lax.ppermute(block, axis, [(i, (i + distance) % size) for i in range(size)])]
  transfers between devices with their start and end apart: 24 -> 22, of which waited for: 12 -> 12; matrix products, arithmetic and copies ran while one was open for 0% -> 0% of each run, Pallas kernels for 39% -> 38%
where the time goes in v12:
time: 96.8 us; the launch traced here: 96.3 us
  Pallas kernels  41.9 us (43%)
  starting transfers between devices  34.2 us (35%)
  waiting for transfers between devices  19.1 us (20%)
    ppermute x11, starting transfers between devices, rotate(): lax.ppermute(block, axis, [(i, (i + distance) % size) for i in range(size)])  22.1 us
    pallas_call x3, Pallas kernels, run_slot(): pl.pallas_call(lambda *refs: slot_kernel(kind, spot, layout, len(tables),...  19.7 us
    pallas_call x5, Pallas kernels, cut(): pl.pallas_call(lambda *refs: cut_kernel(spots, layout, measured is not No...  10.5 us
    pallas_call x1, Pallas kernels, early(): pl.pallas_call(lambda *refs: early_kernel(metas, layout, *refs), in_specs...  6.86 us
    ppermute x11, waiting for transfers between devices, rotate(): lax.ppermute(block, axis, [(i, (i + distance) % size) for i in range(size)])  6.64 us
    ppermute x8, waiting for transfers between devices, swap(): return lax.ppermute(block, axis, route)  6.41 us
    ppermute x2, starting transfers between devices, rotate_last(): return lax.ppermute(block, ('tile', 'slab'), route)  6.24 us
    ppermute x8, starting transfers between devices, swap(): return lax.ppermute(block, axis, route)  4.55 us
  transfers between devices with their start and end apart: 22, of which 12 were waited for; matrix products, arithmetic and copies ran while one was open for 0% of the time, Pallas kernels for 38%

profile of v12, /device:TPU:29, one launch (start us, length us, event | category | flops | bytes accessed | tf_op | source)
XLA Modules:
  0.0 96.3 jit_solution(15919776369041596657)
XLA Ops:
  0.0 1.3 %collective-permute-start = (s32[2,4]{1,0:T(2,128)}, s32[2,4]{1,0:T(2,128)S(1)}, u32[]{:S(2)}, u32[]{:S(2)}) collective-permute-start(s32[2,4]{1,0:T(2,128)} %bitcast.1), channel_id=1, source_target_pairs={{0,4},{4,8},{8,12},{1,5},{5,9},{9,13},{2,6},{6,10},{10,14},{3,7},{... | collective-permute-start | bytes 104 | tf_op jit(solution)/shard_map/ppermute | solution.py:33
  1.3 3.2 %collective-permute-done.refs_1_ = s32[2,4]{1,0:T(2,128)S(1)} collective-permute-done((s32[2,4]{1,0:T(2,128)}, s32[2,4]{1,0:T(2,128)S(1)}, u32[]{:S(2)}, u32[]{:S(2)}) %collective-permute-start) | collective-permute-done | bytes 64 | tf_op jit(solution)/shard_map/ppermute | solution.py:33
  4.5 0.7 copy-done.2
  5.2 2.2 %cut.5 = (f32[2,256,256]{2,1,0:T(8,128)S(1)}, f32[2,256,256]{2,1,0:T(8,128)S(1)}) custom-call(s32[2,4]{1,0:T(2,128)S(1)} %bitcast.2, s32[2,4]{1,0:T(2,128)S(1)} %collective-permute-done.refs_1_, f32[1,256,4096]{2,1,0:T(8,128)} %refs_2_.12, f32[1,256,4096]{2,1,0:T(8,128)} %refs_3_.12), custom_call_target="tpu_custom_call" | custom-call | tf_op jit(solution)/shard_map/cut/pallas_call | solution.py:328
  7.4 0.2 collective-permute-start.3
  7.6 2.0 %cut.6 = f32[3,256,256]{2,1,0:T(8,128)S(1)} custom-call(s32[2,4]{1,0:T(2,128)S(1)} %bitcast.3, s32[2,4]{1,0:T(2,128)S(1)} %collective-permute-done.refs_1_, f32[1,256,4096]{2,1,0:T(8,128)} %refs_2_.12, f32[1,256,4096]{2,1,0:T(8,128)} %refs_3_.12, f32[4,256,256]{2,1,0:T(8,128)} %refs_3_.15), custom_call_target="tpu_custom_call" | custom-call | tf_op jit(solution)/shard_map/cut/pallas_call | solution.py:328
  9.6 1.3 %collective-permute-start.6 = (f32[3,256,256]{2,1,0:T(8,128)S(1)}, f32[3,256,256]{2,1,0:T(8,128)S(1)}, u32[]{:S(2)}, u32[]{:S(2)}) collective-permute-start(f32[3,256,256]{2,1,0:T(8,128)S(1)} %cut.6), channel_id=1, source_target_pairs={{0,4},{4,0},{8,12},{12,8},{1,5},{5,1},{9,13},{13,9},{2,6},{6,2},{1... | collective-permute-start | bytes 2359304 | tf_op jit(solution)/shard_map/ppermute | solution.py:46
  10.9 0.7 collective-permute-start.5
  11.6 3.1 %collective-permute-start.4 = (f32[2,256,256]{2,1,0:T(8,128)S(1)}, f32[2,256,256]{2,1,0:T(8,128)S(1)}, u32[]{:S(2)}, u32[]{:S(2)}) collective-permute-start(f32[2,256,256]{2,1,0:T(8,128)S(1)} %get-tuple-element.45), channel_id=1, source_target_pairs={{12,14},{14,12},{13,15},{15,13},{28,30},{30,28},{29,31},{31,29}} | collective-permute-start | bytes 1572872 | tf_op jit(solution)/shard_map/ppermute | solution.py:53
  14.7 1.9 %cut.7.refs_4_ = f32[3,256,256]{2,1,0:T(8,128)S(1)} custom-call(s32[2,4]{1,0:T(2,128)S(1)} %bitcast.4, s32[2,4]{1,0:T(2,128)S(1)} %collective-permute-done.refs_1_, f32[1,256,4096]{2,1,0:T(8,128)} %refs_2_.12, f32[1,256,4096]{2,1,0:T(8,128)} %refs_3_.12, f32[4,256,256]{2,1,0:T(8,128)} %refs_3_.15), custom_call_target="tpu_custom_call" | custom-call | tf_op jit(solution)/shard_map/cut/pallas_call | solution.py:328
  16.7 2.2 %cut.8 = (f32[2,256,256]{2,1,0:T(8,128)S(1)}, f32[2,256,256]{2,1,0:T(8,128)S(1)}) custom-call(s32[2,4]{1,0:T(2,128)S(1)} %bitcast.5, s32[2,4]{1,0:T(2,128)S(1)} %collective-permute-done.refs_1_, f32[1,256,4096]{2,1,0:T(8,128)} %refs_2_.12, f32[1,256,4096]{2,1,0:T(8,128)} %refs_3_.12), custom_call_target="tpu_custom_call" | custom-call | tf_op jit(solution)/shard_map/cut/pallas_call | solution.py:328
  18.9 2.2 %cut.9 = (f32[2,256,256]{2,1,0:T(8,128)S(1)}, f32[2,256,256]{2,1,0:T(8,128)S(1)}) custom-call(s32[2,4]{1,0:T(2,128)S(1)} %bitcast.6, s32[2,4]{1,0:T(2,128)S(1)} %collective-permute-done.refs_1_, f32[1,256,4096]{2,1,0:T(8,128)} %refs_2_.12, f32[1,256,4096]{2,1,0:T(8,128)} %refs_3_.12), custom_call_target="tpu_custom_call" | custom-call | tf_op jit(solution)/shard_map/cut/pallas_call | solution.py:328
  21.1 0.6 join.2
  21.8 0.3 collective-permute-start.7
  22.1 0.7 collective-permute-start.8
  22.8 0.2 expand.1
  23.0 1.3 %collective-permute-done.4.refs_5_ = f32[2,256,256]{2,1,0:T(8,128)S(1)} collective-permute-done((f32[2,256,256]{2,1,0:T(8,128)S(1)}, f32[2,256,256]{2,1,0:T(8,128)S(1)}, u32[]{:S(2)}, u32[]{:S(2)}) %collective-permute-start.4) | collective-permute-done | bytes 524320 | tf_op jit(solution)/shard_map/ppermute | solution.py:53
  24.3 6.3 %collective-permute-start.1 = (s32[2,4]{1,0:T(2,128)S(1)}, s32[2,4]{1,0:T(2,128)S(1)}, u32[]{:S(2)}, u32[]{:S(2)}) collective-permute-start(s32[2,4]{1,0:T(2,128)S(1)} %bitcast.8), channel_id=1, source_target_pairs={{0,1},{1,0},{2,3},{3,2},{4,5},{5,4},{6,7},{7,6},{8,9},{9,8},{10,11... | collective-permute-start | bytes 104 | tf_op jit(solution)/shard_map/ppermute | solution.py:38
  30.7 0.6 join.3
  31.3 0.2 collective-permute-done.1.refs_2_
  31.5 1.3 %collective-permute-start.9 = (f32[2,256,256]{2,1,0:T(8,128)S(1)}, f32[2,256,256]{2,1,0:T(8,128)S(1)}, u32[]{:S(2)}, u32[]{:S(2)}) collective-permute-start(f32[2,256,256]{2,1,0:T(8,128)S(1)} %join.3), channel_id=1, source_target_pairs={{0,2},{2,0},{1,3},{3,1},{4,6},{6,4},{5,7},{7,5},{8,10},{10,8},{9,1... | collective-permute-start | bytes 1572872 | tf_op jit(solution)/shard_map/ppermute | solution.py:38
  32.8 2.9 %collective-permute-done.6.refs_5_ = f32[3,256,256]{2,1,0:T(8,128)S(1)} collective-permute-done((f32[3,256,256]{2,1,0:T(8,128)S(1)}, f32[3,256,256]{2,1,0:T(8,128)S(1)}, u32[]{:S(2)}, u32[]{:S(2)}) %collective-permute-start.6) | collective-permute-done | bytes 786464 | tf_op jit(solution)/shard_map/ppermute | solution.py:46
  35.7 0.2 collective-permute-done.7.refs_6_
  35.9 6.5 %slot_0.1 = (f32[2,256,256]{2,1,0:T(8,128)S(1)}, f32[2,256,256]{2,1,0:T(8,128)S(1)}) custom-call(s32[2,4]{1,0:T(2,128)S(1)} %bitcast.10, s32[2,4]{1,0:T(2,128)S(1)} %collective-permute-done.refs_1_, f32[2,256,256]{2,1,0:T(8,128)S(1)} %copy-done, f32[4,256,256]{2,1,0:T(8,128)} %refs_3_.15, f32[2,256,256]{2,1,0:T(8,128)S(1)} %get-tuple-element.40.refs_4_, ...), custom_call_target="tpu_custom_call" | custom-call | tf_op jit(solution)/shard_map/slot_0/pallas_call | solution.py:260
  42.4 1.4 %collective-permute-start.10 = (f32[2,256,256]{2,1,0:T(8,128)S(1)}, f32[2,256,256]{2,1,0:T(8,128)S(1)}, u32[]{:S(2)}, u32[]{:S(2)}) collective-permute-start(f32[2,256,256]{2,1,0:T(8,128)S(1)} %get-tuple-element.56), channel_id=1, source_target_pairs={{0,2},{2,0},{1,3},{3,1},{4,6},{6,4},{5,7},{7,5},{8,10},{10,8},{9,1... | collective-permute-start | bytes 1572872 | tf_op jit(solution)/shard_map/ppermute | solution.py:38
  43.8 0.2 collective-permute-start.11
  43.9 3.2 %collective-permute-done.9.refs_6_ = f32[2,256,256]{2,1,0:T(8,128)S(1)} collective-permute-done((f32[2,256,256]{2,1,0:T(8,128)S(1)}, f32[2,256,256]{2,1,0:T(8,128)S(1)}, u32[]{:S(2)}, u32[]{:S(2)}) %collective-permute-start.9) | collective-permute-done | bytes 524320 | tf_op jit(solution)/shard_map/ppermute | solution.py:38
  47.1 6.5 %slot_1.1 = (f32[2,256,256]{2,1,0:T(8,128)S(1)}, f32[2,256,256]{2,1,0:T(8,128)S(1)}) custom-call(s32[2,4]{1,0:T(2,128)S(1)} %bitcast.11, s32[2,4]{1,0:T(2,128)S(1)} %collective-permute-done.refs_1_, f32[2,256,256]{2,1,0:T(8,128)S(1)} %copy-done, f32[4,256,256]{2,1,0:T(8,128)} %refs_3_.15, f32[2,256,256]{2,1,0:T(8,128)S(1)} %get-tuple-element.42.refs_4_, ...), custom_call_target="tpu_custom_call" | custom-call | tf_op jit(solution)/shard_map/slot_1/pallas_call | solution.py:260
  53.6 0.7 collective-permute-start.14
  54.3 1.2 %collective-permute-start.13 = (f32[2,256,256]{2,1,0:T(8,128)S(1)}, f32[2,256,256]{2,1,0:T(8,128)S(1)}, u32[]{:S(2)}, u32[]{:S(2)}) collective-permute-start(f32[2,256,256]{2,1,0:T(8,128)S(1)} %get-tuple-element.57), channel_id=1, source_target_pairs={{0,2},{2,0},{1,3},{3,1},{4,6},{6,4},{5,7},{7,5},{8,10},{10,8},{9,1... | collective-permute-start | bytes 1572872 | tf_op jit(solution)/shard_map/ppermute | solution.py:38
  55.6 6.6 %slot_last.1 = (f32[2,256,256]{2,1,0:T(8,128)S(1)}, f32[2,256,256]{2,1,0:T(8,128)S(1)}) custom-call(s32[2,4]{1,0:T(2,128)S(1)} %bitcast.12, s32[2,4]{1,0:T(2,128)S(1)} %collective-permute-done.refs_1_, f32[2,256,256]{2,1,0:T(8,128)S(1)} %copy-done, f32[4,256,256]{2,1,0:T(8,128)} %refs_3_.15, f32[3,256,256]{2,1,0:T(8,128)S(1)} %cut.7.refs_4_, ...), custom_call_target="tpu_custom_call" | custom-call | tf_op jit(solution)/shard_map/slot_last/pallas_call | solution.py:260
  62.2 0.1 pack.2
  62.4 6.6 %collective-permute-start.12 = (f32[4,2,256,256]{3,2,1,0:T(8,128)S(1)}, f32[4,2,256,256]{3,2,1,0:T(8,128)S(1)}, u32[]{:S(2)}, u32[]{:S(2)}) collective-permute-start(f32[4,2,256,256]{3,2,1,0:T(8,128)S(1)} %pack.2), channel_id=1, source_target_pairs={{0,1},{1,0},{2,3},{3,2},{4,5},{5,4},{6,7},{7,6},{8,9},{9,8},{10,11... | collective-permute-start | bytes 6291464 | tf_op jit(solution)/shard_map/ppermute | solution.py:38
  68.9 0.6 collective-permute-done.13.refs_1_.refs_10_
  69.6 0.1 pack.3
  69.7 3.3 %collective-permute-start.15 = (f32[3,2,256,256]{3,2,1,0:T(8,128)S(1)}, f32[3,2,256,256]{3,2,1,0:T(8,128)S(1)}, u32[]{:S(2)}, u32[]{:S(2)}) collective-permute-start(f32[3,2,256,256]{3,2,1,0:T(8,128)S(1)} %pack.3), channel_id=1, source_target_pairs={{0,1},{1,0},{2,3},{3,2},{4,5},{5,4},{6,7},{7,6},{8,9},{9,8},{10,11... | collective-permute-start | bytes 4718600 | tf_op jit(solution)/shard_map/ppermute | solution.py:38
  73.0 0.7 collective-permute-start.20
  73.7 0.1 collective-permute-start.18
  73.7 3.1 %collective-permute-start.16 = (f32[2,256,256]{2,1,0:T(8,128)S(1)}, f32[2,256,256]{2,1,0:T(8,128)S(1)}, u32[]{:S(2)}, u32[]{:S(2)}) collective-permute-start(f32[2,256,256]{2,1,0:T(8,128)S(1)} %get-tuple-element.60), channel_id=1, source_target_pairs={{12,14},{14,12},{13,15},{15,13},{28,30},{30,28},{29,31},{31,29}} | collective-permute-start | bytes 1572872 | tf_op jit(solution)/shard_map/ppermute | solution.py:53
  76.9 6.9 %early.1 = (f32[2,256,4096]{2,1,0:T(8,128)S(1)}, f32[2,1,256,4096]{3,2,1,0:T(8,128)}) custom-call(s32[2,4]{1,0:T(2,128)S(1)} %bitcast.13, s32[2,4]{1,0:T(2,128)S(1)} %collective-permute-done.refs_1_, s32[2,4]{1,0:T(2,128)S(1)} %collective-permute-done.1.refs_2_, s32[2,4]{1,0:T(2,128)S(1)} %collective-permute-done.2.refs_3_, ...), custom_call_target="tpu_custom_call" | custom-call | tf_op jit(solution)/shard_map/early/pallas_call | solution.py:433
  83.8 3.5 %collective-permute-done.18.refs_7_ = f32[2,256,256]{2,1,0:T(8,128)S(1)} collective-permute-done((f32[2,256,256]{2,1,0:T(8,128)S(1)}, f32[2,256,256]{2,1,0:T(8,128)S(1)}, u32[]{:S(2)}, u32[]{:S(2)}) %collective-permute-start.18) | collective-permute-done | bytes 524320 | tf_op jit(solution)/shard_map/ppermute | solution.py:46
  87.3 1.6 %collective-permute-done.16.refs_5_ = f32[2,256,256]{2,1,0:T(8,128)S(1)} collective-permute-done((f32[2,256,256]{2,1,0:T(8,128)S(1)}, f32[2,256,256]{2,1,0:T(8,128)S(1)}, u32[]{:S(2)}, u32[]{:S(2)}) %collective-permute-start.16) | collective-permute-done | bytes 524320 | tf_op jit(solution)/shard_map/ppermute | solution.py:53
  88.8 1.1 %collective-permute-start.17 = (f32[2,256,256]{2,1,0:T(8,128)S(1)}, f32[2,256,256]{2,1,0:T(8,128)S(1)}, u32[]{:S(2)}, u32[]{:S(2)}) collective-permute-start(f32[2,256,256]{2,1,0:T(8,128)S(1)} %collective-permute-done.16.refs_5_), channel_id=1, source_target_pairs={{0,1},{1,0},{2,3},{3,2},{4,5},{5,4},{6,7},{7,6},{8,9},{9,8},{10,11... | collective-permute-start | bytes 1572872 | tf_op jit(solution)/shard_map/ppermute | solution.py:38
  90.0 0.5 collective-permute-start.21
  90.5 1.0 %collective-permute-done.17.refs_6_ = f32[2,256,256]{2,1,0:T(8,128)S(1)} collective-permute-done((f32[2,256,256]{2,1,0:T(8,128)S(1)}, f32[2,256,256]{2,1,0:T(8,128)S(1)}, u32[]{:S(2)}, u32[]{:S(2)}) %collective-permute-start.17) | collective-permute-done | bytes 524320 | tf_op jit(solution)/shard_map/ppermute | solution.py:38
  91.5 0.7 collective-permute-done.19.refs_8_
  92.3 0.7 collective-permute-done.21.refs_10_
  93.0 3.1 %late.1 = f32[2,1,256,4096]{3,2,1,0:T(8,128)} custom-call(s32[2,4]{1,0:T(2,128)S(1)} %bitcast.14, s32[2,4]{1,0:T(2,128)S(1)} %collective-permute-done.refs_1_, s32[2,4]{1,0:T(2,128)S(1)} %collective-permute-done.1.refs_2_, s32[2,4]{1,0:T(2,128)S(1)} %collective-permute-done.2.refs_3_, ...), custom_call_target="tpu_custom_call", output_to_operand_aliasing={{}: (11, {})} | custom-call | tf_op jit(solution)/shard_map/late/pallas_call | solution.py:498
  (19 shorter events, 0.1 us)
Async XLA Ops:
  0.0 4.5 %collective-permute-start = (s32[2,4]{1,0:T(2,128)}, s32[2,4]{1,0:T(2,128)S(1)}, u32[]{:S(2)}, u32[]{:S(2)}) collective-permute-start(s32[2,4]{1,0:T(2,128)} %bitcast.1), channel_id=1, source_target_pairs={{0,4},{4,8},{8,12},{1,5},{5,9},{9,13},{2,6},{6,10},{10,14},{3,7},{... | collective-permute-start | bytes 104 | tf_op jit(solution)/shard_map/ppermute | solution.py:33
  4.5 0.7 copy-start.2
  7.4 13.7 %collective-permute-start.3 = (f32[2,256,256]{2,1,0:T(8,128)S(1)}, f32[2,256,256]{2,1,0:T(8,128)S(1)}, u32[]{:S(2)}, u32[]{:S(2)}) collective-permute-start(f32[2,256,256]{2,1,0:T(8,128)S(1)} %get-tuple-element.36), channel_id=1, source_target_pairs={{0,4},{4,0},{8,12},{12,8},{1,5},{5,1},{9,13},{13,9},{2,6},{6,2},{1... | collective-permute-start | bytes 1572872 | tf_op jit(solution)/shard_map/ppermute | solution.py:46
  9.6 26.1 %collective-permute-start.6 = (f32[3,256,256]{2,1,0:T(8,128)S(1)}, f32[3,256,256]{2,1,0:T(8,128)S(1)}, u32[]{:S(2)}, u32[]{:S(2)}) collective-permute-start(f32[3,256,256]{2,1,0:T(8,128)S(1)} %cut.6), channel_id=1, source_target_pairs={{0,4},{4,0},{8,12},{12,8},{1,5},{5,1},{9,13},{13,9},{2,6},{6,2},{1... | collective-permute-start | bytes 2359304 | tf_op jit(solution)/shard_map/ppermute | solution.py:46
  10.9 19.8 %collective-permute-start.5 = (f32[2,256,256]{2,1,0:T(8,128)S(1)}, f32[2,256,256]{2,1,0:T(8,128)S(1)}, u32[]{:S(2)}, u32[]{:S(2)}) collective-permute-start(f32[2,256,256]{2,1,0:T(8,128)S(1)} %get-tuple-element.45), channel_id=1, source_target_pairs={{4,8},{8,4},{5,9},{9,5},{6,10},{10,6},{7,11},{11,7},{20,24},{24,20... | collective-permute-start | bytes 1572872 | tf_op jit(solution)/shard_map/ppermute | solution.py:46
  11.6 12.7 %collective-permute-start.4 = (f32[2,256,256]{2,1,0:T(8,128)S(1)}, f32[2,256,256]{2,1,0:T(8,128)S(1)}, u32[]{:S(2)}, u32[]{:S(2)}) collective-permute-start(f32[2,256,256]{2,1,0:T(8,128)S(1)} %get-tuple-element.45), channel_id=1, source_target_pairs={{12,14},{14,12},{13,15},{15,13},{28,30},{30,28},{29,31},{31,29}} | collective-permute-start | bytes 1572872 | tf_op jit(solution)/shard_map/ppermute | solution.py:53
  21.1 1.7 %copy-start.1 = (bf16[8,256,256]{2,1,0:T(8,128)(2,1)S(1)}, bf16[8,256,256]{2,1,0:T(8,128)(2,1)}, u32[]{:S(2)}) copy-start(bf16[8,256,256]{2,1,0:T(8,128)(2,1)} %constant.2.clone.pieces) | copy-start | bytes 3145732
  21.1 14.7 %copy-start = (f32[2,256,256]{2,1,0:T(8,128)S(1)}, f32[2,256,256]{2,1,0:T(8,128)}, u32[]{:S(2)}) copy-start(f32[2,256,256]{2,1,0:T(8,128)} %refs_2_.15) | copy-start | bytes 1572868
  21.1 14.7 %copy-start.3 = (s32[4,2]{0,1:T(2,128)S(1)}, s32[4,2]{0,1:T(2,128)}, u32[]{:S(2)}) copy-start(s32[4,2]{0,1:T(2,128)} %param.10) | copy-start | bytes 100
  21.8 14.1 %collective-permute-start.7 = (f32[2,256,256]{2,1,0:T(8,128)S(1)}, f32[2,256,256]{2,1,0:T(8,128)S(1)}, u32[]{:S(2)}, u32[]{:S(2)}) collective-permute-start(f32[2,256,256]{2,1,0:T(8,128)S(1)} %join.2), channel_id=1, source_target_pairs={{0,2},{2,0},{1,3},{3,1},{4,6},{6,4},{5,7},{7,5},{8,10},{10,8},{9,1... | collective-permute-start | bytes 1572872 | tf_op jit(solution)/shard_map/ppermute | solution.py:38
  22.1 21.8 %collective-permute-start.8 = (f32[3,256,256]{2,1,0:T(8,128)S(1)}, f32[3,256,256]{2,1,0:T(8,128)S(1)}, u32[]{:S(2)}, u32[]{:S(2)}) collective-permute-start(f32[3,256,256]{2,1,0:T(8,128)S(1)} %cut.7.refs_4_), channel_id=1, source_target_pairs={{4,8},{8,4},{5,9},{9,5},{6,10},{10,6},{7,11},{11,7},{20,24},{24,20... | collective-permute-start | bytes 2359304 | tf_op jit(solution)/shard_map/ppermute | solution.py:46
  24.3 7.2 %collective-permute-start.1 = (s32[2,4]{1,0:T(2,128)S(1)}, s32[2,4]{1,0:T(2,128)S(1)}, u32[]{:S(2)}, u32[]{:S(2)}) collective-permute-start(s32[2,4]{1,0:T(2,128)S(1)} %bitcast.8), channel_id=1, source_target_pairs={{0,1},{1,0},{2,3},{3,2},{4,5},{5,4},{6,7},{7,6},{8,9},{9,8},{10,11... | collective-permute-start | bytes 104 | tf_op jit(solution)/shard_map/ppermute | solution.py:38
  30.7 2.1 %collective-permute-start.2 = (s32[2,4]{1,0:T(2,128)S(1)}, s32[2,4]{1,0:T(2,128)S(1)}, u32[]{:S(2)}, u32[]{:S(2)}) collective-permute-start(s32[2,4]{1,0:T(2,128)S(1)} %collective-permute-done.refs_1_), channel_id=1, source_target_pairs={{0,1},{1,0},{2,3},{3,2},{4,5},{5,4},{6,7},{7,6},{8,9},{9,8},{10,11... | collective-permute-start | bytes 104 | tf_op jit(solution)/shard_map/ppermute | solution.py:38
  31.5 15.6 %collective-permute-start.9 = (f32[2,256,256]{2,1,0:T(8,128)S(1)}, f32[2,256,256]{2,1,0:T(8,128)S(1)}, u32[]{:S(2)}, u32[]{:S(2)}) collective-permute-start(f32[2,256,256]{2,1,0:T(8,128)S(1)} %join.3), channel_id=1, source_target_pairs={{0,2},{2,0},{1,3},{3,1},{4,6},{6,4},{5,7},{7,5},{8,10},{10,8},{9,1... | collective-permute-start | bytes 1572872 | tf_op jit(solution)/shard_map/ppermute | solution.py:38
  42.4 19.8 %collective-permute-start.10 = (f32[2,256,256]{2,1,0:T(8,128)S(1)}, f32[2,256,256]{2,1,0:T(8,128)S(1)}, u32[]{:S(2)}, u32[]{:S(2)}) collective-permute-start(f32[2,256,256]{2,1,0:T(8,128)S(1)} %get-tuple-element.56), channel_id=1, source_target_pairs={{0,2},{2,0},{1,3},{3,1},{4,6},{6,4},{5,7},{7,5},{8,10},{10,8},{9,1... | collective-permute-start | bytes 1572872 | tf_op jit(solution)/shard_map/ppermute | solution.py:38
  43.8 18.4 %collective-permute-start.11 = (f32[2,256,256]{2,1,0:T(8,128)S(1)}, f32[2,256,256]{2,1,0:T(8,128)S(1)}, u32[]{:S(2)}, u32[]{:S(2)}) collective-permute-start(f32[2,256,256]{2,1,0:T(8,128)S(1)} %get-tuple-element.51.refs_1_.refs_5_), channel_id=1, source_target_pairs={{0,4},{4,0},{8,12},{12,8},{1,5},{5,1},{9,13},{13,9},{2,6},{6,2},{1... | collective-permute-start | bytes 1572872 | tf_op jit(solution)/shard_map/ppermute | solution.py:46
  53.6 15.9 %collective-permute-start.14 = (f32[2,256,256]{2,1,0:T(8,128)S(1)}, f32[2,256,256]{2,1,0:T(8,128)S(1)}, u32[]{:S(2)}, u32[]{:S(2)}) collective-permute-start(f32[2,256,256]{2,1,0:T(8,128)S(1)} %get-tuple-element.53.refs_0_.refs_9_), channel_id=1, source_target_pairs={{4,8},{8,4},{5,9},{9,5},{6,10},{10,6},{7,11},{11,7},{20,24},{24,20... | collective-permute-start | bytes 1572872 | tf_op jit(solution)/shard_map/ppermute | solution.py:46
  54.3 15.2 %collective-permute-start.13 = (f32[2,256,256]{2,1,0:T(8,128)S(1)}, f32[2,256,256]{2,1,0:T(8,128)S(1)}, u32[]{:S(2)}, u32[]{:S(2)}) collective-permute-start(f32[2,256,256]{2,1,0:T(8,128)S(1)} %get-tuple-element.57), channel_id=1, source_target_pairs={{0,2},{2,0},{1,3},{3,1},{4,6},{6,4},{5,7},{7,5},{8,10},{10,8},{9,1... | collective-permute-start | bytes 1572872 | tf_op jit(solution)/shard_map/ppermute | solution.py:38
  62.4 14.5 %collective-permute-start.12 = (f32[4,2,256,256]{3,2,1,0:T(8,128)S(1)}, f32[4,2,256,256]{3,2,1,0:T(8,128)S(1)}, u32[]{:S(2)}, u32[]{:S(2)}) collective-permute-start(f32[4,2,256,256]{3,2,1,0:T(8,128)S(1)} %pack.2), channel_id=1, source_target_pairs={{0,1},{1,0},{2,3},{3,2},{4,5},{5,4},{6,7},{7,6},{8,9},{9,8},{10,11... | collective-permute-start | bytes 6291464 | tf_op jit(solution)/shard_map/ppermute | solution.py:38
  69.7 7.2 %collective-permute-start.15 = (f32[3,2,256,256]{3,2,1,0:T(8,128)S(1)}, f32[3,2,256,256]{3,2,1,0:T(8,128)S(1)}, u32[]{:S(2)}, u32[]{:S(2)}) collective-permute-start(f32[3,2,256,256]{3,2,1,0:T(8,128)S(1)} %pack.3), channel_id=1, source_target_pairs={{0,1},{1,0},{2,3},{3,2},{4,5},{5,4},{6,7},{7,6},{8,9},{9,8},{10,11... | collective-permute-start | bytes 4718600 | tf_op jit(solution)/shard_map/ppermute | solution.py:38
  73.0 10.8 %collective-permute-start.20 = (f32[2,256,256]{2,1,0:T(8,128)S(1)}, f32[2,256,256]{2,1,0:T(8,128)S(1)}, u32[]{:S(2)}, u32[]{:S(2)}) collective-permute-start(f32[2,256,256]{2,1,0:T(8,128)S(1)} %collective-permute-done.13.refs_1_.refs_10_), channel_id=1, source_target_pairs={{4,8},{8,4},{5,9},{9,5},{6,10},{10,6},{7,11},{11,7},{20,24},{24,20... | collective-permute-start | bytes 1572872 | tf_op jit(solution)/shard_map/ppermute | solution.py:46
  73.7 13.6 %collective-permute-start.18 = (f32[2,256,256]{2,1,0:T(8,128)S(1)}, f32[2,256,256]{2,1,0:T(8,128)S(1)}, u32[]{:S(2)}, u32[]{:S(2)}) collective-permute-start(f32[2,256,256]{2,1,0:T(8,128)S(1)} %collective-permute-done.10.refs_2_.refs_6_), channel_id=1, source_target_pairs={{0,4},{4,0},{8,12},{12,8},{1,5},{5,1},{9,13},{13,9},{2,6},{6,2},{1... | collective-permute-start | bytes 1572872 | tf_op jit(solution)/shard_map/ppermute | solution.py:46
  73.7 15.1 %collective-permute-start.16 = (f32[2,256,256]{2,1,0:T(8,128)S(1)}, f32[2,256,256]{2,1,0:T(8,128)S(1)}, u32[]{:S(2)}, u32[]{:S(2)}) collective-permute-start(f32[2,256,256]{2,1,0:T(8,128)S(1)} %get-tuple-element.60), channel_id=1, source_target_pairs={{12,14},{14,12},{13,15},{15,13},{28,30},{30,28},{29,31},{31,29}} | collective-permute-start | bytes 1572872 | tf_op jit(solution)/shard_map/ppermute | solution.py:53
  88.8 2.7 %collective-permute-start.17 = (f32[2,256,256]{2,1,0:T(8,128)S(1)}, f32[2,256,256]{2,1,0:T(8,128)S(1)}, u32[]{:S(2)}, u32[]{:S(2)}) collective-permute-start(f32[2,256,256]{2,1,0:T(8,128)S(1)} %collective-permute-done.16.refs_5_), channel_id=1, source_target_pairs={{0,1},{1,0},{2,3},{3,2},{4,5},{5,4},{6,7},{7,6},{8,9},{9,8},{10,11... | collective-permute-start | bytes 1572872 | tf_op jit(solution)/shard_map/ppermute | solution.py:38
  90.0 2.3 %collective-permute-start.19 = (f32[2,256,256]{2,1,0:T(8,128)S(1)}, f32[2,256,256]{2,1,0:T(8,128)S(1)}, u32[]{:S(2)}, u32[]{:S(2)}) collective-permute-start(f32[2,256,256]{2,1,0:T(8,128)S(1)} %collective-permute-done.18.refs_7_), channel_id=1, source_target_pairs={{0,1},{1,0},{2,3},{3,2},{4,5},{5,4},{6,7},{7,6},{8,9},{9,8},{10,11... | collective-permute-start | bytes 1572872 | tf_op jit(solution)/shard_map/ppermute | solution.py:38
  90.0 3.0 %collective-permute-start.21 = (f32[2,256,256]{2,1,0:T(8,128)S(1)}, f32[2,256,256]{2,1,0:T(8,128)S(1)}, u32[]{:S(2)}, u32[]{:S(2)}) collective-permute-start(f32[2,256,256]{2,1,0:T(8,128)S(1)} %collective-permute-done.20.refs_9_), channel_id=1, source_target_pairs={{0,1},{1,0},{2,3},{3,2},{4,5},{5,4},{6,7},{7,6},{8,9},{9,8},{10,11... | collective-permute-start | bytes 1572872 | tf_op jit(solution)/shard_map/ppermute | solution.py:38

commit v13 on v10

--- a/solution.py
+++ b/solution.py
@@ -86,8 +86,8 @@
                 outs[which][pl.ds(row * side, side), pl.ds(column * side, side)] = block
 
 
-def expand(side):
-    pieces = jnp.asarray(compact_tables(side))
+def expand(side, *gates):
+    pieces = after(jnp.asarray(compact_tables(side)), *gates)
     return pl.pallas_call(
         expand_kernel,
         in_specs=[VMEM],
@@ -570,7 +570,6 @@
     for k, role, send_role, there, home in rounds:
         spots = [("slot", role, k, d) for d in distances]
         held.append(step(lambda p: cut(spots, layout, p, phase, absorption)))
-    constants = expand(side)
     others = []
     for i, (k, role, send_role, there, home) in enumerate(rounds):
         joined = []
@@ -579,7 +578,8 @@
             joined.append(step(lambda p: join(spot, layout, p, held[i][d], got[i][d])))
         others.append([rotate(joined[d - 1], "slab", d) for d in far])
         if i == 0:
-            done += [value for row in extra for value in row]
+            constants = expand(side, *done, *[value for row in extra for value in row])
+            done[:] = [constants[0]]
 
     twin_tables = [rotate(table, "batch", 1) for table in tables]
     done += twin_tables

time: 96.2 us -> 96.1 us (level)
    ppermute x12, starting transfers between devices: 22.2 us -> 21.1 us  [rotate(): lax.ppermute(block, axis, [(i, (i + distance) % size) for i in range(size)])]
  transfers between devices with their start and end apart: 24 -> 24, of which waited for: 12 -> 11; matrix products, arithmetic and copies ran while one was open for 0% -> 0% of each run, Pallas kernels for 39% -> 39%
where the time goes in v13:
time: 96.1 us; the launch traced here: 95.5 us
  Pallas kernels  42.8 us (45%)
  starting transfers between devices  36 us (37%)
  waiting for transfers between devices  15.6 us (16%)
    ppermute x12, starting transfers between devices, rotate(): lax.ppermute(block, axis, [(i, (i + distance) % size) for i in range(size)])  21.1 us
    pallas_call x3, Pallas kernels, run_slot(): pl.pallas_call(lambda *refs: slot_kernel(kind, spot, layout, len(tables),...  20.2 us
    pallas_call x5, Pallas kernels, cut(): pl.pallas_call(lambda *refs: cut_kernel(spots, layout, measured is not No...  10.7 us
    ppermute x10, starting transfers between devices, swap(): return lax.ppermute(block, axis, route)  8.73 us
    pallas_call x1, Pallas kernels, early(): pl.pallas_call(lambda *refs: early_kernel(metas, layout, *refs), in_specs...  6.94 us
    ppermute x10, waiting for transfers between devices, swap(): return lax.ppermute(block, axis, route)  6.88 us
    ppermute x2, starting transfers between devices, rotate_last(): return lax.ppermute(block, ('tile', 'slab'), route)  6.19 us
    ppermute x12, waiting for transfers between devices, rotate(): lax.ppermute(block, axis, [(i, (i + distance) % size) for i in range(size)])  5.89 us
  transfers between devices with their start and end apart: 24, of which 11 were waited for; matrix products, arithmetic and copies ran while one was open for 0% of the time, Pallas kernels for 39%

profile of v13, /device:TPU:29, one launch (start us, length us, event | category | flops | bytes accessed | tf_op | source)
XLA Modules:
  0.0 95.5 jit_solution(7411660260743670200)
XLA Ops:
  0.0 0.6 collective-permute-start.1
  0.7 1.7 %collective-permute-start = (s32[2,4]{1,0:T(2,128)}, s32[2,4]{1,0:T(2,128)S(1)}, u32[]{:S(2)}, u32[]{:S(2)}) collective-permute-start(s32[2,4]{1,0:T(2,128)} %bitcast.2), channel_id=1, source_target_pairs={{0,4},{4,0},{8,12},{12,8},{1,5},{5,1},{9,13},{13,9},{2,6},{6,2},{1... | collective-permute-start | bytes 104 | tf_op jit(solution)/shard_map/ppermute | solution.py:46
  2.3 1.2 %collective-permute-done.refs_1_ = s32[2,4]{1,0:T(2,128)S(1)} collective-permute-done((s32[2,4]{1,0:T(2,128)}, s32[2,4]{1,0:T(2,128)S(1)}, u32[]{:S(2)}, u32[]{:S(2)}) %collective-permute-start) | collective-permute-done | bytes 64 | tf_op jit(solution)/shard_map/ppermute | solution.py:46
  3.5 0.7 copy-done.2
  4.2 2.2 %cut.5 = (f32[2,256,256]{2,1,0:T(8,128)S(1)}, f32[2,256,256]{2,1,0:T(8,128)S(1)}) custom-call(s32[2,4]{1,0:T(2,128)S(1)} %bitcast.3, s32[2,4]{1,0:T(2,128)S(1)} %collective-permute-done.refs_1_, s32[2,4]{1,0:T(2,128)S(1)} %collective-permute-done.1.refs_2_, f32[1,256,4096]{2,1,0:T(8,128)} %refs_3_.12, f32[1,256,4096]{2,1,0:T(8,128)} %refs_4_.12), custom_call_target="tpu_custom_call" | custom-call | tf_op jit(solution)/shard_map/cut/pallas_call | solution.py:328
  6.4 1.5 %collective-permute-start.5 = (f32[2,256,256]{2,1,0:T(8,128)S(1)}, f32[2,256,256]{2,1,0:T(8,128)S(1)}, u32[]{:S(2)}, u32[]{:S(2)}) collective-permute-start(f32[2,256,256]{2,1,0:T(8,128)S(1)} %get-tuple-element.37), channel_id=1, source_target_pairs={{0,4},{4,0},{8,12},{12,8},{1,5},{5,1},{9,13},{13,9},{2,6},{6,2},{1... | collective-permute-start | bytes 1572872 | tf_op jit(solution)/shard_map/ppermute | solution.py:46
  7.9 1.9 %cut.6 = f32[3,256,256]{2,1,0:T(8,128)S(1)} custom-call(s32[2,4]{1,0:T(2,128)S(1)} %bitcast.4, s32[2,4]{1,0:T(2,128)S(1)} %collective-permute-done.refs_1_, s32[2,4]{1,0:T(2,128)S(1)} %collective-permute-done.1.refs_2_, f32[1,256,4096]{2,1,0:T(8,128)} %refs_3_.12, f32[1,256,4096]{2,1,0:T(8,128)} %refs_4_.12, f32[4,256,256]{2,1,0:T(8,128)} %refs_4_.15), custom_call_target="tpu_custom_call" | custom-call | tf_op jit(solution)/shard_map/cut/pallas_call | solution.py:328
  10.0 3.1 %collective-permute-start.6 = (f32[2,256,256]{2,1,0:T(8,128)S(1)}, f32[2,256,256]{2,1,0:T(8,128)S(1)}, u32[]{:S(2)}, u32[]{:S(2)}) collective-permute-start(f32[2,256,256]{2,1,0:T(8,128)S(1)} %get-tuple-element.46), channel_id=1, source_target_pairs={{12,14},{14,12},{13,15},{15,13},{28,30},{30,28},{29,31},{31,29}} | collective-permute-start | bytes 1572872 | tf_op jit(solution)/shard_map/ppermute | solution.py:53
  13.1 0.7 collective-permute-start.7
  13.8 1.9 %cut.7.refs_5_ = f32[3,256,256]{2,1,0:T(8,128)S(1)} custom-call(s32[2,4]{1,0:T(2,128)S(1)} %bitcast.5, s32[2,4]{1,0:T(2,128)S(1)} %collective-permute-done.refs_1_, s32[2,4]{1,0:T(2,128)S(1)} %collective-permute-done.1.refs_2_, f32[1,256,4096]{2,1,0:T(8,128)} %refs_3_.12, f32[1,256,4096]{2,1,0:T(8,128)} %refs_4_.12, f32[4,256,256]{2,1,0:T(8,128)} %refs_4_.15), custom_call_target="tpu_custom_call" | custom-call | tf_op jit(solution)/shard_map/cut/pallas_call | solution.py:328
  15.7 2.4 %cut.8 = (f32[2,256,256]{2,1,0:T(8,128)S(1)}, f32[2,256,256]{2,1,0:T(8,128)S(1)}) custom-call(s32[2,4]{1,0:T(2,128)S(1)} %bitcast.6, s32[2,4]{1,0:T(2,128)S(1)} %collective-permute-done.refs_1_, s32[2,4]{1,0:T(2,128)S(1)} %collective-permute-done.1.refs_2_, f32[1,256,4096]{2,1,0:T(8,128)} %refs_3_.12, f32[1,256,4096]{2,1,0:T(8,128)} %refs_4_.12), custom_call_target="tpu_custom_call" | custom-call | tf_op jit(solution)/shard_map/cut/pallas_call | solution.py:328
  18.1 2.2 %cut.9 = (f32[2,256,256]{2,1,0:T(8,128)S(1)}, f32[2,256,256]{2,1,0:T(8,128)S(1)}) custom-call(s32[2,4]{1,0:T(2,128)S(1)} %bitcast.7, s32[2,4]{1,0:T(2,128)S(1)} %collective-permute-done.refs_1_, s32[2,4]{1,0:T(2,128)S(1)} %collective-permute-done.1.refs_2_, f32[1,256,4096]{2,1,0:T(8,128)} %refs_3_.12, f32[1,256,4096]{2,1,0:T(8,128)} %refs_4_.12), custom_call_target="tpu_custom_call" | custom-call | tf_op jit(solution)/shard_map/cut/pallas_call | solution.py:328
  20.4 0.7 join.2
  21.0 0.3 collective-permute-start.9
  21.3 0.7 collective-permute-start.10
  22.1 0.8 collective-permute-done.6.refs_6_
  22.8 5.2 %collective-permute-start.2 = (s32[2,4]{1,0:T(2,128)S(1)}, s32[2,4]{1,0:T(2,128)S(1)}, u32[]{:S(2)}, u32[]{:S(2)}) collective-permute-start(s32[2,4]{1,0:T(2,128)S(1)} %bitcast.9), channel_id=1, source_target_pairs={{0,1},{1,0},{2,3},{3,2},{4,5},{5,4},{6,7},{7,6},{8,9},{9,8},{10,11... | collective-permute-start | bytes 104 | tf_op jit(solution)/shard_map/ppermute | solution.py:38
  28.1 0.2 expand.1
  28.4 0.7 join.3
  29.1 0.6 collective-permute-start.3
  29.6 2.2 %collective-permute-start.11 = (f32[2,256,256]{2,1,0:T(8,128)S(1)}, f32[2,256,256]{2,1,0:T(8,128)S(1)}, u32[]{:S(2)}, u32[]{:S(2)}) collective-permute-start(f32[2,256,256]{2,1,0:T(8,128)S(1)} %join.3), channel_id=1, source_target_pairs={{0,2},{2,0},{1,3},{3,1},{4,6},{6,4},{5,7},{7,5},{8,10},{10,8},{9,1... | collective-permute-start | bytes 1572872 | tf_op jit(solution)/shard_map/ppermute | solution.py:38
  31.8 3.0 %collective-permute-done.8.refs_6_ = f32[3,256,256]{2,1,0:T(8,128)S(1)} collective-permute-done((f32[3,256,256]{2,1,0:T(8,128)S(1)}, f32[3,256,256]{2,1,0:T(8,128)S(1)}, u32[]{:S(2)}, u32[]{:S(2)}) %collective-permute-start.8) | collective-permute-done | bytes 786464 | tf_op jit(solution)/shard_map/ppermute | solution.py:46
  34.9 0.2 collective-permute-done.9.refs_7_
  35.1 6.7 %slot_0.1 = (f32[2,256,256]{2,1,0:T(8,128)S(1)}, f32[2,256,256]{2,1,0:T(8,128)S(1)}) custom-call(s32[2,4]{1,0:T(2,128)S(1)} %bitcast.11, s32[2,4]{1,0:T(2,128)S(1)} %collective-permute-done.refs_1_, s32[2,4]{1,0:T(2,128)S(1)} %collective-permute-done.1.refs_2_, f32[2,256,256]{2,1,0:T(8,128)S(1)} %copy-done, f32[4,256,256]{2,1,0:T(8,128)} %refs_4_.15, ...), custom_call_target="tpu_custom_call" | custom-call | tf_op jit(solution)/shard_map/slot_0/pallas_call | solution.py:260
  41.8 1.1 %collective-permute-start.12 = (f32[2,256,256]{2,1,0:T(8,128)S(1)}, f32[2,256,256]{2,1,0:T(8,128)S(1)}, u32[]{:S(2)}, u32[]{:S(2)}) collective-permute-start(f32[2,256,256]{2,1,0:T(8,128)S(1)} %get-tuple-element.58), channel_id=1, source_target_pairs={{0,2},{2,0},{1,3},{3,1},{4,6},{6,4},{5,7},{7,5},{8,10},{10,8},{9,1... | collective-permute-start | bytes 1572872 | tf_op jit(solution)/shard_map/ppermute | solution.py:38
  42.9 1.2 %collective-permute-start.13 = (f32[2,256,256]{2,1,0:T(8,128)S(1)}, f32[2,256,256]{2,1,0:T(8,128)S(1)}, u32[]{:S(2)}, u32[]{:S(2)}) collective-permute-start(f32[2,256,256]{2,1,0:T(8,128)S(1)} %get-tuple-element.53.refs_1_.refs_7_), channel_id=1, source_target_pairs={{0,4},{4,0},{8,12},{12,8},{1,5},{5,1},{9,13},{13,9},{2,6},{6,2},{1... | collective-permute-start | bytes 1572872 | tf_op jit(solution)/shard_map/ppermute | solution.py:46
  44.1 2.2 %collective-permute-done.11.refs_7_ = f32[2,256,256]{2,1,0:T(8,128)S(1)} collective-permute-done((f32[2,256,256]{2,1,0:T(8,128)S(1)}, f32[2,256,256]{2,1,0:T(8,128)S(1)}, u32[]{:S(2)}, u32[]{:S(2)}) %collective-permute-start.11) | collective-permute-done | bytes 524320 | tf_op jit(solution)/shard_map/ppermute | solution.py:38
  46.3 6.7 %slot_1.1 = (f32[2,256,256]{2,1,0:T(8,128)S(1)}, f32[2,256,256]{2,1,0:T(8,128)S(1)}) custom-call(s32[2,4]{1,0:T(2,128)S(1)} %bitcast.12, s32[2,4]{1,0:T(2,128)S(1)} %collective-permute-done.refs_1_, s32[2,4]{1,0:T(2,128)S(1)} %collective-permute-done.1.refs_2_, f32[2,256,256]{2,1,0:T(8,128)S(1)} %copy-done, f32[4,256,256]{2,1,0:T(8,128)} %refs_4_.15, ...), custom_call_target="tpu_custom_call" | custom-call | tf_op jit(solution)/shard_map/slot_1/pallas_call | solution.py:260
  53.0 0.7 collective-permute-start.16
  53.7 0.3 collective-permute-start.15
  54.0 6.8 %slot_last.1 = (f32[2,256,256]{2,1,0:T(8,128)S(1)}, f32[2,256,256]{2,1,0:T(8,128)S(1)}) custom-call(s32[2,4]{1,0:T(2,128)S(1)} %bitcast.13, s32[2,4]{1,0:T(2,128)S(1)} %collective-permute-done.refs_1_, s32[2,4]{1,0:T(2,128)S(1)} %collective-permute-done.1.refs_2_, f32[2,256,256]{2,1,0:T(8,128)S(1)} %copy-done, f32[4,256,256]{2,1,0:T(8,128)} %refs_4_.15, ...), custom_call_target="tpu_custom_call" | custom-call | tf_op jit(solution)/shard_map/slot_last/pallas_call | solution.py:260
  60.9 0.1 pack.2
  61.0 6.5 %collective-permute-start.14 = (f32[4,2,256,256]{3,2,1,0:T(8,128)S(1)}, f32[4,2,256,256]{3,2,1,0:T(8,128)S(1)}, u32[]{:S(2)}, u32[]{:S(2)}) collective-permute-start(f32[4,2,256,256]{3,2,1,0:T(8,128)S(1)} %pack.2), channel_id=1, source_target_pairs={{0,1},{1,0},{2,3},{3,2},{4,5},{5,4},{6,7},{7,6},{8,9},{9,8},{10,11... | collective-permute-start | bytes 6291464 | tf_op jit(solution)/shard_map/ppermute | solution.py:38
  67.6 0.9 collective-permute-done.15.refs_1_.refs_12_
  68.5 0.1 pack.3
  68.6 2.7 %collective-permute-start.17 = (f32[3,2,256,256]{3,2,1,0:T(8,128)S(1)}, f32[3,2,256,256]{3,2,1,0:T(8,128)S(1)}, u32[]{:S(2)}, u32[]{:S(2)}) collective-permute-start(f32[3,2,256,256]{3,2,1,0:T(8,128)S(1)} %pack.3), channel_id=1, source_target_pairs={{0,1},{1,0},{2,3},{3,2},{4,5},{5,4},{6,7},{7,6},{8,9},{9,8},{10,11... | collective-permute-start | bytes 4718600 | tf_op jit(solution)/shard_map/ppermute | solution.py:38
  71.3 0.7 collective-permute-start.22
  72.0 0.9 collective-permute-start.20
  72.8 3.1 %collective-permute-start.18 = (f32[2,256,256]{2,1,0:T(8,128)S(1)}, f32[2,256,256]{2,1,0:T(8,128)S(1)}, u32[]{:S(2)}, u32[]{:S(2)}) collective-permute-start(f32[2,256,256]{2,1,0:T(8,128)S(1)} %get-tuple-element.62), channel_id=1, source_target_pairs={{12,14},{14,12},{13,15},{15,13},{28,30},{30,28},{29,31},{31,29}} | collective-permute-start | bytes 1572872 | tf_op jit(solution)/shard_map/ppermute | solution.py:53
  76.0 6.9 %early.1 = (f32[2,256,4096]{2,1,0:T(8,128)S(1)}, f32[2,1,256,4096]{3,2,1,0:T(8,128)}) custom-call(s32[2,4]{1,0:T(2,128)S(1)} %bitcast.14, s32[2,4]{1,0:T(2,128)S(1)} %collective-permute-done.refs_1_, s32[2,4]{1,0:T(2,128)S(1)} %collective-permute-done.1.refs_2_, s32[2,4]{1,0:T(2,128)S(1)} %collective-permute-done.2.refs_3_, ...), custom_call_target="tpu_custom_call" | custom-call | tf_op jit(solution)/shard_map/early/pallas_call | solution.py:433
  82.9 2.7 %collective-permute-done.20.refs_9_ = f32[2,256,256]{2,1,0:T(8,128)S(1)} collective-permute-done((f32[2,256,256]{2,1,0:T(8,128)S(1)}, f32[2,256,256]{2,1,0:T(8,128)S(1)}, u32[]{:S(2)}, u32[]{:S(2)}) %collective-permute-start.20) | collective-permute-done | bytes 524320 | tf_op jit(solution)/shard_map/ppermute | solution.py:46
  85.6 2.0 %collective-permute-done.18.refs_7_ = f32[2,256,256]{2,1,0:T(8,128)S(1)} collective-permute-done((f32[2,256,256]{2,1,0:T(8,128)S(1)}, f32[2,256,256]{2,1,0:T(8,128)S(1)}, u32[]{:S(2)}, u32[]{:S(2)}) %collective-permute-start.18) | collective-permute-done | bytes 524320 | tf_op jit(solution)/shard_map/ppermute | solution.py:53
  87.6 1.4 %collective-permute-start.19 = (f32[2,256,256]{2,1,0:T(8,128)S(1)}, f32[2,256,256]{2,1,0:T(8,128)S(1)}, u32[]{:S(2)}, u32[]{:S(2)}) collective-permute-start(f32[2,256,256]{2,1,0:T(8,128)S(1)} %collective-permute-done.18.refs_7_), channel_id=1, source_target_pairs={{0,1},{1,0},{2,3},{3,2},{4,5},{5,4},{6,7},{7,6},{8,9},{9,8},{10,11... | collective-permute-start | bytes 1572872 | tf_op jit(solution)/shard_map/ppermute | solution.py:38
  89.1 0.5 collective-permute-start.23
  89.6 1.0 %collective-permute-done.19.refs_8_ = f32[2,256,256]{2,1,0:T(8,128)S(1)} collective-permute-done((f32[2,256,256]{2,1,0:T(8,128)S(1)}, f32[2,256,256]{2,1,0:T(8,128)S(1)}, u32[]{:S(2)}, u32[]{:S(2)}) %collective-permute-start.19) | collective-permute-done | bytes 524320 | tf_op jit(solution)/shard_map/ppermute | solution.py:38
  90.6 0.7 collective-permute-done.21.refs_10_
  91.4 0.7 collective-permute-done.23.refs_12_
  92.1 3.3 %late.1 = f32[2,1,256,4096]{3,2,1,0:T(8,128)} custom-call(s32[2,4]{1,0:T(2,128)S(1)} %bitcast.15, s32[2,4]{1,0:T(2,128)S(1)} %collective-permute-done.refs_1_, s32[2,4]{1,0:T(2,128)S(1)} %collective-permute-done.1.refs_2_, s32[2,4]{1,0:T(2,128)S(1)} %collective-permute-done.2.refs_3_, ...), custom_call_target="tpu_custom_call", output_to_operand_aliasing={{}: (13, {})} | custom-call | tf_op jit(solution)/shard_map/late/pallas_call | solution.py:498
  (23 shorter events, 0.2 us)
Async XLA Ops:
  0.0 2.3 %collective-permute-start.1 = (s32[2,4]{1,0:T(2,128)}, s32[2,4]{1,0:T(2,128)S(1)}, u32[]{:S(2)}, u32[]{:S(2)}) collective-permute-start(s32[2,4]{1,0:T(2,128)} %bitcast.1), channel_id=1, source_target_pairs={{4,8},{8,4},{5,9},{9,5},{6,10},{10,6},{7,11},{11,7},{20,24},{24,20... | collective-permute-start | bytes 104 | tf_op jit(solution)/shard_map/ppermute | solution.py:46
  0.7 2.8 %collective-permute-start = (s32[2,4]{1,0:T(2,128)}, s32[2,4]{1,0:T(2,128)S(1)}, u32[]{:S(2)}, u32[]{:S(2)}) collective-permute-start(s32[2,4]{1,0:T(2,128)} %bitcast.2), channel_id=1, source_target_pairs={{0,4},{4,0},{8,12},{12,8},{1,5},{5,1},{9,13},{13,9},{2,6},{6,2},{1... | collective-permute-start | bytes 104 | tf_op jit(solution)/shard_map/ppermute | solution.py:46
  3.5 0.7 copy-start.2
  6.4 13.9 %collective-permute-start.5 = (f32[2,256,256]{2,1,0:T(8,128)S(1)}, f32[2,256,256]{2,1,0:T(8,128)S(1)}, u32[]{:S(2)}, u32[]{:S(2)}) collective-permute-start(f32[2,256,256]{2,1,0:T(8,128)S(1)} %get-tuple-element.37), channel_id=1, source_target_pairs={{0,4},{4,0},{8,12},{12,8},{1,5},{5,1},{9,13},{13,9},{2,6},{6,2},{1... | collective-permute-start | bytes 1572872 | tf_op jit(solution)/shard_map/ppermute | solution.py:46
  9.9 25.0 %collective-permute-start.8 = (f32[3,256,256]{2,1,0:T(8,128)S(1)}, f32[3,256,256]{2,1,0:T(8,128)S(1)}, u32[]{:S(2)}, u32[]{:S(2)}) collective-permute-start(f32[3,256,256]{2,1,0:T(8,128)S(1)} %cut.6), channel_id=1, source_target_pairs={{0,4},{4,0},{8,12},{12,8},{1,5},{5,1},{9,13},{13,9},{2,6},{6,2},{1... | collective-permute-start | bytes 2359304 | tf_op jit(solution)/shard_map/ppermute | solution.py:46
  10.0 12.9 %collective-permute-start.6 = (f32[2,256,256]{2,1,0:T(8,128)S(1)}, f32[2,256,256]{2,1,0:T(8,128)S(1)}, u32[]{:S(2)}, u32[]{:S(2)}) collective-permute-start(f32[2,256,256]{2,1,0:T(8,128)S(1)} %get-tuple-element.46), channel_id=1, source_target_pairs={{12,14},{14,12},{13,15},{15,13},{28,30},{30,28},{29,31},{31,29}} | collective-permute-start | bytes 1572872 | tf_op jit(solution)/shard_map/ppermute | solution.py:53
  13.1 15.2 %collective-permute-start.7 = (f32[2,256,256]{2,1,0:T(8,128)S(1)}, f32[2,256,256]{2,1,0:T(8,128)S(1)}, u32[]{:S(2)}, u32[]{:S(2)}) collective-permute-start(f32[2,256,256]{2,1,0:T(8,128)S(1)} %get-tuple-element.46), channel_id=1, source_target_pairs={{4,8},{8,4},{5,9},{9,5},{6,10},{10,6},{7,11},{11,7},{20,24},{24,20... | collective-permute-start | bytes 1572872 | tf_op jit(solution)/shard_map/ppermute | solution.py:46
  20.3 7.8 %copy-start.1 = (bf16[8,256,256]{2,1,0:T(8,128)(2,1)S(1)}, bf16[8,256,256]{2,1,0:T(8,128)(2,1)}, u32[]{:S(2)}) copy-start(bf16[8,256,256]{2,1,0:T(8,128)(2,1)} %constant.2.clone.pieces) | copy-start | bytes 3145732
  20.3 14.8 %copy-start = (f32[2,256,256]{2,1,0:T(8,128)S(1)}, f32[2,256,256]{2,1,0:T(8,128)}, u32[]{:S(2)}) copy-start(f32[2,256,256]{2,1,0:T(8,128)} %refs_3_.15) | copy-start | bytes 1572868
  20.4 14.8 %copy-start.3 = (s32[4,2]{0,1:T(2,128)S(1)}, s32[4,2]{0,1:T(2,128)}, u32[]{:S(2)}) copy-start(s32[4,2]{0,1:T(2,128)} %param.10) | copy-start | bytes 100
  21.0 14.1 %collective-permute-start.9 = (f32[2,256,256]{2,1,0:T(8,128)S(1)}, f32[2,256,256]{2,1,0:T(8,128)S(1)}, u32[]{:S(2)}, u32[]{:S(2)}) collective-permute-start(f32[2,256,256]{2,1,0:T(8,128)S(1)} %join.2), channel_id=1, source_target_pairs={{0,2},{2,0},{1,3},{3,1},{4,6},{6,4},{5,7},{7,5},{8,10},{10,8},{9,1... | collective-permute-start | bytes 1572872 | tf_op jit(solution)/shard_map/ppermute | solution.py:38
  21.3 22.7 %collective-permute-start.10 = (f32[3,256,256]{2,1,0:T(8,128)S(1)}, f32[3,256,256]{2,1,0:T(8,128)S(1)}, u32[]{:S(2)}, u32[]{:S(2)}) collective-permute-start(f32[3,256,256]{2,1,0:T(8,128)S(1)} %cut.7.refs_5_), channel_id=1, source_target_pairs={{4,8},{8,4},{5,9},{9,5},{6,10},{10,6},{7,11},{11,7},{20,24},{24,20... | collective-permute-start | bytes 2359304 | tf_op jit(solution)/shard_map/ppermute | solution.py:46
  22.8 6.2 %collective-permute-start.2 = (s32[2,4]{1,0:T(2,128)S(1)}, s32[2,4]{1,0:T(2,128)S(1)}, u32[]{:S(2)}, u32[]{:S(2)}) collective-permute-start(s32[2,4]{1,0:T(2,128)S(1)} %bitcast.9), channel_id=1, source_target_pairs={{0,1},{1,0},{2,3},{3,2},{4,5},{5,4},{6,7},{7,6},{8,9},{9,8},{10,11... | collective-permute-start | bytes 104 | tf_op jit(solution)/shard_map/ppermute | solution.py:38
  28.3 1.3 %collective-permute-start.4 = (s32[2,4]{1,0:T(2,128)S(1)}, s32[2,4]{1,0:T(2,128)S(1)}, u32[]{:S(2)}, u32[]{:S(2)}) collective-permute-start(s32[2,4]{1,0:T(2,128)S(1)} %collective-permute-done.1.refs_2_), channel_id=1, source_target_pairs={{0,1},{1,0},{2,3},{3,2},{4,5},{5,4},{6,7},{7,6},{8,9},{9,8},{10,11... | collective-permute-start | bytes 104 | tf_op jit(solution)/shard_map/ppermute | solution.py:38
  29.1 2.8 %collective-permute-start.3 = (s32[2,4]{1,0:T(2,128)S(1)}, s32[2,4]{1,0:T(2,128)S(1)}, u32[]{:S(2)}, u32[]{:S(2)}) collective-permute-start(s32[2,4]{1,0:T(2,128)S(1)} %collective-permute-done.refs_1_), channel_id=1, source_target_pairs={{0,1},{1,0},{2,3},{3,2},{4,5},{5,4},{6,7},{7,6},{8,9},{9,8},{10,11... | collective-permute-start | bytes 104 | tf_op jit(solution)/shard_map/ppermute | solution.py:38
  29.6 16.7 %collective-permute-start.11 = (f32[2,256,256]{2,1,0:T(8,128)S(1)}, f32[2,256,256]{2,1,0:T(8,128)S(1)}, u32[]{:S(2)}, u32[]{:S(2)}) collective-permute-start(f32[2,256,256]{2,1,0:T(8,128)S(1)} %join.3), channel_id=1, source_target_pairs={{0,2},{2,0},{1,3},{3,1},{4,6},{6,4},{5,7},{7,5},{8,10},{10,8},{9,1... | collective-permute-start | bytes 1572872 | tf_op jit(solution)/shard_map/ppermute | solution.py:38
  41.8 19.1 %collective-permute-start.12 = (f32[2,256,256]{2,1,0:T(8,128)S(1)}, f32[2,256,256]{2,1,0:T(8,128)S(1)}, u32[]{:S(2)}, u32[]{:S(2)}) collective-permute-start(f32[2,256,256]{2,1,0:T(8,128)S(1)} %get-tuple-element.58), channel_id=1, source_target_pairs={{0,2},{2,0},{1,3},{3,1},{4,6},{6,4},{5,7},{7,5},{8,10},{10,8},{9,1... | collective-permute-start | bytes 1572872 | tf_op jit(solution)/shard_map/ppermute | solution.py:38
  42.9 18.0 %collective-permute-start.13 = (f32[2,256,256]{2,1,0:T(8,128)S(1)}, f32[2,256,256]{2,1,0:T(8,128)S(1)}, u32[]{:S(2)}, u32[]{:S(2)}) collective-permute-start(f32[2,256,256]{2,1,0:T(8,128)S(1)} %get-tuple-element.53.refs_1_.refs_7_), channel_id=1, source_target_pairs={{0,4},{4,0},{8,12},{12,8},{1,5},{5,1},{9,13},{13,9},{2,6},{6,2},{1... | collective-permute-start | bytes 1572872 | tf_op jit(solution)/shard_map/ppermute | solution.py:46
  53.0 15.4 %collective-permute-start.16 = (f32[2,256,256]{2,1,0:T(8,128)S(1)}, f32[2,256,256]{2,1,0:T(8,128)S(1)}, u32[]{:S(2)}, u32[]{:S(2)}) collective-permute-start(f32[2,256,256]{2,1,0:T(8,128)S(1)} %get-tuple-element.55.refs_0_.refs_11_), channel_id=1, source_target_pairs={{4,8},{8,4},{5,9},{9,5},{6,10},{10,6},{7,11},{11,7},{20,24},{24,20... | collective-permute-start | bytes 1572872 | tf_op jit(solution)/shard_map/ppermute | solution.py:46
  53.7 14.7 %collective-permute-start.15 = (f32[2,256,256]{2,1,0:T(8,128)S(1)}, f32[2,256,256]{2,1,0:T(8,128)S(1)}, u32[]{:S(2)}, u32[]{:S(2)}) collective-permute-start(f32[2,256,256]{2,1,0:T(8,128)S(1)} %get-tuple-element.59), channel_id=1, source_target_pairs={{0,2},{2,0},{1,3},{3,1},{4,6},{6,4},{5,7},{7,5},{8,10},{10,8},{9,1... | collective-permute-start | bytes 1572872 | tf_op jit(solution)/shard_map/ppermute | solution.py:38
  61.0 14.9 %collective-permute-start.14 = (f32[4,2,256,256]{3,2,1,0:T(8,128)S(1)}, f32[4,2,256,256]{3,2,1,0:T(8,128)S(1)}, u32[]{:S(2)}, u32[]{:S(2)}) collective-permute-start(f32[4,2,256,256]{3,2,1,0:T(8,128)S(1)} %pack.2), channel_id=1, source_target_pairs={{0,1},{1,0},{2,3},{3,2},{4,5},{5,4},{6,7},{7,6},{8,9},{9,8},{10,11... | collective-permute-start | bytes 6291464 | tf_op jit(solution)/shard_map/ppermute | solution.py:38
  68.6 7.4 %collective-permute-start.17 = (f32[3,2,256,256]{3,2,1,0:T(8,128)S(1)}, f32[3,2,256,256]{3,2,1,0:T(8,128)S(1)}, u32[]{:S(2)}, u32[]{:S(2)}) collective-permute-start(f32[3,2,256,256]{3,2,1,0:T(8,128)S(1)} %pack.3), channel_id=1, source_target_pairs={{0,1},{1,0},{2,3},{3,2},{4,5},{5,4},{6,7},{7,6},{8,9},{9,8},{10,11... | collective-permute-start | bytes 4718600 | tf_op jit(solution)/shard_map/ppermute | solution.py:38
  71.3 11.6 %collective-permute-start.22 = (f32[2,256,256]{2,1,0:T(8,128)S(1)}, f32[2,256,256]{2,1,0:T(8,128)S(1)}, u32[]{:S(2)}, u32[]{:S(2)}) collective-permute-start(f32[2,256,256]{2,1,0:T(8,128)S(1)} %collective-permute-done.15.refs_1_.refs_12_), channel_id=1, source_target_pairs={{4,8},{8,4},{5,9},{9,5},{6,10},{10,6},{7,11},{11,7},{20,24},{24,20... | collective-permute-start | bytes 1572872 | tf_op jit(solution)/shard_map/ppermute | solution.py:46
  72.0 13.6 %collective-permute-start.20 = (f32[2,256,256]{2,1,0:T(8,128)S(1)}, f32[2,256,256]{2,1,0:T(8,128)S(1)}, u32[]{:S(2)}, u32[]{:S(2)}) collective-permute-start(f32[2,256,256]{2,1,0:T(8,128)S(1)} %collective-permute-done.12.refs_2_.refs_8_), channel_id=1, source_target_pairs={{0,4},{4,0},{8,12},{12,8},{1,5},{5,1},{9,13},{13,9},{2,6},{6,2},{1... | collective-permute-start | bytes 1572872 | tf_op jit(solution)/shard_map/ppermute | solution.py:46
  72.8 14.8 %collective-permute-start.18 = (f32[2,256,256]{2,1,0:T(8,128)S(1)}, f32[2,256,256]{2,1,0:T(8,128)S(1)}, u32[]{:S(2)}, u32[]{:S(2)}) collective-permute-start(f32[2,256,256]{2,1,0:T(8,128)S(1)} %get-tuple-element.62), channel_id=1, source_target_pairs={{12,14},{14,12},{13,15},{15,13},{28,30},{30,28},{29,31},{31,29}} | collective-permute-start | bytes 1572872 | tf_op jit(solution)/shard_map/ppermute | solution.py:53
  87.6 3.0 %collective-permute-start.19 = (f32[2,256,256]{2,1,0:T(8,128)S(1)}, f32[2,256,256]{2,1,0:T(8,128)S(1)}, u32[]{:S(2)}, u32[]{:S(2)}) collective-permute-start(f32[2,256,256]{2,1,0:T(8,128)S(1)} %collective-permute-done.18.refs_7_), channel_id=1, source_target_pairs={{0,1},{1,0},{2,3},{3,2},{4,5},{5,4},{6,7},{7,6},{8,9},{9,8},{10,11... | collective-permute-start | bytes 1572872 | tf_op jit(solution)/shard_map/ppermute | solution.py:38
  89.1 2.3 %collective-permute-start.21 = (f32[2,256,256]{2,1,0:T(8,128)S(1)}, f32[2,256,256]{2,1,0:T(8,128)S(1)}, u32[]{:S(2)}, u32[]{:S(2)}) collective-permute-start(f32[2,256,256]{2,1,0:T(8,128)S(1)} %collective-permute-done.20.refs_9_), channel_id=1, source_target_pairs={{0,1},{1,0},{2,3},{3,2},{4,5},{5,4},{6,7},{7,6},{8,9},{9,8},{10,11... | collective-permute-start | bytes 1572872 | tf_op jit(solution)/shard_map/ppermute | solution.py:38
  89.1 3.0 %collective-permute-start.23 = (f32[2,256,256]{2,1,0:T(8,128)S(1)}, f32[2,256,256]{2,1,0:T(8,128)S(1)}, u32[]{:S(2)}, u32[]{:S(2)}) collective-permute-start(f32[2,256,256]{2,1,0:T(8,128)S(1)} %collective-permute-done.22.refs_11_), channel_id=1, source_target_pairs={{0,1},{1,0},{2,3},{3,2},{4,5},{5,4},{6,7},{7,6},{8,9},{9,8},{10,11... | collective-permute-start | bytes 1572872 | tf_op jit(solution)/shard_map/ppermute | solution.py:38

commit v14 on v13

--- a/solution.py
+++ b/solution.py
@@ -153,7 +153,7 @@
     here, up = owner * n_here + k, sections * n_here + owner * n_up + k
     width = len(tables) // 2 if len(tables) > 3 else len(tables)
     pairs = tables[width * twin]
-    below = tables[width * twin + 1 + (0 if isinstance(phase, str) else phase)]
+    below = tables[width * twin + 1]
     lower = True if which == "last" else is_lower(phase)
     own, other = (here, up) if which == "slot" else (up, here)
     row = lax.rem(pick(lower, pairs[0, own], below[0, other]), side)
@@ -521,10 +521,7 @@
 
     layout = (sections, n_here, n_up, side)
     pairs = offsets.T
-    if n_here == n_up:
-        tables = [pairs] + [swap(pairs, "tile", parity) for parity in range(2)]
-    else:
-        tables = [pairs, move(pairs, "tile", 1)]
+    tables = [pairs, move(pairs, "tile", 1)]
     back = lambda d: (sections - d) % sections
     far = distances[1:]
     phase = pltpu.with_memory_space_constraint(phase, pltpu.HBM)

time: 96.1 us -> 96.9 us (level)
  waiting for transfers between devices: 15.6 us -> 19.3 us
  starting transfers between devices: 36 us -> 34 us
    ppermute x10 -> x8, starting transfers between devices: 8.73 us -> 4.43 us  [swap(): return lax.ppermute(block, axis, route)]
    ppermute x0 -> x1, waiting for transfers between devices: none -> 3.23 us  [move(): return lax.ppermute(block, axis, route)]
    ppermute x0 -> x1, starting transfers between devices: none -> 1.28 us  [move(): return lax.ppermute(block, axis, route)]
    ppermute x12 -> x11, waiting for transfers between devices: 5.89 us -> 6.78 us  [rotate(): lax.ppermute(block, axis, [(i, (i + distance) % size) for i in range(size)])]
    ppermute x10 -> x8, waiting for transfers between devices: 6.88 us -> 6.17 us  [swap(): return lax.ppermute(block, axis, route)]
    ppermute x12 -> x11, starting transfers between devices: 21.1 us -> 21.7 us  [rotate(): lax.ppermute(block, axis, [(i, (i + distance) % size) for i in range(size)])]
  transfers between devices with their start and end apart: 24 -> 22, of which waited for: 11 -> 11; matrix products, arithmetic and copies ran while one was open for 0% -> 0% of each run, Pallas kernels for 39% -> 38%
where the time goes in v14:
time: 96.9 us; the launch traced here: 96.4 us
  Pallas kernels  42 us (43%)
  starting transfers between devices  34 us (35%)
  waiting for transfers between devices  19.3 us (20%)
    ppermute x11, starting transfers between devices, rotate(): lax.ppermute(block, axis, [(i, (i + distance) % size) for i in range(size)])  21.7 us
    pallas_call x3, Pallas kernels, run_slot(): pl.pallas_call(lambda *refs: slot_kernel(kind, spot, layout, len(tables),...  19.7 us
    pallas_call x5, Pallas kernels, cut(): pl.pallas_call(lambda *refs: cut_kernel(spots, layout, measured is not No...  10.5 us
    pallas_call x1, Pallas kernels, early(): pl.pallas_call(lambda *refs: early_kernel(metas, layout, *refs), in_specs...  6.85 us
    ppermute x11, waiting for transfers between devices, rotate(): lax.ppermute(block, axis, [(i, (i + distance) % size) for i in range(size)])  6.78 us
    ppermute x2, starting transfers between devices, rotate_last(): return lax.ppermute(block, ('tile', 'slab'), route)  6.5 us
    ppermute x8, waiting for transfers between devices, swap(): return lax.ppermute(block, axis, route)  6.17 us
    ppermute x8, starting transfers between devices, swap(): return lax.ppermute(block, axis, route)  4.43 us
  transfers between devices with their start and end apart: 22, of which 11 were waited for; matrix products, arithmetic and copies ran while one was open for 0% of the time, Pallas kernels for 38%

profile of v14, /device:TPU:29, one launch (start us, length us, event | category | flops | bytes accessed | tf_op | source)
XLA Modules:
  0.0 96.4 jit_solution(10497154854831573923)
XLA Ops:
  0.0 1.3 %collective-permute-start = (s32[2,4]{1,0:T(2,128)}, s32[2,4]{1,0:T(2,128)S(1)}, u32[]{:S(2)}, u32[]{:S(2)}) collective-permute-start(s32[2,4]{1,0:T(2,128)} %bitcast.1), channel_id=1, source_target_pairs={{0,4},{4,8},{8,12},{1,5},{5,9},{9,13},{2,6},{6,10},{10,14},{3,7},{... | collective-permute-start | bytes 104 | tf_op jit(solution)/shard_map/ppermute | solution.py:33
  1.3 3.2 %collective-permute-done.refs_1_ = s32[2,4]{1,0:T(2,128)S(1)} collective-permute-done((s32[2,4]{1,0:T(2,128)}, s32[2,4]{1,0:T(2,128)S(1)}, u32[]{:S(2)}, u32[]{:S(2)}) %collective-permute-start) | collective-permute-done | bytes 64 | tf_op jit(solution)/shard_map/ppermute | solution.py:33
  4.5 0.7 copy-done.2
  5.2 2.2 %cut.5 = (f32[2,256,256]{2,1,0:T(8,128)S(1)}, f32[2,256,256]{2,1,0:T(8,128)S(1)}) custom-call(s32[2,4]{1,0:T(2,128)S(1)} %bitcast.2, s32[2,4]{1,0:T(2,128)S(1)} %collective-permute-done.refs_1_, f32[1,256,4096]{2,1,0:T(8,128)} %refs_2_.12, f32[1,256,4096]{2,1,0:T(8,128)} %refs_3_.12), custom_call_target="tpu_custom_call" | custom-call | tf_op jit(solution)/shard_map/cut/pallas_call | solution.py:328
  7.4 0.2 collective-permute-start.3
  7.6 1.9 %cut.6 = f32[3,256,256]{2,1,0:T(8,128)S(1)} custom-call(s32[2,4]{1,0:T(2,128)S(1)} %bitcast.3, s32[2,4]{1,0:T(2,128)S(1)} %collective-permute-done.refs_1_, f32[1,256,4096]{2,1,0:T(8,128)} %refs_2_.12, f32[1,256,4096]{2,1,0:T(8,128)} %refs_3_.12, f32[4,256,256]{2,1,0:T(8,128)} %refs_3_.15), custom_call_target="tpu_custom_call" | custom-call | tf_op jit(solution)/shard_map/cut/pallas_call | solution.py:328
  9.6 1.4 %collective-permute-start.6 = (f32[3,256,256]{2,1,0:T(8,128)S(1)}, f32[3,256,256]{2,1,0:T(8,128)S(1)}, u32[]{:S(2)}, u32[]{:S(2)}) collective-permute-start(f32[3,256,256]{2,1,0:T(8,128)S(1)} %cut.6), channel_id=1, source_target_pairs={{0,4},{4,0},{8,12},{12,8},{1,5},{5,1},{9,13},{13,9},{2,6},{6,2},{1... | collective-permute-start | bytes 2359304 | tf_op jit(solution)/shard_map/ppermute | solution.py:46
  10.9 0.7 collective-permute-start.5
  11.6 3.3 %collective-permute-start.4 = (f32[2,256,256]{2,1,0:T(8,128)S(1)}, f32[2,256,256]{2,1,0:T(8,128)S(1)}, u32[]{:S(2)}, u32[]{:S(2)}) collective-permute-start(f32[2,256,256]{2,1,0:T(8,128)S(1)} %get-tuple-element.46), channel_id=1, source_target_pairs={{12,14},{14,12},{13,15},{15,13},{28,30},{30,28},{29,31},{31,29}} | collective-permute-start | bytes 1572872 | tf_op jit(solution)/shard_map/ppermute | solution.py:53
  14.9 2.0 %cut.7.refs_4_ = f32[3,256,256]{2,1,0:T(8,128)S(1)} custom-call(s32[2,4]{1,0:T(2,128)S(1)} %bitcast.4, s32[2,4]{1,0:T(2,128)S(1)} %collective-permute-done.refs_1_, f32[1,256,4096]{2,1,0:T(8,128)} %refs_2_.12, f32[1,256,4096]{2,1,0:T(8,128)} %refs_3_.12, f32[4,256,256]{2,1,0:T(8,128)} %refs_3_.15), custom_call_target="tpu_custom_call" | custom-call | tf_op jit(solution)/shard_map/cut/pallas_call | solution.py:328
  16.8 2.2 %cut.8 = (f32[2,256,256]{2,1,0:T(8,128)S(1)}, f32[2,256,256]{2,1,0:T(8,128)S(1)}) custom-call(s32[2,4]{1,0:T(2,128)S(1)} %bitcast.5, s32[2,4]{1,0:T(2,128)S(1)} %collective-permute-done.refs_1_, f32[1,256,4096]{2,1,0:T(8,128)} %refs_2_.12, f32[1,256,4096]{2,1,0:T(8,128)} %refs_3_.12), custom_call_target="tpu_custom_call" | custom-call | tf_op jit(solution)/shard_map/cut/pallas_call | solution.py:328
  19.0 2.2 %cut.9 = (f32[2,256,256]{2,1,0:T(8,128)S(1)}, f32[2,256,256]{2,1,0:T(8,128)S(1)}) custom-call(s32[2,4]{1,0:T(2,128)S(1)} %bitcast.6, s32[2,4]{1,0:T(2,128)S(1)} %collective-permute-done.refs_1_, f32[1,256,4096]{2,1,0:T(8,128)} %refs_2_.12, f32[1,256,4096]{2,1,0:T(8,128)} %refs_3_.12), custom_call_target="tpu_custom_call" | custom-call | tf_op jit(solution)/shard_map/cut/pallas_call | solution.py:328
  21.3 0.0 copy-start.1
  21.3 0.6 join.2
  21.9 0.2 collective-permute-start.7
  22.1 0.7 collective-permute-start.8
  22.8 1.6 %collective-permute-done.4.refs_5_ = f32[2,256,256]{2,1,0:T(8,128)S(1)} collective-permute-done((f32[2,256,256]{2,1,0:T(8,128)S(1)}, f32[2,256,256]{2,1,0:T(8,128)S(1)}, u32[]{:S(2)}, u32[]{:S(2)}) %collective-permute-start.4) | collective-permute-done | bytes 524320 | tf_op jit(solution)/shard_map/ppermute | solution.py:53
  24.4 6.1 %collective-permute-start.1 = (s32[2,4]{1,0:T(2,128)S(1)}, s32[2,4]{1,0:T(2,128)S(1)}, u32[]{:S(2)}, u32[]{:S(2)}) collective-permute-start(s32[2,4]{1,0:T(2,128)S(1)} %bitcast.8), channel_id=1, source_target_pairs={{0,1},{1,0},{2,3},{3,2},{4,5},{5,4},{6,7},{7,6},{8,9},{9,8},{10,11... | collective-permute-start | bytes 104 | tf_op jit(solution)/shard_map/ppermute | solution.py:38
  30.5 0.2 expand.1
  30.7 0.1 collective-permute-start.2
  30.8 0.6 join.3
  31.5 1.5 %collective-permute-start.9 = (f32[2,256,256]{2,1,0:T(8,128)S(1)}, f32[2,256,256]{2,1,0:T(8,128)S(1)}, u32[]{:S(2)}, u32[]{:S(2)}) collective-permute-start(f32[2,256,256]{2,1,0:T(8,128)S(1)} %join.3), channel_id=1, source_target_pairs={{0,2},{2,0},{1,3},{3,1},{4,6},{6,4},{5,7},{7,5},{8,10},{10,8},{9,1... | collective-permute-start | bytes 1572872 | tf_op jit(solution)/shard_map/ppermute | solution.py:38
  33.0 2.8 %collective-permute-done.6.refs_5_ = f32[3,256,256]{2,1,0:T(8,128)S(1)} collective-permute-done((f32[3,256,256]{2,1,0:T(8,128)S(1)}, f32[3,256,256]{2,1,0:T(8,128)S(1)}, u32[]{:S(2)}, u32[]{:S(2)}) %collective-permute-start.6) | collective-permute-done | bytes 786464 | tf_op jit(solution)/shard_map/ppermute | solution.py:46
  35.8 0.2 collective-permute-done.7.refs_6_
  36.0 6.5 %slot_0.1 = (f32[2,256,256]{2,1,0:T(8,128)S(1)}, f32[2,256,256]{2,1,0:T(8,128)S(1)}) custom-call(s32[2,4]{1,0:T(2,128)S(1)} %bitcast.10, s32[2,4]{1,0:T(2,128)S(1)} %collective-permute-done.refs_1_, f32[2,256,256]{2,1,0:T(8,128)S(1)} %copy-done, f32[4,256,256]{2,1,0:T(8,128)} %refs_3_.15, f32[2,256,256]{2,1,0:T(8,128)S(1)} %get-tuple-element.41.refs_4_, ...), custom_call_target="tpu_custom_call" | custom-call | tf_op jit(solution)/shard_map/slot_0/pallas_call | solution.py:260
  42.6 1.5 %collective-permute-start.10 = (f32[2,256,256]{2,1,0:T(8,128)S(1)}, f32[2,256,256]{2,1,0:T(8,128)S(1)}, u32[]{:S(2)}, u32[]{:S(2)}) collective-permute-start(f32[2,256,256]{2,1,0:T(8,128)S(1)} %get-tuple-element.58), channel_id=1, source_target_pairs={{0,2},{2,0},{1,3},{3,1},{4,6},{6,4},{5,7},{7,5},{8,10},{10,8},{9,1... | collective-permute-start | bytes 1572872 | tf_op jit(solution)/shard_map/ppermute | solution.py:38
  44.1 3.2 %collective-permute-done.9.refs_6_ = f32[2,256,256]{2,1,0:T(8,128)S(1)} collective-permute-done((f32[2,256,256]{2,1,0:T(8,128)S(1)}, f32[2,256,256]{2,1,0:T(8,128)S(1)}, u32[]{:S(2)}, u32[]{:S(2)}) %collective-permute-start.9) | collective-permute-done | bytes 524320 | tf_op jit(solution)/shard_map/ppermute | solution.py:38
  47.3 6.5 %slot_1.1 = (f32[2,256,256]{2,1,0:T(8,128)S(1)}, f32[2,256,256]{2,1,0:T(8,128)S(1)}) custom-call(s32[2,4]{1,0:T(2,128)S(1)} %bitcast.11, s32[2,4]{1,0:T(2,128)S(1)} %collective-permute-done.refs_1_, f32[2,256,256]{2,1,0:T(8,128)S(1)} %copy-done, f32[4,256,256]{2,1,0:T(8,128)} %refs_3_.15, f32[2,256,256]{2,1,0:T(8,128)S(1)} %get-tuple-element.43.refs_4_, ...), custom_call_target="tpu_custom_call" | custom-call | tf_op jit(solution)/shard_map/slot_1/pallas_call | solution.py:260
  53.8 0.7 collective-permute-start.14
  54.5 1.3 %collective-permute-start.13 = (f32[2,256,256]{2,1,0:T(8,128)S(1)}, f32[2,256,256]{2,1,0:T(8,128)S(1)}, u32[]{:S(2)}, u32[]{:S(2)}) collective-permute-start(f32[2,256,256]{2,1,0:T(8,128)S(1)} %get-tuple-element.59), channel_id=1, source_target_pairs={{0,2},{2,0},{1,3},{3,1},{4,6},{6,4},{5,7},{7,5},{8,10},{10,8},{9,1... | collective-permute-start | bytes 1572872 | tf_op jit(solution)/shard_map/ppermute | solution.py:38
  55.8 6.6 %slot_last.1 = (f32[2,256,256]{2,1,0:T(8,128)S(1)}, f32[2,256,256]{2,1,0:T(8,128)S(1)}) custom-call(s32[2,4]{1,0:T(2,128)S(1)} %bitcast.12, s32[2,4]{1,0:T(2,128)S(1)} %collective-permute-done.refs_1_, f32[2,256,256]{2,1,0:T(8,128)S(1)} %copy-done, f32[4,256,256]{2,1,0:T(8,128)} %refs_3_.15, f32[3,256,256]{2,1,0:T(8,128)S(1)} %cut.7.refs_4_, ...), custom_call_target="tpu_custom_call" | custom-call | tf_op jit(solution)/shard_map/slot_last/pallas_call | solution.py:260
  62.5 0.1 pack.2
  62.6 6.3 %collective-permute-start.12 = (f32[4,2,256,256]{3,2,1,0:T(8,128)S(1)}, f32[4,2,256,256]{3,2,1,0:T(8,128)S(1)}, u32[]{:S(2)}, u32[]{:S(2)}) collective-permute-start(f32[4,2,256,256]{3,2,1,0:T(8,128)S(1)} %pack.2), channel_id=1, source_target_pairs={{0,1},{1,0},{2,3},{3,2},{4,5},{5,4},{6,7},{7,6},{8,9},{9,8},{10,11... | collective-permute-start | bytes 6291464 | tf_op jit(solution)/shard_map/ppermute | solution.py:38
  68.9 0.8 collective-permute-done.13.refs_1_.refs_10_
  69.7 0.1 pack.3
  69.8 3.1 %collective-permute-start.15 = (f32[3,2,256,256]{3,2,1,0:T(8,128)S(1)}, f32[3,2,256,256]{3,2,1,0:T(8,128)S(1)}, u32[]{:S(2)}, u32[]{:S(2)}) collective-permute-start(f32[3,2,256,256]{3,2,1,0:T(8,128)S(1)} %pack.3), channel_id=1, source_target_pairs={{0,1},{1,0},{2,3},{3,2},{4,5},{5,4},{6,7},{7,6},{8,9},{9,8},{10,11... | collective-permute-start | bytes 4718600 | tf_op jit(solution)/shard_map/ppermute | solution.py:38
  73.0 0.7 collective-permute-start.20
  73.7 0.1 collective-permute-start.18
  73.7 3.3 %collective-permute-start.16 = (f32[2,256,256]{2,1,0:T(8,128)S(1)}, f32[2,256,256]{2,1,0:T(8,128)S(1)}, u32[]{:S(2)}, u32[]{:S(2)}) collective-permute-start(f32[2,256,256]{2,1,0:T(8,128)S(1)} %get-tuple-element.62), channel_id=1, source_target_pairs={{12,14},{14,12},{13,15},{15,13},{28,30},{30,28},{29,31},{31,29}} | collective-permute-start | bytes 1572872 | tf_op jit(solution)/shard_map/ppermute | solution.py:53
  77.0 6.8 %early.1 = (f32[2,256,4096]{2,1,0:T(8,128)S(1)}, f32[2,1,256,4096]{3,2,1,0:T(8,128)}) custom-call(s32[2,4]{1,0:T(2,128)S(1)} %bitcast.13, s32[2,4]{1,0:T(2,128)S(1)} %collective-permute-done.refs_1_, s32[2,4]{1,0:T(2,128)S(1)} %collective-permute-done.1.refs_2_, s32[2,4]{1,0:T(2,128)S(1)} %collective-permute-done.2.refs_3_, ...), custom_call_target="tpu_custom_call" | custom-call | tf_op jit(solution)/shard_map/early/pallas_call | solution.py:433
  83.9 3.4 %collective-permute-done.18.refs_7_ = f32[2,256,256]{2,1,0:T(8,128)S(1)} collective-permute-done((f32[2,256,256]{2,1,0:T(8,128)S(1)}, f32[2,256,256]{2,1,0:T(8,128)S(1)}, u32[]{:S(2)}, u32[]{:S(2)}) %collective-permute-start.18) | collective-permute-done | bytes 524320 | tf_op jit(solution)/shard_map/ppermute | solution.py:46
  87.3 1.6 %collective-permute-done.16.refs_5_ = f32[2,256,256]{2,1,0:T(8,128)S(1)} collective-permute-done((f32[2,256,256]{2,1,0:T(8,128)S(1)}, f32[2,256,256]{2,1,0:T(8,128)S(1)}, u32[]{:S(2)}, u32[]{:S(2)}) %collective-permute-start.16) | collective-permute-done | bytes 524320 | tf_op jit(solution)/shard_map/ppermute | solution.py:53
  88.8 1.1 %collective-permute-start.17 = (f32[2,256,256]{2,1,0:T(8,128)S(1)}, f32[2,256,256]{2,1,0:T(8,128)S(1)}, u32[]{:S(2)}, u32[]{:S(2)}) collective-permute-start(f32[2,256,256]{2,1,0:T(8,128)S(1)} %collective-permute-done.16.refs_5_), channel_id=1, source_target_pairs={{0,1},{1,0},{2,3},{3,2},{4,5},{5,4},{6,7},{7,6},{8,9},{9,8},{10,11... | collective-permute-start | bytes 1572872 | tf_op jit(solution)/shard_map/ppermute | solution.py:38
  90.0 0.5 collective-permute-start.21
  90.5 1.0 %collective-permute-done.17.refs_6_ = f32[2,256,256]{2,1,0:T(8,128)S(1)} collective-permute-done((f32[2,256,256]{2,1,0:T(8,128)S(1)}, f32[2,256,256]{2,1,0:T(8,128)S(1)}, u32[]{:S(2)}, u32[]{:S(2)}) %collective-permute-start.17) | collective-permute-done | bytes 524320 | tf_op jit(solution)/shard_map/ppermute | solution.py:38
  91.5 0.7 collective-permute-done.19.refs_8_
  92.3 0.7 collective-permute-done.21.refs_10_
  93.0 3.2 %late.1 = f32[2,1,256,4096]{3,2,1,0:T(8,128)} custom-call(s32[2,4]{1,0:T(2,128)S(1)} %bitcast.14, s32[2,4]{1,0:T(2,128)S(1)} %collective-permute-done.refs_1_, s32[2,4]{1,0:T(2,128)S(1)} %collective-permute-done.1.refs_2_, s32[2,4]{1,0:T(2,128)S(1)} %collective-permute-done.2.refs_3_, ...), custom_call_target="tpu_custom_call", output_to_operand_aliasing={{}: (11, {})} | custom-call | tf_op jit(solution)/shard_map/late/pallas_call | solution.py:498
  (19 shorter events, 0.1 us)
Async XLA Ops:
  0.0 4.5 %collective-permute-start = (s32[2,4]{1,0:T(2,128)}, s32[2,4]{1,0:T(2,128)S(1)}, u32[]{:S(2)}, u32[]{:S(2)}) collective-permute-start(s32[2,4]{1,0:T(2,128)} %bitcast.1), channel_id=1, source_target_pairs={{0,4},{4,8},{8,12},{1,5},{5,9},{9,13},{2,6},{6,10},{10,14},{3,7},{... | collective-permute-start | bytes 104 | tf_op jit(solution)/shard_map/ppermute | solution.py:33
  4.5 0.7 copy-start.2
  7.4 13.9 %collective-permute-start.3 = (f32[2,256,256]{2,1,0:T(8,128)S(1)}, f32[2,256,256]{2,1,0:T(8,128)S(1)}, u32[]{:S(2)}, u32[]{:S(2)}) collective-permute-start(f32[2,256,256]{2,1,0:T(8,128)S(1)} %get-tuple-element.37), channel_id=1, source_target_pairs={{0,4},{4,0},{8,12},{12,8},{1,5},{5,1},{9,13},{13,9},{2,6},{6,2},{1... | collective-permute-start | bytes 1572872 | tf_op jit(solution)/shard_map/ppermute | solution.py:46
  9.6 26.2 %collective-permute-start.6 = (f32[3,256,256]{2,1,0:T(8,128)S(1)}, f32[3,256,256]{2,1,0:T(8,128)S(1)}, u32[]{:S(2)}, u32[]{:S(2)}) collective-permute-start(f32[3,256,256]{2,1,0:T(8,128)S(1)} %cut.6), channel_id=1, source_target_pairs={{0,4},{4,0},{8,12},{12,8},{1,5},{5,1},{9,13},{13,9},{2,6},{6,2},{1... | collective-permute-start | bytes 2359304 | tf_op jit(solution)/shard_map/ppermute | solution.py:46
  10.9 19.8 %collective-permute-start.5 = (f32[2,256,256]{2,1,0:T(8,128)S(1)}, f32[2,256,256]{2,1,0:T(8,128)S(1)}, u32[]{:S(2)}, u32[]{:S(2)}) collective-permute-start(f32[2,256,256]{2,1,0:T(8,128)S(1)} %get-tuple-element.46), channel_id=1, source_target_pairs={{4,8},{8,4},{5,9},{9,5},{6,10},{10,6},{7,11},{11,7},{20,24},{24,20... | collective-permute-start | bytes 1572872 | tf_op jit(solution)/shard_map/ppermute | solution.py:46
  11.6 12.8 %collective-permute-start.4 = (f32[2,256,256]{2,1,0:T(8,128)S(1)}, f32[2,256,256]{2,1,0:T(8,128)S(1)}, u32[]{:S(2)}, u32[]{:S(2)}) collective-permute-start(f32[2,256,256]{2,1,0:T(8,128)S(1)} %get-tuple-element.46), channel_id=1, source_target_pairs={{12,14},{14,12},{13,15},{15,13},{28,30},{30,28},{29,31},{31,29}} | collective-permute-start | bytes 1572872 | tf_op jit(solution)/shard_map/ppermute | solution.py:53
  21.3 9.3 %copy-start.1 = (bf16[8,256,256]{2,1,0:T(8,128)(2,1)S(1)}, bf16[8,256,256]{2,1,0:T(8,128)(2,1)}, u32[]{:S(2)}) copy-start(bf16[8,256,256]{2,1,0:T(8,128)(2,1)} %constant.2.clone.pieces) | copy-start | bytes 3145732
  21.3 14.7 %copy-start = (f32[2,256,256]{2,1,0:T(8,128)S(1)}, f32[2,256,256]{2,1,0:T(8,128)}, u32[]{:S(2)}) copy-start(f32[2,256,256]{2,1,0:T(8,128)} %refs_2_.15) | copy-start | bytes 1572868
  21.3 14.7 %copy-start.3 = (s32[4,2]{0,1:T(2,128)S(1)}, s32[4,2]{0,1:T(2,128)}, u32[]{:S(2)}) copy-start(s32[4,2]{0,1:T(2,128)} %param.10) | copy-start | bytes 100
  21.9 14.1 %collective-permute-start.7 = (f32[2,256,256]{2,1,0:T(8,128)S(1)}, f32[2,256,256]{2,1,0:T(8,128)S(1)}, u32[]{:S(2)}, u32[]{:S(2)}) collective-permute-start(f32[2,256,256]{2,1,0:T(8,128)S(1)} %join.2), channel_id=1, source_target_pairs={{0,2},{2,0},{1,3},{3,1},{4,6},{6,4},{5,7},{7,5},{8,10},{10,8},{9,1... | collective-permute-start | bytes 1572872 | tf_op jit(solution)/shard_map/ppermute | solution.py:38
  22.1 21.9 %collective-permute-start.8 = (f32[3,256,256]{2,1,0:T(8,128)S(1)}, f32[3,256,256]{2,1,0:T(8,128)S(1)}, u32[]{:S(2)}, u32[]{:S(2)}) collective-permute-start(f32[3,256,256]{2,1,0:T(8,128)S(1)} %cut.7.refs_4_), channel_id=1, source_target_pairs={{4,8},{8,4},{5,9},{9,5},{6,10},{10,6},{7,11},{11,7},{20,24},{24,20... | collective-permute-start | bytes 2359304 | tf_op jit(solution)/shard_map/ppermute | solution.py:46
  24.4 7.0 %collective-permute-start.1 = (s32[2,4]{1,0:T(2,128)S(1)}, s32[2,4]{1,0:T(2,128)S(1)}, u32[]{:S(2)}, u32[]{:S(2)}) collective-permute-start(s32[2,4]{1,0:T(2,128)S(1)} %bitcast.8), channel_id=1, source_target_pairs={{0,1},{1,0},{2,3},{3,2},{4,5},{5,4},{6,7},{7,6},{8,9},{9,8},{10,11... | collective-permute-start | bytes 104 | tf_op jit(solution)/shard_map/ppermute | solution.py:38
  30.7 2.3 %collective-permute-start.2 = (s32[2,4]{1,0:T(2,128)S(1)}, s32[2,4]{1,0:T(2,128)S(1)}, u32[]{:S(2)}, u32[]{:S(2)}) collective-permute-start(s32[2,4]{1,0:T(2,128)S(1)} %collective-permute-done.refs_1_), channel_id=1, source_target_pairs={{0,1},{1,0},{2,3},{3,2},{4,5},{5,4},{6,7},{7,6},{8,9},{9,8},{10,11... | collective-permute-start | bytes 104 | tf_op jit(solution)/shard_map/ppermute | solution.py:38
  31.5 15.8 %collective-permute-start.9 = (f32[2,256,256]{2,1,0:T(8,128)S(1)}, f32[2,256,256]{2,1,0:T(8,128)S(1)}, u32[]{:S(2)}, u32[]{:S(2)}) collective-permute-start(f32[2,256,256]{2,1,0:T(8,128)S(1)} %join.3), channel_id=1, source_target_pairs={{0,2},{2,0},{1,3},{3,1},{4,6},{6,4},{5,7},{7,5},{8,10},{10,8},{9,1... | collective-permute-start | bytes 1572872 | tf_op jit(solution)/shard_map/ppermute | solution.py:38
  42.6 19.9 %collective-permute-start.10 = (f32[2,256,256]{2,1,0:T(8,128)S(1)}, f32[2,256,256]{2,1,0:T(8,128)S(1)}, u32[]{:S(2)}, u32[]{:S(2)}) collective-permute-start(f32[2,256,256]{2,1,0:T(8,128)S(1)} %get-tuple-element.58), channel_id=1, source_target_pairs={{0,2},{2,0},{1,3},{3,1},{4,6},{6,4},{5,7},{7,5},{8,10},{10,8},{9,1... | collective-permute-start | bytes 1572872 | tf_op jit(solution)/shard_map/ppermute | solution.py:38
  44.0 18.4 %collective-permute-start.11 = (f32[2,256,256]{2,1,0:T(8,128)S(1)}, f32[2,256,256]{2,1,0:T(8,128)S(1)}, u32[]{:S(2)}, u32[]{:S(2)}) collective-permute-start(f32[2,256,256]{2,1,0:T(8,128)S(1)} %get-tuple-element.53.refs_1_.refs_5_), channel_id=1, source_target_pairs={{0,4},{4,0},{8,12},{12,8},{1,5},{5,1},{9,13},{13,9},{2,6},{6,2},{1... | collective-permute-start | bytes 1572872 | tf_op jit(solution)/shard_map/ppermute | solution.py:46
  53.8 15.9 %collective-permute-start.14 = (f32[2,256,256]{2,1,0:T(8,128)S(1)}, f32[2,256,256]{2,1,0:T(8,128)S(1)}, u32[]{:S(2)}, u32[]{:S(2)}) collective-permute-start(f32[2,256,256]{2,1,0:T(8,128)S(1)} %get-tuple-element.55.refs_0_.refs_9_), channel_id=1, source_target_pairs={{4,8},{8,4},{5,9},{9,5},{6,10},{10,6},{7,11},{11,7},{20,24},{24,20... | collective-permute-start | bytes 1572872 | tf_op jit(solution)/shard_map/ppermute | solution.py:46
  54.5 15.2 %collective-permute-start.13 = (f32[2,256,256]{2,1,0:T(8,128)S(1)}, f32[2,256,256]{2,1,0:T(8,128)S(1)}, u32[]{:S(2)}, u32[]{:S(2)}) collective-permute-start(f32[2,256,256]{2,1,0:T(8,128)S(1)} %get-tuple-element.59), channel_id=1, source_target_pairs={{0,2},{2,0},{1,3},{3,1},{4,6},{6,4},{5,7},{7,5},{8,10},{10,8},{9,1... | collective-permute-start | bytes 1572872 | tf_op jit(solution)/shard_map/ppermute | solution.py:38
  62.6 14.4 %collective-permute-start.12 = (f32[4,2,256,256]{3,2,1,0:T(8,128)S(1)}, f32[4,2,256,256]{3,2,1,0:T(8,128)S(1)}, u32[]{:S(2)}, u32[]{:S(2)}) collective-permute-start(f32[4,2,256,256]{3,2,1,0:T(8,128)S(1)} %pack.2), channel_id=1, source_target_pairs={{0,1},{1,0},{2,3},{3,2},{4,5},{5,4},{6,7},{7,6},{8,9},{9,8},{10,11... | collective-permute-start | bytes 6291464 | tf_op jit(solution)/shard_map/ppermute | solution.py:38
  69.8 7.2 %collective-permute-start.15 = (f32[3,2,256,256]{3,2,1,0:T(8,128)S(1)}, f32[3,2,256,256]{3,2,1,0:T(8,128)S(1)}, u32[]{:S(2)}, u32[]{:S(2)}) collective-permute-start(f32[3,2,256,256]{3,2,1,0:T(8,128)S(1)} %pack.3), channel_id=1, source_target_pairs={{0,1},{1,0},{2,3},{3,2},{4,5},{5,4},{6,7},{7,6},{8,9},{9,8},{10,11... | collective-permute-start | bytes 4718600 | tf_op jit(solution)/shard_map/ppermute | solution.py:38
  73.0 10.9 %collective-permute-start.20 = (f32[2,256,256]{2,1,0:T(8,128)S(1)}, f32[2,256,256]{2,1,0:T(8,128)S(1)}, u32[]{:S(2)}, u32[]{:S(2)}) collective-permute-start(f32[2,256,256]{2,1,0:T(8,128)S(1)} %collective-permute-done.13.refs_1_.refs_10_), channel_id=1, source_target_pairs={{4,8},{8,4},{5,9},{9,5},{6,10},{10,6},{7,11},{11,7},{20,24},{24,20... | collective-permute-start | bytes 1572872 | tf_op jit(solution)/shard_map/ppermute | solution.py:46
  73.7 13.6 %collective-permute-start.18 = (f32[2,256,256]{2,1,0:T(8,128)S(1)}, f32[2,256,256]{2,1,0:T(8,128)S(1)}, u32[]{:S(2)}, u32[]{:S(2)}) collective-permute-start(f32[2,256,256]{2,1,0:T(8,128)S(1)} %collective-permute-done.10.refs_2_.refs_6_), channel_id=1, source_target_pairs={{0,4},{4,0},{8,12},{12,8},{1,5},{5,1},{9,13},{13,9},{2,6},{6,2},{1... | collective-permute-start | bytes 1572872 | tf_op jit(solution)/shard_map/ppermute | solution.py:46
  73.7 15.1 %collective-permute-start.16 = (f32[2,256,256]{2,1,0:T(8,128)S(1)}, f32[2,256,256]{2,1,0:T(8,128)S(1)}, u32[]{:S(2)}, u32[]{:S(2)}) collective-permute-start(f32[2,256,256]{2,1,0:T(8,128)S(1)} %get-tuple-element.62), channel_id=1, source_target_pairs={{12,14},{14,12},{13,15},{15,13},{28,30},{30,28},{29,31},{31,29}} | collective-permute-start | bytes 1572872 | tf_op jit(solution)/shard_map/ppermute | solution.py:53
  88.8 2.7 %collective-permute-start.17 = (f32[2,256,256]{2,1,0:T(8,128)S(1)}, f32[2,256,256]{2,1,0:T(8,128)S(1)}, u32[]{:S(2)}, u32[]{:S(2)}) collective-permute-start(f32[2,256,256]{2,1,0:T(8,128)S(1)} %collective-permute-done.16.refs_5_), channel_id=1, source_target_pairs={{0,1},{1,0},{2,3},{3,2},{4,5},{5,4},{6,7},{7,6},{8,9},{9,8},{10,11... | collective-permute-start | bytes 1572872 | tf_op jit(solution)/shard_map/ppermute | solution.py:38
  90.0 2.3 %collective-permute-start.19 = (f32[2,256,256]{2,1,0:T(8,128)S(1)}, f32[2,256,256]{2,1,0:T(8,128)S(1)}, u32[]{:S(2)}, u32[]{:S(2)}) collective-permute-start(f32[2,256,256]{2,1,0:T(8,128)S(1)} %collective-permute-done.18.refs_7_), channel_id=1, source_target_pairs={{0,1},{1,0},{2,3},{3,2},{4,5},{5,4},{6,7},{7,6},{8,9},{9,8},{10,11... | collective-permute-start | bytes 1572872 | tf_op jit(solution)/shard_map/ppermute | solution.py:38
  90.0 3.0 %collective-permute-start.21 = (f32[2,256,256]{2,1,0:T(8,128)S(1)}, f32[2,256,256]{2,1,0:T(8,128)S(1)}, u32[]{:S(2)}, u32[]{:S(2)}) collective-permute-start(f32[2,256,256]{2,1,0:T(8,128)S(1)} %collective-permute-done.20.refs_9_), channel_id=1, source_target_pairs={{0,1},{1,0},{2,3},{3,2},{4,5},{5,4},{6,7},{7,6},{8,9},{9,8},{10,11... | collective-permute-start | bytes 1572872 | tf_op jit(solution)/shard_map/ppermute | solution.py:38

commit v15 on v13

--- a/solution.py
+++ b/solution.py
@@ -611,8 +611,6 @@
     ending = [
         [rotate_last(after(last_outs[n][d], *backs[-1]), d) for d in far] for n in range(len(ends))
     ]
-    for n, k in enumerate(ends):
-        final += [(ending[n][d - 1], ("last", "lo", k, back(d))) for d in far]
     last_items = [(last_outs[n][0], ("last", "lo", k, 0)) for n, k in enumerate(ends)]
     for i, (k, role, send_role, there, home) in enumerate(rounds):
         items = [(outs[i][0], ("slot", role, k, 0))]
@@ -623,6 +621,9 @@
         twins = group(items)
         for d in far:
             final.append((home(backs[i][d - 1]), ("swap", send_role, k, back(d))))
+        if i == 0:
+            for n, k in enumerate(ends):
+                final += [(ending[n][d - 1], ("last", "lo", k, back(d))) for d in far]
     total, copied = early(kinds, layout, tables + twin_tables, terms, cols_total)
     values = []
     for value, spot in final:

time: 96.1 us -> 96.4 us (level)
  waiting for transfers between devices: 15.6 us -> 16.6 us
    ppermute x2, waiting for transfers between devices: 2.83 us -> 6.13 us  [rotate_last(): return lax.ppermute(block, ('tile', 'slab'), route)]
    ppermute x10, waiting for transfers between devices: 6.88 us -> 4.99 us  [swap(): return lax.ppermute(block, axis, route)]
where the time goes in v15:
time: 96.4 us; the launch traced here: 96 us
  Pallas kernels  42.7 us (44%)
  starting transfers between devices  35.6 us (37%)
  waiting for transfers between devices  16.6 us (17%)
    ppermute x12, starting transfers between devices, rotate(): lax.ppermute(block, axis, [(i, (i + distance) % size) for i in range(size)])  21.3 us
    pallas_call x3, Pallas kernels, run_slot(): pl.pallas_call(lambda *refs: slot_kernel(kind, spot, layout, len(tables),...  20.2 us
    pallas_call x5, Pallas kernels, cut(): pl.pallas_call(lambda *refs: cut_kernel(spots, layout, measured is not No...  10.5 us
    ppermute x10, starting transfers between devices, swap(): return lax.ppermute(block, axis, route)  8.1 us
    pallas_call x1, Pallas kernels, early(): pl.pallas_call(lambda *refs: early_kernel(metas, layout, *refs), in_specs...  6.94 us
    ppermute x2, starting transfers between devices, rotate_last(): return lax.ppermute(block, ('tile', 'slab'), route)  6.16 us
    ppermute x2, waiting for transfers between devices, rotate_last(): return lax.ppermute(block, ('tile', 'slab'), route)  6.13 us
    ppermute x12, waiting for transfers between devices, rotate(): lax.ppermute(block, axis, [(i, (i + distance) % size) for i in range(size)])  5.46 us
  transfers between devices with their start and end apart: 24, of which 11 were waited for; matrix products, arithmetic and copies ran while one was open for 0% of the time, Pallas kernels for 39%

profile of v15, /device:TPU:29, one launch (start us, length us, event | category | flops | bytes accessed | tf_op | source)
XLA Modules:
  0.0 96.0 jit_solution(18160438498132542911)
XLA Ops:
  0.0 0.6 collective-permute-start.1
  0.7 1.7 %collective-permute-start = (s32[2,4]{1,0:T(2,128)}, s32[2,4]{1,0:T(2,128)S(1)}, u32[]{:S(2)}, u32[]{:S(2)}) collective-permute-start(s32[2,4]{1,0:T(2,128)} %bitcast.2), channel_id=1, source_target_pairs={{0,4},{4,0},{8,12},{12,8},{1,5},{5,1},{9,13},{13,9},{2,6},{6,2},{1... | collective-permute-start | bytes 104 | tf_op jit(solution)/shard_map/ppermute | solution.py:46
  2.3 1.2 %collective-permute-done.refs_1_ = s32[2,4]{1,0:T(2,128)S(1)} collective-permute-done((s32[2,4]{1,0:T(2,128)}, s32[2,4]{1,0:T(2,128)S(1)}, u32[]{:S(2)}, u32[]{:S(2)}) %collective-permute-start) | collective-permute-done | bytes 64 | tf_op jit(solution)/shard_map/ppermute | solution.py:46
  3.5 0.7 copy-done.2
  4.2 2.2 %cut.5 = (f32[2,256,256]{2,1,0:T(8,128)S(1)}, f32[2,256,256]{2,1,0:T(8,128)S(1)}) custom-call(s32[2,4]{1,0:T(2,128)S(1)} %bitcast.3, s32[2,4]{1,0:T(2,128)S(1)} %collective-permute-done.refs_1_, s32[2,4]{1,0:T(2,128)S(1)} %collective-permute-done.1.refs_2_, f32[1,256,4096]{2,1,0:T(8,128)} %refs_3_.12, f32[1,256,4096]{2,1,0:T(8,128)} %refs_4_.12), custom_call_target="tpu_custom_call" | custom-call | tf_op jit(solution)/shard_map/cut/pallas_call | solution.py:328
  6.4 1.6 %collective-permute-start.5 = (f32[2,256,256]{2,1,0:T(8,128)S(1)}, f32[2,256,256]{2,1,0:T(8,128)S(1)}, u32[]{:S(2)}, u32[]{:S(2)}) collective-permute-start(f32[2,256,256]{2,1,0:T(8,128)S(1)} %get-tuple-element.37), channel_id=1, source_target_pairs={{0,4},{4,0},{8,12},{12,8},{1,5},{5,1},{9,13},{13,9},{2,6},{6,2},{1... | collective-permute-start | bytes 1572872 | tf_op jit(solution)/shard_map/ppermute | solution.py:46
  8.0 1.9 %cut.6 = f32[3,256,256]{2,1,0:T(8,128)S(1)} custom-call(s32[2,4]{1,0:T(2,128)S(1)} %bitcast.4, s32[2,4]{1,0:T(2,128)S(1)} %collective-permute-done.refs_1_, s32[2,4]{1,0:T(2,128)S(1)} %collective-permute-done.1.refs_2_, f32[1,256,4096]{2,1,0:T(8,128)} %refs_3_.12, f32[1,256,4096]{2,1,0:T(8,128)} %refs_4_.12, f32[4,256,256]{2,1,0:T(8,128)} %refs_4_.15), custom_call_target="tpu_custom_call" | custom-call | tf_op jit(solution)/shard_map/cut/pallas_call | solution.py:328
  9.9 0.1 collective-permute-start.8
  10.0 3.1 %collective-permute-start.6 = (f32[2,256,256]{2,1,0:T(8,128)S(1)}, f32[2,256,256]{2,1,0:T(8,128)S(1)}, u32[]{:S(2)}, u32[]{:S(2)}) collective-permute-start(f32[2,256,256]{2,1,0:T(8,128)S(1)} %get-tuple-element.46), channel_id=1, source_target_pairs={{12,14},{14,12},{13,15},{15,13},{28,30},{30,28},{29,31},{31,29}} | collective-permute-start | bytes 1572872 | tf_op jit(solution)/shard_map/ppermute | solution.py:53
  13.1 0.7 collective-permute-start.7
  13.8 1.9 %cut.7.refs_5_ = f32[3,256,256]{2,1,0:T(8,128)S(1)} custom-call(s32[2,4]{1,0:T(2,128)S(1)} %bitcast.5, s32[2,4]{1,0:T(2,128)S(1)} %collective-permute-done.refs_1_, s32[2,4]{1,0:T(2,128)S(1)} %collective-permute-done.1.refs_2_, f32[1,256,4096]{2,1,0:T(8,128)} %refs_3_.12, f32[1,256,4096]{2,1,0:T(8,128)} %refs_4_.12, f32[4,256,256]{2,1,0:T(8,128)} %refs_4_.15), custom_call_target="tpu_custom_call" | custom-call | tf_op jit(solution)/shard_map/cut/pallas_call | solution.py:328
  15.7 2.2 %cut.8 = (f32[2,256,256]{2,1,0:T(8,128)S(1)}, f32[2,256,256]{2,1,0:T(8,128)S(1)}) custom-call(s32[2,4]{1,0:T(2,128)S(1)} %bitcast.6, s32[2,4]{1,0:T(2,128)S(1)} %collective-permute-done.refs_1_, s32[2,4]{1,0:T(2,128)S(1)} %collective-permute-done.1.refs_2_, f32[1,256,4096]{2,1,0:T(8,128)} %refs_3_.12, f32[1,256,4096]{2,1,0:T(8,128)} %refs_4_.12), custom_call_target="tpu_custom_call" | custom-call | tf_op jit(solution)/shard_map/cut/pallas_call | solution.py:328
  17.9 2.2 %cut.9 = (f32[2,256,256]{2,1,0:T(8,128)S(1)}, f32[2,256,256]{2,1,0:T(8,128)S(1)}) custom-call(s32[2,4]{1,0:T(2,128)S(1)} %bitcast.7, s32[2,4]{1,0:T(2,128)S(1)} %collective-permute-done.refs_1_, s32[2,4]{1,0:T(2,128)S(1)} %collective-permute-done.1.refs_2_, f32[1,256,4096]{2,1,0:T(8,128)} %refs_3_.12, f32[1,256,4096]{2,1,0:T(8,128)} %refs_4_.12), custom_call_target="tpu_custom_call" | custom-call | tf_op jit(solution)/shard_map/cut/pallas_call | solution.py:328
  20.2 0.7 join.2
  20.9 0.4 collective-permute-start.9
  21.2 0.7 collective-permute-start.10
  21.9 0.9 collective-permute-done.6.refs_6_
  22.8 5.5 %collective-permute-start.2 = (s32[2,4]{1,0:T(2,128)S(1)}, s32[2,4]{1,0:T(2,128)S(1)}, u32[]{:S(2)}, u32[]{:S(2)}) collective-permute-start(s32[2,4]{1,0:T(2,128)S(1)} %bitcast.9), channel_id=1, source_target_pairs={{0,1},{1,0},{2,3},{3,2},{4,5},{5,4},{6,7},{7,6},{8,9},{9,8},{10,11... | collective-permute-start | bytes 104 | tf_op jit(solution)/shard_map/ppermute | solution.py:38
  28.3 0.2 expand.1
  28.6 0.7 join.3
  29.3 0.6 collective-permute-start.3
  29.8 2.1 %collective-permute-start.11 = (f32[2,256,256]{2,1,0:T(8,128)S(1)}, f32[2,256,256]{2,1,0:T(8,128)S(1)}, u32[]{:S(2)}, u32[]{:S(2)}) collective-permute-start(f32[2,256,256]{2,1,0:T(8,128)S(1)} %join.3), channel_id=1, source_target_pairs={{0,2},{2,0},{1,3},{3,1},{4,6},{6,4},{5,7},{7,5},{8,10},{10,8},{9,1... | collective-permute-start | bytes 1572872 | tf_op jit(solution)/shard_map/ppermute | solution.py:38
  32.0 2.9 %collective-permute-done.8.refs_6_ = f32[3,256,256]{2,1,0:T(8,128)S(1)} collective-permute-done((f32[3,256,256]{2,1,0:T(8,128)S(1)}, f32[3,256,256]{2,1,0:T(8,128)S(1)}, u32[]{:S(2)}, u32[]{:S(2)}) %collective-permute-start.8) | collective-permute-done | bytes 786464 | tf_op jit(solution)/shard_map/ppermute | solution.py:46
  34.8 0.1 collective-permute-done.9.refs_7_
  35.0 6.7 %slot_0.1 = (f32[2,256,256]{2,1,0:T(8,128)S(1)}, f32[2,256,256]{2,1,0:T(8,128)S(1)}) custom-call(s32[2,4]{1,0:T(2,128)S(1)} %bitcast.11, s32[2,4]{1,0:T(2,128)S(1)} %collective-permute-done.refs_1_, s32[2,4]{1,0:T(2,128)S(1)} %collective-permute-done.1.refs_2_, f32[2,256,256]{2,1,0:T(8,128)S(1)} %copy-done, f32[4,256,256]{2,1,0:T(8,128)} %refs_4_.15, ...), custom_call_target="tpu_custom_call" | custom-call | tf_op jit(solution)/shard_map/slot_0/pallas_call | solution.py:260
  41.6 1.1 %collective-permute-start.12 = (f32[2,256,256]{2,1,0:T(8,128)S(1)}, f32[2,256,256]{2,1,0:T(8,128)S(1)}, u32[]{:S(2)}, u32[]{:S(2)}) collective-permute-start(f32[2,256,256]{2,1,0:T(8,128)S(1)} %get-tuple-element.58), channel_id=1, source_target_pairs={{0,2},{2,0},{1,3},{3,1},{4,6},{6,4},{5,7},{7,5},{8,10},{10,8},{9,1... | collective-permute-start | bytes 1572872 | tf_op jit(solution)/shard_map/ppermute | solution.py:38
  42.8 1.3 %collective-permute-start.13 = (f32[2,256,256]{2,1,0:T(8,128)S(1)}, f32[2,256,256]{2,1,0:T(8,128)S(1)}, u32[]{:S(2)}, u32[]{:S(2)}) collective-permute-start(f32[2,256,256]{2,1,0:T(8,128)S(1)} %get-tuple-element.53.refs_1_.refs_7_), channel_id=1, source_target_pairs={{0,4},{4,0},{8,12},{12,8},{1,5},{5,1},{9,13},{13,9},{2,6},{6,2},{1... | collective-permute-start | bytes 1572872 | tf_op jit(solution)/shard_map/ppermute | solution.py:46
  44.1 2.1 %collective-permute-done.11.refs_7_ = f32[2,256,256]{2,1,0:T(8,128)S(1)} collective-permute-done((f32[2,256,256]{2,1,0:T(8,128)S(1)}, f32[2,256,256]{2,1,0:T(8,128)S(1)}, u32[]{:S(2)}, u32[]{:S(2)}) %collective-permute-start.11) | collective-permute-done | bytes 524320 | tf_op jit(solution)/shard_map/ppermute | solution.py:38
  46.2 6.7 %slot_1.1 = (f32[2,256,256]{2,1,0:T(8,128)S(1)}, f32[2,256,256]{2,1,0:T(8,128)S(1)}) custom-call(s32[2,4]{1,0:T(2,128)S(1)} %bitcast.12, s32[2,4]{1,0:T(2,128)S(1)} %collective-permute-done.refs_1_, s32[2,4]{1,0:T(2,128)S(1)} %collective-permute-done.1.refs_2_, f32[2,256,256]{2,1,0:T(8,128)S(1)} %copy-done, f32[4,256,256]{2,1,0:T(8,128)} %refs_4_.15, ...), custom_call_target="tpu_custom_call" | custom-call | tf_op jit(solution)/shard_map/slot_1/pallas_call | solution.py:260
  52.9 0.7 collective-permute-start.16
  53.6 0.3 collective-permute-start.15
  53.9 6.8 %slot_last.1 = (f32[2,256,256]{2,1,0:T(8,128)S(1)}, f32[2,256,256]{2,1,0:T(8,128)S(1)}) custom-call(s32[2,4]{1,0:T(2,128)S(1)} %bitcast.13, s32[2,4]{1,0:T(2,128)S(1)} %collective-permute-done.refs_1_, s32[2,4]{1,0:T(2,128)S(1)} %collective-permute-done.1.refs_2_, f32[2,256,256]{2,1,0:T(8,128)S(1)} %copy-done, f32[4,256,256]{2,1,0:T(8,128)} %refs_4_.15, ...), custom_call_target="tpu_custom_call" | custom-call | tf_op jit(solution)/shard_map/slot_last/pallas_call | solution.py:260
  60.8 0.1 pack.2
  60.9 6.8 %collective-permute-start.14 = (f32[4,2,256,256]{3,2,1,0:T(8,128)S(1)}, f32[4,2,256,256]{3,2,1,0:T(8,128)S(1)}, u32[]{:S(2)}, u32[]{:S(2)}) collective-permute-start(f32[4,2,256,256]{3,2,1,0:T(8,128)S(1)} %pack.2), channel_id=1, source_target_pairs={{0,1},{1,0},{2,3},{3,2},{4,5},{5,4},{6,7},{7,6},{8,9},{9,8},{10,11... | collective-permute-start | bytes 6291464 | tf_op jit(solution)/shard_map/ppermute | solution.py:38
  67.7 0.7 collective-permute-done.15.refs_1_.refs_12_
  68.4 0.1 pack.3
  68.5 2.8 %collective-permute-start.17 = (f32[3,2,256,256]{3,2,1,0:T(8,128)S(1)}, f32[3,2,256,256]{3,2,1,0:T(8,128)S(1)}, u32[]{:S(2)}, u32[]{:S(2)}) collective-permute-start(f32[3,2,256,256]{3,2,1,0:T(8,128)S(1)} %pack.3), channel_id=1, source_target_pairs={{0,1},{1,0},{2,3},{3,2},{4,5},{5,4},{6,7},{7,6},{8,9},{9,8},{10,11... | collective-permute-start | bytes 4718600 | tf_op jit(solution)/shard_map/ppermute | solution.py:38
  71.3 0.7 collective-permute-start.22
  72.0 3.1 %collective-permute-start.20 = (f32[2,256,256]{2,1,0:T(8,128)S(1)}, f32[2,256,256]{2,1,0:T(8,128)S(1)}, u32[]{:S(2)}, u32[]{:S(2)}) collective-permute-start(f32[2,256,256]{2,1,0:T(8,128)S(1)} %get-tuple-element.63), channel_id=1, source_target_pairs={{12,14},{14,12},{13,15},{15,13},{28,30},{30,28},{29,31},{31,29}} | collective-permute-start | bytes 1572872 | tf_op jit(solution)/shard_map/ppermute | solution.py:53
  75.2 6.9 %early.1 = (f32[2,256,4096]{2,1,0:T(8,128)S(1)}, f32[2,1,256,4096]{3,2,1,0:T(8,128)}) custom-call(s32[2,4]{1,0:T(2,128)S(1)} %bitcast.14, s32[2,4]{1,0:T(2,128)S(1)} %collective-permute-done.refs_1_, s32[2,4]{1,0:T(2,128)S(1)} %collective-permute-done.1.refs_2_, s32[2,4]{1,0:T(2,128)S(1)} %collective-permute-done.2.refs_3_, ...), custom_call_target="tpu_custom_call" | custom-call | tf_op jit(solution)/shard_map/early/pallas_call | solution.py:433
  82.2 5.3 %collective-permute-done.20.refs_9_ = f32[2,256,256]{2,1,0:T(8,128)S(1)} collective-permute-done((f32[2,256,256]{2,1,0:T(8,128)S(1)}, f32[2,256,256]{2,1,0:T(8,128)S(1)}, u32[]{:S(2)}, u32[]{:S(2)}) %collective-permute-start.20) | collective-permute-done | bytes 524320 | tf_op jit(solution)/shard_map/ppermute | solution.py:53
  87.4 0.9 collective-permute-done.18.refs_7_
  88.4 1.1 %collective-permute-start.19 = (f32[2,256,256]{2,1,0:T(8,128)S(1)}, f32[2,256,256]{2,1,0:T(8,128)S(1)}, u32[]{:S(2)}, u32[]{:S(2)}) collective-permute-start(f32[2,256,256]{2,1,0:T(8,128)S(1)} %collective-permute-done.18.refs_7_), channel_id=1, source_target_pairs={{0,1},{1,0},{2,3},{3,2},{4,5},{5,4},{6,7},{7,6},{8,9},{9,8},{10,11... | collective-permute-start | bytes 1572872 | tf_op jit(solution)/shard_map/ppermute | solution.py:38
  89.5 0.5 collective-permute-start.23
  90.0 1.0 %collective-permute-done.19.refs_8_ = f32[2,256,256]{2,1,0:T(8,128)S(1)} collective-permute-done((f32[2,256,256]{2,1,0:T(8,128)S(1)}, f32[2,256,256]{2,1,0:T(8,128)S(1)}, u32[]{:S(2)}, u32[]{:S(2)}) %collective-permute-start.19) | collective-permute-done | bytes 524320 | tf_op jit(solution)/shard_map/ppermute | solution.py:38
  91.0 0.7 collective-permute-done.21.refs_10_
  91.8 0.7 collective-permute-done.23.refs_12_
  92.5 3.3 %late.1 = f32[2,1,256,4096]{3,2,1,0:T(8,128)} custom-call(s32[2,4]{1,0:T(2,128)S(1)} %bitcast.15, s32[2,4]{1,0:T(2,128)S(1)} %collective-permute-done.refs_1_, s32[2,4]{1,0:T(2,128)S(1)} %collective-permute-done.1.refs_2_, s32[2,4]{1,0:T(2,128)S(1)} %collective-permute-done.2.refs_3_, ...), custom_call_target="tpu_custom_call", output_to_operand_aliasing={{}: (13, {})} | custom-call | tf_op jit(solution)/shard_map/late/pallas_call | solution.py:498
  (23 shorter events, 0.2 us)
Async XLA Ops:
  0.0 2.3 %collective-permute-start.1 = (s32[2,4]{1,0:T(2,128)}, s32[2,4]{1,0:T(2,128)S(1)}, u32[]{:S(2)}, u32[]{:S(2)}) collective-permute-start(s32[2,4]{1,0:T(2,128)} %bitcast.1), channel_id=1, source_target_pairs={{4,8},{8,4},{5,9},{9,5},{6,10},{10,6},{7,11},{11,7},{20,24},{24,20... | collective-permute-start | bytes 104 | tf_op jit(solution)/shard_map/ppermute | solution.py:46
  0.7 2.8 %collective-permute-start = (s32[2,4]{1,0:T(2,128)}, s32[2,4]{1,0:T(2,128)S(1)}, u32[]{:S(2)}, u32[]{:S(2)}) collective-permute-start(s32[2,4]{1,0:T(2,128)} %bitcast.2), channel_id=1, source_target_pairs={{0,4},{4,0},{8,12},{12,8},{1,5},{5,1},{9,13},{13,9},{2,6},{6,2},{1... | collective-permute-start | bytes 104 | tf_op jit(solution)/shard_map/ppermute | solution.py:46
  3.5 0.7 copy-start.2
  6.4 13.8 %collective-permute-start.5 = (f32[2,256,256]{2,1,0:T(8,128)S(1)}, f32[2,256,256]{2,1,0:T(8,128)S(1)}, u32[]{:S(2)}, u32[]{:S(2)}) collective-permute-start(f32[2,256,256]{2,1,0:T(8,128)S(1)} %get-tuple-element.37), channel_id=1, source_target_pairs={{0,4},{4,0},{8,12},{12,8},{1,5},{5,1},{9,13},{13,9},{2,6},{6,2},{1... | collective-permute-start | bytes 1572872 | tf_op jit(solution)/shard_map/ppermute | solution.py:46
  9.9 24.9 %collective-permute-start.8 = (f32[3,256,256]{2,1,0:T(8,128)S(1)}, f32[3,256,256]{2,1,0:T(8,128)S(1)}, u32[]{:S(2)}, u32[]{:S(2)}) collective-permute-start(f32[3,256,256]{2,1,0:T(8,128)S(1)} %cut.6), channel_id=1, source_target_pairs={{0,4},{4,0},{8,12},{12,8},{1,5},{5,1},{9,13},{13,9},{2,6},{6,2},{1... | collective-permute-start | bytes 2359304 | tf_op jit(solution)/shard_map/ppermute | solution.py:46
  10.0 12.8 %collective-permute-start.6 = (f32[2,256,256]{2,1,0:T(8,128)S(1)}, f32[2,256,256]{2,1,0:T(8,128)S(1)}, u32[]{:S(2)}, u32[]{:S(2)}) collective-permute-start(f32[2,256,256]{2,1,0:T(8,128)S(1)} %get-tuple-element.46), channel_id=1, source_target_pairs={{12,14},{14,12},{13,15},{15,13},{28,30},{30,28},{29,31},{31,29}} | collective-permute-start | bytes 1572872 | tf_op jit(solution)/shard_map/ppermute | solution.py:53
  13.1 15.4 %collective-permute-start.7 = (f32[2,256,256]{2,1,0:T(8,128)S(1)}, f32[2,256,256]{2,1,0:T(8,128)S(1)}, u32[]{:S(2)}, u32[]{:S(2)}) collective-permute-start(f32[2,256,256]{2,1,0:T(8,128)S(1)} %get-tuple-element.46), channel_id=1, source_target_pairs={{4,8},{8,4},{5,9},{9,5},{6,10},{10,6},{7,11},{11,7},{20,24},{24,20... | collective-permute-start | bytes 1572872 | tf_op jit(solution)/shard_map/ppermute | solution.py:46
  20.2 8.1 %copy-start.1 = (bf16[8,256,256]{2,1,0:T(8,128)(2,1)S(1)}, bf16[8,256,256]{2,1,0:T(8,128)(2,1)}, u32[]{:S(2)}) copy-start(bf16[8,256,256]{2,1,0:T(8,128)(2,1)} %constant.2.clone.pieces) | copy-start | bytes 3145732
  20.2 14.8 %copy-start = (f32[2,256,256]{2,1,0:T(8,128)S(1)}, f32[2,256,256]{2,1,0:T(8,128)}, u32[]{:S(2)}) copy-start(f32[2,256,256]{2,1,0:T(8,128)} %refs_3_.15) | copy-start | bytes 1572868
  20.2 14.8 %copy-start.3 = (s32[4,2]{0,1:T(2,128)S(1)}, s32[4,2]{0,1:T(2,128)}, u32[]{:S(2)}) copy-start(s32[4,2]{0,1:T(2,128)} %param.10) | copy-start | bytes 100
  20.9 14.1 %collective-permute-start.9 = (f32[2,256,256]{2,1,0:T(8,128)S(1)}, f32[2,256,256]{2,1,0:T(8,128)S(1)}, u32[]{:S(2)}, u32[]{:S(2)}) collective-permute-start(f32[2,256,256]{2,1,0:T(8,128)S(1)} %join.2), channel_id=1, source_target_pairs={{0,2},{2,0},{1,3},{3,1},{4,6},{6,4},{5,7},{7,5},{8,10},{10,8},{9,1... | collective-permute-start | bytes 1572872 | tf_op jit(solution)/shard_map/ppermute | solution.py:38
  21.2 22.9 %collective-permute-start.10 = (f32[3,256,256]{2,1,0:T(8,128)S(1)}, f32[3,256,256]{2,1,0:T(8,128)S(1)}, u32[]{:S(2)}, u32[]{:S(2)}) collective-permute-start(f32[3,256,256]{2,1,0:T(8,128)S(1)} %cut.7.refs_5_), channel_id=1, source_target_pairs={{4,8},{8,4},{5,9},{9,5},{6,10},{10,6},{7,11},{11,7},{20,24},{24,20... | collective-permute-start | bytes 2359304 | tf_op jit(solution)/shard_map/ppermute | solution.py:46
  22.8 6.5 %collective-permute-start.2 = (s32[2,4]{1,0:T(2,128)S(1)}, s32[2,4]{1,0:T(2,128)S(1)}, u32[]{:S(2)}, u32[]{:S(2)}) collective-permute-start(s32[2,4]{1,0:T(2,128)S(1)} %bitcast.9), channel_id=1, source_target_pairs={{0,1},{1,0},{2,3},{3,2},{4,5},{5,4},{6,7},{7,6},{8,9},{9,8},{10,11... | collective-permute-start | bytes 104 | tf_op jit(solution)/shard_map/ppermute | solution.py:38
  28.5 1.3 %collective-permute-start.4 = (s32[2,4]{1,0:T(2,128)S(1)}, s32[2,4]{1,0:T(2,128)S(1)}, u32[]{:S(2)}, u32[]{:S(2)}) collective-permute-start(s32[2,4]{1,0:T(2,128)S(1)} %collective-permute-done.1.refs_2_), channel_id=1, source_target_pairs={{0,1},{1,0},{2,3},{3,2},{4,5},{5,4},{6,7},{7,6},{8,9},{9,8},{10,11... | collective-permute-start | bytes 104 | tf_op jit(solution)/shard_map/ppermute | solution.py:38
  29.3 2.7 %collective-permute-start.3 = (s32[2,4]{1,0:T(2,128)S(1)}, s32[2,4]{1,0:T(2,128)S(1)}, u32[]{:S(2)}, u32[]{:S(2)}) collective-permute-start(s32[2,4]{1,0:T(2,128)S(1)} %collective-permute-done.refs_1_), channel_id=1, source_target_pairs={{0,1},{1,0},{2,3},{3,2},{4,5},{5,4},{6,7},{7,6},{8,9},{9,8},{10,11... | collective-permute-start | bytes 104 | tf_op jit(solution)/shard_map/ppermute | solution.py:38
  29.8 16.4 %collective-permute-start.11 = (f32[2,256,256]{2,1,0:T(8,128)S(1)}, f32[2,256,256]{2,1,0:T(8,128)S(1)}, u32[]{:S(2)}, u32[]{:S(2)}) collective-permute-start(f32[2,256,256]{2,1,0:T(8,128)S(1)} %join.3), channel_id=1, source_target_pairs={{0,2},{2,0},{1,3},{3,1},{4,6},{6,4},{5,7},{7,5},{8,10},{10,8},{9,1... | collective-permute-start | bytes 1572872 | tf_op jit(solution)/shard_map/ppermute | solution.py:38
  41.6 19.1 %collective-permute-start.12 = (f32[2,256,256]{2,1,0:T(8,128)S(1)}, f32[2,256,256]{2,1,0:T(8,128)S(1)}, u32[]{:S(2)}, u32[]{:S(2)}) collective-permute-start(f32[2,256,256]{2,1,0:T(8,128)S(1)} %get-tuple-element.58), channel_id=1, source_target_pairs={{0,2},{2,0},{1,3},{3,1},{4,6},{6,4},{5,7},{7,5},{8,10},{10,8},{9,1... | collective-permute-start | bytes 1572872 | tf_op jit(solution)/shard_map/ppermute | solution.py:38
  42.8 18.0 %collective-permute-start.13 = (f32[2,256,256]{2,1,0:T(8,128)S(1)}, f32[2,256,256]{2,1,0:T(8,128)S(1)}, u32[]{:S(2)}, u32[]{:S(2)}) collective-permute-start(f32[2,256,256]{2,1,0:T(8,128)S(1)} %get-tuple-element.53.refs_1_.refs_7_), channel_id=1, source_target_pairs={{0,4},{4,0},{8,12},{12,8},{1,5},{5,1},{9,13},{13,9},{2,6},{6,2},{1... | collective-permute-start | bytes 1572872 | tf_op jit(solution)/shard_map/ppermute | solution.py:46
  52.9 15.5 %collective-permute-start.16 = (f32[2,256,256]{2,1,0:T(8,128)S(1)}, f32[2,256,256]{2,1,0:T(8,128)S(1)}, u32[]{:S(2)}, u32[]{:S(2)}) collective-permute-start(f32[2,256,256]{2,1,0:T(8,128)S(1)} %get-tuple-element.55.refs_0_.refs_11_), channel_id=1, source_target_pairs={{4,8},{8,4},{5,9},{9,5},{6,10},{10,6},{7,11},{11,7},{20,24},{24,20... | collective-permute-start | bytes 1572872 | tf_op jit(solution)/shard_map/ppermute | solution.py:46
  53.6 14.8 %collective-permute-start.15 = (f32[2,256,256]{2,1,0:T(8,128)S(1)}, f32[2,256,256]{2,1,0:T(8,128)S(1)}, u32[]{:S(2)}, u32[]{:S(2)}) collective-permute-start(f32[2,256,256]{2,1,0:T(8,128)S(1)} %get-tuple-element.59), channel_id=1, source_target_pairs={{0,2},{2,0},{1,3},{3,1},{4,6},{6,4},{5,7},{7,5},{8,10},{10,8},{9,1... | collective-permute-start | bytes 1572872 | tf_op jit(solution)/shard_map/ppermute | solution.py:38
  60.9 14.3 %collective-permute-start.14 = (f32[4,2,256,256]{3,2,1,0:T(8,128)S(1)}, f32[4,2,256,256]{3,2,1,0:T(8,128)S(1)}, u32[]{:S(2)}, u32[]{:S(2)}) collective-permute-start(f32[4,2,256,256]{3,2,1,0:T(8,128)S(1)} %pack.2), channel_id=1, source_target_pairs={{0,1},{1,0},{2,3},{3,2},{4,5},{5,4},{6,7},{7,6},{8,9},{9,8},{10,11... | collective-permute-start | bytes 6291464 | tf_op jit(solution)/shard_map/ppermute | solution.py:38
  68.5 6.7 %collective-permute-start.17 = (f32[3,2,256,256]{3,2,1,0:T(8,128)S(1)}, f32[3,2,256,256]{3,2,1,0:T(8,128)S(1)}, u32[]{:S(2)}, u32[]{:S(2)}) collective-permute-start(f32[3,2,256,256]{3,2,1,0:T(8,128)S(1)} %pack.3), channel_id=1, source_target_pairs={{0,1},{1,0},{2,3},{3,2},{4,5},{5,4},{6,7},{7,6},{8,9},{9,8},{10,11... | collective-permute-start | bytes 4718600 | tf_op jit(solution)/shard_map/ppermute | solution.py:38
  71.3 10.8 %collective-permute-start.22 = (f32[2,256,256]{2,1,0:T(8,128)S(1)}, f32[2,256,256]{2,1,0:T(8,128)S(1)}, u32[]{:S(2)}, u32[]{:S(2)}) collective-permute-start(f32[2,256,256]{2,1,0:T(8,128)S(1)} %collective-permute-done.15.refs_1_.refs_12_), channel_id=1, source_target_pairs={{4,8},{8,4},{5,9},{9,5},{6,10},{10,6},{7,11},{11,7},{20,24},{24,20... | collective-permute-start | bytes 1572872 | tf_op jit(solution)/shard_map/ppermute | solution.py:46
  72.0 15.4 %collective-permute-start.20 = (f32[2,256,256]{2,1,0:T(8,128)S(1)}, f32[2,256,256]{2,1,0:T(8,128)S(1)}, u32[]{:S(2)}, u32[]{:S(2)}) collective-permute-start(f32[2,256,256]{2,1,0:T(8,128)S(1)} %get-tuple-element.63), channel_id=1, source_target_pairs={{12,14},{14,12},{13,15},{15,13},{28,30},{30,28},{29,31},{31,29}} | collective-permute-start | bytes 1572872 | tf_op jit(solution)/shard_map/ppermute | solution.py:53
  75.1 13.3 %collective-permute-start.18 = (f32[2,256,256]{2,1,0:T(8,128)S(1)}, f32[2,256,256]{2,1,0:T(8,128)S(1)}, u32[]{:S(2)}, u32[]{:S(2)}) collective-permute-start(f32[2,256,256]{2,1,0:T(8,128)S(1)} %collective-permute-done.12.refs_2_.refs_8_), channel_id=1, source_target_pairs={{0,4},{4,0},{8,12},{12,8},{1,5},{5,1},{9,13},{13,9},{2,6},{6,2},{1... | collective-permute-start | bytes 1572872 | tf_op jit(solution)/shard_map/ppermute | solution.py:46
  88.4 2.7 %collective-permute-start.19 = (f32[2,256,256]{2,1,0:T(8,128)S(1)}, f32[2,256,256]{2,1,0:T(8,128)S(1)}, u32[]{:S(2)}, u32[]{:S(2)}) collective-permute-start(f32[2,256,256]{2,1,0:T(8,128)S(1)} %collective-permute-done.18.refs_7_), channel_id=1, source_target_pairs={{0,1},{1,0},{2,3},{3,2},{4,5},{5,4},{6,7},{7,6},{8,9},{9,8},{10,11... | collective-permute-start | bytes 1572872 | tf_op jit(solution)/shard_map/ppermute | solution.py:38
  89.5 2.3 %collective-permute-start.21 = (f32[2,256,256]{2,1,0:T(8,128)S(1)}, f32[2,256,256]{2,1,0:T(8,128)S(1)}, u32[]{:S(2)}, u32[]{:S(2)}) collective-permute-start(f32[2,256,256]{2,1,0:T(8,128)S(1)} %collective-permute-done.20.refs_9_), channel_id=1, source_target_pairs={{0,1},{1,0},{2,3},{3,2},{4,5},{5,4},{6,7},{7,6},{8,9},{9,8},{10,11... | collective-permute-start | bytes 1572872 | tf_op jit(solution)/shard_map/ppermute | solution.py:38
  89.5 3.0 %collective-permute-start.23 = (f32[2,256,256]{2,1,0:T(8,128)S(1)}, f32[2,256,256]{2,1,0:T(8,128)S(1)}, u32[]{:S(2)}, u32[]{:S(2)}) collective-permute-start(f32[2,256,256]{2,1,0:T(8,128)S(1)} %collective-permute-done.22.refs_11_), channel_id=1, source_target_pairs={{0,1},{1,0},{2,3},{3,2},{4,5},{5,4},{6,7},{7,6},{8,9},{9,8},{10,11... | collective-permute-start | bytes 1572872 | tf_op jit(solution)/shard_map/ppermute | solution.py:38
